TPU v7x, 32 devices: a whole 2x2x4 slice. The times are simulated.
32 devices in a mesh: wide: 16 (over z, y, core), narrow: 2 (over x).
Axes of the slice: x: 2, y: 2, z: 4, core: 2. Of those that a mesh axis runs over, the one named last changes fastest.
Arguments:
- tokens: bfloat16 [16384, 1152], P(('wide', 'narrow')), may hold values from -6 to 6
- condition: bfloat16 [256, 1152], replicated, may hold values from -6 to 6
- cotangent: bfloat16 [16384, 1152], P('wide'), may hold values from -6 to 6
- modulator: bfloat16 [1152, 6, 1152], P(None, None, 'narrow'), may hold values from -0.1875 to 0.1875
- modulator_bias: bfloat16 [6, 1152], P(None, 'narrow'), may hold values from -2 to 2
- qkv_weight: bfloat16 [1152, 3, 1152], P(None, None, 'narrow'), may hold values from -0.1875 to 0.1875
- qv_bias: bfloat16 [2, 1152], P(None, 'narrow'), may hold values from -2 to 2
- out_weight: bfloat16 [1152, 1152], P('narrow'), may hold values from -1.5 to 1.5
- out_bias: bfloat16 [1152], replicated, may hold values from -2 to 2
- up_weight: bfloat16 [1152, 4608], P(None, 'narrow'), may hold values from -0.1875 to 0.1875
- up_bias: bfloat16 [4608], P('narrow'), may hold values from -2 to 2
- down_weight: bfloat16 [4608, 1152], P('narrow'), may hold values from -0.09375 to 0.09375
- down_bias: bfloat16 [1152], replicated, may hold values from -2 to 2
- segment_ids: int32 [16384], replicated, may hold values from 0 to 255, as said below
- valid_counts: int32 [16], replicated, may hold values from 640 to 1024, as said below
Outputs:
- layer_out: bfloat16 [16384, 1152], P(('wide', 'narrow'))
- tokens_grad: float32 [16384, 1152], P(('wide', 'narrow'))
- condition_grad: float32 [256, 1152], replicated
- modulator_grad: float32 [1152, 6, 1152], P(None, None, 'narrow')
- modulator_bias_grad: float32 [6, 1152], P(None, 'narrow')
- qkv_weight_grad: float32 [1152, 3, 1152], P(None, None, 'narrow')
- qv_bias_grad: float32 [2, 1152], P(None, 'narrow')
- out_weight_grad: float32 [1152, 1152], P('narrow')
- out_bias_grad: float32 [1152], replicated
- up_weight_grad: float32 [1152, 4608], P(None, 'narrow')
- up_bias_grad: float32 [4608], P('narrow')
- down_weight_grad: float32 [4608, 1152], P('narrow')
- down_bias_grad: float32 [1152], replicated
Inputs may be any that keep to these rules, and one draw needn't show every extreme that they name: `segment_ids`: over the valid slots of the packed stream, in order, ids never fall and each id covers at most 128 slots; some id covers exactly 128, and the last valid slot carries 256 - 1. A padding slot carries the id of its shard's last valid slot. `valid_counts`: the valid slots of a shard come first in it; one shard is full.
All inputs are finite; a program needn't handle non-finite values.
Results may differ from a plain program's by a relative error of at most 0.02.
Values may be sent and summed in bfloat16 or wider, within the bound.
A program may use at most 256 MiB of HBM per device.

v0:
```python
from functools import partial

import jax
import jax.numpy as jnp
from jax import lax
from jax.sharding import PartitionSpec as P

HD = 72
IMG_MAX = 128


EPSILON = 1e-06
NEG_FILL = -1e30
FULL_PRECISION = lax.Precision.HIGHEST


def padded(cells, sides, width):
    for axis, dim in sides:
        count = lax.axis_size(axis)
        ends = count - 1
        head = lax.slice_in_dim(cells, 0, width, axis=dim)
        tail = lax.slice_in_dim(cells, cells.shape[dim] - width, cells.shape[dim], axis=dim)
        cells = jnp.concatenate(
            [
                lax.ppermute(tail, axis, [(i, (i + 1) % count) for i in range(ends)]),
                cells,
                lax.ppermute(head, axis, [((i + 1) % count, i) for i in range(ends)]),
            ],
            axis=dim,
        )
    return cells


def norm_modulate(field, shift, scale):
    centred = field - jnp.mean(field, axis=-1, keepdims=True)
    variance = jnp.mean(centred * centred, axis=-1, keepdims=True)
    return centred * lax.rsqrt(variance + EPSILON) * (1.0 + scale) + shift


def sum_mlp_grads(up_grad, up_bias_grad, down_grad, down_bias_grad):
    return (
        lax.psum(up_grad.astype(jnp.bfloat16), "wide").astype(jnp.float32),
        lax.psum(up_bias_grad.astype(jnp.bfloat16), "wide").astype(jnp.float32),
        lax.psum(down_grad.astype(jnp.bfloat16), "wide").astype(jnp.float32),
        lax.psum(down_bias_grad.astype(jnp.bfloat16), "wide").astype(jnp.float32),
    )


def body(
    tokens,
    condition,
    cotangent,
    modulator,
    modulator_bias,
    qkv_weight,
    qv_bias,
    out_weight,
    out_bias,
    up_weight,
    up_bias,
    down_weight,
    down_bias,
    segment_ids,
    valid_counts,
):
    wide_count = lax.axis_size("wide")
    wide_index = lax.axis_index("wide")
    narrow_index = lax.axis_index("narrow")
    tok_dev = cotangent.shape[0]
    share = tokens.shape[0]
    width = tokens.shape[1]
    part_width = qkv_weight.shape[2]
    heads = part_width // HD
    img_row = condition.shape[0]
    span = IMG_MAX
    block = min(512, tok_dev)
    window = block + 2 * span
    scale_factor = HD ** (-0.5)
    own_count = valid_counts[wide_index]
    positions = jnp.arange(tok_dev, dtype=jnp.int32)
    own_ids = lax.dynamic_slice_in_dim(segment_ids, wide_index * tok_dev, tok_dev)
    live_full = (positions < own_count).astype(jnp.float32)
    share_start = narrow_index * share
    live_share = lax.dynamic_slice_in_dim(live_full, share_start, share)[:, None]
    image_slots = jnp.arange(img_row, dtype=jnp.int32)
    onehot_full = (own_ids[:, None] == image_slots[None, :]).astype(jnp.float32)
    onehot_share = lax.dynamic_slice_in_dim(onehot_full, share_start, share)
    cond_rows = condition.astype(jnp.float32)
    activated = jax.nn.silu(cond_rows).astype(jnp.bfloat16)
    mod_part = jnp.dot(activated, modulator.reshape(width, -1), preferred_element_type=jnp.float32)
    mod_part = mod_part.reshape(img_row, 6, -1) + modulator_bias.astype(jnp.float32)[None]
    mod_rows = lax.all_gather(mod_part, "narrow", axis=2, tiled=True)
    token_mod = jnp.dot(onehot_share, mod_rows.reshape(img_row, -1), precision=FULL_PRECISION)
    token_mod = token_mod.reshape(share, 6, width)
    shift_one = token_mod[:, 0]
    scale_one = token_mod[:, 1]
    gate_one = token_mod[:, 2]
    shift_two = token_mod[:, 3]
    scale_two = token_mod[:, 4]
    gate_two = token_mod[:, 5]
    tokens_share = tokens.astype(jnp.float32)
    normed_one, norm_one_back = jax.vjp(norm_modulate, tokens_share, shift_one, scale_one)
    gathered_one = lax.all_gather(normed_one.astype(jnp.bfloat16), "narrow", axis=0, tiled=True)
    projected = jnp.dot(
        gathered_one, qkv_weight.reshape(width, -1), preferred_element_type=jnp.float32
    )
    bias_pair = qv_bias.astype(jnp.float32)
    queries = (projected[:, :part_width] + bias_pair[0]).astype(jnp.bfloat16)
    key_rows = projected[:, part_width : 2 * part_width].astype(jnp.bfloat16)
    value_rows = (projected[:, 2 * part_width :] + bias_pair[1]).astype(jnp.bfloat16)
    key_value = jnp.concatenate([key_rows, value_rows], axis=1)
    tail_start = own_count - span
    edge_rows = jnp.concatenate(
        [key_value[:span], lax.dynamic_slice_in_dim(key_value, tail_start, span)], axis=0
    )
    rimmed = padded(edge_rows, (("wide", 0),), span)
    extended = jnp.concatenate([rimmed[:span], key_value, rimmed[3 * span :]], axis=0)
    left_index = jnp.maximum(wide_index - 1, 0)
    right_index = jnp.minimum(wide_index + 1, wide_count - 1)
    left_count = valid_counts[left_index]
    left_ids = lax.dynamic_slice_in_dim(segment_ids, left_index * tok_dev + left_count - span, span)
    left_ids = jnp.where(wide_index > 0, left_ids, -2)
    right_ids = lax.dynamic_slice_in_dim(segment_ids, right_index * tok_dev, span)
    right_ids = jnp.where(wide_index < wide_count - 1, right_ids, -2)
    own_keys = jnp.where(positions < own_count, own_ids, -1)
    extended_ids = jnp.concatenate([left_ids, own_keys, right_ids])

    def block_parts(block_idx):
        row_start = block_idx * block
        query_block = queries[row_start : row_start + block].reshape(block, heads, HD)
        pair_block = extended[row_start : row_start + window]
        key_block = pair_block[:, :part_width].reshape(window, heads, HD)
        value_block = pair_block[:, part_width:].reshape(window, heads, HD)
        same_seg = (
            own_keys[row_start : row_start + block, None]
            == extended_ids[None, row_start : row_start + window]
        )
        return (query_block, key_block, value_block, same_seg)

    def masked_scores(query_block, key_block, same_seg):
        raw = (
            jnp.einsum("ihd,jhd->hij", query_block, key_block, preferred_element_type=jnp.float32)
            * scale_factor
        )
        return jnp.where(same_seg[None], raw, NEG_FILL)

    blocks = tok_dev // block
    outputs = []
    log_sums = []
    for block_idx in range(blocks):
        query_block, key_block, value_block, same_seg = block_parts(block_idx)
        masked = masked_scores(query_block, key_block, same_seg)
        top_score = jnp.max(masked, axis=-1, keepdims=True)
        expo = jnp.exp(masked - top_score)
        totals = jnp.sum(expo, axis=-1, keepdims=True)
        attend = expo / totals
        log_sums.append(top_score + jnp.log(totals))
        block_out = jnp.einsum(
            "hij,jhd->ihd",
            attend.astype(jnp.bfloat16),
            value_block,
            preferred_element_type=jnp.float32,
        )
        outputs.append(block_out.reshape(block, part_width))
    context = jnp.concatenate(outputs, axis=0).astype(jnp.bfloat16)
    attn_share = lax.psum_scatter(
        jnp.dot(context, out_weight, preferred_element_type=jnp.float32).astype(jnp.bfloat16),
        "narrow",
        scatter_dimension=0,
        tiled=True,
    ).astype(jnp.float32) + out_bias.astype(jnp.float32)
    middle = tokens_share + live_share * gate_one * attn_share
    normed_two, norm_two_back = jax.vjp(norm_modulate, middle, shift_two, scale_two)
    gathered_two = lax.all_gather(normed_two.astype(jnp.bfloat16), "narrow", axis=0, tiled=True)
    upper = jnp.dot(gathered_two, up_weight, preferred_element_type=jnp.float32) + up_bias.astype(
        jnp.float32
    )
    activated_up, gelu_back = jax.vjp(partial(jax.nn.gelu, approximate=True), upper)
    hidden = activated_up.astype(jnp.bfloat16)
    branch_share = lax.psum_scatter(
        jnp.dot(
            lax.slice_in_dim(hidden, 0, share * lax.axis_size("narrow"), axis=0),
            down_weight,
            preferred_element_type=jnp.float32,
        ).astype(jnp.bfloat16),
        "narrow",
        scatter_dimension=0,
        tiled=True,
    ).astype(jnp.float32) + down_bias.astype(jnp.float32)
    layer_out = (middle + live_share * gate_two * branch_share).astype(jnp.bfloat16)
    upstream = cotangent.astype(jnp.float32)
    gate_two_full = jnp.dot(onehot_full, mod_rows[:, 5, :], precision=FULL_PRECISION)
    d_branch = (live_full[:, None] * gate_two_full * upstream).astype(jnp.bfloat16)
    down_grad = jnp.einsum("tf,td->fd", hidden, d_branch, preferred_element_type=jnp.float32)
    down_bias_grad = jnp.sum(d_branch.astype(jnp.float32), axis=0)
    d_hidden = jnp.einsum("td,fd->tf", d_branch, down_weight, preferred_element_type=jnp.float32)
    d_upper = gelu_back(d_hidden)[0].astype(jnp.bfloat16)
    up_grad = jnp.einsum("td,tf->df", gathered_two, d_upper, preferred_element_type=jnp.float32)
    up_bias_grad = jnp.sum(d_upper.astype(jnp.float32), axis=0)
    d_norm_two = lax.psum_scatter(
        jnp.einsum("tf,df->td", d_upper, up_weight, preferred_element_type=jnp.float32).astype(
            jnp.bfloat16
        ),
        "narrow",
        scatter_dimension=0,
        tiled=True,
    ).astype(jnp.float32)
    upstream_share = lax.dynamic_slice_in_dim(upstream, share_start, share)
    d_gate_two = live_share * upstream_share * branch_share
    d_middle_extra, d_shift_two, d_scale_two = norm_two_back(d_norm_two)
    d_middle = upstream_share + d_middle_extra
    d_gate_one = live_share * d_middle * attn_share
    d_attn_share = (live_share * gate_one * d_middle).astype(jnp.bfloat16)
    d_attn = lax.all_gather(d_attn_share, "narrow", axis=0, tiled=True)
    out_weight_grad = jnp.einsum("tc,td->cd", context, d_attn, preferred_element_type=jnp.float32)
    out_bias_grad = jnp.sum(d_attn.astype(jnp.float32), axis=0)
    d_context = jnp.einsum(
        "td,cd->tc", d_attn, out_weight, preferred_element_type=jnp.float32
    ).astype(jnp.bfloat16)
    d_extended = jnp.zeros((tok_dev + 2 * span, 2 * part_width), jnp.float32)
    query_grads = []
    for block_idx in range(blocks):
        query_block, key_block, value_block, same_seg = block_parts(block_idx)
        attend = jnp.exp(masked_scores(query_block, key_block, same_seg) - log_sums[block_idx])
        row_start = block_idx * block
        grad_block = d_context[row_start : row_start + block].reshape(block, heads, HD)
        d_attend = jnp.einsum(
            "ihd,jhd->hij", grad_block, value_block, preferred_element_type=jnp.float32
        )
        centre = jnp.sum(attend * d_attend, axis=-1, keepdims=True)
        d_scores = (attend * (d_attend - centre)).astype(jnp.bfloat16)
        query_grad = (
            jnp.einsum("hij,jhd->ihd", d_scores, key_block, preferred_element_type=jnp.float32)
            * scale_factor
        )
        query_grads.append(query_grad.reshape(block, part_width))
        key_grad = (
            jnp.einsum("hij,ihd->jhd", d_scores, query_block, preferred_element_type=jnp.float32)
            * scale_factor
        )
        value_grad = jnp.einsum(
            "hij,ihd->jhd",
            attend.astype(jnp.bfloat16),
            grad_block,
            preferred_element_type=jnp.float32,
        )
        pair_grad = jnp.concatenate(
            [key_grad.reshape(window, part_width), value_grad.reshape(window, part_width)], axis=1
        )
        d_extended = d_extended.at[row_start : row_start + window].add(pair_grad)
    back_edges = jnp.concatenate([d_extended[:span], d_extended[span + tok_dev :]], axis=0)
    returned = padded(back_edges.astype(jnp.bfloat16), (("wide", 0),), span).astype(
        back_edges.dtype
    )
    d_local = d_extended[span : span + tok_dev]
    d_local = d_local.at[:span].add(returned[:span])
    tail_sum = lax.dynamic_slice_in_dim(d_local, tail_start, span) + returned[3 * span :]
    d_local = lax.dynamic_update_slice_in_dim(d_local, tail_sum, tail_start, 0)
    d_queries = jnp.concatenate(query_grads, axis=0).astype(jnp.bfloat16)
    d_pairs = d_local.astype(jnp.bfloat16)
    d_projected = jnp.concatenate([d_queries, d_pairs], axis=1)
    qkv_weight_grad = jnp.einsum(
        "td,tc->dc", gathered_one, d_projected, preferred_element_type=jnp.float32
    ).reshape(width, 3, part_width)
    qv_bias_grad = jnp.stack(
        [
            jnp.sum(d_queries.astype(jnp.float32), axis=0),
            jnp.sum(d_pairs[:, part_width:].astype(jnp.float32), axis=0),
        ]
    )
    flat_qkv = qkv_weight.reshape(width, -1)
    d_norm_one = lax.psum_scatter(
        jnp.einsum("tc,dc->td", d_projected, flat_qkv, preferred_element_type=jnp.float32).astype(
            jnp.bfloat16
        ),
        "narrow",
        scatter_dimension=0,
        tiled=True,
    ).astype(jnp.float32)
    d_tokens_extra, d_shift_one, d_scale_one = norm_one_back(d_norm_one)
    tokens_grad = d_middle + d_tokens_extra
    token_terms = jnp.stack(
        [d_shift_one, d_scale_one, d_gate_one, d_shift_two, d_scale_two, d_gate_two], axis=1
    )
    image_terms = jnp.einsum(
        "ti,tk->ik", onehot_share, token_terms.reshape(share, -1), precision=FULL_PRECISION
    )
    image_terms = image_terms.reshape(img_row, 6, width)
    mod_share_grad = lax.psum_scatter(
        image_terms.astype(jnp.bfloat16), "narrow", scatter_dimension=2, tiled=True
    ).astype(jnp.float32)
    modulator_grad = jnp.einsum(
        "md,mjf->djf", activated.astype(jnp.float32), mod_share_grad, precision=FULL_PRECISION
    )
    modulator_bias_grad = jnp.sum(mod_share_grad, axis=0)
    d_activated = jnp.einsum(
        "mjf,djf->md", mod_share_grad, modulator.astype(jnp.float32), precision=FULL_PRECISION
    )
    sigmoid_rows = jax.nn.sigmoid(cond_rows)
    cond_full = d_activated * sigmoid_rows * (1.0 + cond_rows * (1.0 - sigmoid_rows))
    mlp_summed = sum_mlp_grads(up_grad, up_bias_grad, down_grad, down_bias_grad)
    summed = (
        lax.psum(modulator_grad.astype(jnp.bfloat16), "wide").astype(jnp.float32),
        lax.psum(modulator_bias_grad.astype(jnp.bfloat16), "wide").astype(jnp.float32),
        lax.psum(qkv_weight_grad.astype(jnp.bfloat16), "wide").astype(jnp.float32),
        lax.psum(qv_bias_grad.astype(jnp.bfloat16), "wide").astype(jnp.float32),
        lax.psum(out_weight_grad.astype(jnp.bfloat16), "wide").astype(jnp.float32),
        lax.psum(out_bias_grad.astype(jnp.bfloat16), "wide").astype(jnp.float32),
    )
    condition_grad = lax.psum(cond_full, ("wide", "narrow"))
    return (
        layer_out,
        tokens_grad,
        condition_grad,
        summed[0],
        summed[1],
        summed[2],
        summed[3],
        summed[4],
        summed[5],
        mlp_summed[0],
        mlp_summed[1],
        mlp_summed[2],
        mlp_summed[3],
    )


def solution(mesh):
    in_specs = (
        P(("wide", "narrow"), None),
        P(),
        P("wide", None),
        P(None, None, "narrow"),
        P(None, "narrow"),
        P(None, None, "narrow"),
        P(None, "narrow"),
        P("narrow", None),
        P(),
        P(None, "narrow"),
        P("narrow"),
        P("narrow", None),
        P(),
        P(),
        P(),
    )
    out_specs = (
        P(("wide", "narrow"), None),
        P(("wide", "narrow"), None),
        P(),
        P(None, None, "narrow"),
        P(None, "narrow"),
        P(None, None, "narrow"),
        P(None, "narrow"),
        P("narrow", None),
        P(),
        P(None, "narrow"),
        P("narrow"),
        P("narrow", None),
        P(),
    )
    return jax.shard_map(body, mesh=mesh, in_specs=in_specs, out_specs=out_specs, check_vma=False)
```

profile of v0, /device:TPU:0, one launch (start us, length us, event | category | flops | bytes accessed | tf_op | source)
XLA Modules:
  0.0 1224.6 jit_solution(5855689948880088507)
XLA Ops:
  8.0 7.8 fusion.58
  20.0 88.0 %all-gather.5.cloned.1.call-done = f32[256,6,1152]{0,2,1:T(8,128)} async-done(((f32[256,6,576]{0,2,1:T(8,128)}), f32[256,6,1152]{0,2,1:T(8,128)}) %all-gather.5.cloned.1.call-update) | async-done | bytes 7077904 | tf_op jit(solution)/shard_map/all_gather | solution.py:92
  108.0 8.4 fusion.15
  126.3 33.3 %all-gather.7.cloned.1.call-done = bf16[1024,1152]{1,0:T(8,128)(2,1)} async-done(((bf16[512,1152]{1,0:T(8,128)(2,1)}), bf16[1024,1152]{1,0:T(8,128)(2,1)}) %all-gather.7.cloned.1.call-update) | async-done | bytes 2359312 | tf_op jit(solution)/shard_map/all_gather | solution.py:103
  209.9 38.8 %reduce-scatter.6.cloned.1.call-done = bf16[512,1152]{1,0:T(8,128)(2,1)} async-done(((bf16[1024,1152]{1,0:T(8,128)(2,1)}), bf16[512,1152]{1,0:T(8,128)(2,1)}) %reduce-scatter.6.cloned.1.call-update) | async-done | bytes 1179664 | tf_op jit(solution)/shard_map/reduce_scatter | solution.py:166
  263.6 29.3 %all-gather.9.cloned.1.call-done = bf16[1024,1152]{1,0:T(8,128)(2,1)} async-done(((bf16[512,1152]{1,0:T(8,128)(2,1)}), bf16[1024,1152]{1,0:T(8,128)(2,1)}) %all-gather.9.cloned.1.call-update) | async-done | bytes 2359312 | tf_op jit(solution)/shard_map/all_gather | solution.py:174
  293.0 11.6 fusion.104
  304.6 14.8 %fusion.91 = (bf16[2304]{0:T(1024)(128)(2,1)}, bf16[1024,2304]{1,0:T(8,128)(2,1)S(1)}) fusion(f32[1024,2304]{1,0:T(8,128)} %fusion.104, f32[2304]{0:T(1024)S(1)} %convert_element_type.200, bf16[1024,1152]{1,0:T(8,128)(2,1)S(1)} %copy-done.61, bf16[2304,1152]{1,0:T(8,128)(2,1)} %param.32), kind=kOutput, calls=%fused_computation.193 | convolution fusion | flops 5487720448 | bytes 21837312 | tf_op jit(solution)/shard_map/td,fd->tf/dot_general | solution.py:196
  329.1 13.4 %convolution_convert_fusion.5 = bf16[1024,1152]{1,0:T(8,128)(2,1)} fusion(bf16[2304,1152]{1,0:T(8,128)(2,1)} %param.32, f32[1024,2304]{1,0:T(8,128)} %fusion.104, f32[2304]{0:T(1024)S(1)} %convert_element_type.200), kind=kOutput, calls=%fused_computation.48 | convolution fusion | flops 5460590592 | bytes 17114112 | tf_op jit(solution)/shard_map/dot_general | solution.py:181
  346.8 17.2 %reduce-scatter.10.cloned.1.call-done = bf16[512,1152]{1,0:T(8,128)(2,1)} async-done(((bf16[1024,1152]{1,0:T(8,128)(2,1)}), bf16[512,1152]{1,0:T(8,128)(2,1)}) %reduce-scatter.10.cloned.1.call-update) | async-done | bytes 1179664 | tf_op jit(solution)/shard_map/reduce_scatter | solution.py:200
  367.4 33.6 %reduce-scatter.8.cloned.1.call-done = bf16[512,1152]{1,0:T(8,128)(2,1)} async-done(((bf16[1024,1152]{1,0:T(8,128)(2,1)}), bf16[512,1152]{1,0:T(8,128)(2,1)}) %reduce-scatter.8.cloned.1.call-update) | async-done | bytes 1179664 | tf_op jit(solution)/shard_map/reduce_scatter | solution.py:180
  410.6 36.1 %all-gather.11.cloned.1.call-done = bf16[1024,1152]{1,0:T(8,128)(2,1)} async-done(((bf16[512,1152]{1,0:T(8,128)(2,1)}), bf16[1024,1152]{1,0:T(8,128)(2,1)}) %all-gather.11.cloned.1.call-update) | async-done | bytes 2359312 | tf_op jit(solution)/shard_map/all_gather | solution.py:214
  516.6 9.7 convolution_convert_fusion.6
  526.4 38.5 %reduce-scatter.12.cloned.1.call-done = bf16[512,1152]{1,0:T(8,128)(2,1)} async-done(((bf16[1024,1152]{1,0:T(8,128)(2,1)}), bf16[512,1152]{1,0:T(8,128)(2,1)}) %reduce-scatter.12.cloned.1.call-update) | async-done | bytes 1179664 | tf_op jit(solution)/shard_map/reduce_scatter | solution.py:272
  580.3 15.2 %copy.28 = f32[512,6,1152]{0,2,1:T(8,128)} copy(f32[512,6,1152]{2,0,1:T(8,128)} %bitcast_dynamic-update-slice_fusion) | data formatting | bytes 28311552 | tf_op jit(solution)/shard_map/stack | solution.py:282
  595.5 11.2 fusion.26
  607.0 10.6 convolution_convert_fusion.2
  617.6 12.1 convolution_convert_fusion.1
  632.5 10.4 convolution_convert_fusion.3
  642.9 11.7 reduce-scatter.14.cloned.1.call-done
  684.3 64.9 %all-reduce.1 = (bf16[6,576]{1,0:T(8,128)(2,1)S(1)}, bf16[2,576]{1,0:T(2,128)(2,1)S(1)}, bf16[1152]{0:T(1024)(128)(2,1)S(1)}, bf16[2304]{0:T(1024)(128)(2,1)S(1)}, bf16[1152]{0:T(1024)(128)(2,1)S(1)}) all-reduce(bf16[6,576]{1,0:T(8,128)(2,1)S(1)} %reduce_sum.202, ...), channel_id=1, replica_groups=mesh['wide'=16,'narrow'=2] {'wide'}, use_global_device_ids=true, to_apply=%region_22.23 | all-reduce | flops 9216 | bytes 36864 | tf_op jit(solution)/shard_map/psum | solution.py:304
  752.2 325.5 %all-reduce.8.cloned.1.call-done = (bf16[1152,6,576]{0,2,1:T(8,128)(2,1)}, bf16[1152,3,576]{0,2,1:T(8,128)(2,1)}, bf16[576,1152]{1,0:T(8,128)(2,1)}, bf16[1152,2304]{1,0:T(8,128)(2,1)}, bf16[2304,1152]{1,0:T(8,128)(2,1)}) async-done(((bf16[1152,6,576]{0,2,1:T(8,128)(2,1)}, bf16[1152,3,576]{0,2,1:T(8,128)(2,1)}, bf16[576,1152]{1,0:T(8,128)(2,1)}, bf16[1152,2304]{1,0:T(8,128)(2,1)}, ...) | async-done | bytes 23887888 | tf_op jit(solution)/shard_map/psum | solution.py:303
  1080.9 10.3 convert_element_type.223
  1107.0 108.5 %all-reduce.6.cloned.1.call-done = f32[256,1152]{1,0:T(8,128)} async-done(((f32[256,1152]{1,0:T(8,128)}), f32[256,1152]{1,0:T(8,128)}) %all-reduce.6.cloned.1.call-update) | async-done | bytes 1179664 | tf_op jit(solution)/shard_map/psum | solution.py:310
  (287 shorter events, 246.6 us)
Async XLA Ops:
  7.2 198.3 %copy-start = (bf16[576,1152]{1,0:T(8,128)(2,1)S(1)}, bf16[576,1152]{1,0:T(8,128)(2,1)}, u32[]{:S(2)}) copy-start(bf16[576,1152]{1,0:T(8,128)(2,1)} %param.28) | copy-start | bytes 3981316
  7.2 100.8 %all-gather.5.cloned.1.call-start = ((), (), s32[]{:S(2)}) async-start(), calls=%async_computation.5 | async-start | bytes 10616832 | tf_op jit(solution)/shard_map/all_gather | solution.py:92
  15.9 143.7 %all-gather.7.cloned.1.call-start = ((), (), s32[]{:S(2)}) async-start(), calls=%async_computation.6 | async-start | bytes 3538944 | tf_op jit(solution)/shard_map/all_gather | solution.py:103
  18.7 97.7 %copy-start.40 = (f32[512]{0:T(512)}, f32[512]{0:T(512)S(1)}, u32[]{:S(2)}) copy-start(f32[512]{0:T(512)S(1)} %broadcast_multiply_fusion.1) | copy-start | bytes 6148
  19.8 96.7 %copy-start.42 = (f32[512]{0:T(512)}, f32[512]{0:T(512)S(1)}, u32[]{:S(2)}) copy-start(f32[512]{0:T(512)S(1)} %fusion.83) | copy-start | bytes 6148
  20.0 96.5 %copy-start.33 = (pred[1024,256]{1,0:T(32,128)(4,1)}, pred[1024,256]{1,0:T(32,128)(4,1)S(1)}, u32[]{:S(2)}) copy-start(pred[1024,256]{1,0:T(32,128)(4,1)S(1)} %iota_compare_fusion.1) | copy-start | bytes 786436
  123.4 125.3 %reduce-scatter.6.cloned.1.call-start = ((), (), s32[]{:S(2)}) async-start(), calls=%async_computation.7 | async-start | bytes 3538944 | tf_op jit(solution)/shard_map/reduce_scatter | solution.py:166
  168.0 4.4 collective-permute-start
  169.6 4.9 collective-permute-start.1
  209.1 83.9 %all-gather.9.cloned.1.call-start = ((), (), s32[]{:S(2)}) async-start(), calls=%async_computation.8 | async-start | bytes 3538944 | tf_op jit(solution)/shard_map/all_gather | solution.py:174
  209.9 41.4 %copy-start.38 = (f32[1152]{0:T(1024)}, f32[1152]{0:T(1024)S(1)}, u32[]{:S(2)}) copy-start(f32[1152]{0:T(1024)S(1)} %convert_element_type.198) | copy-start | bytes 13828
  256.8 107.3 %reduce-scatter.10.cloned.1.call-start = ((), (), s32[]{:S(2)}) async-start(), calls=%async_computation.10 | async-start | bytes 3538944 | tf_op jit(solution)/shard_map/reduce_scatter | solution.py:200
  329.1 71.9 %reduce-scatter.8.cloned.1.call-start = ((), (), s32[]{:S(2)}) async-start(), calls=%async_computation.9 | async-start | bytes 3538944 | tf_op jit(solution)/shard_map/reduce_scatter | solution.py:180
  342.6 104.2 %all-gather.11.cloned.1.call-start = ((), (), s32[]{:S(2)}) async-start(), calls=%async_computation.11 | async-start | bytes 3538944 | tf_op jit(solution)/shard_map/all_gather | solution.py:214
  410.6 154.4 %reduce-scatter.12.cloned.1.call-start = ((), (), s32[]{:S(2)}) async-start(), calls=%async_computation.12 | async-start | bytes 3538944 | tf_op jit(solution)/shard_map/reduce_scatter | solution.py:272
  497.3 7.4 collective-permute-start.3
  498.6 6.1 collective-permute-start.2
  526.3 41.5 %copy-start.9 = (bf16[512,1152]{1,0:T(8,128)(2,1)S(1)}, bf16[512,1152]{1,0:T(8,128)(2,1)}, u32[]{:S(2)}) copy-start(bf16[512,1152]{1,0:T(8,128)(2,1)} %param.21) | copy-start | bytes 3538948
  526.3 41.5 %copy-start.41 = (f32[512]{0:T(512)S(1)}, f32[512]{0:T(512)}, u32[]{:S(2)}) copy-start(f32[512]{0:T(512)} %copy-done.40) | copy-start | bytes 6148
  526.4 41.5 %copy-start.43 = (f32[512]{0:T(512)S(1)}, f32[512]{0:T(512)}, u32[]{:S(2)}) copy-start(f32[512]{0:T(512)} %copy-done.42) | copy-start | bytes 6148
  526.4 128.2 %reduce-scatter.14.cloned.1.call-start = ((), (), s32[]{:S(2)}) async-start(), calls=%async_computation.13 | async-start | bytes 5308416 | tf_op jit(solution)/shard_map/reduce_scatter | solution.py:289
  606.7 471.0 %all-reduce.8.cloned.1.call-start = ((), (), s32[]{:S(2)}) async-start(), calls=%async_computation.15 | async-start | bytes 47775744 | tf_op jit(solution)/shard_map/psum | solution.py:303
  661.9 553.6 %all-reduce.6.cloned.1.call-start = ((), (), s32[]{:S(2)}) async-start(), calls=%async_computation.14 | async-start | bytes 2359296 | tf_op jit(solution)/shard_map/psum | solution.py:310
  1102.2 115.7 %copy-start.1 = (bf16[576,1152]{1,0:T(8,128)(2,1)S(1)}, bf16[576,1152]{1,0:T(8,128)(2,1)}, u32[]{:S(2)}) copy-start(bf16[576,1152]{1,0:T(8,128)(2,1)} %param.28) | copy-start | bytes 3981316
  (67 other events, 491.2 us)
Sparse Core Ops, SparseCore 0:
  16.0 91.9 all-gather.4
  123.5 36.0 all-gather.6
  209.2 39.4 reduce-scatter.5
  256.9 36.0 all-gather.8
  329.2 34.7 reduce-scatter.9
  366.1 34.7 reduce-scatter.7
  410.7 36.0 all-gather.10
  526.5 38.4 reduce-scatter.11
  606.8 47.7 reduce-scatter.13
  662.0 415.7 all-reduce.7
  1083.7 131.7 all-reduce.5
where the time goes:
time: 1230 us; the launch traced here: 1220 us
  waiting for transfers between devices  763 us (62%)
  matrix products  203 us (17%)
  other arithmetic  124 us (10%)
  blocking collectives  64.9 us (5%)
  local copies, waits for them, and re-layouts  44.8 us (4%)
  between operations  16.9 us (1%)
    psum x1, waiting for transfers between devices, body(): lax.psum(modulator_grad.astype(jnp.bfloat16), 'wide').astype(jnp.float32)  326 us
    psum x1, waiting for transfers between devices, body(): condition_grad = lax.psum(cond_full, ('wide', 'narrow'))  109 us
    all_gather x1, waiting for transfers between devices, body(): mod_rows = lax.all_gather(mod_part, 'narrow', axis=2, tiled=True)  88 us
    psum x1, blocking collectives, body(): lax.psum(modulator_bias_grad.astype(jnp.bfloat16), 'wide')  64.9 us
    reduce_scatter x1, waiting for transfers between devices, body(): lax.psum_scatter(jnp.dot(context, out_weight, preferred_element_type=jnp....  38.8 us
    reduce_scatter x1, waiting for transfers between devices, body(): lax.psum_scatter(jnp.einsum('tc,dc->td', d_projected, flat_qkv, preferred...  38.5 us
    all_gather x1, waiting for transfers between devices, body(): d_attn = lax.all_gather(d_attn_share, 'narrow', axis=0, tiled=True)  36.1 us
    reduce_scatter x1, waiting for transfers between devices, body(): lax.psum_scatter(jnp.dot(lax.slice_in_dim(hidden, 0, share * lax.axis_siz...  33.6 us
  transfers between devices with their start and end apart: 15, of which 12 were waited for; matrix products, arithmetic and copies ran while one was open for 10% of the time, Pallas kernels for 0%

commit v1 on v0

v1 whole, which is shorter than its diff:
```python
import jax
import jax.numpy as jnp
from jax import lax
from jax.sharding import PartitionSpec as P

HD = 72
IMG_MAX = 128
EPSILON = 1e-06
NEG_FILL = -1e30
F32 = jnp.float32
BF16 = jnp.bfloat16


def dot(left, right, dims, out=F32):
    return lax.dot_general(left, right, (dims, ((), ())), preferred_element_type=F32).astype(out)


def swap(part):
    return lax.ppermute(part, "narrow", [(0, 1), (1, 0)])


def narrow_gather(part):
    if lax.axis_size("narrow") != 2:
        return lax.all_gather(part, "narrow", axis=0, tiled=True)
    other = swap(part)
    first = lax.axis_index("narrow") == 0
    return jnp.where(
        first, jnp.concatenate([part, other], axis=0), jnp.concatenate([other, part], axis=0)
    )


def narrow_sum(part):
    if lax.axis_size("narrow") != 2:
        return lax.psum(part, "narrow").astype(F32)
    return part.astype(F32) + swap(part).astype(F32)


def narrow_scatter(part, dim=0):
    count = lax.axis_size("narrow")
    if count != 2:
        return lax.psum_scatter(part, "narrow", scatter_dimension=dim, tiled=True).astype(F32)
    size = part.shape[dim] // 2
    index = lax.axis_index("narrow")
    mine = lax.dynamic_slice_in_dim(part, index * size, size, axis=dim)
    theirs = lax.dynamic_slice_in_dim(part, (1 - index) * size, size, axis=dim)
    return mine.astype(F32) + swap(theirs).astype(F32)


def padded(cells, width):
    count = lax.axis_size("wide")
    ends = count - 1
    tail = cells[cells.shape[0] - width :]
    return (
        lax.ppermute(tail, "wide", [(i, (i + 1) % count) for i in range(ends)]),
        lax.ppermute(cells[:width], "wide", [((i + 1) % count, i) for i in range(ends)]),
    )


def norm(field):
    centred = field - jnp.mean(field, axis=-1, keepdims=True)
    rstd = lax.rsqrt(jnp.mean(centred * centred, axis=-1, keepdims=True) + EPSILON)
    return centred * rstd, rstd


def norm_back(grad, xhat, rstd):
    return rstd * (
        grad
        - jnp.mean(grad, axis=-1, keepdims=True)
        - xhat * jnp.mean(grad * xhat, axis=-1, keepdims=True)
    )


def gelu_pair(v):
    c = 0.7978845608028654
    sq = v * v
    t = jnp.tanh(c * v * (1.0 + 0.044715 * sq))
    half = 0.5 * (1.0 + t)
    slope = half + 0.5 * v * (1.0 - t * t) * c * (1.0 + 3 * 0.044715 * sq)
    return v * half, slope


def body(
    tokens,
    condition,
    cotangent,
    modulator,
    modulator_bias,
    qkv_weight,
    qv_bias,
    out_weight,
    out_bias,
    up_weight,
    up_bias,
    down_weight,
    down_bias,
    segment_ids,
    valid_counts,
):
    wide_count = lax.axis_size("wide")
    wide_index = lax.axis_index("wide")
    narrow_index = lax.axis_index("narrow")
    tok_dev = cotangent.shape[0]
    share = tokens.shape[0]
    width = tokens.shape[1]
    part_width = qkv_weight.shape[2]
    heads = part_width // HD
    img_row = condition.shape[0]
    span = IMG_MAX
    block = min(512, tok_dev)
    window = block + 2 * span
    scale_factor = HD ** (-0.5)
    own_count = valid_counts[wide_index]
    positions = jnp.arange(tok_dev, dtype=jnp.int32)
    own_ids = lax.dynamic_slice_in_dim(segment_ids, wide_index * tok_dev, tok_dev)
    live_full = (positions < own_count).astype(jnp.float32)
    share_start = narrow_index * share
    live = live_full[:, None]
    image_slots = jnp.arange(img_row, dtype=jnp.int32)
    onehot_full = (own_ids[:, None] == image_slots[None, :]).astype(BF16)
    onehot_share = lax.dynamic_slice_in_dim(onehot_full, share_start, share)
    cond_rows = condition.astype(F32)
    sigmoid_rows = jax.nn.sigmoid(cond_rows)
    activated = (cond_rows * sigmoid_rows).astype(BF16)
    tok_full = narrow_gather(tokens).astype(F32)
    mod_width = modulator.shape[2]
    mod_part = dot(activated, modulator.reshape(width, -1), ((1,), (0,)))
    mod_part = (mod_part.reshape(img_row, 6, -1) + modulator_bias.astype(F32)[None]).astype(BF16)
    mod_rows = jnp.moveaxis(mod_part, 2, 0)

    def per_token(parts):
        rows = narrow_gather(mod_rows[:, :, parts[0] : parts[1]])
        return [
            dot(onehot_full, rows[:, :, i], ((1,), (1,)), BF16).astype(F32)
            for i in range(parts[1] - parts[0])
        ]

    shift_one, scale_one = per_token((0, 2))
    gate_one, shift_two, scale_two, gate_two = per_token((2, 6))
    xhat_one, rstd_one = norm(tok_full)
    norm_one = (xhat_one * (1.0 + scale_one) + shift_one).astype(BF16)
    projected = dot(norm_one, qkv_weight.reshape(width, -1), ((1,), (0,)))
    bias_pair = qv_bias.astype(F32)
    queries = (projected[:, :part_width] + bias_pair[0]).astype(BF16)
    key_rows = projected[:, part_width : 2 * part_width].astype(BF16)
    value_rows = (projected[:, 2 * part_width :] + bias_pair[1]).astype(BF16)
    key_value = jnp.concatenate([key_rows, value_rows], axis=1)
    tail_start = own_count - span
    edge_rows = jnp.concatenate(
        [key_value[:span], lax.dynamic_slice_in_dim(key_value, tail_start, span)], axis=0
    )
    from_left, from_right = padded(edge_rows, span)
    extended = jnp.concatenate([from_left, key_value, from_right], axis=0)
    left_index = jnp.maximum(wide_index - 1, 0)
    right_index = jnp.minimum(wide_index + 1, wide_count - 1)
    left_count = valid_counts[left_index]
    left_ids = lax.dynamic_slice_in_dim(segment_ids, left_index * tok_dev + left_count - span, span)
    left_ids = jnp.where(wide_index > 0, left_ids, -2)
    right_ids = lax.dynamic_slice_in_dim(segment_ids, right_index * tok_dev, span)
    right_ids = jnp.where(wide_index < wide_count - 1, right_ids, -2)
    own_keys = jnp.where(positions < own_count, own_ids, -1)
    extended_ids = jnp.concatenate([left_ids, own_keys, right_ids])

    def block_parts(block_idx):
        row_start = block_idx * block
        query_block = queries[row_start : row_start + block].reshape(block, heads, HD)
        pair_block = extended[row_start : row_start + window]
        key_block = pair_block[:, :part_width].reshape(window, heads, HD)
        value_block = pair_block[:, part_width:].reshape(window, heads, HD)
        same_seg = (
            own_keys[row_start : row_start + block, None]
            == extended_ids[None, row_start : row_start + window]
        )
        return (query_block, key_block, value_block, same_seg)

    def masked_scores(query_block, key_block, same_seg):
        raw = (
            jnp.einsum("ihd,jhd->hij", query_block, key_block, preferred_element_type=jnp.float32)
            * scale_factor
        )
        return jnp.where(same_seg[None], raw, NEG_FILL)

    blocks = tok_dev // block
    outputs = []
    log_sums = []
    for block_idx in range(blocks):
        query_block, key_block, value_block, same_seg = block_parts(block_idx)
        masked = masked_scores(query_block, key_block, same_seg)
        top_score = jnp.max(masked, axis=-1, keepdims=True)
        expo = jnp.exp(masked - top_score)
        totals = jnp.sum(expo, axis=-1, keepdims=True)
        attend = expo / totals
        log_sums.append(top_score + jnp.log(totals))
        block_out = jnp.einsum(
            "hij,jhd->ihd",
            attend.astype(jnp.bfloat16),
            value_block,
            preferred_element_type=jnp.float32,
        )
        outputs.append(block_out.reshape(block, part_width))
    context = jnp.concatenate(outputs, axis=0).astype(jnp.bfloat16)
    attn = narrow_sum(dot(context, out_weight, ((1,), (0,)), BF16)) + out_bias.astype(F32)
    middle = tok_full + live * gate_one * attn
    xhat_two, rstd_two = norm(middle)
    norm_two = (xhat_two * (1.0 + scale_two) + shift_two).astype(BF16)
    upstream = cotangent.astype(F32)
    d_branch = (live * gate_two * upstream).astype(BF16)
    d_hidden = dot(d_branch, down_weight, ((1,), (1,)))
    upper = dot(norm_two, up_weight, ((1,), (0,))) + up_bias.astype(F32)
    gelu, slope = gelu_pair(upper)
    hidden = gelu.astype(BF16)
    d_upper = (d_hidden * slope).astype(BF16)
    d_norm_two = narrow_sum(dot(d_upper, up_weight, ((1,), (1,)), BF16))
    branch = narrow_scatter(dot(hidden, down_weight, ((1,), (0,)), BF16)) + down_bias.astype(F32)

    def own(rows):
        return lax.dynamic_slice_in_dim(rows, share_start, share)

    layer_out = (own(middle) + own(live * gate_two) * branch).astype(BF16)
    up_grad = dot(d_upper, norm_two, ((0,), (0,)), BF16)
    down_grad = dot(hidden, d_branch, ((0,), (0,)), BF16)
    bias_rows = jnp.concatenate(
        [
            jnp.sum(d_upper.astype(F32), axis=0),
            jnp.sum(d_branch.astype(F32), axis=0),
            jnp.zeros(((-d_upper.shape[1] - width) % (8 * width),), F32),
        ]
    ).reshape(-1, width)
    mlp_flat = jnp.concatenate([up_grad, down_grad, bias_rows.astype(BF16)], axis=0)
    mlp_flat = lax.psum(mlp_flat, "wide")
    ff = up_weight.shape[1]
    up_weight_grad = mlp_flat[:ff].T.astype(F32)
    down_weight_grad = mlp_flat[ff : 2 * ff].astype(F32)
    mlp_bias = mlp_flat[2 * ff :].reshape(-1).astype(F32)
    up_bias_grad = mlp_bias[:ff]
    down_bias_grad = mlp_bias[ff : ff + width]

    d_middle = upstream + norm_back(d_norm_two * (1.0 + scale_two), xhat_two, rstd_two)
    d_attn = (live * gate_one * d_middle).astype(BF16)
    out_weight_grad = dot(context, d_attn, ((0,), (0,)), BF16)
    d_context = dot(d_attn, out_weight, ((1,), (1,)), BF16)
    d_extended = jnp.zeros((tok_dev + 2 * span, 2 * part_width), jnp.float32)
    query_grads = []
    for block_idx in range(blocks):
        query_block, key_block, value_block, same_seg = block_parts(block_idx)
        attend = jnp.exp(masked_scores(query_block, key_block, same_seg) - log_sums[block_idx])
        row_start = block_idx * block
        grad_block = d_context[row_start : row_start + block].reshape(block, heads, HD)
        d_attend = jnp.einsum(
            "ihd,jhd->hij", grad_block, value_block, preferred_element_type=jnp.float32
        )
        centre = jnp.sum(attend * d_attend, axis=-1, keepdims=True)
        d_scores = (attend * (d_attend - centre)).astype(jnp.bfloat16)
        query_grad = (
            jnp.einsum("hij,jhd->ihd", d_scores, key_block, preferred_element_type=jnp.float32)
            * scale_factor
        )
        query_grads.append(query_grad.reshape(block, part_width))
        key_grad = (
            jnp.einsum("hij,ihd->jhd", d_scores, query_block, preferred_element_type=jnp.float32)
            * scale_factor
        )
        value_grad = jnp.einsum(
            "hij,ihd->jhd",
            attend.astype(jnp.bfloat16),
            grad_block,
            preferred_element_type=jnp.float32,
        )
        pair_grad = jnp.concatenate(
            [key_grad.reshape(window, part_width), value_grad.reshape(window, part_width)], axis=1
        )
        d_extended = d_extended.at[row_start : row_start + window].add(pair_grad)
    back_edges = jnp.concatenate([d_extended[:span], d_extended[span + tok_dev :]], axis=0)
    back_left, back_right = padded(back_edges.astype(jnp.bfloat16), span)
    d_local = d_extended[span : span + tok_dev]
    d_local = d_local.at[:span].add(back_left.astype(F32))
    tail_sum = lax.dynamic_slice_in_dim(d_local, tail_start, span) + back_right.astype(F32)
    d_local = lax.dynamic_update_slice_in_dim(d_local, tail_sum, tail_start, 0)
    d_queries = jnp.concatenate(query_grads, axis=0).astype(BF16)
    d_pairs = d_local.astype(BF16)
    d_projected = jnp.concatenate([d_queries, d_pairs], axis=1)
    d_norm_one = narrow_scatter(
        dot(d_projected, qkv_weight.reshape(width, -1), ((1,), (1,)), BF16)
    )
    qkv_grad = dot(d_projected, norm_one, ((0,), (0,)), BF16)
    bias_rows = jnp.concatenate(
        [
            jnp.sum(d_queries.astype(F32), axis=0),
            jnp.sum(d_pairs[:, part_width:].astype(F32), axis=0),
            jnp.sum(d_attn.astype(F32), axis=0),
            jnp.zeros(((-2 * part_width - width) % (8 * width),), F32),
        ]
    ).reshape(-1, width)
    xhat_own = own(xhat_one)
    tokens_grad = own(d_middle) + norm_back(
        d_norm_one * (1.0 + own(scale_one)), xhat_own, own(rstd_one)
    )

    def image_sum(hot, term):
        return dot(hot, term.astype(BF16), ((0,), (0,)))

    def feature_part(rows):
        return lax.dynamic_slice_in_dim(rows, narrow_index * mod_width, mod_width, axis=1)

    own_terms = jnp.stack(
        [
            image_sum(onehot_share, d_norm_one),
            image_sum(onehot_share, d_norm_one * xhat_own),
            image_sum(onehot_share, own(live * upstream) * branch),
        ]
    ).astype(BF16)
    own_terms = narrow_scatter(own_terms, 2).astype(BF16)
    full_terms = [
        image_sum(onehot_full, feature_part(live * d_middle * attn)),
        image_sum(onehot_full, feature_part(d_norm_two)),
        image_sum(onehot_full, feature_part(d_norm_two * xhat_two)),
    ]
    full_terms = jnp.stack(full_terms).astype(BF16)
    d_mod = jnp.concatenate([own_terms[:2], full_terms, own_terms[2:]], axis=0)
    attn_flat = jnp.concatenate(
        [qkv_grad, out_weight_grad, bias_rows.astype(BF16), d_mod.reshape(-1, width)], axis=0
    )
    attn_flat = lax.psum(attn_flat, "wide")
    rows_of = [3 * part_width, part_width, bias_rows.shape[0]]
    starts = [0, rows_of[0], rows_of[0] + rows_of[1], sum(rows_of)]
    qkv_weight_grad = (
        attn_flat[: starts[1]].T.reshape(width, 3, part_width).astype(F32)
    )
    out_weight_grad = attn_flat[starts[1] : starts[2]].astype(F32)
    attn_bias = attn_flat[starts[2] : starts[3]].reshape(-1).astype(F32)
    qv_bias_grad = attn_bias[: 2 * part_width].reshape(2, part_width)
    out_bias_grad = attn_bias[2 * part_width : 2 * part_width + width]
    d_mod = attn_flat[starts[3] :].reshape(6, img_row, mod_width)
    modulator_grad = jnp.stack(
        [dot(activated, d_mod[j], ((0,), (0,))) for j in range(6)], axis=1
    )
    modulator_bias_grad = jnp.sum(d_mod.astype(F32), axis=1)
    d_activated = sum(dot(d_mod[j], modulator[:, j], ((1,), (1,))) for j in range(6))
    cond_part = d_activated * sigmoid_rows * (1.0 + cond_rows * (1.0 - sigmoid_rows))
    condition_grad = narrow_sum(cond_part.astype(BF16))
    return (
        layer_out,
        tokens_grad,
        condition_grad,
        modulator_grad,
        modulator_bias_grad,
        qkv_weight_grad,
        qv_bias_grad,
        out_weight_grad,
        out_bias_grad,
        up_weight_grad,
        up_bias_grad,
        down_weight_grad,
        down_bias_grad,
    )


def solution(mesh):
    in_specs = (
        P(("wide", "narrow"), None),
        P(),
        P("wide", None),
        P(None, None, "narrow"),
        P(None, "narrow"),
        P(None, None, "narrow"),
        P(None, "narrow"),
        P("narrow", None),
        P(),
        P(None, "narrow"),
        P("narrow"),
        P("narrow", None),
        P(),
        P(),
        P(),
    )
    out_specs = (
        P(("wide", "narrow"), None),
        P(("wide", "narrow"), None),
        P(),
        P(None, None, "narrow"),
        P(None, "narrow"),
        P(None, None, "narrow"),
        P(None, "narrow"),
        P("narrow", None),
        P(),
        P(None, "narrow"),
        P("narrow"),
        P("narrow", None),
        P(),
    )
    return jax.shard_map(body, mesh=mesh, in_specs=in_specs, out_specs=out_specs, check_vma=False)
```

time: 1230 us -> 885 us (0.72)
  waiting for transfers between devices: 763 us -> 447 us
  blocking collectives: 64.9 us -> 0 us
  starting transfers between devices: 8.24 us -> 21.6 us
    all_gather x4 -> x0, waiting for transfers between devices: 187 us -> none  [the longest x1 88 us: body(): mod_rows = lax.all_gather(mod_part, 'narrow', axis=2, tiled=True)]
    reduce_scatter x5 -> x0, waiting for transfers between devices: 140 us -> none  [the longest x1 38.8 us: body(): lax.psum_scatter(jnp.dot(context, out_weight, preferred_element_type=jnp....]
    ppermute x4 -> x13, waiting for transfers between devices: 2.12 us -> 128 us  [the longest x9 125 us: swap(): return lax.ppermute(part, 'narrow', [(0, 1), (1, 0)])]
    psum x2 -> x1, waiting for transfers between devices: 434 us -> 318 us  [body(): attn_flat = lax.psum(attn_flat, 'wide')]
    psum x1 -> x0, blocking collectives: 64.9 us -> none  [body(): lax.psum(modulator_bias_grad.astype(jnp.bfloat16), 'wide')]
    concatenate x1 -> x4, other arithmetic: 5.44 us -> 29.8 us  [the longest x1 17.9 us: body(): jnp.concatenate([up_grad, down_grad, bias_rows.astype(BF16)], axis=0)]
    convert_element_type x21 -> x13, other arithmetic: 50.6 us -> 30.2 us  [the longest x1 7.86 us: body(): down_weight_grad = mlp_flat[ff:2 * ff].astype(F32)]
    another operation x3 -> x1, local copies, waits for them, and re-layouts: 15.3 us -> 0.07 us  [the longest x1 15.2 us: body(): jnp.stack([d_shift_one, d_scale_one, d_gate_one, d_shift_two, d_scale_two...]
  transfers between devices with their start and end apart: 15 -> 14, of which waited for: 12 -> 6; matrix products, arithmetic and copies ran while one was open for 10% -> 27% of each run, Pallas kernels for 0% -> 0%
where the time goes in v1:
time: 885 us; the launch traced here: 879 us
  waiting for transfers between devices  447 us (51%)
  matrix products  212 us (24%)
  other arithmetic  125 us (14%)
  local copies, waits for them, and re-layouts  56.4 us (6%)
  starting transfers between devices  21.6 us (2%)
  between operations  17.6 us (2%)
    psum x1, waiting for transfers between devices, body(): attn_flat = lax.psum(attn_flat, 'wide')  318 us
    dot_general x37, matrix products, dot(): lax.dot_general(left, right, (dims, ((), ())), preferred_element_type=F32)  171 us
    ppermute x9, waiting for transfers between devices, swap(): return lax.ppermute(part, 'narrow', [(0, 1), (1, 0)])  125 us
    unnamed x176, local copies, waits for them, and re-layouts  28.5 us
    concatenate x1, other arithmetic, body(): jnp.concatenate([up_grad, down_grad, bias_rows.astype(BF16)], axis=0)  17.9 us
  transfers between devices with their start and end apart: 14, of which 6 were waited for; matrix products, arithmetic and copies ran while one was open for 27% of the time, Pallas kernels for 0%

profile of v1, /device:TPU:0, one launch (start us, length us, event | category | flops | bytes accessed | tf_op | source)
XLA Modules:
  0.0 878.9 jit_solution(17819949514260616488)
XLA Ops:
  11.0 6.1 fusion.19
  25.1 24.9 %collective-permute-done.2 = bf16[576,256,2]{1,0,2:T(8,128)(2,1)} collective-permute-done((bf16[576,256,2]{1,0,2:T(8,128)(2,1)S(1)}, bf16[576,256,2]{1,0,2:T(8,128)(2,1)}, u32[]{:S(2)}, u32[]{:S(2)}) %collective-permute-start.2) | collective-permute-done | bytes 589856 | tf_op jit(solution)/shard_map/ppermute | solution.py:19
  74.1 5.6 pad_maximum_fusion.10
  121.3 37.2 %collective-permute-done.5 = bf16[1024,1152]{1,0:T(8,128)(2,1)} collective-permute-done((bf16[1024,1152]{1,0:T(8,128)(2,1)}, bf16[1024,1152]{1,0:T(8,128)(2,1)}, u32[]{:S(2)}, u32[]{:S(2)}) %collective-permute-start.5) | collective-permute-done | bytes 2359328 | tf_op jit(solution)/shard_map/ppermute | solution.py:19
  158.5 8.9 %fusion.136 = (f32[1024]{0:T(1024)S(1)}, f32[1024,1152]{1,0:T(8,128)S(1)}, f32[1024,1152]{1,0:T(8,128)}, f32[1024,1152]{1,0:T(8,128)}, bf16[1024,1152]{1,0:T(8,128)(2,1)}) fusion(f32[1024]{0:T(1024)S(1)} %fusion.121, bf16[512,1152]{1,0:T(8,128)(2,1)S(1)} %copy-done.16, bf16[512,1152]{1,0:T(8,128)(2,1)S(1)} %copy-done.18, pred[]{:T(512)S(6)} %eq.28, ...), kind=kOutput, calls=%fused_computation.265 | convolution fusion | flops 630193152 | bytes 24211456 | tf_op jit(solution)/shard_map/dot_general | solution.py:15
  173.4 8.6 fusion.146
  182.0 11.0 %convolution_convert_fusion.4 = bf16[1024,1152]{1,0:T(8,128)(2,1)S(1)} fusion(bf16[2304,1152]{1,0:T(8,128)(2,1)S(1)} %bitcast.234, f32[1024,2304]{1,0:T(8,128)} %fusion.146, f32[2304]{0:T(1024)S(1)} %convert_element_type.306), kind=kOutput, calls=%fused_computation.59 | convolution fusion | flops 5460590592 | bytes 17114112 | tf_op jit(solution)/shard_map/dot_general | solution.py:15
  193.0 15.0 %fusion.144 = (bf16[2304]{0:T(1024)(128)(2,1)S(1)}, bf16[1024,2304]{1,0:T(8,128)(2,1)}) fusion(f32[1024,2304]{1,0:T(8,128)} %fusion.146, f32[2304]{0:T(1024)S(1)} %convert_element_type.306, bf16[1024,1152]{1,0:T(8,128)(2,1)S(1)} %get-tuple-element.99, bf16[2304,1152]{1,0:T(8,128)(2,1)S(1)} %bitcast.234), kind=kOutput, calls=%fused_computation.273 | convolution fusion | flops 5483001856 | bytes 21837312 | tf_op jit(solution)/shard_map/dot_general | solution.py:15
  208.1 9.5 %convolution_convert_fusion.3 = bf16[1024,1152]{1,0:T(8,128)(2,1)} fusion(bf16[1024,2304]{1,0:T(8,128)(2,1)} %get-tuple-element.158, bf16[1152,2304]{1,0:T(8,128)(2,1)S(1)} %bitcast.238), kind=kOutput, calls=%fused_computation.58 | convolution fusion | flops 5436997632 | bytes 12386304 | tf_op jit(solution)/shard_map/dot_general | solution.py:15
  217.6 8.0 convolution_convert_fusion.1
  228.9 12.8 %convolution_convert_fusion = bf16[2304,1152]{1,0:T(8,128)(2,1)} fusion(bf16[1024,1152]{1,0:T(8,128)(2,1)} %copy-done.38, f32[1024,2304]{1,0:T(8,128)} %fusion.146, f32[2304]{0:T(1024)S(1)} %convert_element_type.306), kind=kOutput, calls=%fused_computation.12 | convolution fusion | flops 5462065152 | bytes 17114112 | tf_op jit(solution)/shard_map/dot_general | solution.py:15
  241.7 61.7 %collective-permute-done.7 = bf16[1024,1152]{1,0:T(8,128)(2,1)S(1)} collective-permute-done((bf16[1024,1152]{1,0:T(8,128)(2,1)}, bf16[1024,1152]{1,0:T(8,128)(2,1)S(1)}, u32[]{:S(2)}, u32[]{:S(2)}) %collective-permute-start.7) | collective-permute-done | bytes 2359328 | tf_op jit(solution)/shard_map/ppermute | solution.py:19
  319.5 6.3 multiply_reduce_fusion
  325.7 7.7 multiply_convert_fusion
  340.3 6.5 multiply_reduce_fusion.1
  346.7 6.5 multiply_convert_fusion.1
  377.2 8.7 convolution_convert_fusion.5
  388.7 17.9 %pad_maximum_fusion = bf16[4616,1152]{1,0:T(8,128)(2,1)} fusion(bf16[8,1152]{1,0:T(8,128)(2,1)S(1)} %convert_element_type.359, bf16[2304,1152]{1,0:T(8,128)(2,1)S(1)} %bitcast.224, bf16[2304,1152]{1,0:T(8,128)(2,1)S(1)} %bitcast.222), kind=kLoop, calls=%fused_computation.16 | loop fusion | flops 31905792 | bytes 21270528 | tf_op jit(solution)/shard_map/concatenate | solution.py:228
  420.0 9.4 %convolution_convert_fusion.2 = bf16[1728,1152]{1,0:T(8,128)(2,1)} fusion(bf16[1024,1152]{1,0:T(8,128)(2,1)} %copy-done.61, bf16[1024,1152]{0,1:T(8,128)(2,1)} %copy-done.35, bf16[512,576]{0,1:T(8,128)(2,1)} %bitcast.230, bf16[512,576]{0,1:T(8,128)(2,1)} %bitcast.232), kind=kOutput, calls=%fused_computation.26 | convolution fusion | flops 4089470976 | bytes 9879552 | tf_op jit(solution)/shard_map/dot_general | solution.py:15
  435.7 5.9 fusion.82
  453.9 6.3 pad_maximum_fusion.1
  474.2 318.4 %all-reduce.4.cloned.1.call-done = (bf16[3080,1152]{1,0:T(8,128)(2,1)}, bf16[4616,1152]{1,0:T(8,128)(2,1)}) async-done(((bf16[3080,1152]{1,0:T(8,128)(2,1)}, bf16[4616,1152]{1,0:T(8,128)(2,1)}), (bf16[3080,1152]{1,0:T(8,128)(2,1)}, bf16[4616,1152]{1,0:T(8,128)(2,1)})) %all-reduce.4.cloned.1.call-update) | async-done | bytes 17731600 | tf_op jit(solution)/shard_map/psum | solution.py:322
  807.7 7.9 slice_convert_fusion
  839.9 12.7 %copy.41 = f32[1152,2304]{1,0:T(8,128)} copy(f32[1152,2304]{0,1:T(8,128)} %get-tuple-element.111) | data formatting | bytes 21233664
  (340 shorter events, 237.8 us)
Async XLA Ops:
  7.2 97.3 %copy-start = (bf16[576,1152]{1,0:T(8,128)(2,1)S(1)}, bf16[576,1152]{1,0:T(8,128)(2,1)}, u32[]{:S(2)}) copy-start(bf16[576,1152]{1,0:T(8,128)(2,1)} %param.28) | copy-start | bytes 3981316
  7.2 785.4 %all-reduce.4.cloned.1.call-start = ((), (), s32[]{:S(2)}) async-start(), calls=%async_computation | async-start | bytes 35463168 | tf_op jit(solution)/shard_map/psum | solution.py:322
  7.2 45.4 %collective-permute-start = (bf16[512,1152]{1,0:T(8,128)(2,1)}, bf16[512,1152]{1,0:T(8,128)(2,1)S(1)}, u32[]{:S(2)}, u32[]{:S(2)}) collective-permute-start(bf16[512,1152]{1,0:T(8,128)(2,1)} %param.21), channel_id=1, source_target_pairs={{0,1},{1,0},{2,3},{3,2},{4,5},{5,4},{6,7},{7,6},{8,9},{9,8},{10,11... | collective-permute-start | bytes 3538952 | tf_op jit(solution)/shard_map/ppermute | solution.py:19
  17.1 32.9 %collective-permute-start.2 = (bf16[576,256,2]{1,0,2:T(8,128)(2,1)S(1)}, bf16[576,256,2]{1,0,2:T(8,128)(2,1)}, u32[]{:S(2)}, u32[]{:S(2)}) collective-permute-start(bf16[576,256,2]{1,0,2:T(8,128)(2,1)S(1)} %slice.351), channel_id=1, source_target_pairs={{0,1},{1,0},{2,3},{3,2},{4,5},{5,4},{6,7},{7,6},{8,9},{9,8},{10,11... | collective-permute-start | bytes 1769480 | tf_op jit(solution)/shard_map/ppermute | solution.py:19
  18.4 94.1 %collective-permute-start.1 = (bf16[576,256,4]{1,0,2:T(8,128)(2,1)}, bf16[576,256,4]{1,0,2:T(8,128)(2,1)}, u32[]{:S(2)}, u32[]{:S(2)}) collective-permute-start(bf16[576,256,4]{1,0,2:T(8,128)(2,1)} %slice.349), channel_id=1, source_target_pairs={{0,1},{1,0},{2,3},{3,2},{4,5},{5,4},{6,7},{7,6},{8,9},{9,8},{10,11... | collective-permute-start | bytes 3538952 | tf_op jit(solution)/shard_map/ppermute | solution.py:19
  22.2 146.3 %copy-start.43 = (s32[1024]{0:T(1024)}, s32[1024]{0:T(1024)S(1)}, u32[]{:S(2)}) copy-start(s32[1024]{0:T(1024)S(1)} %get-tuple-element.109) | copy-start | bytes 12292
  57.0 101.5 %copy-start.47 = (f32[1024]{0:T(1024)}, f32[1024]{0:T(1024)S(1)}, u32[]{:S(2)}) copy-start(f32[1024]{0:T(1024)S(1)} %add_rsqrt_fusion.1) | copy-start | bytes 12292
  67.0 3.9 collective-permute-start.3
  68.4 5.7 collective-permute-start.4
  108.2 50.3 %collective-permute-start.5 = (bf16[1024,1152]{1,0:T(8,128)(2,1)}, bf16[1024,1152]{1,0:T(8,128)(2,1)}, u32[]{:S(2)}, u32[]{:S(2)}) collective-permute-start(bf16[1024,1152]{1,0:T(8,128)(2,1)} %convolution_convert_fusion.9), channel_id=1, source_target_pairs={{0,1},{1,0},{2,3},{3,2},{4,5},{5,4},{6,7},{7,6},{8,9},{9,8},{10,11... | collective-permute-start | bytes 7077896 | tf_op jit(solution)/shard_map/ppermute | solution.py:19
  121.3 71.7 %copy-start.38 = (bf16[1024,1152]{1,0:T(8,128)(2,1)}, bf16[1024,1152]{1,0:T(8,128)(2,1)S(1)}, u32[]{:S(2)}) copy-start(bf16[1024,1152]{1,0:T(8,128)(2,1)S(1)} %get-tuple-element.99) | copy-start | bytes 7077892
  217.6 85.8 %slice-start.6 = ((s8[4718592]{0:T(1024)(128)(4,1)}), s8[524288]{0:T(1024)(128)(4,1)S(1)}, s32[]{:S(2)}) async-start(s8[4718592]{0:T(1024)(128)(4,1)} %bitcast.196), calls=%async_computation.7 | async-start | bytes 1048576
  226.7 179.9 %collective-permute-start.6 = (bf16[512,1152]{1,0:T(8,128)(2,1)}, bf16[512,1152]{1,0:T(8,128)(2,1)}, u32[]{:S(2)}, u32[]{:S(2)}) collective-permute-start(bf16[512,1152]{1,0:T(8,128)(2,1)} %constant_dynamic-slice_fusion.2), channel_id=1, source_target_pairs={{0,1},{1,0},{2,3},{3,2},{4,5},{5,4},{6,7},{7,6},{8,9},{9,8},{10,11... | collective-permute-start | bytes 3538952 | tf_op jit(solution)/shard_map/ppermute | solution.py:19
  228.3 75.1 %slice-start.7 = ((s8[4718592]{0:T(1024)(128)(4,1)}), s8[4194304]{0:T(1024)(128)(4,1)S(1)}, s32[]{:S(2)}) async-start(s8[4718592]{0:T(1024)(128)(4,1)} %bitcast.196), calls=%async_computation.8 | async-start | bytes 8388608
  228.3 75.1 %copy-start.6 = (bf16[1024,1152]{1,0:T(8,128)(2,1)S(1)}, bf16[1024,1152]{1,0:T(8,128)(2,1)}, u32[]{:S(2)}) copy-start(bf16[1024,1152]{1,0:T(8,128)(2,1)} %copy-done.5) | copy-start | bytes 7077892
  228.3 75.1 %copy-start.20 = (bf16[1024,1152]{1,0:T(8,128)(2,1)S(1)}, bf16[1024,1152]{1,0:T(8,128)(2,1)}, u32[]{:S(2)}) copy-start(bf16[1024,1152]{1,0:T(8,128)(2,1)} %convolution_convert_fusion.3) | copy-start | bytes 7077892
  228.3 75.1 %collective-permute-start.7 = (bf16[1024,1152]{1,0:T(8,128)(2,1)}, bf16[1024,1152]{1,0:T(8,128)(2,1)S(1)}, u32[]{:S(2)}, u32[]{:S(2)}) collective-permute-start(bf16[1024,1152]{1,0:T(8,128)(2,1)} %convolution_convert_fusion.3), channel_id=1, source_target_pairs={{0,1},{1,0},{2,3},{3,2},{4,5},{5,4},{6,7},{7,6},{8,9},{9,8},{10,11... | collective-permute-start | bytes 7077896 | tf_op jit(solution)/shard_map/ppermute | solution.py:19
  241.7 65.9 %copy-start.19 = (bf16[1024,1152]{1,0:T(8,128)(2,1)S(1)}, bf16[1024,1152]{1,0:T(8,128)(2,1)}, u32[]{:S(2)}) copy-start(bf16[1024,1152]{1,0:T(8,128)(2,1)} %get-tuple-element.147) | copy-start | bytes 7077892
  241.7 65.9 %copy-start.22 = (bf16[1024,1152]{1,0:T(8,128)(2,1)S(1)}, bf16[1024,1152]{1,0:T(8,128)(2,1)}, u32[]{:S(2)}) copy-start(bf16[1024,1152]{1,0:T(8,128)(2,1)} %param.23) | copy-start | bytes 7077892
  357.2 8.9 %collective-permute-start.9 = (bf16[128,1152]{0,1:T(8,128)(2,1)S(1)}, bf16[128,1152]{0,1:T(8,128)(2,1)S(1)}, u32[]{:S(2)}, u32[]{:S(2)}) collective-permute-start(bf16[128,1152]{0,1:T(8,128)(2,1)S(1)} %slice.464), channel_id=1, source_target_pairs={{2,0},{4,2},{6,4},{8,6},{10,8},{12,10},{14,12},{16,14},{18,16},{20... | collective-permute-start | bytes 884744 | tf_op jit(solution)/shard_map/ppermute | solution.py:55
  358.5 7.4 collective-permute-start.8
  387.1 26.8 %collective-permute-start.10 = (bf16[512,1152]{1,0:T(8,128)(2,1)}, bf16[512,1152]{1,0:T(8,128)(2,1)S(1)}, u32[]{:S(2)}, u32[]{:S(2)}) collective-permute-start(bf16[512,1152]{1,0:T(8,128)(2,1)} %constant_dynamic-slice_fusion.1), channel_id=1, source_target_pairs={{0,1},{1,0},{2,3},{3,2},{4,5},{5,4},{6,7},{7,6},{8,9},{9,8},{10,11... | collective-permute-start | bytes 3538952 | tf_op jit(solution)/shard_map/ppermute | solution.py:19
  417.7 13.2 %collective-permute-start.11 = (bf16[3,256,576]{1,2,0:T(8,128)(2,1)S(1)}, bf16[3,256,576]{1,2,0:T(8,128)(2,1)}, u32[]{:S(2)}, u32[]{:S(2)}) collective-permute-start(bf16[3,256,576]{1,2,0:T(8,128)(2,1)S(1)} %copy.36), channel_id=1, source_target_pairs={{0,1},{1,0},{2,3},{3,2},{4,5},{5,4},{6,7},{7,6},{8,9},{9,8},{10,11... | collective-permute-start | bytes 2654216 | tf_op jit(solution)/shard_map/ppermute | solution.py:19
  833.4 36.3 %collective-permute-start.12 = (bf16[256,1152]{1,0:T(8,128)(2,1)S(1)}, bf16[256,1152]{1,0:T(8,128)(2,1)}, u32[]{:S(2)}, u32[]{:S(2)}) collective-permute-start(bf16[256,1152]{1,0:T(8,128)(2,1)S(1)} %fusion.30), channel_id=1, source_target_pairs={{0,1},{1,0},{2,3},{3,2},{4,5},{5,4},{6,7},{7,6},{8,9},{9,8},{10,11... | collective-permute-start | bytes 1769480 | tf_op jit(solution)/shard_map/ppermute | solution.py:19
  (78 other events, 810.1 us)
Sparse Core Ops, SparseCore 0:
  460.3 332.1 all-reduce.3

commit v2 on v1

--- a/solution.py
+++ b/solution.py
@@ -1,6 +1,8 @@
 import jax
 import jax.numpy as jnp
 from jax import lax
+from jax.experimental import pallas as pl
+from jax.experimental.pallas import tpu as pltpu
 from jax.sharding import PartitionSpec as P
 
 HD = 72
@@ -54,6 +56,133 @@
         lax.ppermute(tail, "wide", [(i, (i + 1) % count) for i in range(ends)]),
         lax.ppermute(cells[:width], "wide", [((i + 1) % count, i) for i in range(ends)]),
     )
+
+
+MESH = pl.DeviceIdType.MESH
+UNIT = 48
+
+
+def ring_kernel(chips, subs, data, out, mine, theirs, slots, copy_sems, core_sems, ring_sems):
+    wide = lax.axis_index("wide")
+    chip, core = wide // 2, wide % 2
+    half = chips // 2
+
+    def place(position):
+        position = lax.rem(position + 2 * chips, chips)
+        side = position // half
+        return (1 - side) * 2 * position + side * (2 * (chips - 1 - position) + 1)
+
+    position = chip // 2 + (chip % 2) * (chips - 1 - 2 * (chip // 2))
+    ahead = 2 * place(position + 1) + core
+    behind = 2 * place(position - 1) + core
+    sibling = 2 * chip + 1 - core
+    barrier = pltpu.get_barrier_semaphore()
+    for device in (ahead, behind, sibling):
+        pl.semaphore_signal(barrier, inc=1, device_id={"wide": device}, device_id_type=MESH)
+    pl.semaphore_wait(barrier, 3)
+
+    def local(lane):
+        return pltpu.make_async_copy(data.at[lane, :, core], mine.at[lane], copy_sems.at[lane])
+
+    def across(lane):
+        return pltpu.make_async_remote_copy(
+            src_ref=data.at[lane, :, 1 - core],
+            dst_ref=theirs.at[lane],
+            send_sem=core_sems.at[0, lane],
+            recv_sem=core_sems.at[1, lane],
+            device_id={"wide": sibling},
+            device_id_type=MESH,
+        )
+
+    for lane in range(2):
+        across(lane).start()
+        local(lane).start()
+
+    def hop(lane, step, sub):
+        rows = pl.ds(sub * UNIT, UNIT)
+        if step == 0:
+            first = place(position - 1 if lane == 0 else position + 1)
+            source = mine.at[lane, first, rows]
+        else:
+            source = slots.at[lane, step - 1, rows]
+        return pltpu.make_async_remote_copy(
+            src_ref=source,
+            dst_ref=slots.at[lane, step, rows],
+            send_sem=ring_sems.at[0, lane, step, sub],
+            recv_sem=ring_sems.at[1, lane, step, sub],
+            device_id={"wide": ahead if lane == 0 else behind},
+            device_id_type=MESH,
+        )
+
+    for lane in range(2):
+        local(lane).wait()
+        across(lane).wait()
+
+        def merge(index, carry, lane=lane):
+            mine[lane, index] = mine[lane, index] + theirs[lane, index]
+            return carry
+
+        lax.fori_loop(0, chips, merge, 0)
+        for sub in range(subs):
+            hop(lane, 0, sub).start()
+    for step in range(chips - 1):
+        for sub in range(subs):
+            for lane in range(2):
+                hop(lane, step, sub).wait_recv()
+                offset = 2 + step
+                index = place(position - offset if lane == 0 else position + offset)
+                rows = pl.ds(sub * UNIT, UNIT)
+                total = slots[lane, step, rows] + mine[lane, index, rows]
+                if step == chips - 2:
+                    out[lane, rows] = total
+                else:
+                    slots[lane, step, rows] = total
+                    hop(lane, step + 1, sub).start()
+    for step in range(chips - 1):
+        for sub in range(subs):
+            for lane in range(2):
+                hop(lane, step, sub).wait_send()
+
+
+def ring_scatter(flat, collective_id):
+    chips = lax.axis_size("wide") // 2
+    shard = flat.shape[0] // (4 * chips)
+    width = flat.shape[1]
+    subs = shard // UNIT
+    data = flat.reshape(2, chips, 2, shard, width)
+    return pl.pallas_call(
+        lambda *refs: ring_kernel(chips, subs, *refs),
+        out_shape=jax.ShapeDtypeStruct((2, shard, width), BF16),
+        in_specs=[pl.BlockSpec(memory_space=pl.ANY)],
+        out_specs=pl.BlockSpec(memory_space=pltpu.VMEM),
+        scratch_shapes=[
+            pltpu.VMEM((2, chips, shard, width), BF16),
+            pltpu.VMEM((2, chips, shard, width), BF16),
+            pltpu.VMEM((2, chips - 1, shard, width), BF16),
+            pltpu.SemaphoreType.DMA((2,)),
+            pltpu.SemaphoreType.DMA((2, 2)),
+            pltpu.SemaphoreType.DMA((2, 2, chips - 1, subs)),
+        ],
+        compiler_params=pltpu.CompilerParams(
+            collective_id=collective_id, has_side_effects=True, vmem_limit_bytes=40 << 20
+        ),
+        name="ring_scatter",
+    )(data)
+
+
+def wide_sum(flat, loose, collective_id):
+    count = lax.axis_size("wide")
+    rows, width = flat.shape
+    if lax.axis_size("narrow") != 2 or rows % (2 * count * UNIT):
+        return lax.psum(flat, "wide"), jnp.sum(
+            lax.all_gather(loose, "wide", axis=0).astype(F32), axis=0
+        )
+    mine = ring_scatter(flat, collective_id)
+    shard = rows // (2 * count)
+    parts = jnp.concatenate([mine.reshape(2 * shard, width), loose], axis=0)
+    parts = lax.all_gather(parts, "wide", axis=0)
+    lanes = [parts[:, lane * shard : (lane + 1) * shard].reshape(-1, width) for lane in range(2)]
+    return jnp.concatenate(lanes, axis=0), jnp.sum(parts[:, 2 * shard :].astype(F32), axis=0)
 
 
 def norm(field):
@@ -180,8 +309,17 @@
         return jnp.where(same_seg[None], raw, NEG_FILL)
 
     blocks = tok_dev // block
-    outputs = []
-    log_sums = []
+
+    def rows_of(rows, block_idx):
+        return rows[block_idx * block : (block_idx + 1) * block]
+
+    def own(parts):
+        rows = jnp.concatenate(parts, axis=0)
+        return lax.dynamic_slice_in_dim(rows, share_start, share)
+
+    upstream = cotangent.astype(F32)
+    contexts, log_sums, attns, middles, xhats, rstds = [], [], [], [], [], []
+    norms, hiddens, d_uppers, d_branches, d_norms, branches = [], [], [], [], [], []
     for block_idx in range(blocks):
         query_block, key_block, value_block, same_seg = block_parts(block_idx)
         masked = masked_scores(query_block, key_block, same_seg)
@@ -191,53 +329,71 @@
         attend = expo / totals
         log_sums.append(top_score + jnp.log(totals))
         block_out = jnp.einsum(
-            "hij,jhd->ihd",
-            attend.astype(jnp.bfloat16),
-            value_block,
-            preferred_element_type=jnp.float32,
-        )
-        outputs.append(block_out.reshape(block, part_width))
-    context = jnp.concatenate(outputs, axis=0).astype(jnp.bfloat16)
-    attn = narrow_sum(dot(context, out_weight, ((1,), (0,)), BF16)) + out_bias.astype(F32)
-    middle = tok_full + live * gate_one * attn
-    xhat_two, rstd_two = norm(middle)
-    norm_two = (xhat_two * (1.0 + scale_two) + shift_two).astype(BF16)
-    upstream = cotangent.astype(F32)
-    d_branch = (live * gate_two * upstream).astype(BF16)
-    d_hidden = dot(d_branch, down_weight, ((1,), (1,)))
-    upper = dot(norm_two, up_weight, ((1,), (0,))) + up_bias.astype(F32)
-    gelu, slope = gelu_pair(upper)
-    hidden = gelu.astype(BF16)
-    d_upper = (d_hidden * slope).astype(BF16)
-    d_norm_two = narrow_sum(dot(d_upper, up_weight, ((1,), (1,)), BF16))
-    branch = narrow_scatter(dot(hidden, down_weight, ((1,), (0,)), BF16)) + down_bias.astype(F32)
-
-    def own(rows):
-        return lax.dynamic_slice_in_dim(rows, share_start, share)
-
-    layer_out = (own(middle) + own(live * gate_two) * branch).astype(BF16)
+            "hij,jhd->ihd", attend.astype(BF16), value_block, preferred_element_type=F32
+        )
+        contexts.append(block_out.reshape(block, part_width).astype(BF16))
+        attn_part = dot(contexts[-1], out_weight, ((1,), (0,)), BF16)
+        attns.append(narrow_sum(attn_part) + out_bias.astype(F32))
+    for block_idx in range(blocks):
+        gate_b = rows_of(live * gate_two, block_idx)
+        d_branches.append((gate_b * rows_of(upstream, block_idx)).astype(BF16))
+        d_hidden = dot(d_branches[-1], down_weight, ((1,), (1,)), BF16).astype(F32)
+        middle = rows_of(tok_full, block_idx) + rows_of(live * gate_one, block_idx) * attns[block_idx]
+        xhat, rstd = norm(middle)
+        middles.append(middle)
+        xhats.append(xhat)
+        rstds.append(rstd)
+        scale_b, shift_b = rows_of(scale_two, block_idx), rows_of(shift_two, block_idx)
+        norms.append((xhat * (1.0 + scale_b) + shift_b).astype(BF16))
+        upper = dot(norms[-1], up_weight, ((1,), (0,))) + up_bias.astype(F32)
+        gelu, slope = gelu_pair(upper)
+        hiddens.append(gelu.astype(BF16))
+        d_uppers.append((d_hidden * slope).astype(BF16))
+        d_norms.append(narrow_sum(dot(d_uppers[-1], up_weight, ((1,), (1,)), BF16)))
+    hidden = jnp.concatenate(hiddens, axis=0)
+    d_upper = jnp.concatenate(d_uppers, axis=0)
+    d_branch = jnp.concatenate(d_branches, axis=0)
+    norm_two = jnp.concatenate(norms, axis=0)
+    context = jnp.concatenate(contexts, axis=0)
+    down_grad = dot(hidden, d_branch, ((0,), (0,)), BF16)
     up_grad = dot(d_upper, norm_two, ((0,), (0,)), BF16)
-    down_grad = dot(hidden, d_branch, ((0,), (0,)), BF16)
-    bias_rows = jnp.concatenate(
-        [
-            jnp.sum(d_upper.astype(F32), axis=0),
-            jnp.sum(d_branch.astype(F32), axis=0),
-            jnp.zeros(((-d_upper.shape[1] - width) % (8 * width),), F32),
-        ]
-    ).reshape(-1, width)
-    mlp_flat = jnp.concatenate([up_grad, down_grad, bias_rows.astype(BF16)], axis=0)
-    mlp_flat = lax.psum(mlp_flat, "wide")
-    ff = up_weight.shape[1]
-    up_weight_grad = mlp_flat[:ff].T.astype(F32)
-    down_weight_grad = mlp_flat[ff : 2 * ff].astype(F32)
-    mlp_bias = mlp_flat[2 * ff :].reshape(-1).astype(F32)
-    up_bias_grad = mlp_bias[:ff]
-    down_bias_grad = mlp_bias[ff : ff + width]
-
-    d_middle = upstream + norm_back(d_norm_two * (1.0 + scale_two), xhat_two, rstd_two)
-    d_attn = (live * gate_one * d_middle).astype(BF16)
+    up_grad, down_grad = lax.psum((up_grad, down_grad), "wide")
+    up_weight_grad = up_grad.T.astype(F32)
+    down_weight_grad = down_grad.astype(F32)
+    branch_part = dot(hidden, down_weight, ((1,), (0,)), BF16)
+    branch = narrow_scatter(branch_part) + down_bias.astype(F32)
+    layer_out = (
+        own(middles) + own([live * gate_two]) * branch
+    ).astype(BF16)
+
+    def image_sum(hot, term):
+        return dot(hot, term.astype(BF16), ((0,), (0,)))
+
+    def feature_part(rows):
+        return lax.dynamic_slice_in_dim(rows, narrow_index * mod_width, mod_width, axis=1)
+
+    first_bias = jnp.where(narrow_index == 0, down_bias.astype(F32), 0.0)
+    d_gate_two = image_sum(onehot_full, live * upstream * (branch_part.astype(F32) + first_bias))
+    d_gate_two = narrow_scatter(d_gate_two.astype(BF16), 1)
+    d_middles, d_attns, d_contexts = [], [], []
+    d_gate_one = d_shift_two = d_scale_two = 0.0
+    for block_idx in range(blocks):
+        scale_b = rows_of(scale_two, block_idx)
+        d_norm = d_norms[block_idx]
+        d_middle = rows_of(upstream, block_idx) + norm_back(
+            d_norm * (1.0 + scale_b), xhats[block_idx], rstds[block_idx]
+        )
+        d_middles.append(d_middle)
+        hot = rows_of(onehot_full, block_idx)
+        live_b = rows_of(live, block_idx)
+        d_attns.append((rows_of(live * gate_one, block_idx) * d_middle).astype(BF16))
+        d_contexts.append(dot(d_attns[-1], out_weight, ((1,), (1,)), BF16))
+        d_gate_one += image_sum(hot, feature_part(live_b * d_middle * attns[block_idx]))
+        d_shift_two += image_sum(hot, feature_part(d_norm))
+        d_scale_two += image_sum(hot, feature_part(d_norm * xhats[block_idx]))
+    d_attn = jnp.concatenate(d_attns, axis=0)
+    d_context = jnp.concatenate(d_contexts, axis=0)
     out_weight_grad = dot(context, d_attn, ((0,), (0,)), BF16)
-    d_context = dot(d_attn, out_weight, ((1,), (1,)), BF16)
     d_extended = jnp.zeros((tok_dev + 2 * span, 2 * part_width), jnp.float32)
     query_grads = []
     for block_idx in range(blocks):
@@ -278,58 +434,46 @@
     d_queries = jnp.concatenate(query_grads, axis=0).astype(BF16)
     d_pairs = d_local.astype(BF16)
     d_projected = jnp.concatenate([d_queries, d_pairs], axis=1)
-    d_norm_one = narrow_scatter(
-        dot(d_projected, qkv_weight.reshape(width, -1), ((1,), (1,)), BF16)
-    )
-    qkv_grad = dot(d_projected, norm_one, ((0,), (0,)), BF16)
-    bias_rows = jnp.concatenate(
+    d_norm_part = dot(d_projected, qkv_weight.reshape(width, -1), ((1,), (1,)), BF16)
+    early = jnp.stack(
         [
-            jnp.sum(d_queries.astype(F32), axis=0),
-            jnp.sum(d_pairs[:, part_width:].astype(F32), axis=0),
-            jnp.sum(d_attn.astype(F32), axis=0),
-            jnp.zeros(((-2 * part_width - width) % (8 * width),), F32),
-        ]
-    ).reshape(-1, width)
-    xhat_own = own(xhat_one)
-    tokens_grad = own(d_middle) + norm_back(
-        d_norm_one * (1.0 + own(scale_one)), xhat_own, own(rstd_one)
-    )
-
-    def image_sum(hot, term):
-        return dot(hot, term.astype(BF16), ((0,), (0,)))
-
-    def feature_part(rows):
-        return lax.dynamic_slice_in_dim(rows, narrow_index * mod_width, mod_width, axis=1)
-
-    own_terms = jnp.stack(
-        [
-            image_sum(onehot_share, d_norm_one),
-            image_sum(onehot_share, d_norm_one * xhat_own),
-            image_sum(onehot_share, own(live * upstream) * branch),
+            image_sum(onehot_full, d_norm_part),
+            image_sum(onehot_full, d_norm_part.astype(F32) * xhat_one),
         ]
     ).astype(BF16)
-    own_terms = narrow_scatter(own_terms, 2).astype(BF16)
-    full_terms = [
-        image_sum(onehot_full, feature_part(live * d_middle * attn)),
-        image_sum(onehot_full, feature_part(d_norm_two)),
-        image_sum(onehot_full, feature_part(d_norm_two * xhat_two)),
+    early = narrow_scatter(early, 2)
+    d_norm_one = narrow_scatter(d_norm_part)
+    qkv_grad = dot(d_projected, norm_one, ((0,), (0,)), BF16)
+    loose_parts = [
+        jnp.sum(d_upper.astype(F32), axis=0),
+        jnp.sum(d_branch.astype(F32), axis=0),
+        jnp.sum(d_queries.astype(F32), axis=0),
+        jnp.sum(d_pairs[:, part_width:].astype(F32), axis=0),
+        jnp.sum(d_attn.astype(F32), axis=0),
     ]
-    full_terms = jnp.stack(full_terms).astype(BF16)
-    d_mod = jnp.concatenate([own_terms[:2], full_terms, own_terms[2:]], axis=0)
-    attn_flat = jnp.concatenate(
-        [qkv_grad, out_weight_grad, bias_rows.astype(BF16), d_mod.reshape(-1, width)], axis=0
-    )
-    attn_flat = lax.psum(attn_flat, "wide")
-    rows_of = [3 * part_width, part_width, bias_rows.shape[0]]
-    starts = [0, rows_of[0], rows_of[0] + rows_of[1], sum(rows_of)]
+    loose = jnp.concatenate(loose_parts)
+    loose = jnp.pad(loose, (0, (-loose.shape[0]) % (8 * width))).reshape(-1, width).astype(BF16)
+    tokens_grad = own(d_middles) + norm_back(
+        d_norm_one * (1.0 + own([scale_one])), own([xhat_one]), own([rstd_one])
+    )
+    late = jnp.stack([d_gate_one, d_shift_two, d_scale_two, d_gate_two])
+    d_mod = jnp.concatenate([early.astype(BF16), late.astype(BF16)], axis=0)
+    flat = jnp.concatenate([qkv_grad, out_weight_grad, d_mod.reshape(-1, width)], axis=0)
+    flat, loose = wide_sum(flat, loose, 0)
+    starts = [0, 3 * part_width, 4 * part_width]
     qkv_weight_grad = (
-        attn_flat[: starts[1]].T.reshape(width, 3, part_width).astype(F32)
-    )
-    out_weight_grad = attn_flat[starts[1] : starts[2]].astype(F32)
-    attn_bias = attn_flat[starts[2] : starts[3]].reshape(-1).astype(F32)
-    qv_bias_grad = attn_bias[: 2 * part_width].reshape(2, part_width)
-    out_bias_grad = attn_bias[2 * part_width : 2 * part_width + width]
-    d_mod = attn_flat[starts[3] :].reshape(6, img_row, mod_width)
+        flat[: starts[1]].T.reshape(width, 3, part_width).astype(F32)
+    )
+    out_weight_grad = flat[starts[1] : starts[2]].astype(F32)
+    loose = loose.reshape(-1)
+    bounds = [0]
+    for part in loose_parts:
+        bounds.append(bounds[-1] + part.shape[0])
+    up_bias_grad, down_bias_grad, query_bias, value_bias, out_bias_grad = [
+        loose[bounds[i] : bounds[i + 1]] for i in range(5)
+    ]
+    qv_bias_grad = jnp.stack([query_bias, value_bias])
+    d_mod = flat[starts[2] :].reshape(6, img_row, mod_width)
     modulator_grad = jnp.stack(
         [dot(activated, d_mod[j], ((0,), (0,))) for j in range(6)], axis=1
     )

time: 885 us -> 655 us (0.74)
  waiting for transfers between devices: 447 us -> 157 us
  Pallas kernels: 0 us -> 59.9 us
  matrix products: 212 us -> 193 us
    psum x1, waiting for transfers between devices: 318 us -> 0.01 us  [body(): up_grad, down_grad = lax.psum((up_grad, down_grad), 'wide')]
    pallas_call x0 -> x1, Pallas kernels: none -> 59.9 us  [ring_scatter(): pl.pallas_call(lambda *refs: ring_kernel(chips, subs, *refs), out_shape=j...]
    ppermute x9 -> x12, waiting for transfers between devices: 125 us -> 157 us  [swap(): return lax.ppermute(part, 'narrow', [(0, 1), (1, 0)])]
    dot_general x37 -> x45, matrix products: 171 us -> 150 us  [dot(): lax.dot_general(left, right, (dims, ((), ())), preferred_element_type=F32)]
    concatenate x3, other arithmetic: 24.1 us -> 6.44 us  [the longest x1 3.67 us: body(): jnp.concatenate([qkv_grad, out_weight_grad, d_mod.reshape(-1, width)], ax...]
    slice x7 -> x9, local copies, waits for them, and re-layouts: 3.69 us -> 13.8 us  [the longest x1 6.59 us: wide_sum(): parts[:, lane * shard:(lane + 1) * shard].reshape(-1, width)]
    unnamed x176 -> x212, local copies, waits for them, and re-layouts: 28.5 us -> 20.9 us
  transfers between devices with their start and end apart: 14 -> 18, of which waited for: 6 -> 8; matrix products, arithmetic and copies ran while one was open for 27% -> 39% of each run, Pallas kernels for 0% -> 9%
where the time goes in v2:
time: 655 us; the launch traced here: 648 us
  matrix products  193 us (29%)
  waiting for transfers between devices  157 us (24%)
  other arithmetic  132 us (20%)
  local copies, waits for them, and re-layouts  63.4 us (10%)
  Pallas kernels  59.9 us (9%)
  starting transfers between devices  24.8 us (4%)
  between operations  17.9 us (3%)
    ppermute x12, waiting for transfers between devices, swap(): return lax.ppermute(part, 'narrow', [(0, 1), (1, 0)])  157 us
    dot_general x45, matrix products, dot(): lax.dot_general(left, right, (dims, ((), ())), preferred_element_type=F32)  150 us
    pallas_call x1, Pallas kernels, ring_scatter(): pl.pallas_call(lambda *refs: ring_kernel(chips, subs, *refs), out_shape=j...  59.9 us
    unnamed x212, local copies, waits for them, and re-layouts  20.9 us
    ppermute x12, starting transfers between devices, swap(): return lax.ppermute(part, 'narrow', [(0, 1), (1, 0)])  16.6 us
    dot_general x2, matrix products, body(): jnp.einsum('ihd,jhd->hij', grad_block, value_block, preferred_element_typ...  14.3 us
    convert_element_type x2, other arithmetic, body(): d_scores = (attend * (d_attend - centre)).astype(jnp.bfloat16)  13.2 us
  transfers between devices with their start and end apart: 18, of which 8 were waited for; matrix products, arithmetic and copies ran while one was open for 39% of the time, Pallas kernels for 9%

profile of v2, /device:TPU:0, one launch (start us, length us, event | category | flops | bytes accessed | tf_op | source)
XLA Modules:
  0.0 648.4 jit_solution(15642944492591330551)
XLA Ops:
  8.0 6.0 fusion.22
  33.4 49.0 %collective-permute-done.2 = bf16[576,256,2]{1,0,2:T(8,128)(2,1)} collective-permute-done((bf16[576,256,2]{1,0,2:T(8,128)(2,1)S(1)}, bf16[576,256,2]{1,0,2:T(8,128)(2,1)}, u32[]{:S(2)}, u32[]{:S(2)}) %collective-permute-start.2) | collective-permute-done | bytes 589856 | tf_op jit(solution)/shard_map/ppermute | solution.py:21
  162.9 7.5 %collective-permute-done.6 = bf16[512,1152]{1,0:T(8,128)(2,1)} collective-permute-done((bf16[512,1152]{1,0:T(8,128)(2,1)}, bf16[512,1152]{1,0:T(8,128)(2,1)}, u32[]{:S(2)}, u32[]{:S(2)}) %collective-permute-start.6) | collective-permute-done | bytes 1179680 | tf_op jit(solution)/shard_map/ppermute | solution.py:21
  170.4 25.2 %collective-permute-done.4 = bf16[512,1152]{1,0:T(8,128)(2,1)S(1)} collective-permute-done((bf16[512,1152]{1,0:T(8,128)(2,1)S(1)}, bf16[512,1152]{1,0:T(8,128)(2,1)S(1)}, u32[]{:S(2)}, u32[]{:S(2)}) %collective-permute-start.4) | collective-permute-done | bytes 1179680 | tf_op jit(solution)/shard_map/ppermute | solution.py:21
  236.4 8.0 %fusion.2 = bf16[1152,2304]{0,1:T(8,128)(2,1)} fusion(bf16[512,2304]{1,0:T(8,128)(2,1)S(1)} %copy-done.83, bf16[512,2304]{1,0:T(8,128)(2,1)S(1)} %get-tuple-element.190, bf16[512,1152]{1,0:T(8,128)(2,1)S(1)} %get-tuple-element.147, bf16[512,1152]{1,0:T(8,128)(2,1)S(1)} %get-tuple-element.127), kind=kOutput, calls=%fused_computation.16 | convolution fusion | flops 5452627968 | bytes 12386304 | tf_op jit(solution)/shard_map/dot_general | solution.py:17
  246.5 7.8 %convolution_convert_fusion.5 = bf16[1024,1152]{1,0:T(8,128)(2,1)S(1)} fusion(bf16[2304,1152]{1,0:T(8,128)(2,1)S(1)} %bitcast.260, bf16[512,2304]{1,0:T(8,128)(2,1)S(1)} %copy-done.84, bf16[512,2304]{1,0:T(8,128)(2,1)S(1)} %copy-done.85), kind=kOutput, calls=%fused_computation.61 | convolution fusion | flops 5446434816 | bytes 12386304 | tf_op jit(solution)/shard_map/dot_general | solution.py:17
  258.8 8.0 %convolution_convert_fusion = bf16[2304,1152]{1,0:T(8,128)(2,1)} fusion(bf16[512,2304]{1,0:T(8,128)(2,1)S(1)} %copy-done.84, bf16[512,2304]{1,0:T(8,128)(2,1)S(1)} %copy-done.85, bf16[512,1152]{1,0:T(8,128)(2,1)S(1)} %copy-done.52, bf16[512,1152]{1,0:T(8,128)(2,1)S(1)} %copy-done.51), kind=kOutput, calls=%fused_computation.12 | convolution fusion | flops 5452627968 | bytes 12386304 | tf_op jit(solution)/shard_map/dot_general | solution.py:17
  266.9 6.6 %collective-permute-done.9 = bf16[512,1152]{1,0:T(8,128)(2,1)} collective-permute-done((bf16[512,1152]{1,0:T(8,128)(2,1)S(1)}, bf16[512,1152]{1,0:T(8,128)(2,1)}, u32[]{:S(2)}, u32[]{:S(2)}) %collective-permute-start.9) | collective-permute-done | bytes 1179680 | tf_op jit(solution)/shard_map/ppermute | solution.py:21
  273.4 25.3 %collective-permute-done.8 = bf16[512,1152]{1,0:T(8,128)(2,1)} collective-permute-done((bf16[512,1152]{1,0:T(8,128)(2,1)}, bf16[512,1152]{1,0:T(8,128)(2,1)}, u32[]{:S(2)}, u32[]{:S(2)}) %collective-permute-start.8) | collective-permute-done | bytes 1179680 | tf_op jit(solution)/shard_map/ppermute | solution.py:21
  298.7 8.1 %fusion.142 = (f32[512]{0:T(512)S(1)}, f32[512]{0:T(512)S(1)}, f32[512]{0:T(512)S(1)}, f32[512]{0:T(512)S(1)}, f32[512,1152]{1,0:T(8,128)}, /*index=5*/f32[512,1152]{1,0:T(8,128)}) fusion(f32[1024,1152]{1,0:T(8,128)} %copy-done.4, bf16[512,1152]{1,0:T(8,128)(2,1)} %collective-permute-done.9, bf16[512,1152]{1,0:T(8,128)(2,1)S(1)} %convolution_convert_fusion.14, ...), kind=kLoop, calls=%fused_computation.333 | loop fusion | flops 9435136 | bytes 18882560 | tf_op jit(solution)/shard_map/reduce_sum | solution.py:197
  306.9 12.4 %fusion.153 = (bf16[1152]{0:T(1024)(128)(2,1)S(1)}, bf16[512,1152]{1,0:T(8,128)(2,1)}, f32[512,1152]{1,0:T(8,128)}, bf16[1152]{0:T(1024)(128)(2,1)S(1)}, bf16[512,1152]{1,0:T(8,128)(2,1)S(1)}, /*index=5*/f32[512,1152]{1,0:T(8,128)}) fusion(f32[1024,1152]{1,0:T(8,128)} %convert_multiply_fusion.1, f32[512,1152]{1,0:T(8,128)S(1)} %copy-done.10, ...), kind=kLoop, calls=%fused_computation.337 | loop fusion | flops 15333120 | bytes 30687744 | tf_op jit(solution)/shard_map/reduce_sum | solution.py:452
  323.7 7.9 %multiply_reduce_fusion.1 = (f32[8,512]{1,0:T(8,128)S(1)}, f32[8,512,768]{2,1,0:T(8,128)}) fusion(f32[8,512,768]{2,1,0:T(8,128)S(1)} %bitcast.217, f32[8,512]{1,0:T(8,128)S(1)} %log_add_fusion.1, bf16[512,8,72]{0,2,1:T(8,128)(2,1)S(1)} %bitcast.250, bf16[768,8,72]{0,2,1:T(8,128)(2,1)} %bitcast.248), kind=kOutput, calls=%fused_computation.4 | convolution fusion | flops 462417920 | bytes 26673152 | tf_op jit(solution)/shard_map/ihd,jhd->hij/dot_general | solution.py:404
  337.4 6.4 multiply_reduce_fusion
  343.8 6.6 %multiply_convert_fusion = bf16[8,512,768]{2,1,0:T(8,128)(2,1)S(1)} fusion(f32[8,512,768]{2,1,0:T(8,128)} %get-tuple-element.188, f32[8,512,768]{2,1,0:T(8,128)S(1)} %bitcast.215, f32[8,512]{1,0:T(8,128)S(1)} %get-tuple-element.187, f32[8,512]{1,0:T(8,128)S(1)} %log_add_fusion), kind=kLoop, calls=%fused_computation | loop fusion | flops 12582912 | bytes 31490048 | tf_op jit(solution)/shard_map/convert_element_type | solution.py:408
  354.5 6.5 %multiply_convert_fusion.1 = bf16[8,512,768]{2,1,0:T(8,128)(2,1)S(1)} fusion(f32[8,512,768]{2,1,0:T(8,128)} %get-tuple-element.186, f32[8,512,768]{2,1,0:T(8,128)S(1)} %bitcast.217, f32[8,512]{1,0:T(8,128)S(1)} %get-tuple-element.185, f32[8,512]{1,0:T(8,128)S(1)} %log_add_fusion.1), kind=kLoop, calls=%fused_computation.3 | loop fusion | flops 12582912 | bytes 31490048 | tf_op jit(solution)/shard_map/convert_element_type | solution.py:408
  403.5 8.7 %convolution_convert_fusion.6 = bf16[1024,1152]{1,0:T(8,128)(2,1)S(1)} fusion(bf16[1152,1728]{0,1:T(8,128)(2,1)} %bitcast.261, bf16[1024,1152]{0,1:T(8,128)(2,1)} %copy-done.39, bf16[512,576]{0,1:T(8,128)(2,1)S(1)} %bitcast.254, bf16[512,576]{0,1:T(8,128)(2,1)S(1)} %bitcast.256), kind=kOutput, calls=%fused_computation.62 | convolution fusion | flops 4088659968 | bytes 9879552 | tf_op jit(solution)/shard_map/dot_general | solution.py:17
  421.1 9.9 %convolution_convert_fusion.2 = bf16[1728,1152]{1,0:T(8,128)(2,1)} fusion(bf16[1024,1152]{1,0:T(8,128)(2,1)} %copy-done.82, bf16[1024,1152]{0,1:T(8,128)(2,1)} %copy-done.39, bf16[512,576]{0,1:T(8,128)(2,1)} %bitcast.253, bf16[512,576]{0,1:T(8,128)(2,1)} %bitcast.255), kind=kOutput, calls=%fused_computation.21 | convolution fusion | flops 4089470976 | bytes 9879552 | tf_op jit(solution)/shard_map/dot_general | solution.py:17
  448.4 59.9 %ring_scatter.1 = bf16[2,96,1152]{2,1,0:T(8,128)(2,1)S(1)} custom-call(bf16[2,8,2,96,1152]{4,3,2,1,0:T(8,128)(2,1)S(1)} %bitcast.212), custom_call_target="tpu_custom_call" | custom-call | tf_op jit(solution)/shard_map/ring_scatter/pallas_call | solution.py:153
  519.2 21.5 %collective-permute-done.7 = bf16[512,1152]{1,0:T(8,128)(2,1)} collective-permute-done((bf16[512,1152]{1,0:T(8,128)(2,1)}, bf16[512,1152]{1,0:T(8,128)(2,1)}, u32[]{:S(2)}, u32[]{:S(2)}) %collective-permute-start.7) | collective-permute-done | bytes 1179680 | tf_op jit(solution)/shard_map/ppermute | solution.py:21
  545.2 19.2 %collective-permute-done.12 = bf16[512,1152]{1,0:T(8,128)(2,1)S(1)} collective-permute-done((bf16[512,1152]{1,0:T(8,128)(2,1)S(1)}, bf16[512,1152]{1,0:T(8,128)(2,1)S(1)}, u32[]{:S(2)}, u32[]{:S(2)}) %collective-permute-start.12) | collective-permute-done | bytes 1179680 | tf_op jit(solution)/shard_map/ppermute | solution.py:21
  567.6 9.5 %copy.56 = f32[1152,2304]{1,0:T(8,128)} copy(bf16[1152,2304]{0,1:T(8,128)(2,1)} %get-tuple-element.113) | data formatting | bytes 15925248
  577.1 7.3 %convert_element_type.473 = f32[2304,1152]{1,0:T(8,128)} convert(bf16[2304,1152]{1,0:T(8,128)(2,1)} %get-tuple-element.114) | non-fusion elementwise | flops 2654208 | bytes 15925248 | tf_op jit(solution)/shard_map/convert_element_type | solution.py:362
  595.7 6.6 %fusion.161 = (bf16[16,96,1152]{2,1,0:T(8,128)(2,1)}, bf16[16,96,1152]{2,1,0:T(8,128)(2,1)}) fusion(bf16[16,200,1152]{2,1,0:T(8,128)(2,1)} %bitcast.227), kind=kLoop, calls=%fused_computation.343 | loop fusion | bytes 14155776 | tf_op jit(solution)/shard_map/slice | solution.py:184
  630.6 6.0 fusion.18
  (402 shorter events, 290.4 us)
Async XLA Ops:
  7.2 132.2 %copy-start = (bf16[576,1152]{1,0:T(8,128)(2,1)S(1)}, bf16[576,1152]{1,0:T(8,128)(2,1)}, u32[]{:S(2)}) copy-start(bf16[576,1152]{1,0:T(8,128)(2,1)} %param.28) | copy-start | bytes 3981316
  7.2 560.4 %all-reduce.5.cloned.1.call-start = ((), (), s32[]{:S(2)}) async-start(), calls=%async_computation.1 | async-start | bytes 21233664 | tf_op jit(solution)/shard_map/psum | solution.py:360
  15.3 69.6 %collective-permute-start.1 = (bf16[576,256,4]{1,0,2:T(8,128)(2,1)}, bf16[576,256,4]{1,0,2:T(8,128)(2,1)}, u32[]{:S(2)}, u32[]{:S(2)}) collective-permute-start(bf16[576,256,4]{1,0,2:T(8,128)(2,1)} %slice.384), channel_id=1, source_target_pairs={{0,1},{1,0},{2,3},{3,2},{4,5},{5,4},{6,7},{7,6},{8,9},{9,8},{10,11... | collective-permute-start | bytes 3538952 | tf_op jit(solution)/shard_map/ppermute | solution.py:21
  18.2 74.9 %collective-permute-start = (bf16[512,1152]{1,0:T(8,128)(2,1)S(1)}, bf16[512,1152]{1,0:T(8,128)(2,1)}, u32[]{:S(2)}, u32[]{:S(2)}) collective-permute-start(bf16[512,1152]{1,0:T(8,128)(2,1)S(1)} %copy-done.15), channel_id=1, source_target_pairs={{0,1},{1,0},{2,3},{3,2},{4,5},{5,4},{6,7},{7,6},{8,9},{9,8},{10,11... | collective-permute-start | bytes 3538952 | tf_op jit(solution)/shard_map/ppermute | solution.py:21
  18.8 63.6 %collective-permute-start.2 = (bf16[576,256,2]{1,0,2:T(8,128)(2,1)S(1)}, bf16[576,256,2]{1,0,2:T(8,128)(2,1)}, u32[]{:S(2)}, u32[]{:S(2)}) collective-permute-start(bf16[576,256,2]{1,0,2:T(8,128)(2,1)S(1)} %slice.387), channel_id=1, source_target_pairs={{0,1},{1,0},{2,3},{3,2},{4,5},{5,4},{6,7},{7,6},{8,9},{9,8},{10,11... | collective-permute-start | bytes 1769480 | tf_op jit(solution)/shard_map/ppermute | solution.py:21
  21.6 70.6 %copy-start.61 = (f32[1024]{0:T(1024)}, f32[1024]{0:T(1024)S(1)}, u32[]{:S(2)}) copy-start(f32[1024]{0:T(1024)S(1)} %fusion.135) | copy-start | bytes 12292
  111.3 10.3 %collective-permute-start.5 = (bf16[128,1152]{0,1:T(8,128)(2,1)S(1)}, bf16[128,1152]{0,1:T(8,128)(2,1)S(1)}, u32[]{:S(2)}, u32[]{:S(2)}) collective-permute-start(bf16[128,1152]{0,1:T(8,128)(2,1)S(1)} %get-tuple-element.161), channel_id=1, source_target_pairs={{2,0},{4,2},{6,4},{8,6},{10,8},{12,10},{14,12},{16,14},{18,16},{20... | collective-permute-start | bytes 884744 | tf_op jit(solution)/shard_map/ppermute | solution.py:57
  112.7 8.9 %collective-permute-start.3 = (bf16[128,1152]{0,1:T(8,128)(2,1)S(1)}, bf16[128,1152]{0,1:T(8,128)(2,1)S(1)}, u32[]{:S(2)}, u32[]{:S(2)}) collective-permute-start(bf16[128,1152]{0,1:T(8,128)(2,1)S(1)} %get-tuple-element.162), channel_id=1, source_target_pairs={{0,2},{2,4},{4,6},{6,8},{8,10},{10,12},{12,14},{14,16},{16,18},{18... | collective-permute-start | bytes 884744 | tf_op jit(solution)/shard_map/ppermute | solution.py:56
  141.6 28.8 %collective-permute-start.6 = (bf16[512,1152]{1,0:T(8,128)(2,1)}, bf16[512,1152]{1,0:T(8,128)(2,1)}, u32[]{:S(2)}, u32[]{:S(2)}) collective-permute-start(bf16[512,1152]{1,0:T(8,128)(2,1)} %convolution_convert_fusion.16), channel_id=1, source_target_pairs={{0,1},{1,0},{2,3},{3,2},{4,5},{5,4},{6,7},{7,6},{8,9},{9,8},{10,11... | collective-permute-start | bytes 3538952 | tf_op jit(solution)/shard_map/ppermute | solution.py:21
  156.5 39.0 %collective-permute-start.4 = (bf16[512,1152]{1,0:T(8,128)(2,1)S(1)}, bf16[512,1152]{1,0:T(8,128)(2,1)S(1)}, u32[]{:S(2)}, u32[]{:S(2)}) collective-permute-start(bf16[512,1152]{1,0:T(8,128)(2,1)S(1)} %convolution_convert_fusion.17), channel_id=1, source_target_pairs={{0,1},{1,0},{2,3},{3,2},{4,5},{5,4},{6,7},{7,6},{8,9},{9,8},{10,11... | collective-permute-start | bytes 3538952 | tf_op jit(solution)/shard_map/ppermute | solution.py:21
  227.0 71.7 %copy-start.41 = (bf16[512,1152]{1,0:T(8,128)(2,1)}, bf16[512,1152]{1,0:T(8,128)(2,1)S(1)}, u32[]{:S(2)}) copy-start(bf16[512,1152]{1,0:T(8,128)(2,1)S(1)} %convolution_convert_fusion.14) | copy-start | bytes 3538948
  244.5 28.9 %collective-permute-start.9 = (bf16[512,1152]{1,0:T(8,128)(2,1)S(1)}, bf16[512,1152]{1,0:T(8,128)(2,1)}, u32[]{:S(2)}, u32[]{:S(2)}) collective-permute-start(bf16[512,1152]{1,0:T(8,128)(2,1)S(1)} %convolution_convert_fusion.14), channel_id=1, source_target_pairs={{0,1},{1,0},{2,3},{3,2},{4,5},{5,4},{6,7},{7,6},{8,9},{9,8},{10,11... | collective-permute-start | bytes 3538952 | tf_op jit(solution)/shard_map/ppermute | solution.py:21
  246.5 52.2 %collective-permute-start.8 = (bf16[512,1152]{1,0:T(8,128)(2,1)}, bf16[512,1152]{1,0:T(8,128)(2,1)}, u32[]{:S(2)}, u32[]{:S(2)}) collective-permute-start(bf16[512,1152]{1,0:T(8,128)(2,1)} %convolution_convert_fusion.15), channel_id=1, source_target_pairs={{0,1},{1,0},{2,3},{3,2},{4,5},{5,4},{6,7},{7,6},{8,9},{9,8},{10,11... | collective-permute-start | bytes 3538952 | tf_op jit(solution)/shard_map/ppermute | solution.py:21
  256.8 181.9 %collective-permute-start.14 = (bf16[256,576]{1,0:T(8,128)(2,1)}, bf16[256,576]{1,0:T(8,128)(2,1)}, u32[]{:S(2)}, u32[]{:S(2)}) collective-permute-start(bf16[256,576]{1,0:T(8,128)(2,1)} %constant_dynamic-slice_fusion), channel_id=1, source_target_pairs={{0,1},{1,0},{2,3},{3,2},{4,5},{5,4},{6,7},{7,6},{8,9},{9,8},{10,11... | collective-permute-start | bytes 884744 | tf_op jit(solution)/shard_map/ppermute | solution.py:21
  266.8 317.6 %all-gather.3.cloned.1.call-start = ((), (), s32[]{:S(2)}) async-start(), calls=%async_computation | async-start | bytes 7833600 | tf_op jit(solution)/shard_map/all_gather | solution.py:183
  370.9 18.9 %collective-permute-start.10 = (bf16[128,1152]{0,1:T(8,128)(2,1)}, bf16[128,1152]{0,1:T(8,128)(2,1)}, u32[]{:S(2)}, u32[]{:S(2)}) collective-permute-start(bf16[128,1152]{0,1:T(8,128)(2,1)} %slice.565), channel_id=1, source_target_pairs={{0,2},{2,4},{4,6},{6,8},{8,10},{10,12},{12,14},{14,16},{16,18},{18... | collective-permute-start | bytes 884744 | tf_op jit(solution)/shard_map/ppermute | solution.py:56
  373.9 17.9 %collective-permute-start.11 = (bf16[128,1152]{0,1:T(8,128)(2,1)}, bf16[128,1152]{0,1:T(8,128)(2,1)}, u32[]{:S(2)}, u32[]{:S(2)}) collective-permute-start(bf16[128,1152]{0,1:T(8,128)(2,1)} %slice.564), channel_id=1, source_target_pairs={{2,0},{4,2},{6,4},{8,6},{10,8},{12,10},{14,12},{16,14},{18,16},{20... | collective-permute-start | bytes 884744 | tf_op jit(solution)/shard_map/ppermute | solution.py:57
  419.2 14.6 %collective-permute-start.13 = (bf16[2,256,576]{1,2,0:T(8,128)(2,1)}, bf16[2,256,576]{1,2,0:T(8,128)(2,1)}, u32[]{:S(2)}, u32[]{:S(2)}) collective-permute-start(bf16[2,256,576]{1,2,0:T(8,128)(2,1)} %copy.51), channel_id=1, source_target_pairs={{0,1},{1,0},{2,3},{3,2},{4,5},{5,4},{6,7},{7,6},{8,9},{9,8},{10,11... | collective-permute-start | bytes 1769480 | tf_op jit(solution)/shard_map/ppermute | solution.py:21
  511.6 29.2 %collective-permute-start.7 = (bf16[512,1152]{1,0:T(8,128)(2,1)}, bf16[512,1152]{1,0:T(8,128)(2,1)}, u32[]{:S(2)}, u32[]{:S(2)}) collective-permute-start(bf16[512,1152]{1,0:T(8,128)(2,1)} %constant_dynamic-slice_fusion.2), channel_id=1, source_target_pairs={{0,1},{1,0},{2,3},{3,2},{4,5},{5,4},{6,7},{7,6},{8,9},{9,8},{10,11... | collective-permute-start | bytes 3538952 | tf_op jit(solution)/shard_map/ppermute | solution.py:21
  514.6 49.8 %collective-permute-start.12 = (bf16[512,1152]{1,0:T(8,128)(2,1)S(1)}, bf16[512,1152]{1,0:T(8,128)(2,1)S(1)}, u32[]{:S(2)}, u32[]{:S(2)}) collective-permute-start(bf16[512,1152]{1,0:T(8,128)(2,1)S(1)} %constant_dynamic-slice_fusion.1), channel_id=1, source_target_pairs={{0,1},{1,0},{2,3},{3,2},{4,5},{5,4},{6,7},{7,6},{8,9},{9,8},{10,11... | collective-permute-start | bytes 3538952 | tf_op jit(solution)/shard_map/ppermute | solution.py:21
  515.2 49.2 %slice-start.10 = ((s8[4718592]{0:T(1024)(128)(4,1)}), s8[4194304]{0:T(1024)(128)(4,1)S(1)}, s32[]{:S(2)}) async-start(s8[4718592]{0:T(1024)(128)(4,1)} %bitcast.222), calls=%async_computation.12 | async-start | bytes 8388608
  519.2 45.2 %slice-start.11 = ((s8[4718592]{0:T(1024)(128)(4,1)}), s8[524288]{0:T(1024)(128)(4,1)S(1)}, s32[]{:S(2)}) async-start(s8[4718592]{0:T(1024)(128)(4,1)} %bitcast.222), calls=%async_computation.13 | async-start | bytes 1048576
  519.2 45.2 %copy-start.38 = (bf16[1024,1152]{1,0:T(8,128)(2,1)S(1)}, bf16[1024,1152]{1,0:T(8,128)(2,1)}, u32[]{:S(2)}) copy-start(bf16[1024,1152]{1,0:T(8,128)(2,1)} %copy-done.37) | copy-start | bytes 7077892
  617.4 21.6 %collective-permute-start.15 = (bf16[256,1152]{1,0:T(8,128)(2,1)}, bf16[256,1152]{1,0:T(8,128)(2,1)}, u32[]{:S(2)}, u32[]{:S(2)}) collective-permute-start(bf16[256,1152]{1,0:T(8,128)(2,1)} %fusion.31), channel_id=1, source_target_pairs={{0,1},{1,0},{2,3},{3,2},{4,5},{5,4},{6,7},{7,6},{8,9},{9,8},{10,11... | collective-permute-start | bytes 1769480 | tf_op jit(solution)/shard_map/ppermute | solution.py:21
  (99 other events, 876.0 us)
Sparse Core Ops, SparseCore 0:
  266.9 220.4 all-reduce.4
  509.3 67.8 all-gather.2

commit v3 on v2

--- a/solution.py
+++ b/solution.py
@@ -48,21 +48,16 @@
     return mine.astype(F32) + swap(theirs).astype(F32)
 
 
-def padded(cells, width):
-    count = lax.axis_size("wide")
-    ends = count - 1
-    tail = cells[cells.shape[0] - width :]
-    return (
-        lax.ppermute(tail, "wide", [(i, (i + 1) % count) for i in range(ends)]),
-        lax.ppermute(cells[:width], "wide", [((i + 1) % count, i) for i in range(ends)]),
-    )
-
-
 MESH = pl.DeviceIdType.MESH
 UNIT = 48
 
 
-def ring_kernel(chips, subs, data, out, mine, theirs, slots, copy_sems, core_sems, ring_sems):
+def ring_kernel(chips, subs, swapped, *refs):
+    data = refs[:2]
+    out, mine, theirs, slots, copy_sems, core_sems, ring_sems = refs[2 + swapped :][:7]
+    if swapped:
+        part, (out, landing, *rest) = refs[2], refs[3:]
+        mine, theirs, slots, copy_sems, core_sems, ring_sems, swap_sems = rest
     wide = lax.axis_index("wide")
     chip, core = wide // 2, wide % 2
     half = chips // 2
@@ -79,14 +74,28 @@
     barrier = pltpu.get_barrier_semaphore()
     for device in (ahead, behind, sibling):
         pl.semaphore_signal(barrier, inc=1, device_id={"wide": device}, device_id_type=MESH)
-    pl.semaphore_wait(barrier, 3)
+    if swapped:
+        facing = 1 - lax.axis_index("narrow")
+        pl.semaphore_signal(barrier, inc=1, device_id={"narrow": facing}, device_id_type=MESH)
+    pl.semaphore_wait(barrier, 3 + swapped)
+    if swapped:
+        share = landing.shape[0]
+        turn = pltpu.make_async_remote_copy(
+            src_ref=part.at[pl.ds(facing * share, share)],
+            dst_ref=landing,
+            send_sem=swap_sems.at[0],
+            recv_sem=swap_sems.at[1],
+            device_id={"narrow": facing},
+            device_id_type=MESH,
+        )
+        turn.start()
 
     def local(lane):
-        return pltpu.make_async_copy(data.at[lane, :, core], mine.at[lane], copy_sems.at[lane])
+        return pltpu.make_async_copy(data[lane].at[:, core], mine.at[lane], copy_sems.at[lane])
 
     def across(lane):
         return pltpu.make_async_remote_copy(
-            src_ref=data.at[lane, :, 1 - core],
+            src_ref=data[lane].at[:, 1 - core],
             dst_ref=theirs.at[lane],
             send_sem=core_sems.at[0, lane],
             recv_sem=core_sems.at[1, lane],
@@ -142,47 +151,278 @@
         for sub in range(subs):
             for lane in range(2):
                 hop(lane, step, sub).wait_send()
-
-
-def ring_scatter(flat, collective_id):
+    if swapped:
+        turn.wait()
+
+
+def ring_scatter(lanes, part, collective_id):
     chips = lax.axis_size("wide") // 2
-    shard = flat.shape[0] // (4 * chips)
-    width = flat.shape[1]
+    rows, width = lanes[0].shape
+    shard = rows // (2 * chips)
     subs = shard // UNIT
-    data = flat.reshape(2, chips, 2, shard, width)
+    operands = [lane.reshape(chips, 2, shard, width) for lane in lanes]
+    shapes = [jax.ShapeDtypeStruct((2, shard, width), BF16)]
+    specs = [pl.BlockSpec(memory_space=pltpu.VMEM)]
+    scratch = [
+        pltpu.VMEM((2, chips, shard, width), BF16),
+        pltpu.VMEM((2, chips, shard, width), BF16),
+        pltpu.VMEM((2, chips - 1, shard, width), BF16),
+        pltpu.SemaphoreType.DMA((2,)),
+        pltpu.SemaphoreType.DMA((2, 2)),
+        pltpu.SemaphoreType.DMA((2, 2, chips - 1, subs)),
+    ]
+    if part is not None:
+        operands.append(part)
+        shapes.append(jax.ShapeDtypeStruct((part.shape[0] // 2, part.shape[1]), BF16))
+        specs.append(pl.BlockSpec(memory_space=pl.ANY))
+        scratch.append(pltpu.SemaphoreType.DMA((2,)))
     return pl.pallas_call(
-        lambda *refs: ring_kernel(chips, subs, *refs),
-        out_shape=jax.ShapeDtypeStruct((2, shard, width), BF16),
-        in_specs=[pl.BlockSpec(memory_space=pl.ANY)],
-        out_specs=pl.BlockSpec(memory_space=pltpu.VMEM),
-        scratch_shapes=[
-            pltpu.VMEM((2, chips, shard, width), BF16),
-            pltpu.VMEM((2, chips, shard, width), BF16),
-            pltpu.VMEM((2, chips - 1, shard, width), BF16),
-            pltpu.SemaphoreType.DMA((2,)),
-            pltpu.SemaphoreType.DMA((2, 2)),
-            pltpu.SemaphoreType.DMA((2, 2, chips - 1, subs)),
-        ],
+        lambda *refs: ring_kernel(chips, subs, int(part is not None), *refs),
+        out_shape=shapes,
+        in_specs=[pl.BlockSpec(memory_space=pl.ANY)] * len(operands),
+        out_specs=specs,
+        scratch_shapes=scratch,
         compiler_params=pltpu.CompilerParams(
             collective_id=collective_id, has_side_effects=True, vmem_limit_bytes=40 << 20
         ),
         name="ring_scatter",
-    )(data)
-
-
-def wide_sum(flat, loose, collective_id):
+    )(*operands)
+
+
+def ring_fits(lanes):
     count = lax.axis_size("wide")
-    rows, width = flat.shape
-    if lax.axis_size("narrow") != 2 or rows % (2 * count * UNIT):
-        return lax.psum(flat, "wide"), jnp.sum(
-            lax.all_gather(loose, "wide", axis=0).astype(F32), axis=0
-        )
-    mine = ring_scatter(flat, collective_id)
-    shard = rows // (2 * count)
-    parts = jnp.concatenate([mine.reshape(2 * shard, width), loose], axis=0)
+    return lax.axis_size("narrow") == 2 and lanes[0].shape[0] % (count * UNIT) == 0
+
+
+def wide_gather(mine, loose):
+    shard, width = mine.shape[1:]
+    parts = mine.reshape(2 * shard, width)
+    if loose is not None:
+        parts = jnp.concatenate([parts, loose], axis=0)
     parts = lax.all_gather(parts, "wide", axis=0)
     lanes = [parts[:, lane * shard : (lane + 1) * shard].reshape(-1, width) for lane in range(2)]
-    return jnp.concatenate(lanes, axis=0), jnp.sum(parts[:, 2 * shard :].astype(F32), axis=0)
+    return lanes, parts[:, 2 * shard :].astype(F32)
+
+
+TILE = 256
+LOG2E = 1.4426950408889634
+
+
+def head_lanes(part_width):
+    for head in range(part_width // HD):
+        lo = head * HD // 128 * 128
+        hi = min(-(-(head + 1) * HD // 128) * 128, part_width)
+        lanes = lax.broadcasted_iota(jnp.int32, (1, hi - lo), 1) + lo
+        yield head, lo, hi, (lanes >= head * HD) & (lanes < (head + 1) * HD)
+
+
+def extend(first, left, own, right, ext):
+    span = left.shape[1]
+    ends = ext.shape[1] - span
+
+    @pl.when(first)
+    def _():
+        for which in range(2):
+            ext[which, :span] = left[which]
+            ext[which, span:ends] = own[which][...]
+            ext[which, ends:] = right[which]
+
+
+def forward_kernel(tiles, q, k, v, left, right, q_ids, k_ids, out, lse, ext, total):
+    tile = pl.program_id(0)
+    part_width = q.shape[1]
+    span = left.shape[1]
+    ends = ext.shape[1] - span
+    extend(tile == 0, left, (k, v), right, ext)
+    scale = LOG2E * HD ** (-0.5)
+
+    def run(extra):
+        rows = pl.ds(pl.multiple_of(tile * TILE, TILE), TILE + 2 * span)
+        keys, values = ext[0, rows], ext[1, rows]
+        ids = k_ids[:, rows]
+        if extra:
+            keys = jnp.concatenate([keys, ext[0, ends:]], axis=0)
+            values = jnp.concatenate([values, ext[1, ends:]], axis=0)
+            ids = jnp.concatenate([ids, k_ids[:, ends:]], axis=1)
+        same = q_ids[...] == ids
+        queries = q[...]
+        total[...] = jnp.zeros_like(total)
+        packed = jnp.zeros((TILE, 128), F32)
+        column = lax.broadcasted_iota(jnp.int32, (TILE, 128), 1)
+        for head, lo, hi, mask in head_lanes(part_width):
+            chosen = jnp.where(mask, queries[:, lo:hi], 0)
+            scores = lax.dot_general(
+                chosen, keys[:, lo:hi], (((1,), (1,)), ((), ())), preferred_element_type=F32
+            )
+            scores = jnp.where(same, scores * scale, NEG_FILL)
+            top = jnp.max(scores, axis=1, keepdims=True)
+            expo = jnp.exp2(scores - top)
+            count = jnp.sum(expo, axis=1, keepdims=True)
+            part = jnp.dot(expo.astype(BF16), values[:, lo:hi], preferred_element_type=F32)
+            total[:, lo:hi] += jnp.where(mask, part / count, 0.0)
+            packed = jnp.where(column == head, top + jnp.log2(count), packed)
+        out[...] = total[...].astype(BF16)
+        lse[...] = packed.T[: lse.shape[0]]
+
+    split_tiles(tile, tiles, run)
+
+
+def split_tiles(tile, tiles, run):
+    first_extra = tiles - 512 // TILE
+    extra = (tile >= first_extra) & (tile < tiles - 1)
+    pl.when(extra)(lambda: run(True))
+    pl.when(jnp.logical_not(extra))(lambda: run(False))
+
+
+def rim_specs(part_width, span, tok_dev):
+    whole = lambda shape: pl.BlockSpec(shape, lambda i: (0,) * len(shape))
+    return whole((tok_dev, part_width)), whole((2, span, part_width))
+
+
+def attention_forward(q, k, v, left, right, q_ids, k_ids):
+    tok_dev, part_width = q.shape
+    span = left.shape[1]
+    tiles = tok_dev // TILE
+    head_rows = -(-(part_width // HD) // 8) * 8
+    own_spec, rim_spec = rim_specs(part_width, span, tok_dev)
+    return pl.pallas_call(
+        lambda *refs: forward_kernel(tiles, *refs),
+        grid=(tiles,),
+        out_shape=[
+            jax.ShapeDtypeStruct((tok_dev, part_width), BF16),
+            jax.ShapeDtypeStruct((head_rows, tok_dev), F32),
+        ],
+        in_specs=[
+            pl.BlockSpec((TILE, part_width), lambda i: (i, 0)),
+            own_spec,
+            own_spec,
+            rim_spec,
+            rim_spec,
+            pl.BlockSpec((TILE, 1), lambda i: (i, 0)),
+            pl.BlockSpec((1, tok_dev + 2 * span), lambda i: (0, 0)),
+        ],
+        out_specs=[
+            pl.BlockSpec((TILE, part_width), lambda i: (i, 0)),
+            pl.BlockSpec((head_rows, TILE), lambda i: (0, i)),
+        ],
+        scratch_shapes=[
+            pltpu.VMEM((2, tok_dev + 2 * span, part_width), BF16),
+            pltpu.VMEM((TILE, part_width), F32),
+        ],
+        compiler_params=pltpu.CompilerParams(vmem_limit_bytes=40 << 20),
+        cost_estimate=pl.CostEstimate(
+            flops=4 * tok_dev * 512 * part_width,
+            transcendentals=tok_dev * 512 * 8,
+            bytes_accessed=8 * tok_dev * part_width,
+        ),
+        name="attention_forward",
+    )(q, k, v, left, right, q_ids, k_ids)
+
+
+def backward_kernel(tiles, q, k, v, left, right, grad, lse, q_ids, k_ids, *refs):
+    d_q, d_own, d_rim, ext, d_ext, total = refs
+    tile = pl.program_id(0)
+    part_width = q.shape[1]
+    span = left.shape[1]
+    ends = ext.shape[1] - span
+    extend(tile == 0, left, (k, v), right, ext)
+    scale = HD ** (-0.5)
+
+    @pl.when(tile == 0)
+    def _():
+        d_ext[...] = jnp.zeros_like(d_ext)
+
+    def run(extra):
+        rows = pl.ds(pl.multiple_of(tile * TILE, TILE), TILE + 2 * span)
+        keys, values = ext[0, rows], ext[1, rows]
+        ids = k_ids[rows]
+        if extra:
+            keys = jnp.concatenate([keys, ext[0, ends:]], axis=0)
+            values = jnp.concatenate([values, ext[1, ends:]], axis=0)
+            ids = jnp.concatenate([ids, k_ids[ends:]], axis=0)
+        same = ids == q_ids[...]
+        queries, grads = q[...], grad[...]
+        total[...] = jnp.zeros_like(total)
+
+        def across(left_side, right_side, dims):
+            return lax.dot_general(
+                left_side, right_side, (dims, ((), ())), preferred_element_type=F32
+            )
+
+        for head, lo, hi, mask in head_lanes(part_width):
+            chosen = jnp.where(mask, queries[:, lo:hi], 0)
+            pulled = jnp.where(mask, grads[:, lo:hi], 0)
+            scores = across(keys[:, lo:hi], chosen, ((1,), (1,)))
+            scores = jnp.where(same, scores * (scale * LOG2E), NEG_FILL)
+            attend = jnp.exp2(scores - lse[head : head + 1])
+            d_attend = across(values[:, lo:hi], pulled, ((1,), (1,)))
+            centre = jnp.sum(attend * d_attend, axis=0, keepdims=True)
+            d_scores = (attend * (d_attend - centre)).astype(BF16)
+            d_key = across(d_scores, chosen, ((1,), (0,)))
+            d_value = across(attend.astype(BF16), pulled, ((1,), (0,)))
+            length = TILE + 2 * span
+            d_ext[0, rows, lo:hi] += d_key[:length]
+            d_ext[1, rows, lo:hi] += d_value[:length]
+            if extra:
+                d_ext[0, ends:, lo:hi] += d_key[length:]
+                d_ext[1, ends:, lo:hi] += d_value[length:]
+            d_query = across(d_scores, keys[:, lo:hi], ((0,), (0,)))
+            total[:, lo:hi] += jnp.where(mask, d_query, 0.0)
+        d_q[...] = (total[...] * scale).astype(BF16)
+
+    split_tiles(tile, tiles, run)
+
+    @pl.when(tile == tiles - 1)
+    def _():
+        for which, factor in ((0, scale), (1, 1.0)):
+            d_rim[0, which] = (d_ext[which, :span] * factor).astype(BF16)
+            d_own[which] = (d_ext[which, span:ends] * factor).astype(BF16)
+            d_rim[1, which] = (d_ext[which, ends:] * factor).astype(BF16)
+
+
+def attention_backward(q, k, v, left, right, grad, lse, q_ids, k_ids):
+    tok_dev, part_width = q.shape
+    span = left.shape[1]
+    tiles = tok_dev // TILE
+    own_spec, rim_spec = rim_specs(part_width, span, tok_dev)
+    tile_spec = pl.BlockSpec((TILE, part_width), lambda i: (i, 0))
+    return pl.pallas_call(
+        lambda *refs: backward_kernel(tiles, *refs),
+        grid=(tiles,),
+        out_shape=[
+            jax.ShapeDtypeStruct((tok_dev, part_width), BF16),
+            jax.ShapeDtypeStruct((2, tok_dev, part_width), BF16),
+            jax.ShapeDtypeStruct((2, 2, span, part_width), BF16),
+        ],
+        in_specs=[
+            tile_spec,
+            own_spec,
+            own_spec,
+            rim_spec,
+            rim_spec,
+            tile_spec,
+            pl.BlockSpec((lse.shape[0], TILE), lambda i: (0, i)),
+            pl.BlockSpec((1, TILE), lambda i: (0, i)),
+            pl.BlockSpec((tok_dev + 2 * span, 1), lambda i: (0, 0)),
+        ],
+        out_specs=[
+            tile_spec,
+            pl.BlockSpec((2, tok_dev, part_width), lambda i: (0, 0, 0)),
+            pl.BlockSpec((2, 2, span, part_width), lambda i: (0, 0, 0, 0)),
+        ],
+        scratch_shapes=[
+            pltpu.VMEM((2, tok_dev + 2 * span, part_width), BF16),
+            pltpu.VMEM((2, tok_dev + 2 * span, part_width), F32),
+            pltpu.VMEM((TILE, part_width), F32),
+        ],
+        compiler_params=pltpu.CompilerParams(vmem_limit_bytes=48 << 20),
+        cost_estimate=pl.CostEstimate(
+            flops=10 * tok_dev * 512 * part_width,
+            transcendentals=tok_dev * 512 * 8,
+            bytes_accessed=16 * tok_dev * part_width,
+        ),
+        name="attention_backward",
+    )(q, k, v, left, right, grad, lse, q_ids, k_ids)
 
 
 def norm(field):
@@ -232,12 +472,9 @@
     share = tokens.shape[0]
     width = tokens.shape[1]
     part_width = qkv_weight.shape[2]
-    heads = part_width // HD
     img_row = condition.shape[0]
     span = IMG_MAX
     block = min(512, tok_dev)
-    window = block + 2 * span
-    scale_factor = HD ** (-0.5)
     own_count = valid_counts[wide_index]
     positions = jnp.arange(tok_dev, dtype=jnp.int32)
     own_ids = lax.dynamic_slice_in_dim(segment_ids, wide_index * tok_dev, tok_dev)
@@ -250,35 +487,47 @@
     cond_rows = condition.astype(F32)
     sigmoid_rows = jax.nn.sigmoid(cond_rows)
     activated = (cond_rows * sigmoid_rows).astype(BF16)
-    tok_full = narrow_gather(tokens).astype(F32)
+    tok_full = narrow_gather(tokens)
     mod_width = modulator.shape[2]
-    mod_part = dot(activated, modulator.reshape(width, -1), ((1,), (0,)))
-    mod_part = (mod_part.reshape(img_row, 6, -1) + modulator_bias.astype(F32)[None]).astype(BF16)
-    mod_rows = jnp.moveaxis(mod_part, 2, 0)
-
-    def per_token(parts):
-        rows = narrow_gather(mod_rows[:, :, parts[0] : parts[1]])
-        return [
-            dot(onehot_full, rows[:, :, i], ((1,), (1,)), BF16).astype(F32)
-            for i in range(parts[1] - parts[0])
+    mod_rows = jnp.transpose(modulator, (1, 2, 0)).reshape(6 * mod_width, width)
+
+    def per_token(lo, hi, after=None):
+        part = dot(activated, mod_rows[lo * mod_width : hi * mod_width], ((1,), (1,)))
+        part = part + modulator_bias[lo:hi].astype(F32).reshape(1, -1)
+        rows = jnp.moveaxis(part.astype(BF16).reshape(img_row, hi - lo, -1), 2, 0)
+        if after is not None:
+            rows, after = lax.optimization_barrier((rows, after))
+        rows = narrow_gather(rows)
+        vectors = [
+            dot(onehot_full, rows[:, :, i], ((1,), (1,)), BF16).astype(F32) for i in range(hi - lo)
         ]
-
-    shift_one, scale_one = per_token((0, 2))
-    gate_one, shift_two, scale_two, gate_two = per_token((2, 6))
+        return vectors, after
+
+    (shift_one, scale_one), _ = per_token(0, 2)
+    (gate_one, shift_two, scale_two, gate_two), tok_full = per_token(2, 6, tok_full)
+    tok_full = tok_full.astype(F32)
     xhat_one, rstd_one = norm(tok_full)
     norm_one = (xhat_one * (1.0 + scale_one) + shift_one).astype(BF16)
-    projected = dot(norm_one, qkv_weight.reshape(width, -1), ((1,), (0,)))
+    flat_qkv = jnp.transpose(qkv_weight, (1, 2, 0)).reshape(3 * part_width, width)
     bias_pair = qv_bias.astype(F32)
-    queries = (projected[:, :part_width] + bias_pair[0]).astype(BF16)
-    key_rows = projected[:, part_width : 2 * part_width].astype(BF16)
-    value_rows = (projected[:, 2 * part_width :] + bias_pair[1]).astype(BF16)
-    key_value = jnp.concatenate([key_rows, value_rows], axis=1)
+    parts_qkv = [flat_qkv[i * part_width : (i + 1) * part_width] for i in range(3)]
+    queries, key_rows, value_rows = [dot(norm_one, part, ((1,), (1,))) for part in parts_qkv]
+    queries = (queries + bias_pair[0]).astype(BF16)
+    key_rows = key_rows.astype(BF16)
+    value_rows = (value_rows + bias_pair[1]).astype(BF16)
     tail_start = own_count - span
-    edge_rows = jnp.concatenate(
-        [key_value[:span], lax.dynamic_slice_in_dim(key_value, tail_start, span)], axis=0
-    )
-    from_left, from_right = padded(edge_rows, span)
-    extended = jnp.concatenate([from_left, key_value, from_right], axis=0)
+
+    def tail_of(rows):
+        return lax.dynamic_slice_in_dim(rows, tail_start, span)
+
+    def to_right(rows):
+        return lax.ppermute(rows, "wide", [(i, i + 1) for i in range(wide_count - 1)])
+
+    def to_left(rows):
+        return lax.ppermute(rows, "wide", [(i + 1, i) for i in range(wide_count - 1)])
+
+    from_left = to_right(jnp.stack([tail_of(key_rows), tail_of(value_rows)]))
+    from_right = to_left(jnp.stack([key_rows[:span], value_rows[:span]]))
     left_index = jnp.maximum(wide_index - 1, 0)
     right_index = jnp.minimum(wide_index + 1, wide_count - 1)
     left_count = valid_counts[left_index]
@@ -288,26 +537,9 @@
     right_ids = jnp.where(wide_index < wide_count - 1, right_ids, -2)
     own_keys = jnp.where(positions < own_count, own_ids, -1)
     extended_ids = jnp.concatenate([left_ids, own_keys, right_ids])
-
-    def block_parts(block_idx):
-        row_start = block_idx * block
-        query_block = queries[row_start : row_start + block].reshape(block, heads, HD)
-        pair_block = extended[row_start : row_start + window]
-        key_block = pair_block[:, :part_width].reshape(window, heads, HD)
-        value_block = pair_block[:, part_width:].reshape(window, heads, HD)
-        same_seg = (
-            own_keys[row_start : row_start + block, None]
-            == extended_ids[None, row_start : row_start + window]
-        )
-        return (query_block, key_block, value_block, same_seg)
-
-    def masked_scores(query_block, key_block, same_seg):
-        raw = (
-            jnp.einsum("ihd,jhd->hij", query_block, key_block, preferred_element_type=jnp.float32)
-            * scale_factor
-        )
-        return jnp.where(same_seg[None], raw, NEG_FILL)
-
+    context, log_sums = attention_forward(
+        queries, key_rows, value_rows, from_left, from_right, own_keys[:, None], extended_ids[None]
+    )
     blocks = tok_dev // block
 
     def rows_of(rows, block_idx):
@@ -318,21 +550,10 @@
         return lax.dynamic_slice_in_dim(rows, share_start, share)
 
     upstream = cotangent.astype(F32)
-    contexts, log_sums, attns, middles, xhats, rstds = [], [], [], [], [], []
-    norms, hiddens, d_uppers, d_branches, d_norms, branches = [], [], [], [], [], []
+    attns, middles, xhats, rstds = [], [], [], []
+    norms, hiddens, d_uppers, d_branches, d_norms = [], [], [], [], []
     for block_idx in range(blocks):
-        query_block, key_block, value_block, same_seg = block_parts(block_idx)
-        masked = masked_scores(query_block, key_block, same_seg)
-        top_score = jnp.max(masked, axis=-1, keepdims=True)
-        expo = jnp.exp(masked - top_score)
-        totals = jnp.sum(expo, axis=-1, keepdims=True)
-        attend = expo / totals
-        log_sums.append(top_score + jnp.log(totals))
-        block_out = jnp.einsum(
-            "hij,jhd->ihd", attend.astype(BF16), value_block, preferred_element_type=F32
-        )
-        contexts.append(block_out.reshape(block, part_width).astype(BF16))
-        attn_part = dot(contexts[-1], out_weight, ((1,), (0,)), BF16)
+        attn_part = dot(rows_of(context, block_idx), out_weight, ((1,), (0,)), BF16)
         attns.append(narrow_sum(attn_part) + out_bias.astype(F32))
     for block_idx in range(blocks):
         gate_b = rows_of(live * gate_two, block_idx)
@@ -354,10 +575,14 @@
     d_upper = jnp.concatenate(d_uppers, axis=0)
     d_branch = jnp.concatenate(d_branches, axis=0)
     norm_two = jnp.concatenate(norms, axis=0)
-    context = jnp.concatenate(contexts, axis=0)
     down_grad = dot(hidden, d_branch, ((0,), (0,)), BF16)
     up_grad = dot(d_upper, norm_two, ((0,), (0,)), BF16)
-    up_grad, down_grad = lax.psum((up_grad, down_grad), "wide")
+    if ring_fits([up_grad]):
+        mine = ring_scatter([up_grad, down_grad], None, 1)[0]
+        mine, d_norms = lax.optimization_barrier((mine, d_norms))
+        (up_grad, down_grad), _ = wide_gather(mine, None)
+    else:
+        up_grad, down_grad = lax.psum((up_grad, down_grad), "wide")
     up_weight_grad = up_grad.T.astype(F32)
     down_weight_grad = down_grad.astype(F32)
     branch_part = dot(hidden, down_weight, ((1,), (0,)), BF16)
@@ -394,47 +619,23 @@
     d_attn = jnp.concatenate(d_attns, axis=0)
     d_context = jnp.concatenate(d_contexts, axis=0)
     out_weight_grad = dot(context, d_attn, ((0,), (0,)), BF16)
-    d_extended = jnp.zeros((tok_dev + 2 * span, 2 * part_width), jnp.float32)
-    query_grads = []
-    for block_idx in range(blocks):
-        query_block, key_block, value_block, same_seg = block_parts(block_idx)
-        attend = jnp.exp(masked_scores(query_block, key_block, same_seg) - log_sums[block_idx])
-        row_start = block_idx * block
-        grad_block = d_context[row_start : row_start + block].reshape(block, heads, HD)
-        d_attend = jnp.einsum(
-            "ihd,jhd->hij", grad_block, value_block, preferred_element_type=jnp.float32
-        )
-        centre = jnp.sum(attend * d_attend, axis=-1, keepdims=True)
-        d_scores = (attend * (d_attend - centre)).astype(jnp.bfloat16)
-        query_grad = (
-            jnp.einsum("hij,jhd->ihd", d_scores, key_block, preferred_element_type=jnp.float32)
-            * scale_factor
-        )
-        query_grads.append(query_grad.reshape(block, part_width))
-        key_grad = (
-            jnp.einsum("hij,ihd->jhd", d_scores, query_block, preferred_element_type=jnp.float32)
-            * scale_factor
-        )
-        value_grad = jnp.einsum(
-            "hij,ihd->jhd",
-            attend.astype(jnp.bfloat16),
-            grad_block,
-            preferred_element_type=jnp.float32,
-        )
-        pair_grad = jnp.concatenate(
-            [key_grad.reshape(window, part_width), value_grad.reshape(window, part_width)], axis=1
-        )
-        d_extended = d_extended.at[row_start : row_start + window].add(pair_grad)
-    back_edges = jnp.concatenate([d_extended[:span], d_extended[span + tok_dev :]], axis=0)
-    back_left, back_right = padded(back_edges.astype(jnp.bfloat16), span)
-    d_local = d_extended[span : span + tok_dev]
-    d_local = d_local.at[:span].add(back_left.astype(F32))
-    tail_sum = lax.dynamic_slice_in_dim(d_local, tail_start, span) + back_right.astype(F32)
-    d_local = lax.dynamic_update_slice_in_dim(d_local, tail_sum, tail_start, 0)
-    d_queries = jnp.concatenate(query_grads, axis=0).astype(BF16)
-    d_pairs = d_local.astype(BF16)
-    d_projected = jnp.concatenate([d_queries, d_pairs], axis=1)
-    d_norm_part = dot(d_projected, qkv_weight.reshape(width, -1), ((1,), (1,)), BF16)
+    d_queries, d_own, d_rim = attention_backward(
+        queries,
+        key_rows,
+        value_rows,
+        from_left,
+        from_right,
+        d_context,
+        log_sums,
+        own_keys[None],
+        extended_ids[:, None],
+    )
+    back_left, back_right = to_right(d_rim[1]), to_left(d_rim[0])
+    placed = lax.dynamic_update_slice(jnp.zeros_like(d_own), back_right, (0, tail_start, 0))
+    back_left = jnp.pad(back_left, ((0, 0), (0, tok_dev - span), (0, 0)))
+    d_own = (d_own.astype(F32) + placed.astype(F32) + back_left.astype(F32)).astype(BF16)
+    d_parts = [d_queries, d_own[0], d_own[1]]
+    d_norm_part = sum(dot(d_parts[i], parts_qkv[i], ((1,), (0,))) for i in range(3)).astype(BF16)
     early = jnp.stack(
         [
             image_sum(onehot_full, d_norm_part),
@@ -442,27 +643,41 @@
         ]
     ).astype(BF16)
     early = narrow_scatter(early, 2)
-    d_norm_one = narrow_scatter(d_norm_part)
-    qkv_grad = dot(d_projected, norm_one, ((0,), (0,)), BF16)
+    qkv_grads = [dot(part, norm_one, ((0,), (0,)), BF16) for part in d_parts]
     loose_parts = [
         jnp.sum(d_upper.astype(F32), axis=0),
         jnp.sum(d_branch.astype(F32), axis=0),
         jnp.sum(d_queries.astype(F32), axis=0),
-        jnp.sum(d_pairs[:, part_width:].astype(F32), axis=0),
+        jnp.sum(d_own[1].astype(F32), axis=0),
         jnp.sum(d_attn.astype(F32), axis=0),
     ]
     loose = jnp.concatenate(loose_parts)
     loose = jnp.pad(loose, (0, (-loose.shape[0]) % (8 * width))).reshape(-1, width).astype(BF16)
+    late = [d_gate_one, d_shift_two, d_scale_two, d_gate_two]
+    terms = [term.astype(BF16) for term in [early[0], early[1]] + late]
+    d_mod = [jnp.concatenate(terms[2 * i : 2 * i + 2], axis=1) for i in range(3)]
+    if 2 * mod_width == width:
+        d_mod_flat = jnp.concatenate(d_mod, axis=0)
+    else:
+        d_mod_flat = jnp.concatenate(d_mod, axis=1).reshape(-1, width)
+    flat = jnp.concatenate(qkv_grads + [out_weight_grad, d_mod_flat], axis=0)
+    lanes = [flat[: flat.shape[0] // 2], flat[flat.shape[0] // 2 :]]
+    if ring_fits(lanes):
+        mine, d_norm_other = ring_scatter(lanes, d_norm_part, 0)
+        d_norm_one = own([d_norm_part.astype(F32)]) + d_norm_other.astype(F32)
+        lanes, loose = wide_gather(mine, loose)
+        flat = jnp.concatenate(lanes, axis=0)
+    else:
+        d_norm_one = narrow_scatter(d_norm_part)
+        flat = lax.psum(flat, "wide")
+        loose = lax.all_gather(loose, "wide", axis=0).astype(F32)
+    loose = jnp.sum(loose, axis=0)
     tokens_grad = own(d_middles) + norm_back(
         d_norm_one * (1.0 + own([scale_one])), own([xhat_one]), own([rstd_one])
     )
-    late = jnp.stack([d_gate_one, d_shift_two, d_scale_two, d_gate_two])
-    d_mod = jnp.concatenate([early.astype(BF16), late.astype(BF16)], axis=0)
-    flat = jnp.concatenate([qkv_grad, out_weight_grad, d_mod.reshape(-1, width)], axis=0)
-    flat, loose = wide_sum(flat, loose, 0)
     starts = [0, 3 * part_width, 4 * part_width]
-    qkv_weight_grad = (
-        flat[: starts[1]].T.reshape(width, 3, part_width).astype(F32)
+    qkv_weight_grad = jnp.transpose(
+        flat[: starts[1]].astype(F32).reshape(3, part_width, width), (2, 0, 1)
     )
     out_weight_grad = flat[starts[1] : starts[2]].astype(F32)
     loose = loose.reshape(-1)
@@ -473,12 +688,18 @@
         loose[bounds[i] : bounds[i + 1]] for i in range(5)
     ]
     qv_bias_grad = jnp.stack([query_bias, value_bias])
-    d_mod = flat[starts[2] :].reshape(6, img_row, mod_width)
-    modulator_grad = jnp.stack(
-        [dot(activated, d_mod[j], ((0,), (0,))) for j in range(6)], axis=1
-    )
-    modulator_bias_grad = jnp.sum(d_mod.astype(F32), axis=1)
-    d_activated = sum(dot(d_mod[j], modulator[:, j], ((1,), (1,))) for j in range(6))
+    d_mod_flat = flat[starts[2] :]
+    if 2 * mod_width == width:
+        d_mod = d_mod_flat.reshape(3, img_row, width)
+    else:
+        d_mod = jnp.moveaxis(d_mod_flat.reshape(img_row, 3, -1), 1, 0)
+    modulator_grad = lax.dot_general(
+        d_mod, activated, (((1,), (0,)), ((), ())), preferred_element_type=F32
+    )
+    modulator_grad = jnp.transpose(modulator_grad.reshape(6, mod_width, width), (2, 0, 1))
+    modulator_bias_grad = jnp.sum(d_mod.astype(F32), axis=1).reshape(6, mod_width)
+    mod_blocks = mod_rows.reshape(3, 2 * mod_width, width)
+    d_activated = sum(dot(d_mod[i], mod_blocks[i], ((1,), (0,))) for i in range(3))
     cond_part = d_activated * sigmoid_rows * (1.0 + cond_rows * (1.0 - sigmoid_rows))
     condition_grad = narrow_sum(cond_part.astype(BF16))
     return (

time: 655 us -> 686 us (1.047)
  Pallas kernels: 59.9 us -> 154 us
  other arithmetic: 132 us -> 90.1 us
  matrix products: 193 us -> 154 us
  local copies, waits for them, and re-layouts: 63.4 us -> 86.8 us
    pallas_call x1 -> x4, Pallas kernels: 59.9 us -> 154 us  [the longest x2 117 us: ring_scatter(): pl.pallas_call(lambda *refs: ring_kernel(chips, subs, int(part is not Non...]
    ppermute x12 -> x11, waiting for transfers between devices: 157 us -> 75.9 us  [swap(): return lax.ppermute(part, 'narrow', [(0, 1), (1, 0)])]
    all_gather x1 -> x2, waiting for transfers between devices: 0.01 us -> 74.7 us  [wide_gather(): parts = lax.all_gather(parts, 'wide', axis=0)]
    dot_general x12 -> x1, matrix products: 43.7 us -> 8.37 us  [body(): lax.dot_general(d_mod, activated, (((1,), (0,)), ((), ())), preferred_ele...]
    convert_element_type x6 -> x4, other arithmetic: 26.1 us -> 11.8 us  [the longest x1 7.32 us: body(): up_weight_grad = up_grad.T.astype(F32)]
    slice x11 -> x7, local copies, waits for them, and re-layouts: 15.2 us -> 27.8 us  [the longest x2 12.7 us: wide_gather(): parts[:, lane * shard:(lane + 1) * shard].reshape(-1, width)]
    unnamed x212 -> x194, local copies, waits for them, and re-layouts: 20.9 us -> 28.7 us
    reduce_sum x2, other arithmetic: 12.4 us -> 4.8 us  [body(): jnp.sum(d_attn.astype(F32), axis=0)]
  transfers between devices with their start and end apart: 18 -> 17, of which waited for: 8 -> 8; matrix products, arithmetic and copies ran while one was open for 39% -> 24% of each run, Pallas kernels for 9% -> 12%
where the time goes in v3:
time: 686 us; the launch traced here: 678 us
  matrix products  154 us (22%)
  Pallas kernels  154 us (22%)
  waiting for transfers between devices  153 us (22%)
  other arithmetic  90.1 us (13%)
  local copies, waits for them, and re-layouts  86.8 us (13%)
  starting transfers between devices  21.4 us (3%)
  between operations  17.8 us (3%)
    dot_general x43, matrix products, dot(): lax.dot_general(left, right, (dims, ((), ())), preferred_element_type=F32)  146 us
    pallas_call x2, Pallas kernels, ring_scatter(): pl.pallas_call(lambda *refs: ring_kernel(chips, subs, int(part is not Non...  117 us
    ppermute x11, waiting for transfers between devices, swap(): return lax.ppermute(part, 'narrow', [(0, 1), (1, 0)])  75.9 us
    all_gather x2, waiting for transfers between devices, wide_gather(): parts = lax.all_gather(parts, 'wide', axis=0)  74.7 us
    unnamed x194, local copies, waits for them, and re-layouts  28.7 us
    pallas_call x1, Pallas kernels, attention_backward(): pl.pallas_call(lambda *refs: backward_kernel(tiles, *refs), grid=(tiles,)...  26.3 us
  transfers between devices with their start and end apart: 17, of which 8 were waited for; matrix products, arithmetic and copies ran while one was open for 24% of the time, Pallas kernels for 12%

profile of v3, /device:TPU:0, one launch (start us, length us, event | category | flops | bytes accessed | tf_op | source)
XLA Modules:
  0.0 677.7 jit_solution(3443801169100458952)
XLA Ops:
  74.3 10.8 %attention_forward.1 = (bf16[1024,576]{1,0:T(8,128)(2,1)S(1)}, f32[8,1024]{1,0:T(8,128)S(1)}) custom-call(bf16[1024,576]{1,0:T(8,128)(2,1)S(1)} %add_convert_fusion.4.refs_0_, bf16[1024,576]{1,0:T(8,128)(2,1)S(1)} %convolution_convert_fusion.22.refs_1_, bf16[1024,576]{1,0:T(8,128)(2,1)S(1)} %add_convert_fusion.3.refs_2_, ...), custom_call_target="tpu_custom_call" | custom-call | flops 1207959552 | bytes 4718592 | tf_op jit(solution)/shard_map/attention_forward/pallas_call | solution.py:288
  101.2 10.6 %collective-permute-done.6 = bf16[512,1152]{1,0:T(8,128)(2,1)} collective-permute-done((bf16[512,1152]{1,0:T(8,128)(2,1)}, bf16[512,1152]{1,0:T(8,128)(2,1)}, u32[]{:S(2)}, u32[]{:S(2)}) %collective-permute-start.6) | collective-permute-done | bytes 1179680 | tf_op jit(solution)/shard_map/ppermute | solution.py:21
  111.8 25.3 %collective-permute-done.5 = bf16[512,1152]{1,0:T(8,128)(2,1)} collective-permute-done((bf16[512,1152]{1,0:T(8,128)(2,1)}, bf16[512,1152]{1,0:T(8,128)(2,1)}, u32[]{:S(2)}, u32[]{:S(2)}) %collective-permute-start.5) | collective-permute-done | bytes 1179680 | tf_op jit(solution)/shard_map/ppermute | solution.py:21
  148.8 5.9 multiply_convert_fusion.4
  154.7 5.8 multiply_convert_fusion.5
  160.6 7.8 %fusion.123 = (bf16[2304]{0:T(1024)(128)(2,1)S(1)}, bf16[512,2304]{1,0:T(8,128)(2,1)}) fusion(f32[512,2304]{1,0:T(8,128)} %get-tuple-element.147, bf16[512,1152]{1,0:T(8,128)(2,1)S(1)} %get-tuple-element.97, bf16[2304,1152]{1,0:T(8,128)(2,1)S(1)} %bitcast.206), kind=kOutput, calls=%fused_computation.284 | convolution fusion | flops 2742679296 | bytes 13570560 | tf_op jit(solution)/shard_map/dot_general | solution.py:17
  168.3 6.0 convolution_convert_fusion.16
  174.4 8.8 %fusion.124 = (bf16[2304]{0:T(1024)(128)(2,1)S(1)}, bf16[512,2304]{1,0:T(8,128)(2,1)}) fusion(f32[512,2304]{1,0:T(8,128)} %get-tuple-element.145, bf16[512,1152]{1,0:T(8,128)(2,1)S(1)} %copy-done.54, bf16[2304,1152]{1,0:T(8,128)(2,1)} %param.26), kind=kOutput, calls=%fused_computation.285 | convolution fusion | flops 2742679296 | bytes 13570560 | tf_op jit(solution)/shard_map/dot_general | solution.py:17
  183.2 8.0 %convolution_convert_fusion.1 = bf16[2304,1152]{1,0:T(8,128)(2,1)S(1)} fusion(bf16[512,2304]{1,0:T(8,128)(2,1)} %get-tuple-element.155, bf16[512,2304]{1,0:T(8,128)(2,1)S(1)} %copy-done.80, bf16[512,1152]{1,0:T(8,128)(2,1)S(1)} %get-tuple-element.121, bf16[512,1152]{1,0:T(8,128)(2,1)S(1)} %get-tuple-element.99), kind=kOutput, calls=%fused_computation.1 | convolution fusion | flops 5452627968 | bytes 12386304 | tf_op jit(solution)/shard_map/dot_general | solution.py:17
  191.2 6.9 %convolution_convert_fusion.15 = bf16[512,1152]{1,0:T(8,128)(2,1)} fusion(bf16[512,2304]{1,0:T(8,128)(2,1)S(1)} %copy-done.81, bf16[1152,2304]{1,0:T(8,128)(2,1)} %param.24), kind=kOutput, calls=%fused_computation.56 | convolution fusion | flops 2718498816 | bytes 8847360 | tf_op jit(solution)/shard_map/dot_general | solution.py:17
  200.2 10.8 %convolution_convert_fusion.4 = bf16[1024,1152]{1,0:T(8,128)(2,1)S(1)} fusion(bf16[2304,1152]{1,0:T(8,128)(2,1)} %param.26, bf16[512,2304]{1,0:T(8,128)(2,1)S(1)} %copy-done.82, bf16[512,2304]{1,0:T(8,128)(2,1)S(1)} %copy-done.83), kind=kOutput, calls=%fused_computation.37 | convolution fusion | flops 5446434816 | bytes 12386304 | tf_op jit(solution)/shard_map/dot_general | solution.py:17
  214.0 8.2 %convolution_convert_fusion = bf16[2304,1152]{1,0:T(8,128)(2,1)S(1)} fusion(bf16[512,2304]{1,0:T(8,128)(2,1)} %get-tuple-element.144, bf16[512,2304]{1,0:T(8,128)(2,1)} %get-tuple-element.146, bf16[512,1152]{1,0:T(8,128)(2,1)S(1)} %copy-done.54, bf16[512,1152]{1,0:T(8,128)(2,1)S(1)} %get-tuple-element.97), kind=kOutput, calls=%fused_computation | convolution fusion | flops 5452627968 | bytes 12386304 | tf_op jit(solution)/shard_map/dot_general | solution.py:17
  222.2 73.1 %ring_scatter.2 = bf16[2,144,1152]{2,1,0:T(8,128)(2,1)} custom-call(bf16[8,2,144,1152]{3,2,1,0:T(8,128)(2,1)S(1)} %bitcast.160, bf16[8,2,144,1152]{3,2,1,0:T(8,128)(2,1)S(1)} %bitcast.161), custom_call_target="tpu_custom_call" | custom-call | tf_op jit(solution)/shard_map/ring_scatter/pallas_call | solution.py:179
  324.2 26.3 %attention_backward.1 = (bf16[1024,576]{1,0:T(8,128)(2,1)S(1)}, bf16[2,1024,576]{2,1,0:T(8,128)(2,1)}, bf16[2,2,128,576]{3,2,1,0:T(8,128)(2,1)S(1)}) custom-call(bf16[1024,576]{1,0:T(8,128)(2,1)S(1)} %copy-done.16, bf16[1024,576]{1,0:T(8,128)(2,1)S(1)} %copy-done.5, bf16[1024,576]{1,0:T(8,128)(2,1)} %copy-done.6, bf16[2,128,576]{2,1,0:T(8,128)(2,1)S(1)} %copy-done.10, ...), custom_call_target="tpu_custom_call" | custom-call | flops 3019898880 | bytes 9437184 | tf_op jit(solution)/shard_map/attention_backward/pallas_call | solution.py:389
  414.8 10.4 %collective-permute-done.12 = bf16[2,256,576]{1,2,0:T(8,128)(2,1)} collective-permute-done((bf16[2,256,576]{1,2,0:T(8,128)(2,1)}, bf16[2,256,576]{1,2,0:T(8,128)(2,1)}, u32[]{:S(2)}, u32[]{:S(2)}) %collective-permute-start.12) | collective-permute-done | bytes 589856 | tf_op jit(solution)/shard_map/ppermute | solution.py:21
  433.6 43.9 %ring_scatter.3 = (bf16[2,96,1152]{2,1,0:T(8,128)(2,1)S(1)}, bf16[512,1152]{1,0:T(8,128)(2,1)S(1)}) custom-call(bf16[8,2,96,1152]{3,2,1,0:T(8,128)(2,1)S(1)} %bitcast.158, bf16[8,2,96,1152]{3,2,1,0:T(8,128)(2,1)S(1)} %bitcast.159, bf16[1024,1152]{1,0:T(8,128)(2,1)S(1)} %copy-done.3), custom_call_target="tpu_custom_call" | custom-call | tf_op jit(solution)/shard_map/ring_scatter/pallas_call | solution.py:179
  485.0 23.9 %collective-permute-done.7 = bf16[512,1152]{1,0:T(8,128)(2,1)} collective-permute-done((bf16[512,1152]{1,0:T(8,128)(2,1)}, bf16[512,1152]{1,0:T(8,128)(2,1)}, u32[]{:S(2)}, u32[]{:S(2)}) %collective-permute-start.7) | collective-permute-done | bytes 1179680 | tf_op jit(solution)/shard_map/ppermute | solution.py:21
  518.6 26.1 %all-gather.6.cloned.1.call-done = bf16[3200,1152]{1,0:T(8,128)(2,1)} async-done(((bf16[200,1152]{1,0:T(8,128)(2,1)}), bf16[3200,1152]{1,0:T(8,128)(2,1)}) %all-gather.6.cloned.1.call-update) | async-done | bytes 7372816 | tf_op jit(solution)/shard_map/all_gather | solution.py:202
  569.0 8.4 %fusion.73 = f32[1152,6,576]{0,2,1:T(8,128)} fusion(bf16[6,576,256]{2,1,0:T(8,128)(2,1)S(1)} %bitcast.186, bf16[256,1152]{1,0:T(8,128)(2,1)S(1)} %copy-done.59), kind=kOutput, calls=%fused_computation.197 | convolution fusion | flops 2040201216 | bytes 18284544 | tf_op jit(solution)/shard_map/dot_general | solution.py:696
  585.4 48.7 %all-gather.4.cloned.1.call-done = bf16[16,288,1152]{2,1,0:T(8,128)(2,1)} async-done(((bf16[1,288,1152]{2,1,0:T(8,128)(2,1)}), bf16[16,288,1152]{2,1,0:T(8,128)(2,1)}) %all-gather.4.cloned.1.call-update) | async-done | bytes 10616848 | tf_op jit(solution)/shard_map/all_gather | solution.py:202
  634.1 9.0 %fusion.116 = (bf16[16,144,1152]{2,1,0:T(8,128)(2,1)}, bf16[16,144,1152]{2,1,0:T(8,128)(2,1)}) fusion(bf16[16,288,1152]{2,1,0:T(8,128)(2,1)} %all-gather.4.cloned.1.call-done), kind=kLoop, calls=%fused_computation.277 | loop fusion | bytes 21233664 | tf_op jit(solution)/shard_map/slice | solution.py:203
  643.1 7.3 %convert_bitcast_fusion = f32[1152,2304]{0,1:T(8,128)} fusion(bf16[16,144,1152]{2,1,0:T(8,128)(2,1)} %get-tuple-element.115), kind=kLoop, calls=%fused_computation.2 | loop fusion | flops 2654208 | bytes 15925248 | tf_op jit(solution)/shard_map/convert_element_type | solution.py:586
  650.4 12.7 %copy.91 = f32[1152,2304]{1,0:T(8,128)} copy(f32[1152,2304]{0,1:T(8,128)} %convert_bitcast_fusion) | data formatting | bytes 21233664
  663.1 7.3 %bitcast_convert_fusion = f32[2304,1152]{1,0:T(8,128)} fusion(bf16[16,144,1152]{2,1,0:T(8,128)(2,1)} %get-tuple-element.114), kind=kLoop, calls=%fused_computation.4 | loop fusion | flops 2654208 | bytes 15925248 | tf_op jit(solution)/shard_map/convert_element_type | solution.py:587
  (375 shorter events, 247.9 us)
Async XLA Ops:
  7.2 78.0 %copy-start = (bf16[576,1152]{1,0:T(8,128)(2,1)S(1)}, bf16[576,1152]{1,0:T(8,128)(2,1)}, u32[]{:S(2)}) copy-start(bf16[576,1152]{1,0:T(8,128)(2,1)} %param.22) | copy-start | bytes 3981316
  7.2 537.5 %all-gather.6.cloned.1.call-start = ((), (), s32[]{:S(2)}) async-start(), calls=%async_computation.1 | async-start | bytes 7833600 | tf_op jit(solution)/shard_map/all_gather | solution.py:202
  7.2 44.5 %collective-permute-start = (bf16[512,1152]{1,0:T(8,128)(2,1)}, bf16[512,1152]{1,0:T(8,128)(2,1)}, u32[]{:S(2)}, u32[]{:S(2)}) collective-permute-start(bf16[512,1152]{1,0:T(8,128)(2,1)} %param.15), channel_id=1, source_target_pairs={{0,1},{1,0},{2,3},{3,2},{4,5},{5,4},{6,7},{7,6},{8,9},{9,8},{10,11... | collective-permute-start | bytes 3538952 | tf_op jit(solution)/shard_map/ppermute | solution.py:21
  19.1 30.1 %collective-permute-start.2 = (bf16[576,256,2]{1,0,2:T(8,128)(2,1)S(1)}, bf16[576,256,2]{1,0,2:T(8,128)(2,1)}, u32[]{:S(2)}, u32[]{:S(2)}) collective-permute-start(bf16[576,256,2]{1,0,2:T(8,128)(2,1)S(1)} %bitcast.195), channel_id=1, source_target_pairs={{0,1},{1,0},{2,3},{3,2},{4,5},{5,4},{6,7},{7,6},{8,9},{9,8},{10,11... | collective-permute-start | bytes 1769480 | tf_op jit(solution)/shard_map/ppermute | solution.py:21
  43.4 259.0 %copy-start.39 = (pred[1024,256]{1,0:T(32,128)(4,1)}, pred[1024,256]{1,0:T(32,128)(4,1)S(1)}, u32[]{:S(2)}) copy-start(pred[1024,256]{1,0:T(32,128)(4,1)S(1)} %iota_compare_fusion) | copy-start | bytes 786436
  58.0 33.6 %collective-permute-start.1 = (bf16[576,256,4]{1,0,2:T(8,128)(2,1)S(1)}, bf16[576,256,4]{1,0,2:T(8,128)(2,1)S(1)}, u32[]{:S(2)}, u32[]{:S(2)}) collective-permute-start(bf16[576,256,4]{1,0,2:T(8,128)(2,1)S(1)} %bitcast.188), channel_id=1, source_target_pairs={{0,1},{1,0},{2,3},{3,2},{4,5},{5,4},{6,7},{7,6},{8,9},{9,8},{10,11... | collective-permute-start | bytes 3538952 | tf_op jit(solution)/shard_map/ppermute | solution.py:21
  67.6 4.9 collective-permute-start.3
  69.0 5.3 collective-permute-start.4
  87.3 24.5 %collective-permute-start.6 = (bf16[512,1152]{1,0:T(8,128)(2,1)}, bf16[512,1152]{1,0:T(8,128)(2,1)}, u32[]{:S(2)}, u32[]{:S(2)}) collective-permute-start(bf16[512,1152]{1,0:T(8,128)(2,1)} %convolution_convert_fusion.17), channel_id=1, source_target_pairs={{0,1},{1,0},{2,3},{3,2},{4,5},{5,4},{6,7},{7,6},{8,9},{9,8},{10,11... | collective-permute-start | bytes 3538952 | tf_op jit(solution)/shard_map/ppermute | solution.py:21
  90.0 47.0 %collective-permute-start.5 = (bf16[512,1152]{1,0:T(8,128)(2,1)}, bf16[512,1152]{1,0:T(8,128)(2,1)}, u32[]{:S(2)}, u32[]{:S(2)}) collective-permute-start(bf16[512,1152]{1,0:T(8,128)(2,1)} %convolution_convert_fusion.18), channel_id=1, source_target_pairs={{0,1},{1,0},{2,3},{3,2},{4,5},{5,4},{6,7},{7,6},{8,9},{9,8},{10,11... | collective-permute-start | bytes 3538952 | tf_op jit(solution)/shard_map/ppermute | solution.py:21
  101.2 40.2 %copy-start.19 = (f32[1024,1152]{1,0:T(8,128)}, f32[1024,1152]{1,0:T(8,128)S(1)}, u32[]{:S(2)}) copy-start(f32[1024,1152]{1,0:T(8,128)S(1)} %convert_multiply_fusion.1) | copy-start | bytes 14155780
  198.1 98.0 %collective-permute-start.8 = (bf16[512,1152]{1,0:T(8,128)(2,1)}, bf16[512,1152]{1,0:T(8,128)(2,1)}, u32[]{:S(2)}, u32[]{:S(2)}) collective-permute-start(bf16[512,1152]{1,0:T(8,128)(2,1)} %convolution_convert_fusion.16), channel_id=1, source_target_pairs={{0,1},{1,0},{2,3},{3,2},{4,5},{5,4},{6,7},{7,6},{8,9},{9,8},{10,11... | collective-permute-start | bytes 3538952 | tf_op jit(solution)/shard_map/ppermute | solution.py:21
  198.7 99.4 %collective-permute-start.9 = (bf16[512,1152]{1,0:T(8,128)(2,1)}, bf16[512,1152]{1,0:T(8,128)(2,1)}, u32[]{:S(2)}, u32[]{:S(2)}) collective-permute-start(bf16[512,1152]{1,0:T(8,128)(2,1)} %convolution_convert_fusion.15), channel_id=1, source_target_pairs={{0,1},{1,0},{2,3},{3,2},{4,5},{5,4},{6,7},{7,6},{8,9},{9,8},{10,11... | collective-permute-start | bytes 3538952 | tf_op jit(solution)/shard_map/ppermute | solution.py:21
  213.5 81.9 %collective-permute-start.13 = (bf16[256,576]{0,1:T(8,128)(2,1)}, bf16[256,576]{0,1:T(8,128)(2,1)S(1)}, u32[]{:S(2)}, u32[]{:S(2)}) collective-permute-start(bf16[256,576]{0,1:T(8,128)(2,1)} %constant_dynamic-slice_fusion), channel_id=1, source_target_pairs={{0,1},{1,0},{2,3},{3,2},{4,5},{5,4},{6,7},{7,6},{8,9},{9,8},{10,11... | collective-permute-start | bytes 884744 | tf_op jit(solution)/shard_map/ppermute | solution.py:21
  222.2 73.1 %copy-start.61 = (bf16[256,1152]{0,1:T(8,128)(2,1)S(1)}, bf16[256,1152]{0,1:T(8,128)(2,1)}, u32[]{:S(2)}) copy-start(bf16[256,1152]{0,1:T(8,128)(2,1)} %copy-done.60) | copy-start | bytes 1769476
  324.2 32.7 %copy-start.49 = (bf16[1024,1152]{1,0:T(8,128)(2,1)S(1)}, bf16[1024,1152]{1,0:T(8,128)(2,1)}, u32[]{:S(2)}) copy-start(bf16[1024,1152]{1,0:T(8,128)(2,1)} %copy-done.48) | copy-start | bytes 7077892
  351.5 27.0 %collective-permute-start.10 = (bf16[2,128,576]{2,1,0:T(8,128)(2,1)}, bf16[2,128,576]{2,1,0:T(8,128)(2,1)}, u32[]{:S(2)}, u32[]{:S(2)}) collective-permute-start(bf16[2,128,576]{2,1,0:T(8,128)(2,1)} %get-tuple-element.135), channel_id=1, source_target_pairs={{2,0},{4,2},{6,4},{8,6},{10,8},{12,10},{14,12},{16,14},{18,16},{20... | collective-permute-start | bytes 884744 | tf_op jit(solution)/shard_map/ppermute | solution.py:527
  353.2 30.6 %collective-permute-start.11 = (bf16[2,128,576]{2,1,0:T(8,128)(2,1)}, bf16[2,128,576]{2,1,0:T(8,128)(2,1)}, u32[]{:S(2)}, u32[]{:S(2)}) collective-permute-start(bf16[2,128,576]{2,1,0:T(8,128)(2,1)} %get-tuple-element.134), channel_id=1, source_target_pairs={{0,2},{2,4},{4,6},{6,8},{8,10},{10,12},{12,14},{14,16},{16,18},{18... | collective-permute-start | bytes 884744 | tf_op jit(solution)/shard_map/ppermute | solution.py:524
  409.4 15.9 %collective-permute-start.12 = (bf16[2,256,576]{1,2,0:T(8,128)(2,1)}, bf16[2,256,576]{1,2,0:T(8,128)(2,1)}, u32[]{:S(2)}, u32[]{:S(2)}) collective-permute-start(bf16[2,256,576]{1,2,0:T(8,128)(2,1)} %copy.85), channel_id=1, source_target_pairs={{0,1},{1,0},{2,3},{3,2},{4,5},{5,4},{6,7},{7,6},{8,9},{9,8},{10,11... | collective-permute-start | bytes 1769480 | tf_op jit(solution)/shard_map/ppermute | solution.py:21
  478.3 155.8 %all-gather.4.cloned.1.call-start = ((), (), s32[]{:S(2)}) async-start(), calls=%async_computation | async-start | bytes 11280384 | tf_op jit(solution)/shard_map/all_gather | solution.py:202
  481.4 27.4 %collective-permute-start.7 = (bf16[512,1152]{1,0:T(8,128)(2,1)}, bf16[512,1152]{1,0:T(8,128)(2,1)}, u32[]{:S(2)}, u32[]{:S(2)}) collective-permute-start(bf16[512,1152]{1,0:T(8,128)(2,1)} %constant_dynamic-slice_fusion.1), channel_id=1, source_target_pairs={{0,1},{1,0},{2,3},{3,2},{4,5},{5,4},{6,7},{7,6},{8,9},{9,8},{10,11... | collective-permute-start | bytes 3538952 | tf_op jit(solution)/shard_map/ppermute | solution.py:21
  482.5 30.8 %slice-start.4 = ((s8[4718592]{0:T(1024)(128)(4,1)}), s8[4194304]{0:T(1024)(128)(4,1)S(1)}, s32[]{:S(2)}) async-start(s8[4718592]{0:T(1024)(128)(4,1)} %bitcast.169), calls=%async_computation.6 | async-start | bytes 8388608
  484.9 28.4 %slice-start.5 = ((s8[4718592]{0:T(1024)(128)(4,1)}), s8[524288]{0:T(1024)(128)(4,1)S(1)}, s32[]{:S(2)}) async-start(s8[4718592]{0:T(1024)(128)(4,1)} %bitcast.169), calls=%async_computation.7 | async-start | bytes 1048576
  556.8 26.1 %collective-permute-start.14 = (bf16[256,1152]{1,0:T(8,128)(2,1)}, bf16[256,1152]{1,0:T(8,128)(2,1)}, u32[]{:S(2)}, u32[]{:S(2)}) collective-permute-start(bf16[256,1152]{1,0:T(8,128)(2,1)} %fusion.10), channel_id=1, source_target_pairs={{0,1},{1,0},{2,3},{3,2},{4,5},{5,4},{6,7},{7,6},{8,9},{9,8},{10,11... | collective-permute-start | bytes 1769480 | tf_op jit(solution)/shard_map/ppermute | solution.py:21
  (90 other events, 452.9 us)
Sparse Core Ops, SparseCore 0:
  478.4 66.2 all-gather.5
  547.0 87.0 all-gather.3

commit v4 on v3

--- a/solution.py
+++ b/solution.py
@@ -31,10 +31,10 @@
     )
 
 
-def narrow_sum(part):
+def narrow_other(part):
     if lax.axis_size("narrow") != 2:
-        return lax.psum(part, "narrow").astype(F32)
-    return part.astype(F32) + swap(part).astype(F32)
+        return (lax.psum(part.astype(F32), "narrow") - part.astype(F32)).astype(BF16)
+    return swap(part)
 
 
 def narrow_scatter(part, dim=0):
@@ -194,12 +194,16 @@
     return lax.axis_size("narrow") == 2 and lanes[0].shape[0] % (count * UNIT) == 0
 
 
-def wide_gather(mine, loose):
+def wide_gather(mine, loose=None):
     shard, width = mine.shape[1:]
     parts = mine.reshape(2 * shard, width)
     if loose is not None:
         parts = jnp.concatenate([parts, loose], axis=0)
-    parts = lax.all_gather(parts, "wide", axis=0)
+    return lax.all_gather(parts, "wide", axis=0)
+
+
+def lanes_of(parts, shard):
+    width = parts.shape[2]
     lanes = [parts[:, lane * shard : (lane + 1) * shard].reshape(-1, width) for lane in range(2)]
     return lanes, parts[:, 2 * shard :].astype(F32)
 
@@ -448,6 +452,277 @@
     return v * half, slope
 
 
+def matmul(left, right, dims=((1,), (0,))):
+    return lax.dot_general(left, right, (dims, ((), ())), preferred_element_type=F32)
+
+
+def pick(ids, table):
+    slots = lax.broadcasted_iota(jnp.int32, (ids.shape[0], table.shape[0]), 1)
+    return matmul((ids == slots).astype(BF16), table)
+
+
+def gather_images(ids, terms, sums, fresh):
+    slots = lax.broadcasted_iota(jnp.int32, (sums.shape[1], ids.shape[1]), 0)
+    hot = (ids == slots).astype(BF16)
+    for i, term in enumerate(terms):
+        part = matmul(hot, term.astype(BF16))
+        sums[i] = jnp.where(fresh, 0.0, sums[i]) + part
+
+
+def halves_out(sums, out, halves):
+    size = sums.shape[2] // halves
+    for half in range(halves):
+        for i in range(sums.shape[0]):
+            out[half, i] = sums[i, :, half * size : (half + 1) * size].astype(BF16)
+
+
+def whole(shape):
+    return pl.BlockSpec(shape, lambda i: (0,) * len(shape))
+
+
+def tiled(rows, width):
+    return pl.BlockSpec((rows, width), lambda i: (i, 0))
+
+
+def token_call(kernel, tokens, name, out_shape, in_specs, out_specs, scratch, flops, operands):
+    size = sum(x.size * x.dtype.itemsize for x in operands)
+    return pl.pallas_call(
+        kernel,
+        grid=(tokens // TILE,),
+        out_shape=out_shape,
+        in_specs=in_specs,
+        out_specs=out_specs,
+        scratch_shapes=scratch,
+        compiler_params=pltpu.CompilerParams(vmem_limit_bytes=60 << 20),
+        cost_estimate=pl.CostEstimate(
+            flops=flops, transcendentals=0, bytes_accessed=size + size // 2
+        ),
+        name=name,
+    )(*operands)
+
+
+def shaped(shape, dtype=BF16):
+    return jax.ShapeDtypeStruct(shape, dtype)
+
+
+def project_kernel(tokens, ids, table, weight, bias, q, k, v, norm_one):
+    xhat, _ = norm(tokens[...].astype(F32))
+    normed = (xhat * (1.0 + pick(ids[...], table[1])) + pick(ids[...], table[0])).astype(BF16)
+    norm_one[...] = normed
+    size = q.shape[1]
+    for i, out in enumerate((q, k, v)):
+        rows = matmul(normed, weight[i * size : (i + 1) * size], ((1,), (1,)))
+        if i != 1:
+            rows = rows + bias[i // 2 : i // 2 + 1].astype(F32)
+        out[...] = rows.astype(BF16)
+
+
+def project(tokens, ids, table, weight, bias):
+    count, width = tokens.shape
+    size = weight.shape[0] // 3
+    return token_call(
+        project_kernel,
+        count,
+        "project",
+        [shaped((count, size))] * 3 + [shaped((count, width))],
+        [tiled(TILE, width), tiled(TILE, 1), whole(table.shape), whole(weight.shape), whole(bias.shape)],
+        [tiled(TILE, size)] * 3 + [tiled(TILE, width)],
+        [],
+        6 * count * width * size,
+        (tokens, ids, table, weight, bias),
+    )
+
+
+def mlp_kernel(
+    tokens, mine, theirs, cotangent, ids, live, table, out_bias, up, up_bias, down, *outs
+):
+    norm_two, hidden, d_upper, d_branch, d_norm, branch = outs
+    ids, live = ids[...], live[...]
+    attn = mine[...].astype(F32) + theirs[...].astype(F32) + out_bias[...].astype(F32)
+    middle = tokens[...].astype(F32) + live * pick(ids, table[0]) * attn
+    xhat, _ = norm(middle)
+    normed = (xhat * (1.0 + pick(ids, table[2])) + pick(ids, table[1])).astype(BF16)
+    norm_two[...] = normed
+    pulled = (live * pick(ids, table[3]) * cotangent[...].astype(F32)).astype(BF16)
+    d_branch[...] = pulled
+    width = up.shape[1]
+    step = 384 if width % 384 == 0 else width
+    back = ahead = 0.0
+    for lo in range(0, width, step):
+        cols = slice(lo, lo + step)
+        upper = matmul(normed, up[:, cols]) + up_bias[:, cols].astype(F32)
+        d_hidden = matmul(pulled, down[cols], ((1,), (1,)))
+        value, slope = gelu_pair(upper)
+        value = value.astype(BF16)
+        d_up = (d_hidden * slope).astype(BF16)
+        hidden[:, cols] = value
+        d_upper[:, cols] = d_up
+        back += matmul(d_up, up[:, cols], ((1,), (1,)))
+        ahead += matmul(value, down[cols])
+    d_norm[...] = back.astype(BF16)
+    branch[...] = ahead.astype(BF16)
+
+
+def mlp(tokens, mine, theirs, cotangent, ids, live, table, out_bias, up, up_bias, down):
+    count, width = tokens.shape
+    size = up.shape[1]
+    row, col = tiled(TILE, width), tiled(TILE, 1)
+    consts = (table, out_bias, up, up_bias, down)
+    return token_call(
+        mlp_kernel,
+        count,
+        "mlp",
+        [shaped((count, n)) for n in (width, size, size, width, width, width)],
+        [row, row, row, row, col, col] + [whole(x.shape) for x in consts],
+        [tiled(TILE, n) for n in (width, size, size, width, width, width)],
+        [],
+        8 * count * width * size,
+        (tokens, mine, theirs, cotangent, ids, live) + consts,
+    )
+
+
+def middle_kernel(
+    halves, tokens, mine, theirs, cotangent, d_own, d_other, context, ids, live, ids_row, *refs
+):
+    table, out_bias, weight, d_middle, d_context, d_weight, d_images, d_bias, sums, total = refs
+    first = pl.program_id(0) == 0
+    last = pl.program_id(0) == pl.num_programs(0) - 1
+    ids, live = ids[...], live[...]
+    gate = live * pick(ids, table[0])
+    attn = mine[...].astype(F32) + theirs[...].astype(F32) + out_bias[...].astype(F32)
+    xhat, rstd = norm(tokens[...].astype(F32) + gate * attn)
+    d_norm = d_own[...].astype(F32) + d_other[...].astype(F32)
+    grad = cotangent[...].astype(F32) + norm_back(d_norm * (1.0 + pick(ids, table[2])), xhat, rstd)
+    d_middle[...] = grad
+    d_attn = (gate * grad).astype(BF16)
+    d_context[...] = matmul(d_attn, weight[...], ((1,), (1,))).astype(BF16)
+    part = matmul(context[...], d_attn, ((0,), (0,)))
+    total[...] = jnp.where(first, 0.0, total[...]) + part
+    column = jnp.sum(d_attn.astype(F32), axis=0, keepdims=True)
+    d_bias[...] = jnp.where(first, 0.0, d_bias[...]) + column
+    gather_images(ids_row[...], (live * grad * attn, d_norm, d_norm * xhat), sums, first)
+
+    @pl.when(last)
+    def _():
+        d_weight[...] = total[...].astype(BF16)
+        halves_out(sums, d_images, halves)
+
+
+def middle_back(
+    halves, tokens, mine, theirs, cotangent, d_own, d_other, context, ids, live, ids_row, table, out_bias, weight
+):
+    count, width = tokens.shape
+    size = context.shape[1]
+    images = table.shape[1]
+    row, col = tiled(TILE, width), tiled(TILE, 1)
+    consts = (table, out_bias, weight)
+    return token_call(
+        lambda *refs: middle_kernel(halves, *refs),
+        count,
+        "middle_back",
+        [
+            shaped((count, width), F32),
+            shaped((count, size)),
+            shaped((size, width)),
+            shaped((halves, 3, images, width // halves)),
+            shaped((1, width), F32),
+        ],
+        [row] * 6
+        + [tiled(TILE, size), col, col, pl.BlockSpec((1, TILE), lambda i: (0, i))]
+        + [whole(x.shape) for x in consts],
+        [
+            row,
+            tiled(TILE, size),
+            whole((size, width)),
+            whole((halves, 3, images, width // halves)),
+            whole((1, width)),
+        ],
+        [pltpu.VMEM((3, images, width), F32), pltpu.VMEM((size, width), F32)],
+        4 * count * width * size,
+        (tokens, mine, theirs, cotangent, d_own, d_other, context, ids, live, ids_row) + consts,
+    )
+
+
+def project_back_kernel(
+    halves, split, tokens, norm_one, d_q, d_own, rims, tail_start, ids_row, weight, *refs
+):
+    d_norm, top, bottom, d_images, d_bias, sums, total = refs
+    tile = pl.program_id(0)
+    first = tile == 0
+    last = tile == pl.num_programs(0) - 1
+    span, size = rims.shape[2], d_q.shape[1]
+    rows = lax.broadcasted_iota(jnp.int32, (TILE, span), 0) + tile * TILE
+    cols = lax.broadcasted_iota(jnp.int32, (TILE, span), 1)
+    head_rim = (rows == cols).astype(BF16)
+    tail_rim = (rows == cols + tail_start[0]).astype(BF16)
+    parts = [d_q[...]]
+    for which in range(2):
+        rim = matmul(head_rim, rims[0, which]) + matmul(tail_rim, rims[1, which])
+        parts.append((d_own[which].astype(F32) + rim).astype(BF16))
+    normed = norm_one[...]
+    back = 0.0
+    for i, part in enumerate(parts):
+        span_rows = slice(i * size, (i + 1) * size)
+        back += matmul(part, weight[span_rows])
+        grown = matmul(part, normed, ((0,), (0,)))
+        total[span_rows] = jnp.where(first, 0.0, total[span_rows]) + grown
+    back = back.astype(BF16)
+    d_norm[...] = back
+    for i, part in ((0, parts[0]), (1, parts[2])):
+        column = jnp.sum(part.astype(F32), axis=0, keepdims=True)
+        d_bias[i : i + 1] = jnp.where(first, 0.0, d_bias[i : i + 1]) + column
+    xhat, _ = norm(tokens[...].astype(F32))
+    back = back.astype(F32)
+    gather_images(ids_row[...], (back, back * xhat), sums, first)
+
+    @pl.when(last)
+    def _():
+        top[...] = total[:split].astype(BF16)
+        bottom[...] = total[split:].astype(BF16)
+        halves_out(sums, d_images, halves)
+
+
+def project_back(
+    halves, split, images, tokens, norm_one, d_q, d_own, rims, tail_start, ids_row, weight
+):
+    count, width = tokens.shape
+    size = d_q.shape[1]
+    row = tiled(TILE, width)
+    rest = 3 * size - split
+    return token_call(
+        lambda *refs: project_back_kernel(halves, split, *refs),
+        count,
+        "project_back",
+        [
+            shaped((count, width)),
+            shaped((split, width)),
+            shaped((rest, width)),
+            shaped((halves, 2, images, width // halves)),
+            shaped((2, size), F32),
+        ],
+        [
+            row,
+            row,
+            tiled(TILE, size),
+            pl.BlockSpec((2, TILE, size), lambda i: (0, i, 0)),
+            whole(rims.shape),
+            pl.BlockSpec(memory_space=pltpu.SMEM),
+            pl.BlockSpec((1, TILE), lambda i: (0, i)),
+            whole(weight.shape),
+        ],
+        [
+            row,
+            whole((split, width)),
+            whole((rest, width)),
+            whole((halves, 2, images, width // halves)),
+            whole((2, size)),
+        ],
+        [pltpu.VMEM((2, images, width), F32), pltpu.VMEM((3 * size, width), F32)],
+        12 * count * width * size,
+        (tokens, norm_one, d_q, d_own, rims, tail_start, ids_row, weight),
+    )
+
+
 def body(
     tokens,
     condition,
@@ -466,55 +741,46 @@
     valid_counts,
 ):
     wide_count = lax.axis_size("wide")
+    narrow_count = lax.axis_size("narrow")
     wide_index = lax.axis_index("wide")
     narrow_index = lax.axis_index("narrow")
-    tok_dev = cotangent.shape[0]
+    tok_dev, width = cotangent.shape
     share = tokens.shape[0]
-    width = tokens.shape[1]
     part_width = qkv_weight.shape[2]
+    mod_width = modulator.shape[2]
     img_row = condition.shape[0]
     span = IMG_MAX
-    block = min(512, tok_dev)
     own_count = valid_counts[wide_index]
     positions = jnp.arange(tok_dev, dtype=jnp.int32)
     own_ids = lax.dynamic_slice_in_dim(segment_ids, wide_index * tok_dev, tok_dev)
-    live_full = (positions < own_count).astype(jnp.float32)
+    live = (positions < own_count).astype(F32)[:, None]
     share_start = narrow_index * share
-    live = live_full[:, None]
-    image_slots = jnp.arange(img_row, dtype=jnp.int32)
-    onehot_full = (own_ids[:, None] == image_slots[None, :]).astype(BF16)
-    onehot_share = lax.dynamic_slice_in_dim(onehot_full, share_start, share)
+    ids_col, ids_row = own_ids[:, None], own_ids[None]
+    onehot_full = (ids_col == jnp.arange(img_row, dtype=jnp.int32)[None]).astype(BF16)
+
+    def own(rows):
+        return lax.dynamic_slice_in_dim(rows, share_start, share)
+
     cond_rows = condition.astype(F32)
     sigmoid_rows = jax.nn.sigmoid(cond_rows)
     activated = (cond_rows * sigmoid_rows).astype(BF16)
     tok_full = narrow_gather(tokens)
-    mod_width = modulator.shape[2]
     mod_rows = jnp.transpose(modulator, (1, 2, 0)).reshape(6 * mod_width, width)
 
-    def per_token(lo, hi, after=None):
+    def vectors(lo, hi, after=None):
         part = dot(activated, mod_rows[lo * mod_width : hi * mod_width], ((1,), (1,)))
         part = part + modulator_bias[lo:hi].astype(F32).reshape(1, -1)
         rows = jnp.moveaxis(part.astype(BF16).reshape(img_row, hi - lo, -1), 2, 0)
         if after is not None:
             rows, after = lax.optimization_barrier((rows, after))
-        rows = narrow_gather(rows)
-        vectors = [
-            dot(onehot_full, rows[:, :, i], ((1,), (1,)), BF16).astype(F32) for i in range(hi - lo)
-        ]
-        return vectors, after
-
-    (shift_one, scale_one), _ = per_token(0, 2)
-    (gate_one, shift_two, scale_two, gate_two), tok_full = per_token(2, 6, tok_full)
-    tok_full = tok_full.astype(F32)
-    xhat_one, rstd_one = norm(tok_full)
-    norm_one = (xhat_one * (1.0 + scale_one) + shift_one).astype(BF16)
+        return jnp.transpose(narrow_gather(rows), (2, 1, 0)), after
+
+    table_one, _ = vectors(0, 2)
+    table_two, tok_full = vectors(2, 6, tok_full)
     flat_qkv = jnp.transpose(qkv_weight, (1, 2, 0)).reshape(3 * part_width, width)
-    bias_pair = qv_bias.astype(F32)
-    parts_qkv = [flat_qkv[i * part_width : (i + 1) * part_width] for i in range(3)]
-    queries, key_rows, value_rows = [dot(norm_one, part, ((1,), (1,))) for part in parts_qkv]
-    queries = (queries + bias_pair[0]).astype(BF16)
-    key_rows = key_rows.astype(BF16)
-    value_rows = (value_rows + bias_pair[1]).astype(BF16)
+    queries, key_rows, value_rows, norm_one = project(
+        tok_full, ids_col, table_one, flat_qkv, qv_bias
+    )
     tail_start = own_count - span
 
     def tail_of(rows):
@@ -540,85 +806,73 @@
     context, log_sums = attention_forward(
         queries, key_rows, value_rows, from_left, from_right, own_keys[:, None], extended_ids[None]
     )
+    block = min(512, tok_dev)
     blocks = tok_dev // block
 
     def rows_of(rows, block_idx):
         return rows[block_idx * block : (block_idx + 1) * block]
 
-    def own(parts):
-        rows = jnp.concatenate(parts, axis=0)
-        return lax.dynamic_slice_in_dim(rows, share_start, share)
-
-    upstream = cotangent.astype(F32)
-    attns, middles, xhats, rstds = [], [], [], []
-    norms, hiddens, d_uppers, d_branches, d_norms = [], [], [], [], []
-    for block_idx in range(blocks):
-        attn_part = dot(rows_of(context, block_idx), out_weight, ((1,), (0,)), BF16)
-        attns.append(narrow_sum(attn_part) + out_bias.astype(F32))
-    for block_idx in range(blocks):
-        gate_b = rows_of(live * gate_two, block_idx)
-        d_branches.append((gate_b * rows_of(upstream, block_idx)).astype(BF16))
-        d_hidden = dot(d_branches[-1], down_weight, ((1,), (1,)), BF16).astype(F32)
-        middle = rows_of(tok_full, block_idx) + rows_of(live * gate_one, block_idx) * attns[block_idx]
-        xhat, rstd = norm(middle)
-        middles.append(middle)
-        xhats.append(xhat)
-        rstds.append(rstd)
-        scale_b, shift_b = rows_of(scale_two, block_idx), rows_of(shift_two, block_idx)
-        norms.append((xhat * (1.0 + scale_b) + shift_b).astype(BF16))
-        upper = dot(norms[-1], up_weight, ((1,), (0,))) + up_bias.astype(F32)
-        gelu, slope = gelu_pair(upper)
-        hiddens.append(gelu.astype(BF16))
-        d_uppers.append((d_hidden * slope).astype(BF16))
-        d_norms.append(narrow_sum(dot(d_uppers[-1], up_weight, ((1,), (1,)), BF16)))
-    hidden = jnp.concatenate(hiddens, axis=0)
-    d_upper = jnp.concatenate(d_uppers, axis=0)
-    d_branch = jnp.concatenate(d_branches, axis=0)
-    norm_two = jnp.concatenate(norms, axis=0)
+    out_row = out_bias[None]
+    attn_parts, attn_others, mlp_outs, d_others = [], [], [], []
+    for i in range(blocks):
+        attn_parts.append(dot(rows_of(context, i), out_weight, ((1,), (0,)), BF16))
+        attn_others.append(narrow_other(attn_parts[i]))
+    for i in range(blocks):
+        operands = [rows_of(rows, i) for rows in (tok_full, cotangent, ids_col, live)]
+        mlp_outs.append(
+            mlp(
+                operands[0],
+                attn_parts[i],
+                attn_others[i],
+                *operands[1:],
+                table_two,
+                out_row,
+                up_weight,
+                up_bias[None],
+                down_weight,
+            )
+        )
+        d_others.append(narrow_other(mlp_outs[i][4]))
+    norm_two, hidden, d_upper, d_branch, d_norm, branch_part = [
+        jnp.concatenate(parts, axis=0) for parts in zip(*mlp_outs)
+    ]
+    up_grad = dot(d_upper, norm_two, ((0,), (0,)), BF16)
     down_grad = dot(hidden, d_branch, ((0,), (0,)), BF16)
-    up_grad = dot(d_upper, norm_two, ((0,), (0,)), BF16)
     if ring_fits([up_grad]):
         mine = ring_scatter([up_grad, down_grad], None, 1)[0]
-        mine, d_norms = lax.optimization_barrier((mine, d_norms))
-        (up_grad, down_grad), _ = wide_gather(mine, None)
+        mine, d_others = lax.optimization_barrier((mine, d_others))
+        gathered = wide_gather(mine)
     else:
-        up_grad, down_grad = lax.psum((up_grad, down_grad), "wide")
-    up_weight_grad = up_grad.T.astype(F32)
-    down_weight_grad = down_grad.astype(F32)
-    branch_part = dot(hidden, down_weight, ((1,), (0,)), BF16)
+        gathered = lax.psum((up_grad, down_grad), "wide")
+    attn_part, attn_other, d_other = [
+        jnp.concatenate(parts, axis=0) for parts in (attn_parts, attn_others, d_others)
+    ]
     branch = narrow_scatter(branch_part) + down_bias.astype(F32)
-    layer_out = (
-        own(middles) + own([live * gate_two]) * branch
-    ).astype(BF16)
 
     def image_sum(hot, term):
         return dot(hot, term.astype(BF16), ((0,), (0,)))
 
-    def feature_part(rows):
-        return lax.dynamic_slice_in_dim(rows, narrow_index * mod_width, mod_width, axis=1)
-
     first_bias = jnp.where(narrow_index == 0, down_bias.astype(F32), 0.0)
-    d_gate_two = image_sum(onehot_full, live * upstream * (branch_part.astype(F32) + first_bias))
+    d_gate_two = image_sum(
+        onehot_full, live * cotangent.astype(F32) * (branch_part.astype(F32) + first_bias)
+    )
     d_gate_two = narrow_scatter(d_gate_two.astype(BF16), 1)
-    d_middles, d_attns, d_contexts = [], [], []
-    d_gate_one = d_shift_two = d_scale_two = 0.0
-    for block_idx in range(blocks):
-        scale_b = rows_of(scale_two, block_idx)
-        d_norm = d_norms[block_idx]
-        d_middle = rows_of(upstream, block_idx) + norm_back(
-            d_norm * (1.0 + scale_b), xhats[block_idx], rstds[block_idx]
-        )
-        d_middles.append(d_middle)
-        hot = rows_of(onehot_full, block_idx)
-        live_b = rows_of(live, block_idx)
-        d_attns.append((rows_of(live * gate_one, block_idx) * d_middle).astype(BF16))
-        d_contexts.append(dot(d_attns[-1], out_weight, ((1,), (1,)), BF16))
-        d_gate_one += image_sum(hot, feature_part(live_b * d_middle * attns[block_idx]))
-        d_shift_two += image_sum(hot, feature_part(d_norm))
-        d_scale_two += image_sum(hot, feature_part(d_norm * xhats[block_idx]))
-    d_attn = jnp.concatenate(d_attns, axis=0)
-    d_context = jnp.concatenate(d_contexts, axis=0)
-    out_weight_grad = dot(context, d_attn, ((0,), (0,)), BF16)
+    d_middle, d_context, out_weight_grad, images_two, out_bias_sum = middle_back(
+        narrow_count,
+        tok_full,
+        attn_part,
+        attn_other,
+        cotangent,
+        d_norm,
+        d_other,
+        context,
+        ids_col,
+        live,
+        ids_row,
+        table_two,
+        out_row,
+        out_weight,
+    )
     d_queries, d_own, d_rim = attention_backward(
         queries,
         key_rows,
@@ -630,56 +884,76 @@
         own_keys[None],
         extended_ids[:, None],
     )
-    back_left, back_right = to_right(d_rim[1]), to_left(d_rim[0])
-    placed = lax.dynamic_update_slice(jnp.zeros_like(d_own), back_right, (0, tail_start, 0))
-    back_left = jnp.pad(back_left, ((0, 0), (0, tok_dev - span), (0, 0)))
-    d_own = (d_own.astype(F32) + placed.astype(F32) + back_left.astype(F32)).astype(BF16)
-    d_parts = [d_queries, d_own[0], d_own[1]]
-    d_norm_part = sum(dot(d_parts[i], parts_qkv[i], ((1,), (0,))) for i in range(3)).astype(BF16)
-    early = jnp.stack(
-        [
-            image_sum(onehot_full, d_norm_part),
-            image_sum(onehot_full, d_norm_part.astype(F32) * xhat_one),
-        ]
-    ).astype(BF16)
-    early = narrow_scatter(early, 2)
-    qkv_grads = [dot(part, norm_one, ((0,), (0,)), BF16) for part in d_parts]
+    rims = jnp.stack([to_right(d_rim[1]), to_left(d_rim[0])])
+    lane_rows = (4 * part_width * width + 6 * img_row * mod_width) // (2 * width)
+    split = min(lane_rows, 3 * part_width - 16)
+    d_norm_part, top, bottom, images_one, qv_sums = project_back(
+        narrow_count,
+        split,
+        img_row,
+        tok_full,
+        norm_one,
+        d_queries,
+        d_own,
+        rims,
+        tail_start[None],
+        ids_row,
+        flat_qkv,
+    )
+
+    def mine_of(images):
+        return lax.dynamic_index_in_dim(images, narrow_index, 0, keepdims=False)
+
+    if narrow_count == 2:
+        theirs = lax.dynamic_index_in_dim(images_one, 1 - narrow_index, 0, keepdims=False)
+        early = mine_of(images_one).astype(F32) + swap(theirs).astype(F32)
+    else:
+        early = mine_of(lax.psum(images_one, "narrow"))
+    images_two = mine_of(images_two)
     loose_parts = [
         jnp.sum(d_upper.astype(F32), axis=0),
         jnp.sum(d_branch.astype(F32), axis=0),
-        jnp.sum(d_queries.astype(F32), axis=0),
-        jnp.sum(d_own[1].astype(F32), axis=0),
-        jnp.sum(d_attn.astype(F32), axis=0),
+        qv_sums[0],
+        qv_sums[1],
+        out_bias_sum[0],
     ]
     loose = jnp.concatenate(loose_parts)
     loose = jnp.pad(loose, (0, (-loose.shape[0]) % (8 * width))).reshape(-1, width).astype(BF16)
-    late = [d_gate_one, d_shift_two, d_scale_two, d_gate_two]
-    terms = [term.astype(BF16) for term in [early[0], early[1]] + late]
+    terms = [early[0], early[1], images_two[0], images_two[1], images_two[2], d_gate_two]
+    terms = [term.astype(BF16) for term in terms]
     d_mod = [jnp.concatenate(terms[2 * i : 2 * i + 2], axis=1) for i in range(3)]
     if 2 * mod_width == width:
         d_mod_flat = jnp.concatenate(d_mod, axis=0)
     else:
         d_mod_flat = jnp.concatenate(d_mod, axis=1).reshape(-1, width)
-    flat = jnp.concatenate(qkv_grads + [out_weight_grad, d_mod_flat], axis=0)
-    lanes = [flat[: flat.shape[0] // 2], flat[flat.shape[0] // 2 :]]
-    if ring_fits(lanes):
-        mine, d_norm_other = ring_scatter(lanes, d_norm_part, 0)
-        d_norm_one = own([d_norm_part.astype(F32)]) + d_norm_other.astype(F32)
-        lanes, loose = wide_gather(mine, loose)
-        flat = jnp.concatenate(lanes, axis=0)
+    rest = jnp.concatenate([bottom, out_weight_grad, d_mod_flat], axis=0)
+    if ring_fits([top]) and top.shape == rest.shape:
+        gathered, rest = lax.optimization_barrier((gathered, rest))
+        mine, d_norm_other = ring_scatter([top, rest], d_norm_part, 0)
+        (up_grad, down_grad), _ = lanes_of(gathered, gathered.shape[1] // 2)
+        d_norm_one = own(d_norm_part).astype(F32) + d_norm_other.astype(F32)
+        (top, rest), loose = lanes_of(wide_gather(mine, loose), mine.shape[1])
     else:
+        up_grad, down_grad = gathered
         d_norm_one = narrow_scatter(d_norm_part)
-        flat = lax.psum(flat, "wide")
+        top, rest = lax.psum((top, rest), "wide")
         loose = lax.all_gather(loose, "wide", axis=0).astype(F32)
+    tok_own = tokens.astype(F32)
+    xhat_one, rstd_one = norm(tok_own)
+    hot_own = own(onehot_full)
+    scale_one = dot(hot_own, table_one[1], ((1,), (0,)))
+    tokens_grad = own(d_middle) + norm_back(d_norm_one * (1.0 + scale_one), xhat_one, rstd_one)
+    attn_own = own(attn_part).astype(F32) + own(attn_other).astype(F32) + out_bias.astype(F32)
+    live_own = own(live)
+    gates = [dot(hot_own, table_two[j], ((1,), (0,))) for j in (0, 3)]
+    layer_out = (tok_own + live_own * (gates[0] * attn_own + gates[1] * branch)).astype(BF16)
+    up_weight_grad = up_grad.T.astype(F32)
+    down_weight_grad = down_grad.astype(F32)
     loose = jnp.sum(loose, axis=0)
-    tokens_grad = own(d_middles) + norm_back(
-        d_norm_one * (1.0 + own([scale_one])), own([xhat_one]), own([rstd_one])
-    )
-    starts = [0, 3 * part_width, 4 * part_width]
-    qkv_weight_grad = jnp.transpose(
-        flat[: starts[1]].astype(F32).reshape(3, part_width, width), (2, 0, 1)
-    )
-    out_weight_grad = flat[starts[1] : starts[2]].astype(F32)
+    keep = 3 * part_width - split
+    qkv_flat = jnp.concatenate([top.astype(F32), rest[:keep].astype(F32)], axis=0)
+    qkv_weight_grad = jnp.transpose(qkv_flat.reshape(3, part_width, width), (2, 0, 1))
+    out_weight_grad = rest[keep : keep + part_width].astype(F32)
     loose = loose.reshape(-1)
     bounds = [0]
     for part in loose_parts:
@@ -688,7 +962,7 @@
         loose[bounds[i] : bounds[i + 1]] for i in range(5)
     ]
     qv_bias_grad = jnp.stack([query_bias, value_bias])
-    d_mod_flat = flat[starts[2] :]
+    d_mod_flat = rest[keep + part_width :]
     if 2 * mod_width == width:
         d_mod = d_mod_flat.reshape(3, img_row, width)
     else:
@@ -701,7 +975,8 @@
     mod_blocks = mod_rows.reshape(3, 2 * mod_width, width)
     d_activated = sum(dot(d_mod[i], mod_blocks[i], ((1,), (0,))) for i in range(3))
     cond_part = d_activated * sigmoid_rows * (1.0 + cond_rows * (1.0 - sigmoid_rows))
-    condition_grad = narrow_sum(cond_part.astype(BF16))
+    cond_part = cond_part.astype(BF16)
+    condition_grad = cond_part.astype(F32) + narrow_other(cond_part).astype(F32)
     return (
         layer_out,
         tokens_grad,

time: 686 us -> 591 us (0.86)
  Pallas kernels: 154 us -> 268 us
  matrix products: 154 us -> 54 us
  waiting for transfers between devices: 153 us -> 62.6 us
  other arithmetic: 90.1 us -> 64.1 us
  local copies, waits for them, and re-layouts: 86.8 us -> 95.8 us
    pallas_call x0 -> x5, Pallas kernels: none -> 108 us  [token_call(): pl.pallas_call(kernel, grid=(tokens // TILE,), out_shape=out_shape, in_sp...]
    dot_general x43 -> x13, matrix products: 146 us -> 43.8 us  [dot(): lax.dot_general(left, right, (dims, ((), ())), preferred_element_type=F32)]
    all_gather x2, waiting for transfers between devices: 74.7 us -> 0.02 us  [wide_gather(): return lax.all_gather(parts, 'wide', axis=0)]
    convert_element_type x11 -> x5, other arithmetic: 20.5 us -> 4.85 us  [the longest x2 2.15 us: body(): live = (positions < own_count).astype(F32)[:, None]]
    ppermute x11, waiting for transfers between devices: 75.9 us -> 62.5 us  [swap(): return lax.ppermute(part, 'narrow', [(0, 1), (1, 0)])]
    reduce_sum x6 -> x0, other arithmetic: 10.7 us -> none  [the longest x2 5.33 us: norm_back(): jnp.mean(grad, axis=-1, keepdims=True)]
    transpose x1 -> x3, other arithmetic: 3.77 us -> 10.9 us  [the longest x2 7.11 us: vectors(): return (jnp.transpose(narrow_gather(rows), (2, 1, 0)), after)]
    unnamed x194 -> x131, local copies, waits for them, and re-layouts: 28.7 us -> 32.5 us
  transfers between devices with their start and end apart: 17 -> 17, of which waited for: 8 -> 5; matrix products, arithmetic and copies ran while one was open for 24% -> 30% of each run, Pallas kernels for 12% -> 35%
where the time goes in v4:
time: 591 us; the launch traced here: 583 us
  Pallas kernels  268 us (45%)
  local copies, waits for them, and re-layouts  95.8 us (16%)
  other arithmetic  64.1 us (11%)
  waiting for transfers between devices  62.6 us (11%)
  matrix products  54 us (9%)
  starting transfers between devices  21 us (4%)
  between operations  17.1 us (3%)
    pallas_call x2, Pallas kernels, ring_scatter(): pl.pallas_call(lambda *refs: ring_kernel(chips, subs, int(part is not Non...  123 us
    pallas_call x5, Pallas kernels, token_call(): pl.pallas_call(kernel, grid=(tokens // TILE,), out_shape=out_shape, in_sp...  108 us
    ppermute x11, waiting for transfers between devices, swap(): return lax.ppermute(part, 'narrow', [(0, 1), (1, 0)])  62.5 us
    dot_general x13, matrix products, dot(): lax.dot_general(left, right, (dims, ((), ())), preferred_element_type=F32)  43.8 us
    unnamed x131, local copies, waits for them, and re-layouts  32.5 us
    pallas_call x1, Pallas kernels, attention_backward(): pl.pallas_call(lambda *refs: backward_kernel(tiles, *refs), grid=(tiles,)...  26.2 us
    ppermute x11, starting transfers between devices, swap(): return lax.ppermute(part, 'narrow', [(0, 1), (1, 0)])  13.1 us
  transfers between devices with their start and end apart: 17, of which 5 were waited for; matrix products, arithmetic and copies ran while one was open for 30% of the time, Pallas kernels for 35%

profile of v4, /device:TPU:0, one launch (start us, length us, event | category | flops | bytes accessed | tf_op | source)
XLA Modules:
  0.0 582.6 jit_solution(1053211666390284579)
XLA Ops:
  10.3 5.2 fusion.62
  18.9 5.3 slice.234
  38.1 11.1 %collective-permute-done.2 = bf16[576,256,2]{1,0,2:T(8,128)(2,1)} collective-permute-done((bf16[576,256,2]{1,0,2:T(8,128)(2,1)S(1)}, bf16[576,256,2]{1,0,2:T(8,128)(2,1)}, u32[]{:S(2)}, u32[]{:S(2)}) %collective-permute-start.2) | collective-permute-done | bytes 589856 | tf_op jit(solution)/shard_map/ppermute | solution.py:21
  56.5 12.8 %project.1 = (bf16[1024,576]{1,0:T(8,128)(2,1)}, bf16[1024,576]{1,0:T(8,128)(2,1)}, bf16[1024,576]{1,0:T(8,128)(2,1)}, bf16[1024,1152]{1,0:T(8,128)(2,1)}) custom-call(bf16[1024,1152]{1,0:T(8,128)(2,1)} %maximum_select_fusion.tokens.refs_0_, s32[1024,1]{1,0:T(8,128)} %copy.74.ids.refs_7_, bf16[2,256,1152]{2,1,0:T(8,128)(2,1)} %fusion.38.table, ...), custom_call_target="tpu_custom_call" | custom-call | flops 4076863488 | bytes 11289984 | tf_op jit(solution)/shard_map/project/pallas_call | solution.py:489
  86.7 10.8 %attention_forward.1 = (bf16[1024,576]{1,0:T(8,128)(2,1)S(1)}, f32[8,1024]{1,0:T(8,128)S(1)}) custom-call(bf16[1024,576]{1,0:T(8,128)(2,1)S(1)} %copy-done.11, bf16[1024,576]{1,0:T(8,128)(2,1)S(1)} %copy-done.4, bf16[1024,576]{1,0:T(8,128)(2,1)S(1)} %copy-done.5, bf16[2,128,576]{2,1,0:T(8,128)(2,1)S(1)} %collective-permute-done.3.refs_3_, ...), custom_call_target="tpu_custom_call" | custom-call | flops 1207959552 | bytes 4718592 | tf_op jit(solution)/shard_map/attention_forward/pallas_call | solution.py:292
  110.0 5.2 fusion.22.table.refs_10_
  115.2 17.7 %collective-permute-done.5.theirs = bf16[512,1152]{1,0:T(8,128)(2,1)} collective-permute-done((bf16[512,1152]{1,0:T(8,128)(2,1)}, bf16[512,1152]{1,0:T(8,128)(2,1)}, u32[]{:S(2)}, u32[]{:S(2)}) %collective-permute-start.5) | collective-permute-done | bytes 1179680 | tf_op jit(solution)/shard_map/ppermute | solution.py:21
  132.9 27.3 %mlp.2 = (bf16[512,1152]{1,0:T(8,128)(2,1)}, bf16[512,2304]{1,0:T(8,128)(2,1)}, bf16[512,2304]{1,0:T(8,128)(2,1)}, bf16[512,1152]{1,0:T(8,128)(2,1)}, bf16[512,1...) custom-call(bf16[512,1152]{1,0:T(8,128)(2,1)} %get-tuple-element.174.tokens, ...), custom_call_target="tpu_custom_call" | custom-call | flops 10871635968 | bytes 26558592 | tf_op jit(solution)/shard_map/mlp/pallas_call | solution.py:489
  162.3 27.1 %mlp.3 = (bf16[512,1152]{1,0:T(8,128)(2,1)}, bf16[512,2304]{1,0:T(8,128)(2,1)}, bf16[512,2304]{1,0:T(8,128)(2,1)}, bf16[512,1152]{1,0:T(8,128)(2,1)}, bf16[512,1...) custom-call(bf16[512,1152]{1,0:T(8,128)(2,1)} %get-tuple-element.175.tokens, ...), custom_call_target="tpu_custom_call" | custom-call | flops 10871635968 | bytes 26558592 | tf_op jit(solution)/shard_map/mlp/pallas_call | solution.py:489
  189.5 9.5 %convolution_convert_fusion.1 = bf16[2304,1152]{1,0:T(8,128)(2,1)S(1)} fusion(bf16[512,2304]{1,0:T(8,128)(2,1)} %get-tuple-element.64, bf16[512,2304]{1,0:T(8,128)(2,1)} %get-tuple-element.63, bf16[512,1152]{1,0:T(8,128)(2,1)} %get-tuple-element.66, bf16[512,1152]{1,0:T(8,128)(2,1)} %get-tuple-element.65), kind=kOutput, calls=%fused_computation.1 | convolution fusion | flops 5452627968 | bytes 12386304 | tf_op jit(solution)/shard_map/dot_general | solution.py:17
  199.0 6.6 %convolution_convert_fusion = bf16[2304,1152]{1,0:T(8,128)(2,1)S(1)} fusion(bf16[512,2304]{1,0:T(8,128)(2,1)S(1)} %copy-done.60, bf16[512,2304]{1,0:T(8,128)(2,1)S(1)} %copy-done.59, bf16[512,1152]{1,0:T(8,128)(2,1)S(1)} %copy-done.37, bf16[512,1152]{1,0:T(8,128)(2,1)S(1)} %copy-done.35), kind=kOutput, calls=%fused_computation | convolution fusion | flops 5452627968 | bytes 12386304 | tf_op jit(solution)/shard_map/dot_general | solution.py:17
  205.7 70.9 %ring_scatter.2 = bf16[2,144,1152]{2,1,0:T(8,128)(2,1)} custom-call(bf16[8,2,144,1152]{3,2,1,0:T(8,128)(2,1)S(1)} %bitcast.119, bf16[8,2,144,1152]{3,2,1,0:T(8,128)(2,1)S(1)} %bitcast.120), custom_call_target="tpu_custom_call" | custom-call | tf_op jit(solution)/shard_map/ring_scatter/pallas_call | solution.py:179
  306.1 19.1 %middle_back.1 = (f32[1024,1152]{1,0:T(8,128)}, bf16[1024,576]{1,0:T(8,128)(2,1)}, bf16[576,1152]{1,0:T(8,128)(2,1)}, bf16[2,3,256,576]{3,2,1,0:T(8,128)(2,1)}, f32[1,1152]{1,0:T(1,128)}) custom-call(bf16[1024,1152]{1,0:T(8,128)(2,1)} %maximum_select_fusion.tokens.refs_0_, bf16[1024,1152]{1,0:T(8,128)(2,1)} %pad_maximum_fusion.1.refs_1_, ...), custom_call_target="tpu_custom_call" | custom-call | flops 2717908992 | bytes 28554624 | tf_op jit(solution)/shard_map/middle_back/pallas_call | solution.py:489
  326.6 26.2 %attention_backward.1 = (bf16[1024,576]{1,0:T(8,128)(2,1)S(1)}, bf16[2,1024,576]{2,1,0:T(8,128)(2,1)}, bf16[2,2,128,576]{3,2,1,0:T(8,128)(2,1)S(1)}) custom-call(bf16[1024,576]{1,0:T(8,128)(2,1)S(1)} %copy-done.12, bf16[1024,576]{1,0:T(8,128)(2,1)S(1)} %copy-done.4, bf16[1024,576]{1,0:T(8,128)(2,1)} %get-tuple-element.57.refs_2_, ...), custom_call_target="tpu_custom_call" | custom-call | flops 3019898880 | bytes 9437184 | tf_op jit(solution)/shard_map/attention_backward/pallas_call | solution.py:393
  360.6 21.5 %project_back.1 = (bf16[1024,1152]{1,0:T(8,128)(2,1)}, bf16[1536,1152]{1,0:T(8,128)(2,1)}, bf16[192,1152]{1,0:T(8,128)(2,1)}, bf16[2,2,256,576]{3,2,1,0:T(8,128)(2,1)}, f32[2,576]{1,0:T(2,128)}) custom-call(bf16[1024,1152]{1,0:T(8,128)(2,1)} %maximum_select_fusion.tokens.refs_0_, bf16[1024,1152]{1,0:T(8,128)(2,1)} %get-tuple-element.74.refs_1_, ...), custom_call_target="tpu_custom_call" | custom-call | flops 8153726976 | bytes 19249158 | tf_op jit(solution)/shard_map/project_back/pallas_call | solution.py:489
  387.7 8.8 %collective-permute-done.12 = bf16[2,256,576]{1,2,0:T(8,128)(2,1)} collective-permute-done((bf16[2,256,576]{1,2,0:T(8,128)(2,1)}, bf16[2,256,576]{1,2,0:T(8,128)(2,1)}, u32[]{:S(2)}, u32[]{:S(2)}) %collective-permute-start.12) | collective-permute-done | bytes 589856 | tf_op jit(solution)/shard_map/ppermute | solution.py:21
  405.0 52.2 %ring_scatter.3 = (bf16[2,96,1152]{2,1,0:T(8,128)(2,1)S(1)}, bf16[512,1152]{1,0:T(8,128)(2,1)S(1)}) custom-call(bf16[8,2,96,1152]{3,2,1,0:T(8,128)(2,1)S(1)} %bitcast.122, bf16[8,2,96,1152]{3,2,1,0:T(8,128)(2,1)S(1)} %bitcast.121, bf16[1024,1152]{1,0:T(8,128)(2,1)S(1)} %copy-done.1), custom_call_target="tpu_custom_call" | custom-call | tf_op jit(solution)/shard_map/ring_scatter/pallas_call | solution.py:179
  463.2 23.7 %collective-permute-done.7 = bf16[512,1152]{1,0:T(8,128)(2,1)S(1)} collective-permute-done((bf16[512,1152]{1,0:T(8,128)(2,1)S(1)}, bf16[512,1152]{1,0:T(8,128)(2,1)S(1)}, u32[]{:S(2)}, u32[]{:S(2)}) %collective-permute-start.7) | collective-permute-done | bytes 1179680 | tf_op jit(solution)/shard_map/ppermute | solution.py:21
  486.9 4.4 fusion.21
  491.3 9.0 %fusion.61 = (bf16[16,144,1152]{2,1,0:T(8,128)(2,1)}, bf16[16,144,1152]{2,1,0:T(8,128)(2,1)}) fusion(bf16[16,288,1152]{2,1,0:T(8,128)(2,1)} %all-gather.4.cloned.1.call-done), kind=kLoop, calls=%fused_computation.145 | loop fusion | bytes 21233664 | tf_op jit(solution)/shard_map/slice | solution.py:207
  500.3 7.3 %convert_bitcast_fusion = f32[1152,2304]{0,1:T(8,128)} fusion(bf16[16,144,1152]{2,1,0:T(8,128)(2,1)} %get-tuple-element.141), kind=kLoop, calls=%fused_computation.2 | loop fusion | flops 2654208 | bytes 15925248 | tf_op jit(solution)/shard_map/convert_element_type | solution.py:950
  507.6 13.3 %copy.85 = f32[1152,2304]{1,0:T(8,128)} copy(f32[1152,2304]{0,1:T(8,128)} %convert_bitcast_fusion) | data formatting | bytes 21233664
  527.7 5.2 bitcast_convert_fusion
  552.7 10.2 %fusion.44 = f32[1152,6,576]{0,2,1:T(8,128)} fusion(bf16[6,576,256]{2,1,0:T(8,128)(2,1)} %bitcast.140, bf16[256,1152]{1,0:T(8,128)(2,1)} %param.16), kind=kOutput, calls=%fused_computation.89 | convolution fusion | flops 2040201216 | bytes 18284544 | tf_op jit(solution)/shard_map/dot_general | solution.py:970
  (272 shorter events, 155.0 us)
Async XLA Ops:
  7.2 394.2 %all-gather.4.cloned.1.call-start = ((), (), s32[]{:S(2)}) async-start(), calls=%async_computation | async-start | bytes 11280384 | tf_op jit(solution)/shard_map/all_gather | solution.py:202
  7.2 45.3 %collective-permute-start = (bf16[512,1152]{1,0:T(8,128)(2,1)}, bf16[512,1152]{1,0:T(8,128)(2,1)}, u32[]{:S(2)}, u32[]{:S(2)}) collective-permute-start(bf16[512,1152]{1,0:T(8,128)(2,1)} %param.15), channel_id=1, source_target_pairs={{0,1},{1,0},{2,3},{3,2},{4,5},{5,4},{6,7},{7,6},{8,9},{9,8},{10,11... | collective-permute-start | bytes 3538952 | tf_op jit(solution)/shard_map/ppermute | solution.py:21
  18.8 30.4 %collective-permute-start.2 = (bf16[576,256,2]{1,0,2:T(8,128)(2,1)S(1)}, bf16[576,256,2]{1,0,2:T(8,128)(2,1)}, u32[]{:S(2)}, u32[]{:S(2)}) collective-permute-start(bf16[576,256,2]{1,0,2:T(8,128)(2,1)S(1)} %bitcast.152), channel_id=1, source_target_pairs={{0,1},{1,0},{2,3},{3,2},{4,5},{5,4},{6,7},{7,6},{8,9},{9,8},{10,11... | collective-permute-start | bytes 1769480 | tf_op jit(solution)/shard_map/ppermute | solution.py:21
  32.7 259.3 %copy-start.48 = (s32[1024]{0:T(1024)}, s32[1024]{0:T(1024)S(1)}, u32[]{:S(2)}) copy-start(s32[1024]{0:T(1024)S(1)} %get-tuple-element.139) | copy-start | bytes 12292
  70.6 11.7 %collective-permute-start.3 = (bf16[2,128,576]{2,1,0:T(8,128)(2,1)S(1)}, bf16[2,128,576]{2,1,0:T(8,128)(2,1)S(1)}, u32[]{:S(2)}, u32[]{:S(2)}) collective-permute-start(bf16[2,128,576]{2,1,0:T(8,128)(2,1)S(1)} %pad_maximum_fusion.6), channel_id=1, source_target_pairs={{0,2},{2,4},{4,6},{6,8},{8,10},{10,12},{12,14},{14,16},{16,18},{18... | collective-permute-start | bytes 884744 | tf_op jit(solution)/shard_map/ppermute | solution.py:790
  72.1 10.2 %collective-permute-start.4 = (bf16[2,128,576]{2,1,0:T(8,128)(2,1)S(1)}, bf16[2,128,576]{2,1,0:T(8,128)(2,1)S(1)}, u32[]{:S(2)}, u32[]{:S(2)}) collective-permute-start(bf16[2,128,576]{2,1,0:T(8,128)(2,1)S(1)} %pad_maximum_fusion.7), channel_id=1, source_target_pairs={{2,0},{4,2},{6,4},{8,6},{10,8},{12,10},{14,12},{16,14},{18,16},{20... | collective-permute-start | bytes 884744 | tf_op jit(solution)/shard_map/ppermute | solution.py:793
  80.6 27.0 %collective-permute-start.1 = (bf16[576,256,4]{1,0,2:T(8,128)(2,1)}, bf16[576,256,4]{1,0,2:T(8,128)(2,1)}, u32[]{:S(2)}, u32[]{:S(2)}) collective-permute-start(bf16[576,256,4]{1,0,2:T(8,128)(2,1)} %copy.66), channel_id=1, source_target_pairs={{0,1},{1,0},{2,3},{3,2},{4,5},{5,4},{6,7},{7,6},{8,9},{9,8},{10,11... | collective-permute-start | bytes 3538952 | tf_op jit(solution)/shard_map/ppermute | solution.py:21
  99.8 33.1 %collective-permute-start.5 = (bf16[512,1152]{1,0:T(8,128)(2,1)}, bf16[512,1152]{1,0:T(8,128)(2,1)}, u32[]{:S(2)}, u32[]{:S(2)}) collective-permute-start(bf16[512,1152]{1,0:T(8,128)(2,1)} %convolution_convert_fusion.3.mine), channel_id=1, source_target_pairs={{0,1},{1,0},{2,3},{3,2},{4,5},{5,4},{6,7},{7,6},{8,9},{9,8},{10,11... | collective-permute-start | bytes 3538952 | tf_op jit(solution)/shard_map/ppermute | solution.py:21
  104.7 57.6 %collective-permute-start.6 = (bf16[512,1152]{1,0:T(8,128)(2,1)}, bf16[512,1152]{1,0:T(8,128)(2,1)}, u32[]{:S(2)}, u32[]{:S(2)}) collective-permute-start(bf16[512,1152]{1,0:T(8,128)(2,1)} %convolution_convert_fusion.2.mine), channel_id=1, source_target_pairs={{0,1},{1,0},{2,3},{3,2},{4,5},{5,4},{6,7},{7,6},{8,9},{9,8},{10,11... | collective-permute-start | bytes 3538952 | tf_op jit(solution)/shard_map/ppermute | solution.py:21
  160.2 116.3 %collective-permute-start.8 = (bf16[512,1152]{1,0:T(8,128)(2,1)}, bf16[512,1152]{1,0:T(8,128)(2,1)S(1)}, u32[]{:S(2)}, u32[]{:S(2)}) collective-permute-start(bf16[512,1152]{1,0:T(8,128)(2,1)} %get-tuple-element.61), channel_id=1, source_target_pairs={{0,1},{1,0},{2,3},{3,2},{4,5},{5,4},{6,7},{7,6},{8,9},{9,8},{10,11... | collective-permute-start | bytes 3538952 | tf_op jit(solution)/shard_map/ppermute | solution.py:21
  189.4 87.2 %collective-permute-start.9 = (bf16[512,1152]{1,0:T(8,128)(2,1)}, bf16[512,1152]{1,0:T(8,128)(2,1)}, u32[]{:S(2)}, u32[]{:S(2)}) collective-permute-start(bf16[512,1152]{1,0:T(8,128)(2,1)} %get-tuple-element.62), channel_id=1, source_target_pairs={{0,1},{1,0},{2,3},{3,2},{4,5},{5,4},{6,7},{7,6},{8,9},{9,8},{10,11... | collective-permute-start | bytes 3538952 | tf_op jit(solution)/shard_map/ppermute | solution.py:21
  205.6 73.7 %copy-start.51 = (bf16[1152]{0:T(1024)(128)(2,1)S(1)}, bf16[1152]{0:T(1024)(128)(2,1)}, u32[]{:S(2)}) copy-start(bf16[1152]{0:T(1024)(128)(2,1)} %param.27) | copy-start | bytes 6916
  276.6 256.3 %all-gather.6.cloned.1.call-start = ((), (), s32[]{:S(2)}) async-start(), calls=%async_computation.1 | async-start | bytes 7833600 | tf_op jit(solution)/shard_map/all_gather | solution.py:202
  295.0 62.7 %collective-permute-start.13 = (bf16[256,576]{1,0:T(8,128)(2,1)}, bf16[256,576]{1,0:T(8,128)(2,1)S(1)}, u32[]{:S(2)}, u32[]{:S(2)}) collective-permute-start(bf16[256,576]{1,0:T(8,128)(2,1)} %constant_dynamic-slice_fusion), channel_id=1, source_target_pairs={{0,1},{1,0},{2,3},{3,2},{4,5},{5,4},{6,7},{7,6},{8,9},{9,8},{10,11... | collective-permute-start | bytes 884744 | tf_op jit(solution)/shard_map/ppermute | solution.py:21
  306.1 19.2 %copy-start.10 = (bf16[2,128,576]{2,1,0:T(8,128)(2,1)S(1)}, bf16[2,128,576]{2,1,0:T(8,128)(2,1)}, u32[]{:S(2)}) copy-start(bf16[2,128,576]{2,1,0:T(8,128)(2,1)} %copy-done.8) | copy-start | bytes 884740
  326.6 32.0 %copy-start.57 = (f32[1,1152]{1,0:T(1,128)S(1)}, f32[1,1152]{1,0:T(1,128)}, u32[]{:S(2)}) copy-start(f32[1,1152]{1,0:T(1,128)} %get-tuple-element.91) | copy-start | bytes 13828
  352.8 6.8 %collective-permute-start.11 = (bf16[2,128,576]{2,1,0:T(8,128)(2,1)S(1)}, bf16[2,128,576]{2,1,0:T(8,128)(2,1)S(1)}, u32[]{:S(2)}, u32[]{:S(2)}) collective-permute-start(bf16[2,128,576]{2,1,0:T(8,128)(2,1)S(1)} %get-tuple-element.159), channel_id=1, source_target_pairs={{2,0},{4,2},{6,4},{8,6},{10,8},{12,10},{14,12},{16,14},{18,16},{20... | collective-permute-start | bytes 884744 | tf_op jit(solution)/shard_map/ppermute | solution.py:793
  354.6 5.0 collective-permute-start.10
  384.3 12.2 %collective-permute-start.12 = (bf16[2,256,576]{1,2,0:T(8,128)(2,1)}, bf16[2,256,576]{1,2,0:T(8,128)(2,1)}, u32[]{:S(2)}, u32[]{:S(2)}) collective-permute-start(bf16[2,256,576]{1,2,0:T(8,128)(2,1)} %bitcast.39), channel_id=1, source_target_pairs={{0,1},{1,0},{2,3},{3,2},{4,5},{5,4},{6,7},{7,6},{8,9},{9,8},{10,11... | collective-permute-start | bytes 1769480 | tf_op jit(solution)/shard_map/ppermute | solution.py:21
  405.0 53.3 %copy-start.50 = (bf16[8,1152]{1,0:T(8,128)(2,1)S(1)}, bf16[8,1152]{1,0:T(8,128)(2,1)}, u32[]{:S(2)}) copy-start(bf16[8,1152]{1,0:T(8,128)(2,1)} %convert_element_type.199) | copy-start | bytes 55300
  460.7 26.2 %collective-permute-start.7 = (bf16[512,1152]{1,0:T(8,128)(2,1)S(1)}, bf16[512,1152]{1,0:T(8,128)(2,1)S(1)}, u32[]{:S(2)}, u32[]{:S(2)}) collective-permute-start(bf16[512,1152]{1,0:T(8,128)(2,1)S(1)} %constant_dynamic-slice_fusion.2), channel_id=1, source_target_pairs={{0,1},{1,0},{2,3},{3,2},{4,5},{5,4},{6,7},{7,6},{8,9},{9,8},{10,11... | collective-permute-start | bytes 3538952 | tf_op jit(solution)/shard_map/ppermute | solution.py:21
  461.9 25.0 %copy-start.28 = (bf16[1024,1152]{1,0:T(8,128)(2,1)S(1)}, bf16[1024,1152]{1,0:T(8,128)(2,1)}, u32[]{:S(2)}) copy-start(bf16[1024,1152]{1,0:T(8,128)(2,1)} %copy-done.27) | copy-start | bytes 7077892
  462.7 24.2 %copy-start.45 = (pred[1024,256]{1,0:T(32,128)(4,1)}, pred[1024,256]{1,0:T(32,128)(4,1)S(1)}, u32[]{:S(2)}) copy-start(pred[1024,256]{1,0:T(32,128)(4,1)S(1)} %iota_compare_fusion) | copy-start | bytes 786436
  548.8 24.4 %collective-permute-start.14 = (bf16[256,1152]{1,0:T(8,128)(2,1)}, bf16[256,1152]{1,0:T(8,128)(2,1)}, u32[]{:S(2)}, u32[]{:S(2)}) collective-permute-start(bf16[256,1152]{1,0:T(8,128)(2,1)} %fusion.14), channel_id=1, source_target_pairs={{0,1},{1,0},{2,3},{3,2},{4,5},{5,4},{6,7},{7,6},{8,9},{9,8},{10,11... | collective-permute-start | bytes 1769480 | tf_op jit(solution)/shard_map/ppermute | solution.py:21
  (57 other events, 284.7 us)
Sparse Core Ops, SparseCore 0:
  276.7 88.9 all-gather.3
  459.3 67.0 all-gather.5

commit v5 on v4

--- a/solution.py
+++ b/solution.py
@@ -52,12 +52,11 @@
 UNIT = 48
 
 
-def ring_kernel(chips, subs, swapped, *refs):
-    data = refs[:2]
-    out, mine, theirs, slots, copy_sems, core_sems, ring_sems = refs[2 + swapped :][:7]
-    if swapped:
-        part, (out, landing, *rest) = refs[2], refs[3:]
-        mine, theirs, slots, copy_sems, core_sems, ring_sems, swap_sems = rest
+def ring_kernel(chips, subs, *refs):
+    data, part, loose, out, landing, loose_out = refs[:2], *refs[2:7]
+    mine, theirs, slots, last, loose_pair, loose_rows = refs[7:13]
+    copy_sems, core_sems, ring_sems, swap_sems, gather_sems, pair_sems, own_sems = refs[13:20]
+    loose_pair_sems, loose_sems = refs[20:]
     wide = lax.axis_index("wide")
     chip, core = wide // 2, wide % 2
     half = chips // 2
@@ -71,24 +70,41 @@
     ahead = 2 * place(position + 1) + core
     behind = 2 * place(position - 1) + core
     sibling = 2 * chip + 1 - core
+    facing = 1 - lax.axis_index("narrow")
     barrier = pltpu.get_barrier_semaphore()
     for device in (ahead, behind, sibling):
         pl.semaphore_signal(barrier, inc=1, device_id={"wide": device}, device_id_type=MESH)
-    if swapped:
-        facing = 1 - lax.axis_index("narrow")
-        pl.semaphore_signal(barrier, inc=1, device_id={"narrow": facing}, device_id_type=MESH)
-    pl.semaphore_wait(barrier, 3 + swapped)
-    if swapped:
-        share = landing.shape[0]
-        turn = pltpu.make_async_remote_copy(
-            src_ref=part.at[pl.ds(facing * share, share)],
-            dst_ref=landing,
-            send_sem=swap_sems.at[0],
-            recv_sem=swap_sems.at[1],
-            device_id={"narrow": facing},
+    pl.semaphore_signal(barrier, inc=1, device_id={"narrow": facing}, device_id_type=MESH)
+    pl.semaphore_wait(barrier, 4)
+    share = landing.shape[0]
+    turn = pltpu.make_async_remote_copy(
+        src_ref=part.at[pl.ds(facing * share, share)],
+        dst_ref=landing,
+        send_sem=swap_sems.at[0],
+        recv_sem=swap_sems.at[1],
+        device_id={"narrow": facing},
+        device_id_type=MESH,
+    )
+    turn.start()
+    loose_swap = pltpu.make_async_remote_copy(
+        src_ref=loose,
+        dst_ref=loose_pair,
+        send_sem=loose_pair_sems.at[0],
+        recv_sem=loose_pair_sems.at[1],
+        device_id={"wide": sibling},
+        device_id_type=MESH,
+    )
+    loose_swap.start()
+
+    def loose_hop(step, index):
+        return pltpu.make_async_remote_copy(
+            src_ref=loose_rows.at[index],
+            dst_ref=loose_rows.at[index],
+            send_sem=loose_sems.at[0, step],
+            recv_sem=loose_sems.at[1, step],
+            device_id={"wide": ahead},
             device_id_type=MESH,
         )
-        turn.start()
 
     def local(lane):
         return pltpu.make_async_copy(data[lane].at[:, core], mine.at[lane], copy_sems.at[lane])
@@ -107,8 +123,11 @@
         across(lane).start()
         local(lane).start()
 
+    def rows_of(sub):
+        return pl.ds(sub * UNIT, UNIT)
+
     def hop(lane, step, sub):
-        rows = pl.ds(sub * UNIT, UNIT)
+        rows = rows_of(sub)
         if step == 0:
             first = place(position - 1 if lane == 0 else position + 1)
             source = mine.at[lane, first, rows]
@@ -123,6 +142,50 @@
             device_id_type=MESH,
         )
 
+    def held(lane, step, sub, side):
+        index = place(position - step if lane == 0 else position + step)
+        return out.at[lane, index, side, rows_of(sub)]
+
+    def send_on(lane, step, sub):
+        source = last.at[lane, rows_of(sub)] if step == 0 else held(lane, step, sub, core)
+        return pltpu.make_async_remote_copy(
+            src_ref=source,
+            dst_ref=held(lane, step, sub, core),
+            send_sem=gather_sems.at[0, lane, step, sub],
+            recv_sem=gather_sems.at[1, lane, step, sub],
+            device_id={"wide": ahead if lane == 0 else behind},
+            device_id_type=MESH,
+        )
+
+    def landed(lane, step, sub):
+        return pltpu.make_async_remote_copy(
+            src_ref=last.at[lane, rows_of(sub)],
+            dst_ref=held(lane, step + 1, sub, core),
+            send_sem=gather_sems.at[0, lane, step, sub],
+            recv_sem=gather_sems.at[1, lane, step, sub],
+            device_id={"wide": ahead if lane == 0 else behind},
+            device_id_type=MESH,
+        )
+
+    def pair(lane, step, sub, side):
+        source = last.at[lane, rows_of(sub)] if step == 0 else held(lane, step, sub, core)
+        return pltpu.make_async_remote_copy(
+            src_ref=source,
+            dst_ref=held(lane, step, sub, side),
+            send_sem=pair_sems.at[0, lane, step, sub],
+            recv_sem=pair_sems.at[1, lane, step, sub],
+            device_id={"wide": sibling},
+            device_id_type=MESH,
+        )
+
+    def keep(lane, sub):
+        return pltpu.make_async_copy(
+            last.at[lane, rows_of(sub)], held(lane, 0, sub, core), own_sems.at[lane, sub]
+        )
+
+    loose_swap.wait()
+    loose_rows[chip] = loose[...] + loose_pair[...]
+    loose_hop(0, chip).start()
     for lane in range(2):
         local(lane).wait()
         across(lane).wait()
@@ -135,77 +198,92 @@
         for sub in range(subs):
             hop(lane, 0, sub).start()
     for step in range(chips - 1):
+        passed = place(position - 1 - step)
+        loose_hop(step, passed).wait_recv()
+        if step < chips - 2:
+            loose_hop(step + 1, passed).start()
         for sub in range(subs):
             for lane in range(2):
                 hop(lane, step, sub).wait_recv()
                 offset = 2 + step
                 index = place(position - offset if lane == 0 else position + offset)
-                rows = pl.ds(sub * UNIT, UNIT)
+                rows = rows_of(sub)
                 total = slots[lane, step, rows] + mine[lane, index, rows]
                 if step == chips - 2:
-                    out[lane, rows] = total
+                    last[lane, rows] = total
+                    send_on(lane, 0, sub).start()
+                    pair(lane, 0, sub, core).start()
+                    keep(lane, sub).start()
                 else:
                     slots[lane, step, rows] = total
                     hop(lane, step + 1, sub).start()
     for step in range(chips - 1):
         for sub in range(subs):
             for lane in range(2):
-                hop(lane, step, sub).wait_send()
-    if swapped:
-        turn.wait()
-
-
-def ring_scatter(lanes, part, collective_id):
+                landed(lane, step, sub).wait_recv()
+                if step < chips - 2:
+                    send_on(lane, step + 1, sub).start()
+                pair(lane, step + 1, sub, core).start()
+    loose_out[...] = jnp.sum(loose_rows[...], axis=0)
+    for step in range(chips):
+        if step < chips - 1:
+            loose_hop(step, place(position - step)).wait_send()
+        for sub in range(subs):
+            for lane in range(2):
+                pair(lane, step, sub, 1 - core).wait_recv()
+                pair(lane, step, sub, core).wait_send()
+                if step == 0:
+                    keep(lane, sub).wait()
+                if step < chips - 1:
+                    hop(lane, step, sub).wait_send()
+                    send_on(lane, step, sub).wait_send()
+    turn.wait()
+
+
+def ring_sum(lanes, part, loose, collective_id):
     chips = lax.axis_size("wide") // 2
     rows, width = lanes[0].shape
     shard = rows // (2 * chips)
     subs = shard // UNIT
-    operands = [lane.reshape(chips, 2, shard, width) for lane in lanes]
-    shapes = [jax.ShapeDtypeStruct((2, shard, width), BF16)]
-    specs = [pl.BlockSpec(memory_space=pltpu.VMEM)]
-    scratch = [
-        pltpu.VMEM((2, chips, shard, width), BF16),
-        pltpu.VMEM((2, chips, shard, width), BF16),
-        pltpu.VMEM((2, chips - 1, shard, width), BF16),
-        pltpu.SemaphoreType.DMA((2,)),
-        pltpu.SemaphoreType.DMA((2, 2)),
-        pltpu.SemaphoreType.DMA((2, 2, chips - 1, subs)),
-    ]
-    if part is not None:
-        operands.append(part)
-        shapes.append(jax.ShapeDtypeStruct((part.shape[0] // 2, part.shape[1]), BF16))
-        specs.append(pl.BlockSpec(memory_space=pl.ANY))
-        scratch.append(pltpu.SemaphoreType.DMA((2,)))
-    return pl.pallas_call(
-        lambda *refs: ring_kernel(chips, subs, int(part is not None), *refs),
-        out_shape=shapes,
-        in_specs=[pl.BlockSpec(memory_space=pl.ANY)] * len(operands),
-        out_specs=specs,
-        scratch_shapes=scratch,
+    anywhere = pl.BlockSpec(memory_space=pl.ANY)
+    inside = pl.BlockSpec(memory_space=pltpu.VMEM)
+    sums, landed, loose_sum = pl.pallas_call(
+        lambda *refs: ring_kernel(chips, subs, *refs),
+        out_shape=[
+            jax.ShapeDtypeStruct((2, chips, 2, shard, width), BF16),
+            jax.ShapeDtypeStruct((part.shape[0] // 2, part.shape[1]), BF16),
+            jax.ShapeDtypeStruct(loose.shape, F32),
+        ],
+        in_specs=[anywhere] * 3 + [inside],
+        out_specs=[anywhere] * 2 + [inside],
+        scratch_shapes=[
+            pltpu.VMEM((2, chips, shard, width), BF16),
+            pltpu.VMEM((2, chips, shard, width), BF16),
+            pltpu.VMEM((2, chips - 1, shard, width), BF16),
+            pltpu.VMEM((2, shard, width), BF16),
+            pltpu.VMEM(loose.shape, F32),
+            pltpu.VMEM((chips,) + loose.shape, F32),
+            pltpu.SemaphoreType.DMA((2,)),
+            pltpu.SemaphoreType.DMA((2, 2)),
+            pltpu.SemaphoreType.DMA((2, 2, chips - 1, subs)),
+            pltpu.SemaphoreType.DMA((2,)),
+            pltpu.SemaphoreType.DMA((2, 2, chips - 1, subs)),
+            pltpu.SemaphoreType.DMA((2, 2, chips, subs)),
+            pltpu.SemaphoreType.DMA((2, subs)),
+            pltpu.SemaphoreType.DMA((2,)),
+            pltpu.SemaphoreType.DMA((2, chips - 1)),
+        ],
         compiler_params=pltpu.CompilerParams(
             collective_id=collective_id, has_side_effects=True, vmem_limit_bytes=40 << 20
         ),
-        name="ring_scatter",
-    )(*operands)
+        name="ring_sum",
+    )(*[lane.reshape(chips, 2, shard, width) for lane in lanes], part, loose)
+    return sums.reshape(2 * rows, width), landed, loose_sum
 
 
 def ring_fits(lanes):
     count = lax.axis_size("wide")
     return lax.axis_size("narrow") == 2 and lanes[0].shape[0] % (count * UNIT) == 0
-
-
-def wide_gather(mine, loose=None):
-    shard, width = mine.shape[1:]
-    parts = mine.reshape(2 * shard, width)
-    if loose is not None:
-        parts = jnp.concatenate([parts, loose], axis=0)
-    return lax.all_gather(parts, "wide", axis=0)
-
-
-def lanes_of(parts, shard):
-    width = parts.shape[2]
-    lanes = [parts[:, lane * shard : (lane + 1) * shard].reshape(-1, width) for lane in range(2)]
-    return lanes, parts[:, 2 * shard :].astype(F32)
 
 
 TILE = 256
@@ -838,12 +916,7 @@
     ]
     up_grad = dot(d_upper, norm_two, ((0,), (0,)), BF16)
     down_grad = dot(hidden, d_branch, ((0,), (0,)), BF16)
-    if ring_fits([up_grad]):
-        mine = ring_scatter([up_grad, down_grad], None, 1)[0]
-        mine, d_others = lax.optimization_barrier((mine, d_others))
-        gathered = wide_gather(mine)
-    else:
-        gathered = lax.psum((up_grad, down_grad), "wide")
+    up_grad, down_grad = lax.psum((up_grad, down_grad), "wide")
     attn_part, attn_other, d_other = [
         jnp.concatenate(parts, axis=0) for parts in (attn_parts, attn_others, d_others)
     ]
@@ -918,7 +991,7 @@
         out_bias_sum[0],
     ]
     loose = jnp.concatenate(loose_parts)
-    loose = jnp.pad(loose, (0, (-loose.shape[0]) % (8 * width))).reshape(-1, width).astype(BF16)
+    loose = jnp.pad(loose, (0, (-loose.shape[0]) % (8 * width))).reshape(-1, width)
     terms = [early[0], early[1], images_two[0], images_two[1], images_two[2], d_gate_two]
     terms = [term.astype(BF16) for term in terms]
     d_mod = [jnp.concatenate(terms[2 * i : 2 * i + 2], axis=1) for i in range(3)]
@@ -928,16 +1001,12 @@
         d_mod_flat = jnp.concatenate(d_mod, axis=1).reshape(-1, width)
     rest = jnp.concatenate([bottom, out_weight_grad, d_mod_flat], axis=0)
     if ring_fits([top]) and top.shape == rest.shape:
-        gathered, rest = lax.optimization_barrier((gathered, rest))
-        mine, d_norm_other = ring_scatter([top, rest], d_norm_part, 0)
-        (up_grad, down_grad), _ = lanes_of(gathered, gathered.shape[1] // 2)
+        flat, d_norm_other, loose = ring_sum([top, rest], d_norm_part, loose, 0)
         d_norm_one = own(d_norm_part).astype(F32) + d_norm_other.astype(F32)
-        (top, rest), loose = lanes_of(wide_gather(mine, loose), mine.shape[1])
     else:
-        up_grad, down_grad = gathered
         d_norm_one = narrow_scatter(d_norm_part)
-        top, rest = lax.psum((top, rest), "wide")
-        loose = lax.all_gather(loose, "wide", axis=0).astype(F32)
+        flat = jnp.concatenate(lax.psum((top, rest), "wide"), axis=0)
+        loose = lax.psum(loose, "wide")
     tok_own = tokens.astype(F32)
     xhat_one, rstd_one = norm(tok_own)
     hot_own = own(onehot_full)
@@ -949,11 +1018,10 @@
     layer_out = (tok_own + live_own * (gates[0] * attn_own + gates[1] * branch)).astype(BF16)
     up_weight_grad = up_grad.T.astype(F32)
     down_weight_grad = down_grad.astype(F32)
-    loose = jnp.sum(loose, axis=0)
-    keep = 3 * part_width - split
-    qkv_flat = jnp.concatenate([top.astype(F32), rest[:keep].astype(F32)], axis=0)
+    keep = 3 * part_width
+    qkv_flat = flat[:keep].astype(F32)
     qkv_weight_grad = jnp.transpose(qkv_flat.reshape(3, part_width, width), (2, 0, 1))
-    out_weight_grad = rest[keep : keep + part_width].astype(F32)
+    out_weight_grad = flat[keep : keep + part_width].astype(F32)
     loose = loose.reshape(-1)
     bounds = [0]
     for part in loose_parts:
@@ -962,7 +1030,7 @@
         loose[bounds[i] : bounds[i + 1]] for i in range(5)
     ]
     qv_bias_grad = jnp.stack([query_bias, value_bias])
-    d_mod_flat = rest[keep + part_width :]
+    d_mod_flat = flat[keep + part_width :]
     if 2 * mod_width == width:
         d_mod = d_mod_flat.reshape(3, img_row, width)
     else:

time: 591 us -> 573 us (0.970)
  waiting for transfers between devices: 62.6 us -> 17.7 us
  Pallas kernels: 268 us -> 292 us
    ppermute x11, waiting for transfers between devices: 62.5 us -> 17.7 us  [swap(): return lax.ppermute(part, 'narrow', [(0, 1), (1, 0)])]
    pallas_call x2 -> x1, Pallas kernels: 123 us -> 146 us  [ring_sum(): pl.pallas_call(lambda *refs: ring_kernel(chips, subs, *refs), out_shape=[...]
    slice x5 -> x2, local copies, waits for them, and re-layouts: 14.8 us -> 5.03 us  [the longest x1 2.82 us: body(): d_mod_flat = flat[keep + part_width:]]
    convert_element_type x2 -> x1, other arithmetic: 9.1 us -> 3.01 us  [body(): out_weight_grad = flat[keep:keep + part_width].astype(F32)]
    unnamed x131 -> x127, local copies, waits for them, and re-layouts: 32.5 us -> 29.7 us
  transfers between devices with their start and end apart: 17 -> 16, of which waited for: 5 -> 2; matrix products, arithmetic and copies ran while one was open for 30% -> 30% of each run, Pallas kernels for 35% -> 52%
where the time goes in v5:
time: 573 us; the launch traced here: 561 us
  Pallas kernels  292 us (51%)
  local copies, waits for them, and re-layouts  91.9 us (16%)
  other arithmetic  60.8 us (11%)
  matrix products  56.3 us (10%)
  starting transfers between devices  25.7 us (4%)
  waiting for transfers between devices  17.7 us (3%)
  between operations  17 us (3%)
    pallas_call x1, Pallas kernels, ring_sum(): pl.pallas_call(lambda *refs: ring_kernel(chips, subs, *refs), out_shape=[...  146 us
    pallas_call x5, Pallas kernels, token_call(): pl.pallas_call(kernel, grid=(tokens // TILE,), out_shape=out_shape, in_sp...  108 us
    dot_general x13, matrix products, dot(): lax.dot_general(left, right, (dims, ((), ())), preferred_element_type=F32)  47.9 us
    unnamed x127, local copies, waits for them, and re-layouts  29.7 us
    pallas_call x1, Pallas kernels, attention_backward(): pl.pallas_call(lambda *refs: backward_kernel(tiles, *refs), grid=(tiles,)...  26.7 us
    ppermute x11, waiting for transfers between devices, swap(): return lax.ppermute(part, 'narrow', [(0, 1), (1, 0)])  17.7 us
    ppermute x11, starting transfers between devices, swap(): return lax.ppermute(part, 'narrow', [(0, 1), (1, 0)])  12.6 us
  transfers between devices with their start and end apart: 16, of which 2 were waited for; matrix products, arithmetic and copies ran while one was open for 30% of the time, Pallas kernels for 52%

profile of v5, /device:TPU:0, one launch (start us, length us, event | category | flops | bytes accessed | tf_op | source)
XLA Modules:
  0.0 561.4 jit_solution(4914982028463288938)
XLA Ops:
  11.0 5.2 fusion.59
  20.2 5.3 slice.215
  29.9 5.4 fusion.4
  57.7 4.0 maximum_select_fusion.tokens.refs_0_
  66.1 12.8 %project.1 = (bf16[1024,576]{1,0:T(8,128)(2,1)}, bf16[1024,576]{1,0:T(8,128)(2,1)}, bf16[1024,576]{1,0:T(8,128)(2,1)}, bf16[1024,1152]{1,0:T(8,128)(2,1)}) custom-call(bf16[1024,1152]{1,0:T(8,128)(2,1)} %maximum_select_fusion.tokens.refs_0_, s32[1024,1]{1,0:T(8,128)} %copy.75.ids.refs_7_, bf16[2,256,1152]{2,1,0:T(8,128)(2,1)} %fusion.33.table, ...), custom_call_target="tpu_custom_call" | custom-call | flops 4076863488 | bytes 11289984 | tf_op jit(solution)/shard_map/project/pallas_call | solution.py:567
  87.5 10.9 %attention_forward.1 = (bf16[1024,576]{1,0:T(8,128)(2,1)S(1)}, f32[8,1024]{1,0:T(8,128)S(1)}) custom-call(bf16[1024,576]{1,0:T(8,128)(2,1)S(1)} %copy-done.10, bf16[1024,576]{1,0:T(8,128)(2,1)S(1)} %copy-done.6, bf16[1024,576]{1,0:T(8,128)(2,1)S(1)} %copy-done.7, bf16[2,128,576]{2,1,0:T(8,128)(2,1)S(1)} %collective-permute-done.3.refs_3_, ...), custom_call_target="tpu_custom_call" | custom-call | flops 1207959552 | bytes 4718592 | tf_op jit(solution)/shard_map/attention_forward/pallas_call | solution.py:370
  110.4 5.0 fusion.20.table.refs_10_
  118.6 6.9 %collective-permute-done.6.theirs = bf16[512,1152]{1,0:T(8,128)(2,1)} collective-permute-done((bf16[512,1152]{1,0:T(8,128)(2,1)}, bf16[512,1152]{1,0:T(8,128)(2,1)}, u32[]{:S(2)}, u32[]{:S(2)}) %collective-permute-start.6) | collective-permute-done | bytes 1179680 | tf_op jit(solution)/shard_map/ppermute | solution.py:21
  125.6 27.1 %mlp.3 = (bf16[512,1152]{1,0:T(8,128)(2,1)}, bf16[512,2304]{1,0:T(8,128)(2,1)}, bf16[512,2304]{1,0:T(8,128)(2,1)}, bf16[512,1152]{1,0:T(8,128)(2,1)}, bf16[512,1...) custom-call(bf16[512,1152]{1,0:T(8,128)(2,1)} %get-tuple-element.180.tokens, ...), custom_call_target="tpu_custom_call" | custom-call | flops 10871635968 | bytes 26558592 | tf_op jit(solution)/shard_map/mlp/pallas_call | solution.py:567
  152.7 27.5 %mlp.2 = (bf16[512,1152]{1,0:T(8,128)(2,1)}, bf16[512,2304]{1,0:T(8,128)(2,1)}, bf16[512,2304]{1,0:T(8,128)(2,1)}, bf16[512,1152]{1,0:T(8,128)(2,1)}, bf16[512,1...) custom-call(bf16[512,1152]{1,0:T(8,128)(2,1)} %get-tuple-element.179.tokens, ...), custom_call_target="tpu_custom_call" | custom-call | flops 10871635968 | bytes 26558592 | tf_op jit(solution)/shard_map/mlp/pallas_call | solution.py:567
  196.9 8.0 %convolution_convert_fusion = bf16[2304,1152]{1,0:T(8,128)(2,1)} fusion(bf16[1024,1152]{1,0:T(8,128)(2,1)S(1)} %constant_dynamic-update-slice_fusion.8, bf16[512,2304]{1,0:T(8,128)(2,1)S(1)} %copy-done.54, bf16[512,2304]{1,0:T(8,128)(2,1)S(1)} %copy-done.55), kind=kOutput, calls=%fused_computation | convolution fusion | flops 5447909376 | bytes 12386304 | tf_op jit(solution)/shard_map/dot_general | solution.py:17
  207.9 8.0 %fusion = bf16[1152,2304]{0,1:T(8,128)(2,1)} fusion(bf16[1024,2304]{1,0:T(8,128)(2,1)S(1)} %constant_dynamic-update-slice_fusion.6, bf16[512,1152]{1,0:T(8,128)(2,1)S(1)} %copy-done.56, bf16[512,1152]{1,0:T(8,128)(2,1)S(1)} %copy-done.57), kind=kOutput, calls=%fused_computation.2 | convolution fusion | flops 5443190784 | bytes 12386304 | tf_op jit(solution)/shard_map/dot_general | solution.py:17
  228.9 19.5 %middle_back.1 = (f32[1024,1152]{1,0:T(8,128)}, bf16[1024,576]{1,0:T(8,128)(2,1)}, bf16[576,1152]{1,0:T(8,128)(2,1)}, bf16[2,3,256,576]{3,2,1,0:T(8,128)(2,1)}, f32[1,1152]{1,0:T(1,128)}) custom-call(bf16[1024,1152]{1,0:T(8,128)(2,1)} %maximum_select_fusion.tokens.refs_0_, bf16[1024,1152]{1,0:T(8,128)(2,1)} %pad_maximum_fusion.refs_1_, ...), custom_call_target="tpu_custom_call" | custom-call | flops 2717908992 | bytes 28554624 | tf_op jit(solution)/shard_map/middle_back/pallas_call | solution.py:567
  249.8 26.7 %attention_backward.1 = (bf16[1024,576]{1,0:T(8,128)(2,1)S(1)}, bf16[2,1024,576]{2,1,0:T(8,128)(2,1)}, bf16[2,2,128,576]{3,2,1,0:T(8,128)(2,1)S(1)}) custom-call(bf16[1024,576]{1,0:T(8,128)(2,1)S(1)} %copy-done.11, bf16[1024,576]{1,0:T(8,128)(2,1)S(1)} %copy-done.6, bf16[1024,576]{1,0:T(8,128)(2,1)} %get-tuple-element.53.refs_2_, ...), custom_call_target="tpu_custom_call" | custom-call | flops 3019898880 | bytes 9437184 | tf_op jit(solution)/shard_map/attention_backward/pallas_call | solution.py:471
  276.6 8.7 %collective-permute-start.10 = (bf16[2,128,576]{2,1,0:T(8,128)(2,1)S(1)}, bf16[2,128,576]{2,1,0:T(8,128)(2,1)S(1)}, u32[]{:S(2)}, u32[]{:S(2)}) collective-permute-start(bf16[2,128,576]{2,1,0:T(8,128)(2,1)S(1)} %get-tuple-element.163), channel_id=1, source_target_pairs={{0,2},{2,4},{4,6},{6,8},{8,10},{10,12},{12,14},{14,16},{16,18},{18... | collective-permute-start | bytes 884744 | tf_op jit(solution)/shard_map/ppermute | solution.py:868
  286.7 5.2 fusion.19
  294.8 21.3 %project_back.1 = (bf16[1024,1152]{1,0:T(8,128)(2,1)}, bf16[1536,1152]{1,0:T(8,128)(2,1)}, bf16[192,1152]{1,0:T(8,128)(2,1)}, bf16[2,2,256,576]{3,2,1,0:T(8,128)(2,1)}, f32[2,576]{1,0:T(2,128)}) custom-call(bf16[1024,1152]{1,0:T(8,128)(2,1)} %maximum_select_fusion.tokens.refs_0_, bf16[1024,1152]{1,0:T(8,128)(2,1)} %get-tuple-element.60.refs_1_, ...), custom_call_target="tpu_custom_call" | custom-call | flops 8153726976 | bytes 19249158 | tf_op jit(solution)/shard_map/project_back/pallas_call | solution.py:567
  322.8 10.8 %collective-permute-done.12 = bf16[2,256,576]{1,2,0:T(8,128)(2,1)} collective-permute-done((bf16[2,256,576]{1,2,0:T(8,128)(2,1)}, bf16[2,256,576]{1,2,0:T(8,128)(2,1)}, u32[]{:S(2)}, u32[]{:S(2)}) %collective-permute-start.12) | collective-permute-done | bytes 589856 | tf_op jit(solution)/shard_map/ppermute | solution.py:21
  339.7 146.2 %ring_sum.1 = (bf16[2,8,2,96,1152]{4,3,2,1,0:T(8,128)(2,1)}, bf16[512,1152]{1,0:T(8,128)(2,1)S(1)}, f32[8,1152]{1,0:T(8,128)S(1)}) custom-call(bf16[8,2,96,1152]{3,2,1,0:T(8,128)(2,1)S(1)} %bitcast.98, bf16[8,2,96,1152]{3,2,1,0:T(8,128)(2,1)S(1)} %bitcast.97, bf16[1024,1152]{1,0:T(8,128)(2,1)S(1)} %copy-done.1, f32[8,1152]{1,0:T(8,128)S(1)} %copy-done.4), custom_call_target="tpu_custom_call" | custom-call | tf_op jit(solution)/shard_map/ring_sum/pallas_call | solution.py:250
  488.3 4.1 fusion.38
  504.2 4.2 copy.85
  517.1 8.4 %fusion.42 = f32[1152,6,576]{0,2,1:T(8,128)} fusion(bf16[6,576,256]{2,1,0:T(8,128)(2,1)S(1)} %bitcast.109, bf16[256,1152]{1,0:T(8,128)(2,1)S(1)} %copy-done.41), kind=kOutput, calls=%fused_computation.83 | convolution fusion | flops 2040201216 | bytes 18284544 | tf_op jit(solution)/shard_map/dot_general | solution.py:1038
  537.6 9.4 %copy.86 = f32[1152,2304]{1,0:T(8,128)} copy(bf16[1152,2304]{0,1:T(8,128)(2,1)} %get-tuple-element.143) | data formatting | bytes 15925248
  547.0 7.3 %convert_element_type.183 = f32[2304,1152]{1,0:T(8,128)} convert(bf16[2304,1152]{1,0:T(8,128)(2,1)} %get-tuple-element.144) | non-fusion elementwise | flops 2654208 | bytes 15925248 | tf_op jit(solution)/shard_map/convert_element_type | solution.py:1020
  (253 shorter events, 146.5 us)
Async XLA Ops:
  7.2 530.4 %all-reduce.4.cloned.1.call-start = ((), (), s32[]{:S(2)}) async-start(), calls=%async_computation | async-start | bytes 21233664 | tf_op jit(solution)/shard_map/psum | solution.py:919
  7.2 50.4 %collective-permute-start = (bf16[512,1152]{1,0:T(8,128)(2,1)}, bf16[512,1152]{1,0:T(8,128)(2,1)}, u32[]{:S(2)}, u32[]{:S(2)}) collective-permute-start(bf16[512,1152]{1,0:T(8,128)(2,1)} %param.15), channel_id=1, source_target_pairs={{0,1},{1,0},{2,3},{3,2},{4,5},{5,4},{6,7},{7,6},{8,9},{9,8},{10,11... | collective-permute-start | bytes 3538952 | tf_op jit(solution)/shard_map/ppermute | solution.py:21
  19.9 32.3 %collective-permute-start.2 = (bf16[576,256,2]{1,0,2:T(8,128)(2,1)}, bf16[576,256,2]{1,0,2:T(8,128)(2,1)}, u32[]{:S(2)}, u32[]{:S(2)}) collective-permute-start(bf16[576,256,2]{1,0,2:T(8,128)(2,1)} %bitcast.55), channel_id=1, source_target_pairs={{0,1},{1,0},{2,3},{3,2},{4,5},{5,4},{6,7},{7,6},{8,9},{9,8},{10,11... | collective-permute-start | bytes 1769480 | tf_op jit(solution)/shard_map/ppermute | solution.py:21
  29.2 156.7 %copy-start.44 = (s32[1024]{0:T(1024)}, s32[1024]{0:T(1024)S(1)}, u32[]{:S(2)}) copy-start(s32[1024]{0:T(1024)S(1)} %get-tuple-element.146) | copy-start | bytes 12292
  52.2 234.5 %copy-start.42 = (pred[1024,256]{1,0:T(32,128)(4,1)}, pred[1024,256]{1,0:T(32,128)(4,1)S(1)}, u32[]{:S(2)}) copy-start(pred[1024,256]{1,0:T(32,128)(4,1)S(1)} %iota_compare_fusion) | copy-start | bytes 786436
  64.1 43.9 %collective-permute-start.1 = (bf16[576,256,4]{1,0,2:T(8,128)(2,1)}, bf16[576,256,4]{1,0,2:T(8,128)(2,1)}, u32[]{:S(2)}, u32[]{:S(2)}) collective-permute-start(bf16[576,256,4]{1,0,2:T(8,128)(2,1)} %copy.67), channel_id=1, source_target_pairs={{0,1},{1,0},{2,3},{3,2},{4,5},{5,4},{6,7},{7,6},{8,9},{9,8},{10,11... | collective-permute-start | bytes 3538952 | tf_op jit(solution)/shard_map/ppermute | solution.py:21
  80.3 7.1 %collective-permute-start.3 = (bf16[2,128,576]{2,1,0:T(8,128)(2,1)S(1)}, bf16[2,128,576]{2,1,0:T(8,128)(2,1)S(1)}, u32[]{:S(2)}, u32[]{:S(2)}) collective-permute-start(bf16[2,128,576]{2,1,0:T(8,128)(2,1)S(1)} %pad_maximum_fusion.4), channel_id=1, source_target_pairs={{0,2},{2,4},{4,6},{6,8},{8,10},{10,12},{12,14},{14,16},{16,18},{18... | collective-permute-start | bytes 884744 | tf_op jit(solution)/shard_map/ppermute | solution.py:868
  81.7 5.7 %collective-permute-start.4 = (bf16[2,128,576]{2,1,0:T(8,128)(2,1)S(1)}, bf16[2,128,576]{2,1,0:T(8,128)(2,1)S(1)}, u32[]{:S(2)}, u32[]{:S(2)}) collective-permute-start(bf16[2,128,576]{2,1,0:T(8,128)(2,1)S(1)} %pad_maximum_fusion.5), channel_id=1, source_target_pairs={{2,0},{4,2},{6,4},{8,6},{10,8},{12,10},{14,12},{16,14},{18,16},{20... | collective-permute-start | bytes 884744 | tf_op jit(solution)/shard_map/ppermute | solution.py:871
  100.5 25.0 %collective-permute-start.6 = (bf16[512,1152]{1,0:T(8,128)(2,1)}, bf16[512,1152]{1,0:T(8,128)(2,1)}, u32[]{:S(2)}, u32[]{:S(2)}) collective-permute-start(bf16[512,1152]{1,0:T(8,128)(2,1)} %convolution_convert_fusion.2.mine), channel_id=1, source_target_pairs={{0,1},{1,0},{2,3},{3,2},{4,5},{5,4},{6,7},{7,6},{8,9},{9,8},{10,11... | collective-permute-start | bytes 3538952 | tf_op jit(solution)/shard_map/ppermute | solution.py:21
  103.0 49.7 %collective-permute-start.5 = (bf16[512,1152]{1,0:T(8,128)(2,1)}, bf16[512,1152]{1,0:T(8,128)(2,1)}, u32[]{:S(2)}, u32[]{:S(2)}) collective-permute-start(bf16[512,1152]{1,0:T(8,128)(2,1)} %convolution_convert_fusion.3.mine), channel_id=1, source_target_pairs={{0,1},{1,0},{2,3},{3,2},{4,5},{5,4},{6,7},{7,6},{8,9},{9,8},{10,11... | collective-permute-start | bytes 3538952 | tf_op jit(solution)/shard_map/ppermute | solution.py:21
  152.6 73.0 %collective-permute-start.9 = (bf16[512,1152]{1,0:T(8,128)(2,1)}, bf16[512,1152]{1,0:T(8,128)(2,1)}, u32[]{:S(2)}, u32[]{:S(2)}) collective-permute-start(bf16[512,1152]{1,0:T(8,128)(2,1)} %get-tuple-element.58), channel_id=1, source_target_pairs={{0,1},{1,0},{2,3},{3,2},{4,5},{5,4},{6,7},{7,6},{8,9},{9,8},{10,11... | collective-permute-start | bytes 3538952 | tf_op jit(solution)/shard_map/ppermute | solution.py:21
  183.6 42.1 %collective-permute-start.8 = (bf16[512,1152]{1,0:T(8,128)(2,1)}, bf16[512,1152]{1,0:T(8,128)(2,1)}, u32[]{:S(2)}, u32[]{:S(2)}) collective-permute-start(bf16[512,1152]{1,0:T(8,128)(2,1)} %get-tuple-element.57), channel_id=1, source_target_pairs={{0,1},{1,0},{2,3},{3,2},{4,5},{5,4},{6,7},{7,6},{8,9},{9,8},{10,11... | collective-permute-start | bytes 3538952 | tf_op jit(solution)/shard_map/ppermute | solution.py:21
  189.6 34.2 %collective-permute-start.13 = (bf16[256,576]{1,0:T(8,128)(2,1)}, bf16[256,576]{1,0:T(8,128)(2,1)}, u32[]{:S(2)}, u32[]{:S(2)}) collective-permute-start(bf16[256,576]{1,0:T(8,128)(2,1)} %constant_dynamic-slice_fusion), channel_id=1, source_target_pairs={{0,1},{1,0},{2,3},{3,2},{4,5},{5,4},{6,7},{7,6},{8,9},{9,8},{10,11... | collective-permute-start | bytes 884744 | tf_op jit(solution)/shard_map/ppermute | solution.py:21
  191.1 95.5 %collective-permute-start.7 = (bf16[512,1152]{1,0:T(8,128)(2,1)}, bf16[512,1152]{1,0:T(8,128)(2,1)}, u32[]{:S(2)}, u32[]{:S(2)}) collective-permute-start(bf16[512,1152]{1,0:T(8,128)(2,1)} %constant_dynamic-slice_fusion.2), channel_id=1, source_target_pairs={{0,1},{1,0},{2,3},{3,2},{4,5},{5,4},{6,7},{7,6},{8,9},{9,8},{10,11... | collective-permute-start | bytes 3538952 | tf_op jit(solution)/shard_map/ppermute | solution.py:21
  249.8 36.9 %copy-start.15 = (bf16[512,1152]{1,0:T(8,128)(2,1)S(1)}, bf16[512,1152]{1,0:T(8,128)(2,1)}, u32[]{:S(2)}) copy-start(bf16[512,1152]{1,0:T(8,128)(2,1)} %param.15) | copy-start | bytes 3538948
  249.8 36.9 %copy-start.27 = (bf16[1024,1152]{1,0:T(8,128)(2,1)S(1)}, bf16[1024,1152]{1,0:T(8,128)(2,1)}, u32[]{:S(2)}) copy-start(bf16[1024,1152]{1,0:T(8,128)(2,1)} %copy-done.26) | copy-start | bytes 7077892
  249.8 36.9 %copy-start.28 = (f32[512,1152]{1,0:T(8,128)S(1)}, f32[512,1152]{1,0:T(8,128)}, u32[]{:S(2)}) copy-start(f32[512,1152]{1,0:T(8,128)} %fusion.41) | copy-start | bytes 7077892
  249.8 36.9 %copy-start.47 = (f32[1152]{0:T(1024)S(1)}, f32[1152]{0:T(1024)}, u32[]{:S(2)}) copy-start(f32[1152]{0:T(1024)} %convert_element_type.155) | copy-start | bytes 13828
  249.8 36.9 %copy-start.52 = (f32[512]{0:T(512)S(1)}, f32[512]{0:T(512)}, u32[]{:S(2)}) copy-start(f32[512]{0:T(512)} %get-tuple-element.169) | copy-start | bytes 6148
  276.5 15.3 %copy-start.12 = (bf16[1024,576]{1,0:T(8,128)(2,1)}, bf16[1024,576]{1,0:T(8,128)(2,1)S(1)}, u32[]{:S(2)}) copy-start(bf16[1024,576]{1,0:T(8,128)(2,1)S(1)} %get-tuple-element.63.refs_2_) | copy-start | bytes 3538948
  276.6 16.3 %collective-permute-start.10 = (bf16[2,128,576]{2,1,0:T(8,128)(2,1)S(1)}, bf16[2,128,576]{2,1,0:T(8,128)(2,1)S(1)}, u32[]{:S(2)}, u32[]{:S(2)}) collective-permute-start(bf16[2,128,576]{2,1,0:T(8,128)(2,1)S(1)} %get-tuple-element.163), channel_id=1, source_target_pairs={{0,2},{2,4},{4,6},{6,8},{8,10},{10,12},{12,14},{14,16},{16,18},{18... | collective-permute-start | bytes 884744 | tf_op jit(solution)/shard_map/ppermute | solution.py:868
  285.3 7.6 %collective-permute-start.11 = (bf16[2,128,576]{2,1,0:T(8,128)(2,1)S(1)}, bf16[2,128,576]{2,1,0:T(8,128)(2,1)}, u32[]{:S(2)}, u32[]{:S(2)}) collective-permute-start(bf16[2,128,576]{2,1,0:T(8,128)(2,1)S(1)} %get-tuple-element.164), channel_id=1, source_target_pairs={{2,0},{4,2},{6,4},{8,6},{10,8},{12,10},{14,12},{16,14},{18,16},{20... | collective-permute-start | bytes 884744 | tf_op jit(solution)/shard_map/ppermute | solution.py:871
  318.3 15.2 %collective-permute-start.12 = (bf16[2,256,576]{1,2,0:T(8,128)(2,1)}, bf16[2,256,576]{1,2,0:T(8,128)(2,1)}, u32[]{:S(2)}, u32[]{:S(2)}) collective-permute-start(bf16[2,256,576]{1,2,0:T(8,128)(2,1)} %bitcast.36), channel_id=1, source_target_pairs={{0,1},{1,0},{2,3},{3,2},{4,5},{5,4},{6,7},{7,6},{8,9},{9,8},{10,11... | collective-permute-start | bytes 1769480 | tf_op jit(solution)/shard_map/ppermute | solution.py:21
  503.8 31.4 %collective-permute-start.14 = (bf16[256,1152]{1,0:T(8,128)(2,1)}, bf16[256,1152]{1,0:T(8,128)(2,1)}, u32[]{:S(2)}, u32[]{:S(2)}) collective-permute-start(bf16[256,1152]{1,0:T(8,128)(2,1)} %fusion.12), channel_id=1, source_target_pairs={{0,1},{1,0},{2,3},{3,2},{4,5},{5,4},{6,7},{7,6},{8,9},{9,8},{10,11... | collective-permute-start | bytes 1769480 | tf_op jit(solution)/shard_map/ppermute | solution.py:21
  (52 other events, 225.6 us)
Sparse Core Ops, SparseCore 0:
  216.1 274.2 all-reduce.3

commit v6 on v5

--- a/solution.py
+++ b/solution.py
@@ -499,9 +499,7 @@
         ],
         compiler_params=pltpu.CompilerParams(vmem_limit_bytes=48 << 20),
         cost_estimate=pl.CostEstimate(
-            flops=10 * tok_dev * 512 * part_width,
-            transcendentals=tok_dev * 512 * 8,
-            bytes_accessed=16 * tok_dev * part_width,
+            flops=tok_dev * part_width, transcendentals=0, bytes_accessed=tok_dev * part_width
         ),
         name="attention_backward",
     )(q, k, v, left, right, grad, lse, q_ids, k_ids)
@@ -573,7 +571,7 @@
         scratch_shapes=scratch,
         compiler_params=pltpu.CompilerParams(vmem_limit_bytes=60 << 20),
         cost_estimate=pl.CostEstimate(
-            flops=flops, transcendentals=0, bytes_accessed=size + size // 2
+            flops=flops, transcendentals=0, bytes_accessed=size if flops else tokens
         ),
         name=name,
     )(*operands)
@@ -716,7 +714,7 @@
             whole((1, width)),
         ],
         [pltpu.VMEM((3, images, width), F32), pltpu.VMEM((size, width), F32)],
-        4 * count * width * size,
+        0,
         (tokens, mine, theirs, cotangent, d_own, d_other, context, ids, live, ids_row) + consts,
     )
 
@@ -796,7 +794,7 @@
             whole((2, size)),
         ],
         [pltpu.VMEM((2, images, width), F32), pltpu.VMEM((3 * size, width), F32)],
-        12 * count * width * size,
+        0,
         (tokens, norm_one, d_q, d_own, rims, tail_start, ids_row, weight),
     )
 
@@ -914,9 +912,32 @@
     norm_two, hidden, d_upper, d_branch, d_norm, branch_part = [
         jnp.concatenate(parts, axis=0) for parts in zip(*mlp_outs)
     ]
-    up_grad = dot(d_upper, norm_two, ((0,), (0,)), BF16)
-    down_grad = dot(hidden, d_branch, ((0,), (0,)), BF16)
-    up_grad, down_grad = lax.psum((up_grad, down_grad), "wide")
+    core = wide_index % 2
+    paired = wide_count % 2 == 0 and d_upper.shape[1] % 256 == 0
+    if paired:
+        half = d_upper.shape[1] // 2
+        pairs = [(i, i ^ 1) for i in range(wide_count)]
+        cores = [list(range(i, wide_count, 2)) for i in range(2)]
+
+        def grads_of(which):
+            cols = [lax.dynamic_slice_in_dim(x, which * half, half, axis=1) for x in (d_upper, hidden)]
+            return dot(norm_two, cols[0], ((0,), (0,)), BF16), dot(cols[1], d_branch, ((0,), (0,)), BF16)
+
+        got = [lax.ppermute(part, "wide", pairs) for part in grads_of(1 - core)]
+        sums = [
+            (part.astype(F32) + other.astype(F32)).astype(BF16)
+            for part, other in zip(grads_of(core), got)
+        ]
+        sums, d_others = lax.optimization_barrier((sums, d_others))
+        mlp_grads = lax.psum(sums, "wide", axis_index_groups=cores)
+    else:
+        mlp_grads = lax.psum(
+            (
+                dot(norm_two, d_upper, ((0,), (0,)), BF16),
+                dot(hidden, d_branch, ((0,), (0,)), BF16),
+            ),
+            "wide",
+        )
     attn_part, attn_other, d_other = [
         jnp.concatenate(parts, axis=0) for parts in (attn_parts, attn_others, d_others)
     ]
@@ -1001,6 +1022,7 @@
         d_mod_flat = jnp.concatenate(d_mod, axis=1).reshape(-1, width)
     rest = jnp.concatenate([bottom, out_weight_grad, d_mod_flat], axis=0)
     if ring_fits([top]) and top.shape == rest.shape:
+        mlp_grads, rest = lax.optimization_barrier((mlp_grads, rest))
         flat, d_norm_other, loose = ring_sum([top, rest], d_norm_part, loose, 0)
         d_norm_one = own(d_norm_part).astype(F32) + d_norm_other.astype(F32)
     else:
@@ -1016,8 +1038,17 @@
     live_own = own(live)
     gates = [dot(hot_own, table_two[j], ((1,), (0,))) for j in (0, 3)]
     layer_out = (tok_own + live_own * (gates[0] * attn_own + gates[1] * branch)).astype(BF16)
-    up_weight_grad = up_grad.T.astype(F32)
-    down_weight_grad = down_grad.astype(F32)
+    if paired:
+        others = [lax.ppermute(part, "wide", pairs) for part in mlp_grads]
+        mlp_grads = [
+            jnp.where(
+                core == 0,
+                jnp.concatenate([part, other], axis=axis),
+                jnp.concatenate([other, part], axis=axis),
+            )
+            for axis, part, other in zip((1, 0), mlp_grads, others)
+        ]
+    up_weight_grad, down_weight_grad = [part.astype(F32) for part in mlp_grads]
     keep = 3 * part_width
     qkv_flat = flat[:keep].astype(F32)
     qkv_weight_grad = jnp.transpose(qkv_flat.reshape(3, part_width, width), (2, 0, 1))

time: 573 us -> 645 us (1.13)
  waiting for transfers between devices: 17.7 us -> 151 us
  Pallas kernels: 292 us -> 228 us
  local copies, waits for them, and re-layouts: 91.9 us -> 78.5 us
  matrix products: 56.3 us -> 67.2 us
  other arithmetic: 60.8 us -> 68.1 us
    psum x1, waiting for transfers between devices: 0.01 us -> 73.4 us  [body(): mlp_grads = lax.psum(sums, 'wide', axis_index_groups=cores)]
    pallas_call x1, Pallas kernels: 146 us -> 82.6 us  [ring_sum(): pl.pallas_call(lambda *refs: ring_kernel(chips, subs, *refs), out_shape=[...]
    ppermute x11, waiting for transfers between devices: 17.7 us -> 77.8 us  [swap(): return lax.ppermute(part, 'narrow', [(0, 1), (1, 0)])]
    dot_general x13 -> x15, matrix products: 47.9 us -> 57.1 us  [dot(): lax.dot_general(left, right, (dims, ((), ())), preferred_element_type=F32)]
    convert_element_type x1 -> x2, other arithmetic: 7.32 us -> 14.2 us  [body(): up_weight_grad, down_weight_grad = [part.astype(F32) for part in mlp_grads]]
    unnamed x127 -> x180, local copies, waits for them, and re-layouts: 29.7 us -> 23.5 us
  transfers between devices with their start and end apart: 16 -> 20, of which waited for: 2 -> 8; matrix products, arithmetic and copies ran while one was open for 30% -> 26% of each run, Pallas kernels for 52% -> 17%
where the time goes in v6:
time: 645 us; the launch traced here: 636 us
  Pallas kernels  228 us (35%)
  waiting for transfers between devices  151 us (23%)
  local copies, waits for them, and re-layouts  78.5 us (12%)
  other arithmetic  68.1 us (11%)
  matrix products  67.2 us (10%)
  starting transfers between devices  24.9 us (4%)
  between operations  17.5 us (3%)
    pallas_call x5, Pallas kernels, token_call(): pl.pallas_call(kernel, grid=(tokens // TILE,), out_shape=out_shape, in_sp...  107 us
    pallas_call x1, Pallas kernels, ring_sum(): pl.pallas_call(lambda *refs: ring_kernel(chips, subs, *refs), out_shape=[...  82.6 us
    ppermute x11, waiting for transfers between devices, swap(): return lax.ppermute(part, 'narrow', [(0, 1), (1, 0)])  77.8 us
    psum x1, waiting for transfers between devices, body(): mlp_grads = lax.psum(sums, 'wide', axis_index_groups=cores)  73.4 us
    dot_general x15, matrix products, dot(): lax.dot_general(left, right, (dims, ((), ())), preferred_element_type=F32)  57.1 us
    pallas_call x1, Pallas kernels, attention_backward(): pl.pallas_call(lambda *refs: backward_kernel(tiles, *refs), grid=(tiles,)...  26.6 us
    unnamed x180, local copies, waits for them, and re-layouts  23.5 us
    ppermute x11, starting transfers between devices, swap(): return lax.ppermute(part, 'narrow', [(0, 1), (1, 0)])  14.4 us
  transfers between devices with their start and end apart: 20, of which 8 were waited for; matrix products, arithmetic and copies ran while one was open for 26% of the time, Pallas kernels for 17%

profile of v6, /device:TPU:0, one launch (start us, length us, event | category | flops | bytes accessed | tf_op | source)
XLA Modules:
  0.0 635.9 jit_solution(15386914287559022167)
XLA Ops:
  19.6 5.3 slice.215
  26.0 5.4 fusion.8
  55.2 12.8 %project.1 = (bf16[1024,576]{1,0:T(8,128)(2,1)}, bf16[1024,576]{1,0:T(8,128)(2,1)}, bf16[1024,576]{1,0:T(8,128)(2,1)}, bf16[1024,1152]{1,0:T(8,128)(2,1)}) custom-call(bf16[1024,1152]{1,0:T(8,128)(2,1)} %maximum_select_fusion.2.tokens.refs_0_, s32[1024,1]{1,0:T(8,128)} %copy.72.ids.refs_7_, bf16[2,256,1152]{2,1,0:T(8,128)(2,1)} %fusion.38.table, ...), custom_call_target="tpu_custom_call" | custom-call | flops 4076863488 | bytes 7526656 | tf_op jit(solution)/shard_map/project/pallas_call | solution.py:565
  84.8 12.1 %attention_forward.1 = (bf16[1024,576]{1,0:T(8,128)(2,1)S(1)}, f32[8,1024]{1,0:T(8,128)S(1)}) custom-call(bf16[1024,576]{1,0:T(8,128)(2,1)S(1)} %copy-done.6, bf16[1024,576]{1,0:T(8,128)(2,1)S(1)} %copy-done.2, bf16[1024,576]{1,0:T(8,128)(2,1)S(1)} %copy-done.3, bf16[2,128,576]{2,1,0:T(8,128)(2,1)} %collective-permute-done.3.refs_3_, ...), custom_call_target="tpu_custom_call" | custom-call | flops 1207959552 | bytes 4718592 | tf_op jit(solution)/shard_map/attention_forward/pallas_call | solution.py:370
  111.9 5.2 fusion.24.table.refs_10_
  117.1 17.7 %collective-permute-done.5.theirs = bf16[512,1152]{1,0:T(8,128)(2,1)} collective-permute-done((bf16[512,1152]{1,0:T(8,128)(2,1)}, bf16[512,1152]{1,0:T(8,128)(2,1)}, u32[]{:S(2)}, u32[]{:S(2)}) %collective-permute-start.5) | collective-permute-done | bytes 1179680 | tf_op jit(solution)/shard_map/ppermute | solution.py:21
  134.8 27.3 %mlp.2 = (bf16[512,1152]{1,0:T(8,128)(2,1)}, bf16[512,2304]{1,0:T(8,128)(2,1)}, bf16[512,2304]{1,0:T(8,128)(2,1)}, bf16[512,1152]{1,0:T(8,128)(2,1)}, bf16[512,1...) custom-call(bf16[512,1152]{1,0:T(8,128)(2,1)} %get-tuple-element.141.tokens, ...), custom_call_target="tpu_custom_call" | custom-call | flops 10871635968 | bytes 17705728 | tf_op jit(solution)/shard_map/mlp/pallas_call | solution.py:565
  167.3 27.2 %mlp.3 = (bf16[512,1152]{1,0:T(8,128)(2,1)}, bf16[512,2304]{1,0:T(8,128)(2,1)}, bf16[512,2304]{1,0:T(8,128)(2,1)}, bf16[512,1152]{1,0:T(8,128)(2,1)}, bf16[512,1...) custom-call(bf16[512,1152]{1,0:T(8,128)(2,1)} %get-tuple-element.142.tokens, ...), custom_call_target="tpu_custom_call" | custom-call | flops 10871635968 | bytes 17705728 | tf_op jit(solution)/shard_map/mlp/pallas_call | solution.py:565
  199.7 6.6 %convolution_convert_fusion.2 = bf16[1152,1152]{1,0:T(8,128)(2,1)} fusion(bf16[1024,1152]{1,0:T(8,128)(2,1)S(1)} %copy-done.57, bf16[1024,2304]{1,0:T(8,128)(2,1)} %constant_dynamic-update-slice_fusion.6, s32[]{:T(128)S(6)} %select_n.145), kind=kOutput, calls=%fused_computation.6 | convolution fusion | flops 2719236096 | bytes 7372804 | tf_op jit(solution)/shard_map/dot_general | solution.py:17
  234.2 7.4 %fusion.4 = bf16[1152,1152]{1,0:T(8,128)(2,1)} fusion(bf16[1024,1152]{1,0:T(8,128)(2,1)S(1)} %copy-done.58, bf16[1152,1152]{1,0:T(8,128)(2,1)} %collective-permute-done.8, bf16[1024,2304]{1,0:T(8,128)(2,1)S(1)} %bitcast.109, s32[]{:T(128)S(6)} %select_n.144), kind=kOutput, calls=%fused_computation.10 | convolution fusion | flops 2724544512 | bytes 10027012 | tf_op jit(solution)/shard_map/dot_general | solution.py:17
  241.6 6.6 %fusion.5 = bf16[1152,1152]{1,0:T(8,128)(2,1)} fusion(bf16[1024,1152]{1,0:T(8,128)(2,1)S(1)} %copy-done.23, bf16[1152,1152]{1,0:T(8,128)(2,1)} %collective-permute-done.9, bf16[1024,2304]{1,0:T(8,128)(2,1)S(1)} %bitcast.131, s32[]{:T(128)S(6)} %select_n.144), kind=kOutput, calls=%fused_computation.11 | convolution fusion | flops 2724544512 | bytes 10027012 | tf_op jit(solution)/shard_map/dot_general | solution.py:17
  248.2 7.5 %collective-permute-done.11 = bf16[512,1152]{1,0:T(8,128)(2,1)} collective-permute-done((bf16[512,1152]{1,0:T(8,128)(2,1)}, bf16[512,1152]{1,0:T(8,128)(2,1)}, u32[]{:S(2)}, u32[]{:S(2)}) %collective-permute-start.11) | collective-permute-done | bytes 1179680 | tf_op jit(solution)/shard_map/ppermute | solution.py:21
  255.6 31.8 %collective-permute-done.10 = bf16[512,1152]{1,0:T(8,128)(2,1)} collective-permute-done((bf16[512,1152]{1,0:T(8,128)(2,1)S(1)}, bf16[512,1152]{1,0:T(8,128)(2,1)}, u32[]{:S(2)}, u32[]{:S(2)}) %collective-permute-start.10) | collective-permute-done | bytes 1179680 | tf_op jit(solution)/shard_map/ppermute | solution.py:21
  305.5 18.4 %middle_back.1 = (f32[1024,1152]{1,0:T(8,128)}, bf16[1024,576]{1,0:T(8,128)(2,1)}, bf16[576,1152]{1,0:T(8,128)(2,1)}, bf16[2,3,256,576]{3,2,1,0:T(8,128)(2,1)}, f32[1,1152]{1,0:T(1,128)}) custom-call(bf16[1024,1152]{1,0:T(8,128)(2,1)} %maximum_select_fusion.2.tokens.refs_0_, bf16[1024,1152]{1,0:T(8,128)(2,1)} %pad_maximum_fusion.refs_1_, ...), custom_call_target="tpu_custom_call" | custom-call | bytes 1024 | tf_op jit(solution)/shard_map/middle_back/pallas_call | solution.py:565
  324.0 26.6 %attention_backward.1 = (bf16[1024,576]{1,0:T(8,128)(2,1)S(1)}, bf16[2,1024,576]{2,1,0:T(8,128)(2,1)}, bf16[2,2,128,576]{3,2,1,0:T(8,128)(2,1)S(1)}) custom-call(bf16[1024,576]{1,0:T(8,128)(2,1)S(1)} %copy-done.7, bf16[1024,576]{1,0:T(8,128)(2,1)S(1)} %copy-done.2, bf16[1024,576]{1,0:T(8,128)(2,1)} %get-tuple-element.60.refs_2_, ...), custom_call_target="tpu_custom_call" | custom-call | flops 589824 | bytes 589824 | tf_op jit(solution)/shard_map/attention_backward/pallas_call | solution.py:471
  354.0 5.3 fusion.23
  361.4 21.4 %project_back.1 = (bf16[1024,1152]{1,0:T(8,128)(2,1)}, bf16[1536,1152]{1,0:T(8,128)(2,1)}, bf16[192,1152]{1,0:T(8,128)(2,1)}, bf16[2,2,256,576]{3,2,1,0:T(8,128)(2,1)}, f32[2,576]{1,0:T(2,128)}) custom-call(bf16[1024,1152]{1,0:T(8,128)(2,1)} %maximum_select_fusion.2.tokens.refs_0_, bf16[1024,1152]{1,0:T(8,128)(2,1)} %get-tuple-element.77.refs_1_, ...), custom_call_target="tpu_custom_call" | custom-call | bytes 1024 | tf_op jit(solution)/shard_map/project_back/pallas_call | solution.py:565
  389.4 10.0 %collective-permute-done.14 = bf16[2,256,576]{1,2,0:T(8,128)(2,1)} collective-permute-done((bf16[2,256,576]{1,2,0:T(8,128)(2,1)}, bf16[2,256,576]{1,2,0:T(8,128)(2,1)}, u32[]{:S(2)}, u32[]{:S(2)}) %collective-permute-start.14) | collective-permute-done | bytes 589856 | tf_op jit(solution)/shard_map/ppermute | solution.py:21
  404.4 73.4 %all-reduce.4.cloned.1.call-done = (bf16[1152,1152]{1,0:T(8,128)(2,1)}, bf16[1152,1152]{1,0:T(8,128)(2,1)}) async-done(((bf16[1152,1152]{1,0:T(8,128)(2,1)}, bf16[1152,1152]{1,0:T(8,128)(2,1)}), (bf16[1152,1152]{1,0:T(8,128)(2,1)}, bf16[1152,1152]{1,0:T(8,128)(2,1)})) %all-reduce.4.cloned.1.call-update) | async-done | bytes 5308432 | tf_op jit(solution)/shard_map/psum | solution.py:932
  482.2 82.6 %ring_sum.1 = (bf16[2,8,2,96,1152]{4,3,2,1,0:T(8,128)(2,1)}, bf16[512,1152]{1,0:T(8,128)(2,1)S(1)}, f32[8,1152]{1,0:T(8,128)S(1)}) custom-call(bf16[8,2,96,1152]{3,2,1,0:T(8,128)(2,1)S(1)} %bitcast.98, bf16[8,2,96,1152]{3,2,1,0:T(8,128)(2,1)S(1)} %bitcast.97, bf16[1024,1152]{1,0:T(8,128)(2,1)S(1)} %copy-done.1, f32[8,1152]{1,0:T(8,128)S(1)} %copy-done.8), custom_call_target="tpu_custom_call" | custom-call | tf_op jit(solution)/shard_map/ring_sum/pallas_call | solution.py:250
  575.4 10.2 %fusion.47 = f32[1152,6,576]{0,2,1:T(8,128)} fusion(bf16[6,576,256]{2,1,0:T(8,128)(2,1)} %bitcast.111, bf16[256,1152]{1,0:T(8,128)(2,1)} %param.16), kind=kOutput, calls=%fused_computation.92 | convolution fusion | flops 2040201216 | bytes 18284544 | tf_op jit(solution)/shard_map/dot_general | solution.py:1069
  599.7 5.9 convert_bitcast_fusion
  614.4 6.9 %fusion.7 = f32[2304,1152]{1,0:T(8,128)} fusion(bf16[1152,1152]{1,0:T(8,128)(2,1)} %collective-permute-done.18, bf16[1152,1152]{1,0:T(8,128)(2,1)S(1)} %copy-done.26, pred[]{:T(512)S(6)} %eq.29), kind=kLoop, calls=%fused_computation.15 | loop fusion | flops 26542080 | bytes 15925249 | tf_op jit(solution)/shard_map/convert_element_type | solution.py:1051
  621.3 7.3 %fusion.6 = f32[1152,2304]{1,0:T(8,128)} fusion(bf16[1152,1152]{1,0:T(8,128)(2,1)} %collective-permute-done.17, bf16[1152,1152]{1,0:T(8,128)(2,1)S(1)} %copy-done.25, pred[]{:T(512)S(6)} %eq.29), kind=kLoop, calls=%fused_computation.13 | loop fusion | flops 26542080 | bytes 15925249 | tf_op jit(solution)/shard_map/convert_element_type | solution.py:1051
  (321 shorter events, 177.6 us)
Async XLA Ops:
  7.2 470.6 %all-reduce.4.cloned.1.call-start = ((), (), s32[]{:S(2)}) async-start(), calls=%async_computation | async-start | bytes 10616832 | tf_op jit(solution)/shard_map/psum | solution.py:932
  7.2 44.1 %collective-permute-start = (bf16[512,1152]{1,0:T(8,128)(2,1)}, bf16[512,1152]{1,0:T(8,128)(2,1)}, u32[]{:S(2)}, u32[]{:S(2)}) collective-permute-start(bf16[512,1152]{1,0:T(8,128)(2,1)} %param.15), channel_id=1, source_target_pairs={{0,1},{1,0},{2,3},{3,2},{4,5},{5,4},{6,7},{7,6},{8,9},{9,8},{10,11... | collective-permute-start | bytes 3538952 | tf_op jit(solution)/shard_map/ppermute | solution.py:21
  19.1 30.0 %collective-permute-start.2 = (bf16[576,256,2]{1,0,2:T(8,128)(2,1)S(1)}, bf16[576,256,2]{1,0,2:T(8,128)(2,1)S(1)}, u32[]{:S(2)}, u32[]{:S(2)}) collective-permute-start(bf16[576,256,2]{1,0,2:T(8,128)(2,1)S(1)} %bitcast.128), channel_id=1, source_target_pairs={{0,1},{1,0},{2,3},{3,2},{4,5},{5,4},{6,7},{7,6},{8,9},{9,8},{10,11... | collective-permute-start | bytes 1769480 | tf_op jit(solution)/shard_map/ppermute | solution.py:21
  33.4 194.9 %copy-start.61 = (s32[1024]{0:T(1024)}, s32[1024]{0:T(1024)S(1)}, u32[]{:S(2)}) copy-start(s32[1024]{0:T(1024)S(1)} %get-tuple-element.108) | copy-start | bytes 12292
  70.1 13.4 %collective-permute-start.3 = (bf16[2,128,576]{2,1,0:T(8,128)(2,1)}, bf16[2,128,576]{2,1,0:T(8,128)(2,1)}, u32[]{:S(2)}, u32[]{:S(2)}) collective-permute-start(bf16[2,128,576]{2,1,0:T(8,128)(2,1)} %pad_maximum_fusion.4), channel_id=1, source_target_pairs={{0,2},{2,4},{4,6},{6,8},{8,10},{10,12},{12,14},{14,16},{16,18},{18... | collective-permute-start | bytes 884744 | tf_op jit(solution)/shard_map/ppermute | solution.py:866
  72.9 10.6 %collective-permute-start.4 = (bf16[2,128,576]{2,1,0:T(8,128)(2,1)}, bf16[2,128,576]{2,1,0:T(8,128)(2,1)}, u32[]{:S(2)}, u32[]{:S(2)}) collective-permute-start(bf16[2,128,576]{2,1,0:T(8,128)(2,1)} %pad_maximum_fusion.5), channel_id=1, source_target_pairs={{2,0},{4,2},{6,4},{8,6},{10,8},{12,10},{14,12},{16,14},{18,16},{20... | collective-permute-start | bytes 884744 | tf_op jit(solution)/shard_map/ppermute | solution.py:869
  79.3 144.0 %copy-start.54 = (pred[1024,256]{1,0:T(32,128)(4,1)}, pred[1024,256]{1,0:T(32,128)(4,1)S(1)}, u32[]{:S(2)}) copy-start(pred[1024,256]{1,0:T(32,128)(4,1)S(1)} %iota_compare_fusion) | copy-start | bytes 786436
  81.8 27.7 %collective-permute-start.1 = (bf16[576,256,4]{1,0,2:T(8,128)(2,1)}, bf16[576,256,4]{1,0,2:T(8,128)(2,1)}, u32[]{:S(2)}, u32[]{:S(2)}) collective-permute-start(bf16[576,256,4]{1,0,2:T(8,128)(2,1)} %copy.64), channel_id=1, source_target_pairs={{0,1},{1,0},{2,3},{3,2},{4,5},{5,4},{6,7},{7,6},{8,9},{9,8},{10,11... | collective-permute-start | bytes 3538952 | tf_op jit(solution)/shard_map/ppermute | solution.py:21
  99.1 35.7 %collective-permute-start.5 = (bf16[512,1152]{1,0:T(8,128)(2,1)}, bf16[512,1152]{1,0:T(8,128)(2,1)}, u32[]{:S(2)}, u32[]{:S(2)}) collective-permute-start(bf16[512,1152]{1,0:T(8,128)(2,1)} %convolution_convert_fusion.5.mine), channel_id=1, source_target_pairs={{0,1},{1,0},{2,3},{3,2},{4,5},{5,4},{6,7},{7,6},{8,9},{9,8},{10,11... | collective-permute-start | bytes 3538952 | tf_op jit(solution)/shard_map/ppermute | solution.py:21
  103.8 63.5 %collective-permute-start.6 = (bf16[512,1152]{1,0:T(8,128)(2,1)}, bf16[512,1152]{1,0:T(8,128)(2,1)}, u32[]{:S(2)}, u32[]{:S(2)}) collective-permute-start(bf16[512,1152]{1,0:T(8,128)(2,1)} %convolution_convert_fusion.4.mine), channel_id=1, source_target_pairs={{0,1},{1,0},{2,3},{3,2},{4,5},{5,4},{6,7},{7,6},{8,9},{9,8},{10,11... | collective-permute-start | bytes 3538952 | tf_op jit(solution)/shard_map/ppermute | solution.py:21
  206.3 27.9 %collective-permute-start.8 = (bf16[1152,1152]{1,0:T(8,128)(2,1)}, bf16[1152,1152]{1,0:T(8,128)(2,1)}, u32[]{:S(2)}, u32[]{:S(2)}) collective-permute-start(bf16[1152,1152]{1,0:T(8,128)(2,1)} %convolution_convert_fusion.2), channel_id=1, source_target_pairs={{0,2},{2,0},{4,6},{6,4},{8,10},{10,8},{12,14},{14,12},{16,18},{18,... | collective-permute-start | bytes 7962632 | tf_op jit(solution)/shard_map/ppermute | solution.py:926
  217.6 23.9 %collective-permute-start.9 = (bf16[1152,1152]{1,0:T(8,128)(2,1)}, bf16[1152,1152]{1,0:T(8,128)(2,1)}, u32[]{:S(2)}, u32[]{:S(2)}) collective-permute-start(bf16[1152,1152]{1,0:T(8,128)(2,1)} %convolution_convert_fusion), channel_id=1, source_target_pairs={{0,2},{2,0},{4,6},{6,4},{8,10},{10,8},{12,14},{14,12},{16,18},{18,... | collective-permute-start | bytes 7962632 | tf_op jit(solution)/shard_map/ppermute | solution.py:926
  226.5 29.2 %collective-permute-start.11 = (bf16[512,1152]{1,0:T(8,128)(2,1)}, bf16[512,1152]{1,0:T(8,128)(2,1)}, u32[]{:S(2)}, u32[]{:S(2)}) collective-permute-start(bf16[512,1152]{1,0:T(8,128)(2,1)} %get-tuple-element.65), channel_id=1, source_target_pairs={{0,1},{1,0},{2,3},{3,2},{4,5},{5,4},{6,7},{7,6},{8,9},{9,8},{10,11... | collective-permute-start | bytes 3538952 | tf_op jit(solution)/shard_map/ppermute | solution.py:21
  232.0 69.1 %collective-permute-start.15 = (bf16[256,576]{1,0:T(8,128)(2,1)}, bf16[256,576]{1,0:T(8,128)(2,1)S(1)}, u32[]{:S(2)}, u32[]{:S(2)}) collective-permute-start(bf16[256,576]{1,0:T(8,128)(2,1)} %constant_dynamic-slice_fusion), channel_id=1, source_target_pairs={{0,1},{1,0},{2,3},{3,2},{4,5},{5,4},{6,7},{7,6},{8,9},{9,8},{10,11... | collective-permute-start | bytes 884744 | tf_op jit(solution)/shard_map/ppermute | solution.py:21
  232.6 54.8 %collective-permute-start.10 = (bf16[512,1152]{1,0:T(8,128)(2,1)S(1)}, bf16[512,1152]{1,0:T(8,128)(2,1)}, u32[]{:S(2)}, u32[]{:S(2)}) collective-permute-start(bf16[512,1152]{1,0:T(8,128)(2,1)S(1)} %copy-done.48), channel_id=1, source_target_pairs={{0,1},{1,0},{2,3},{3,2},{4,5},{5,4},{6,7},{7,6},{8,9},{9,8},{10,11... | collective-permute-start | bytes 3538952 | tf_op jit(solution)/shard_map/ppermute | solution.py:21
  289.9 64.1 %collective-permute-start.7 = (bf16[512,1152]{1,0:T(8,128)(2,1)}, bf16[512,1152]{1,0:T(8,128)(2,1)}, u32[]{:S(2)}, u32[]{:S(2)}) collective-permute-start(bf16[512,1152]{1,0:T(8,128)(2,1)} %constant_dynamic-slice_fusion.2), channel_id=1, source_target_pairs={{0,1},{1,0},{2,3},{3,2},{4,5},{5,4},{6,7},{7,6},{8,9},{9,8},{10,11... | collective-permute-start | bytes 3538952 | tf_op jit(solution)/shard_map/ppermute | solution.py:21
  323.9 30.0 %copy-start.13 = (bf16[512,1152]{1,0:T(8,128)(2,1)S(1)}, bf16[512,1152]{1,0:T(8,128)(2,1)}, u32[]{:S(2)}) copy-start(bf16[512,1152]{1,0:T(8,128)(2,1)} %param.15) | copy-start | bytes 3538948
  350.7 9.7 %collective-permute-start.12 = (bf16[2,128,576]{2,1,0:T(8,128)(2,1)S(1)}, bf16[2,128,576]{2,1,0:T(8,128)(2,1)S(1)}, u32[]{:S(2)}, u32[]{:S(2)}) collective-permute-start(bf16[2,128,576]{2,1,0:T(8,128)(2,1)S(1)} %get-tuple-element.125), channel_id=1, source_target_pairs={{0,2},{2,4},{4,6},{6,8},{8,10},{10,12},{12,14},{14,16},{16,18},{18... | collective-permute-start | bytes 884744 | tf_op jit(solution)/shard_map/ppermute | solution.py:866
  352.6 7.8 %collective-permute-start.13 = (bf16[2,128,576]{2,1,0:T(8,128)(2,1)S(1)}, bf16[2,128,576]{2,1,0:T(8,128)(2,1)S(1)}, u32[]{:S(2)}, u32[]{:S(2)}) collective-permute-start(bf16[2,128,576]{2,1,0:T(8,128)(2,1)S(1)} %get-tuple-element.126), channel_id=1, source_target_pairs={{2,0},{4,2},{6,4},{8,6},{10,8},{12,10},{14,12},{16,14},{18,16},{20... | collective-permute-start | bytes 884744 | tf_op jit(solution)/shard_map/ppermute | solution.py:869
  385.0 14.5 %collective-permute-start.14 = (bf16[2,256,576]{1,2,0:T(8,128)(2,1)}, bf16[2,256,576]{1,2,0:T(8,128)(2,1)}, u32[]{:S(2)}, u32[]{:S(2)}) collective-permute-start(bf16[2,256,576]{1,2,0:T(8,128)(2,1)} %bitcast.36), channel_id=1, source_target_pairs={{0,1},{1,0},{2,3},{3,2},{4,5},{5,4},{6,7},{7,6},{8,9},{9,8},{10,11... | collective-permute-start | bytes 1769480 | tf_op jit(solution)/shard_map/ppermute | solution.py:21
  482.2 82.6 %copy-start.29 = (bf16[2,576,1152]{2,1,0:T(8,128)(2,1)S(1)}, bf16[2,576,1152]{2,1,0:T(8,128)(2,1)}, u32[]{:S(2)}) copy-start(bf16[2,576,1152]{2,1,0:T(8,128)(2,1)} %copy-done.28) | copy-start | bytes 7962628
  575.0 39.4 %collective-permute-start.18 = (bf16[1152,1152]{1,0:T(8,128)(2,1)}, bf16[1152,1152]{1,0:T(8,128)(2,1)}, u32[]{:S(2)}, u32[]{:S(2)}) collective-permute-start(bf16[1152,1152]{1,0:T(8,128)(2,1)} %get-tuple-element.98), channel_id=1, source_target_pairs={{0,2},{2,0},{4,6},{6,4},{8,10},{10,8},{12,14},{14,12},{16,18},{18,... | collective-permute-start | bytes 7962632 | tf_op jit(solution)/shard_map/ppermute | solution.py:1042
  597.8 15.4 %collective-permute-start.16 = (bf16[256,1152]{1,0:T(8,128)(2,1)S(1)}, bf16[256,1152]{1,0:T(8,128)(2,1)S(1)}, u32[]{:S(2)}, u32[]{:S(2)}) collective-permute-start(bf16[256,1152]{1,0:T(8,128)(2,1)S(1)} %copy-done.59), channel_id=1, source_target_pairs={{0,1},{1,0},{2,3},{3,2},{4,5},{5,4},{6,7},{7,6},{8,9},{9,8},{10,11... | collective-permute-start | bytes 1769480 | tf_op jit(solution)/shard_map/ppermute | solution.py:21
  599.1 22.2 %collective-permute-start.17 = (bf16[1152,1152]{1,0:T(8,128)(2,1)}, bf16[1152,1152]{1,0:T(8,128)(2,1)}, u32[]{:S(2)}, u32[]{:S(2)}) collective-permute-start(bf16[1152,1152]{1,0:T(8,128)(2,1)} %get-tuple-element.97), channel_id=1, source_target_pairs={{0,2},{2,0},{4,6},{6,4},{8,10},{10,8},{12,14},{14,12},{16,18},{18,... | collective-permute-start | bytes 7962632 | tf_op jit(solution)/shard_map/ppermute | solution.py:1042
  (82 other events, 551.2 us)
Sparse Core Ops, SparseCore 0:
  287.6 190.1 all-reduce.3

commit v7 on v5

--- a/solution.py
+++ b/solution.py
@@ -52,11 +52,15 @@
 UNIT = 48
 
 
-def ring_kernel(chips, subs, *refs):
-    data, part, loose, out, landing, loose_out = refs[:2], *refs[2:7]
-    mine, theirs, slots, last, loose_pair, loose_rows = refs[7:13]
-    copy_sems, core_sems, ring_sems, swap_sems, gather_sems, pair_sems, own_sems = refs[13:20]
-    loose_pair_sems, loose_sems = refs[20:]
+def ring_kernel(chips, subs, full, *refs):
+    data = refs[:2]
+    if full:
+        part, loose, out, landing, loose_out, *refs = refs[2:]
+        last, loose_pair, loose_rows, *sems = refs[6:]
+        swap_sems, gather_sems, pair_sems, own_sems, loose_pair_sems, loose_sems = sems
+    else:
+        last, *refs = refs[2:]
+    mine, theirs, slots, copy_sems, core_sems, ring_sems = refs[:6]
     wide = lax.axis_index("wide")
     chip, core = wide // 2, wide % 2
     half = chips // 2
@@ -70,31 +74,56 @@
     ahead = 2 * place(position + 1) + core
     behind = 2 * place(position - 1) + core
     sibling = 2 * chip + 1 - core
-    facing = 1 - lax.axis_index("narrow")
     barrier = pltpu.get_barrier_semaphore()
     for device in (ahead, behind, sibling):
         pl.semaphore_signal(barrier, inc=1, device_id={"wide": device}, device_id_type=MESH)
-    pl.semaphore_signal(barrier, inc=1, device_id={"narrow": facing}, device_id_type=MESH)
-    pl.semaphore_wait(barrier, 4)
-    share = landing.shape[0]
-    turn = pltpu.make_async_remote_copy(
-        src_ref=part.at[pl.ds(facing * share, share)],
-        dst_ref=landing,
-        send_sem=swap_sems.at[0],
-        recv_sem=swap_sems.at[1],
-        device_id={"narrow": facing},
-        device_id_type=MESH,
-    )
-    turn.start()
-    loose_swap = pltpu.make_async_remote_copy(
-        src_ref=loose,
-        dst_ref=loose_pair,
-        send_sem=loose_pair_sems.at[0],
-        recv_sem=loose_pair_sems.at[1],
-        device_id={"wide": sibling},
-        device_id_type=MESH,
-    )
-    loose_swap.start()
+    if full:
+        facing = 1 - lax.axis_index("narrow")
+        pl.semaphore_signal(barrier, inc=1, device_id={"narrow": facing}, device_id_type=MESH)
+    pl.semaphore_wait(barrier, 3 + int(full))
+
+    def local(lane):
+        return pltpu.make_async_copy(data[lane].at[:, core], mine.at[lane], copy_sems.at[lane])
+
+    def needed(lane, order):
+        return place(position - 1 - order if lane == 0 else position + 1 + order)
+
+    def across(lane, order):
+        index = needed(lane, order)
+        return pltpu.make_async_remote_copy(
+            src_ref=data[lane].at[index, 1 - core],
+            dst_ref=theirs.at[lane, index],
+            send_sem=core_sems.at[0, lane, order],
+            recv_sem=core_sems.at[1, lane, order],
+            device_id={"wide": sibling},
+            device_id_type=MESH,
+        )
+
+    for order in range(chips):
+        for lane in range(2):
+            across(lane, order).start()
+            if order == 0:
+                local(lane).start()
+    if full:
+        share = landing.shape[0]
+        turn = pltpu.make_async_remote_copy(
+            src_ref=part.at[pl.ds(facing * share, share)],
+            dst_ref=landing,
+            send_sem=swap_sems.at[0],
+            recv_sem=swap_sems.at[1],
+            device_id={"narrow": facing},
+            device_id_type=MESH,
+        )
+        turn.start()
+        loose_swap = pltpu.make_async_remote_copy(
+            src_ref=loose,
+            dst_ref=loose_pair,
+            send_sem=loose_pair_sems.at[0],
+            recv_sem=loose_pair_sems.at[1],
+            device_id={"wide": sibling},
+            device_id_type=MESH,
+        )
+        loose_swap.start()
 
     def loose_hop(step, index):
         return pltpu.make_async_remote_copy(
@@ -105,23 +134,6 @@
             device_id={"wide": ahead},
             device_id_type=MESH,
         )
-
-    def local(lane):
-        return pltpu.make_async_copy(data[lane].at[:, core], mine.at[lane], copy_sems.at[lane])
-
-    def across(lane):
-        return pltpu.make_async_remote_copy(
-            src_ref=data[lane].at[:, 1 - core],
-            dst_ref=theirs.at[lane],
-            send_sem=core_sems.at[0, lane],
-            recv_sem=core_sems.at[1, lane],
-            device_id={"wide": sibling},
-            device_id_type=MESH,
-        )
-
-    for lane in range(2):
-        across(lane).start()
-        local(lane).start()
 
     def rows_of(sub):
         return pl.ds(sub * UNIT, UNIT)
@@ -183,61 +195,97 @@
             last.at[lane, rows_of(sub)], held(lane, 0, sub, core), own_sems.at[lane, sub]
         )
 
-    loose_swap.wait()
-    loose_rows[chip] = loose[...] + loose_pair[...]
-    loose_hop(0, chip).start()
+    def pair_sum(lane, order, rows):
+        index = needed(lane, order)
+        return mine[lane, index, rows].astype(F32) + theirs[lane, index, rows].astype(F32)
+
     for lane in range(2):
         local(lane).wait()
-        across(lane).wait()
-
-        def merge(index, carry, lane=lane):
-            mine[lane, index] = mine[lane, index] + theirs[lane, index]
-            return carry
-
-        lax.fori_loop(0, chips, merge, 0)
+        across(lane, 0).wait_recv()
         for sub in range(subs):
+            mine[lane, needed(lane, 0), rows_of(sub)] = pair_sum(lane, 0, rows_of(sub)).astype(BF16)
             hop(lane, 0, sub).start()
-    for step in range(chips - 1):
-        passed = place(position - 1 - step)
-        loose_hop(step, passed).wait_recv()
-        if step < chips - 2:
-            loose_hop(step + 1, passed).start()
-        for sub in range(subs):
-            for lane in range(2):
-                hop(lane, step, sub).wait_recv()
-                offset = 2 + step
-                index = place(position - offset if lane == 0 else position + offset)
-                rows = rows_of(sub)
-                total = slots[lane, step, rows] + mine[lane, index, rows]
-                if step == chips - 2:
-                    last[lane, rows] = total
-                    send_on(lane, 0, sub).start()
-                    pair(lane, 0, sub, core).start()
-                    keep(lane, sub).start()
-                else:
-                    slots[lane, step, rows] = total
-                    hop(lane, step + 1, sub).start()
+    if full:
+        loose_swap.wait()
+        loose_rows[chip] = loose[...] + loose_pair[...]
+        loose_hop(0, chip).start()
     for step in range(chips - 1):
         for sub in range(subs):
             for lane in range(2):
-                landed(lane, step, sub).wait_recv()
+                if sub == 0:
+                    across(lane, step + 1).wait_recv()
+                rows = rows_of(sub)
+                extra = pair_sum(lane, step + 1, rows)
+                hop(lane, step, sub).wait_recv()
+                total = (slots[lane, step, rows].astype(F32) + extra).astype(BF16)
                 if step < chips - 2:
-                    send_on(lane, step + 1, sub).start()
-                pair(lane, step + 1, sub, core).start()
-    loose_out[...] = jnp.sum(loose_rows[...], axis=0)
+                    slots[lane, step, rows] = total
+                    hop(lane, step + 1, sub).start()
+                else:
+                    last[lane, rows] = total
+                    if full:
+                        send_on(lane, 0, sub).start()
+                        pair(lane, 0, sub, core).start()
+                        keep(lane, sub).start()
+        if full:
+            passed = place(position - 1 - step)
+            loose_hop(step, passed).wait_recv()
+            if step < chips - 2:
+                loose_hop(step + 1, passed).start()
+    if full:
+        for step in range(chips - 1):
+            for sub in range(subs):
+                for lane in range(2):
+                    landed(lane, step, sub).wait_recv()
+                    if step < chips - 2:
+                        send_on(lane, step + 1, sub).start()
+                    pair(lane, step + 1, sub, core).start()
+        loose_out[...] = jnp.sum(loose_rows[...], axis=0)
     for step in range(chips):
-        if step < chips - 1:
+        if full and step < chips - 1:
             loose_hop(step, place(position - step)).wait_send()
-        for sub in range(subs):
-            for lane in range(2):
-                pair(lane, step, sub, 1 - core).wait_recv()
-                pair(lane, step, sub, core).wait_send()
-                if step == 0:
-                    keep(lane, sub).wait()
+        for lane in range(2):
+            across(lane, step).wait_send()
+            for sub in range(subs):
                 if step < chips - 1:
                     hop(lane, step, sub).wait_send()
-                    send_on(lane, step, sub).wait_send()
-    turn.wait()
+                if full:
+                    pair(lane, step, sub, 1 - core).wait_recv()
+                    pair(lane, step, sub, core).wait_send()
+                    if step == 0:
+                        keep(lane, sub).wait()
+                    if step < chips - 1:
+                        send_on(lane, step, sub).wait_send()
+    if full:
+        turn.wait()
+
+
+def ring_scratch(chips, shard, width):
+    return [
+        pltpu.VMEM((2, chips, shard, width), BF16),
+        pltpu.VMEM((2, chips, shard, width), BF16),
+        pltpu.VMEM((2, chips - 1, shard, width), BF16),
+        pltpu.SemaphoreType.DMA((2,)),
+        pltpu.SemaphoreType.DMA((2, 2, chips)),
+        pltpu.SemaphoreType.DMA((2, 2, chips - 1, shard // UNIT)),
+    ]
+
+
+def ring_scatter(lanes, collective_id):
+    chips = lax.axis_size("wide") // 2
+    rows, width = lanes[0].shape
+    shard = rows // (2 * chips)
+    return pl.pallas_call(
+        lambda *refs: ring_kernel(chips, shard // UNIT, False, *refs),
+        out_shape=jax.ShapeDtypeStruct((2, shard, width), BF16),
+        in_specs=[pl.BlockSpec(memory_space=pl.ANY)] * 2,
+        out_specs=pl.BlockSpec(memory_space=pltpu.VMEM),
+        scratch_shapes=ring_scratch(chips, shard, width),
+        compiler_params=pltpu.CompilerParams(
+            collective_id=collective_id, has_side_effects=True, vmem_limit_bytes=40 << 20
+        ),
+        name="ring_scatter",
+    )(*[lane.reshape(chips, 2, shard, width) for lane in lanes])
 
 
 def ring_sum(lanes, part, loose, collective_id):
@@ -248,7 +296,7 @@
     anywhere = pl.BlockSpec(memory_space=pl.ANY)
     inside = pl.BlockSpec(memory_space=pltpu.VMEM)
     sums, landed, loose_sum = pl.pallas_call(
-        lambda *refs: ring_kernel(chips, subs, *refs),
+        lambda *refs: ring_kernel(chips, subs, True, *refs),
         out_shape=[
             jax.ShapeDtypeStruct((2, chips, 2, shard, width), BF16),
             jax.ShapeDtypeStruct((part.shape[0] // 2, part.shape[1]), BF16),
@@ -256,16 +304,11 @@
         ],
         in_specs=[anywhere] * 3 + [inside],
         out_specs=[anywhere] * 2 + [inside],
-        scratch_shapes=[
-            pltpu.VMEM((2, chips, shard, width), BF16),
-            pltpu.VMEM((2, chips, shard, width), BF16),
-            pltpu.VMEM((2, chips - 1, shard, width), BF16),
+        scratch_shapes=ring_scratch(chips, shard, width)
+        + [
             pltpu.VMEM((2, shard, width), BF16),
             pltpu.VMEM(loose.shape, F32),
             pltpu.VMEM((chips,) + loose.shape, F32),
-            pltpu.SemaphoreType.DMA((2,)),
-            pltpu.SemaphoreType.DMA((2, 2)),
-            pltpu.SemaphoreType.DMA((2, 2, chips - 1, subs)),
             pltpu.SemaphoreType.DMA((2,)),
             pltpu.SemaphoreType.DMA((2, 2, chips - 1, subs)),
             pltpu.SemaphoreType.DMA((2, 2, chips, subs)),
@@ -614,7 +657,8 @@
 def mlp_kernel(
     tokens, mine, theirs, cotangent, ids, live, table, out_bias, up, up_bias, down, *outs
 ):
-    norm_two, hidden, d_upper, d_branch, d_norm, branch = outs
+    norm_two, hidden, d_upper, d_branch, d_norm, branch, up_sum, down_sum = outs
+    first = pl.program_id(0) == 0
     ids, live = ids[...], live[...]
     attn = mine[...].astype(F32) + theirs[...].astype(F32) + out_bias[...].astype(F32)
     middle = tokens[...].astype(F32) + live * pick(ids, table[0]) * attn
@@ -623,6 +667,8 @@
     norm_two[...] = normed
     pulled = (live * pick(ids, table[3]) * cotangent[...].astype(F32)).astype(BF16)
     d_branch[...] = pulled
+    column = jnp.sum(pulled.astype(F32), axis=0, keepdims=True)
+    down_sum[...] = jnp.where(first, 0.0, down_sum[...]) + column
     width = up.shape[1]
     step = 384 if width % 384 == 0 else width
     back = ahead = 0.0
@@ -635,6 +681,8 @@
         d_up = (d_hidden * slope).astype(BF16)
         hidden[:, cols] = value
         d_upper[:, cols] = d_up
+        column = jnp.sum(d_up.astype(F32), axis=0, keepdims=True)
+        up_sum[:, cols] = jnp.where(first, 0.0, up_sum[:, cols]) + column
         back += matmul(d_up, up[:, cols], ((1,), (1,)))
         ahead += matmul(value, down[cols])
     d_norm[...] = back.astype(BF16)
@@ -650,26 +698,39 @@
         mlp_kernel,
         count,
         "mlp",
-        [shaped((count, n)) for n in (width, size, size, width, width, width)],
+        [shaped((count, n)) for n in (width, size, size, width, width, width)]
+        + [shaped((1, n), F32) for n in (size, width)],
         [row, row, row, row, col, col] + [whole(x.shape) for x in consts],
-        [tiled(TILE, n) for n in (width, size, size, width, width, width)],
+        [tiled(TILE, n) for n in (width, size, size, width, width, width)]
+        + [whole((1, n)) for n in (size, width)],
         [],
         8 * count * width * size,
         (tokens, mine, theirs, cotangent, ids, live) + consts,
     )
 
 
-def middle_kernel(
-    halves, tokens, mine, theirs, cotangent, d_own, d_other, context, ids, live, ids_row, *refs
-):
-    table, out_bias, weight, d_middle, d_context, d_weight, d_images, d_bias, sums, total = refs
-    first = pl.program_id(0) == 0
-    last = pl.program_id(0) == pl.num_programs(0) - 1
+def middle_kernel(halves, blocks, *refs):
+    tokens, cotangent, context, ids, live, ids_row, *refs = refs
+    parts = [refs[i * blocks : (i + 1) * blocks] for i in range(4)]
+    table, out_bias, weight, d_middle, d_context, d_weight, d_images, d_bias, sums, total = refs[
+        4 * blocks :
+    ]
+    tile = pl.program_id(0)
+    first = tile == 0
+    last = tile == pl.num_programs(0) - 1
+
+    def rows_at(refs):
+        rows = refs[0][...]
+        for i in range(1, blocks):
+            rows = jnp.where(tile >= i * (pl.num_programs(0) // blocks), refs[i][...], rows)
+        return rows.astype(F32)
+
+    mine, theirs, d_own, d_other = [rows_at(part) for part in parts]
     ids, live = ids[...], live[...]
     gate = live * pick(ids, table[0])
-    attn = mine[...].astype(F32) + theirs[...].astype(F32) + out_bias[...].astype(F32)
+    attn = mine + theirs + out_bias[...].astype(F32)
     xhat, rstd = norm(tokens[...].astype(F32) + gate * attn)
-    d_norm = d_own[...].astype(F32) + d_other[...].astype(F32)
+    d_norm = d_own + d_other
     grad = cotangent[...].astype(F32) + norm_back(d_norm * (1.0 + pick(ids, table[2])), xhat, rstd)
     d_middle[...] = grad
     d_attn = (gate * grad).astype(BF16)
@@ -686,16 +747,20 @@
         halves_out(sums, d_images, halves)
 
 
-def middle_back(
-    halves, tokens, mine, theirs, cotangent, d_own, d_other, context, ids, live, ids_row, table, out_bias, weight
-):
+def middle_back(halves, parts, tokens, cotangent, context, ids, live, ids_row, table, out_bias, weight):
     count, width = tokens.shape
     size = context.shape[1]
     images = table.shape[1]
+    blocks = len(parts[0])
+    tiles = count // TILE // blocks
     row, col = tiled(TILE, width), tiled(TILE, 1)
     consts = (table, out_bias, weight)
+
+    def block_spec(i):
+        return pl.BlockSpec((TILE, width), lambda t: (jnp.clip(t - i * tiles, 0, tiles - 1), 0))
+
     return token_call(
-        lambda *refs: middle_kernel(halves, *refs),
+        lambda *refs: middle_kernel(halves, blocks, *refs),
         count,
         "middle_back",
         [
@@ -705,8 +770,8 @@
             shaped((halves, 3, images, width // halves)),
             shaped((1, width), F32),
         ],
-        [row] * 6
-        + [tiled(TILE, size), col, col, pl.BlockSpec((1, TILE), lambda i: (0, i))]
+        [row, row, tiled(TILE, size), col, col, pl.BlockSpec((1, TILE), lambda i: (0, i))]
+        + [block_spec(i) for _ in parts for i in range(blocks)]
         + [whole(x.shape) for x in consts],
         [
             row,
@@ -717,87 +782,99 @@
         ],
         [pltpu.VMEM((3, images, width), F32), pltpu.VMEM((size, width), F32)],
         4 * count * width * size,
-        (tokens, mine, theirs, cotangent, d_own, d_other, context, ids, live, ids_row) + consts,
-    )
-
-
-def project_back_kernel(
-    halves, split, tokens, norm_one, d_q, d_own, rims, tail_start, ids_row, weight, *refs
-):
-    d_norm, top, bottom, d_images, d_bias, sums, total = refs
+        (tokens, cotangent, context, ids, live, ids_row) + tuple(sum(parts, [])) + consts,
+    )
+
+
+def project_back_kernel(halves, tokens, d_q, d_own, rims, tail_start, ids_row, weight, *refs):
+    d_norm, d_kv, d_images, sums = refs
     tile = pl.program_id(0)
-    first = tile == 0
-    last = tile == pl.num_programs(0) - 1
     span, size = rims.shape[2], d_q.shape[1]
     rows = lax.broadcasted_iota(jnp.int32, (TILE, span), 0) + tile * TILE
     cols = lax.broadcasted_iota(jnp.int32, (TILE, span), 1)
     head_rim = (rows == cols).astype(BF16)
     tail_rim = (rows == cols + tail_start[0]).astype(BF16)
-    parts = [d_q[...]]
+    back = matmul(d_q[...], weight[:size])
     for which in range(2):
         rim = matmul(head_rim, rims[0, which]) + matmul(tail_rim, rims[1, which])
-        parts.append((d_own[which].astype(F32) + rim).astype(BF16))
-    normed = norm_one[...]
-    back = 0.0
-    for i, part in enumerate(parts):
-        span_rows = slice(i * size, (i + 1) * size)
-        back += matmul(part, weight[span_rows])
-        grown = matmul(part, normed, ((0,), (0,)))
-        total[span_rows] = jnp.where(first, 0.0, total[span_rows]) + grown
+        part = (d_own[which].astype(F32) + rim).astype(BF16)
+        d_kv[which] = part
+        back += matmul(part, weight[(which + 1) * size : (which + 2) * size])
     back = back.astype(BF16)
     d_norm[...] = back
-    for i, part in ((0, parts[0]), (1, parts[2])):
-        column = jnp.sum(part.astype(F32), axis=0, keepdims=True)
-        d_bias[i : i + 1] = jnp.where(first, 0.0, d_bias[i : i + 1]) + column
     xhat, _ = norm(tokens[...].astype(F32))
     back = back.astype(F32)
-    gather_images(ids_row[...], (back, back * xhat), sums, first)
-
-    @pl.when(last)
+    gather_images(ids_row[...], (back, back * xhat), sums, tile == 0)
+
+    @pl.when(tile == pl.num_programs(0) - 1)
     def _():
-        top[...] = total[:split].astype(BF16)
-        bottom[...] = total[split:].astype(BF16)
-        halves_out(sums, d_images, halves)
-
-
-def project_back(
-    halves, split, images, tokens, norm_one, d_q, d_own, rims, tail_start, ids_row, weight
-):
+        part = sums.shape[2] // halves
+        for half in range(halves):
+            cut = slice(half * part, (half + 1) * part)
+            both = jnp.concatenate([sums[0, :, cut], sums[1, :, cut]], axis=1)
+            d_images[half] = both.astype(BF16)
+
+
+def project_back(halves, images, tokens, d_q, d_own, rims, tail_start, ids_row, weight):
     count, width = tokens.shape
     size = d_q.shape[1]
     row = tiled(TILE, width)
-    rest = 3 * size - split
+    pair = pl.BlockSpec((2, TILE, size), lambda i: (0, i, 0))
+    sums = (halves, images, 2 * width // halves)
     return token_call(
-        lambda *refs: project_back_kernel(halves, split, *refs),
+        lambda *refs: project_back_kernel(halves, *refs),
         count,
         "project_back",
-        [
-            shaped((count, width)),
-            shaped((split, width)),
-            shaped((rest, width)),
-            shaped((halves, 2, images, width // halves)),
-            shaped((2, size), F32),
-        ],
+        [shaped((count, width)), shaped((2, count, size)), shaped(sums)],
         [
             row,
-            row,
             tiled(TILE, size),
-            pl.BlockSpec((2, TILE, size), lambda i: (0, i, 0)),
+            pair,
             whole(rims.shape),
             pl.BlockSpec(memory_space=pltpu.SMEM),
             pl.BlockSpec((1, TILE), lambda i: (0, i)),
             whole(weight.shape),
         ],
-        [
-            row,
-            whole((split, width)),
-            whole((rest, width)),
-            whole((halves, 2, images, width // halves)),
-            whole((2, size)),
-        ],
-        [pltpu.VMEM((2, images, width), F32), pltpu.VMEM((3 * size, width), F32)],
-        12 * count * width * size,
-        (tokens, norm_one, d_q, d_own, rims, tail_start, ids_row, weight),
+        [row, pair, whole(sums)],
+        [pltpu.VMEM((2, images, width), F32)],
+        6 * count * width * size,
+        (tokens, d_q, d_own, rims, tail_start, ids_row, weight),
+    )
+
+
+def qkv_grads_kernel(split, norm_one, d_q, d_kv, top, bottom, d_bias, total):
+    tile = pl.program_id(0)
+    first = tile == 0
+    size = d_q.shape[1]
+    parts = [d_q[...], d_kv[0], d_kv[1]]
+    normed = norm_one[...]
+    for i, part in enumerate(parts):
+        rows = slice(i * size, (i + 1) * size)
+        total[rows] = jnp.where(first, 0.0, total[rows]) + matmul(part, normed, ((0,), (0,)))
+    for i, part in ((0, parts[0]), (1, parts[2])):
+        column = jnp.sum(part.astype(F32), axis=0, keepdims=True)
+        d_bias[i : i + 1] = jnp.where(first, 0.0, d_bias[i : i + 1]) + column
+
+    @pl.when(tile == pl.num_programs(0) - 1)
+    def _():
+        top[...] = total[:split].astype(BF16)
+        bottom[...] = total[split:].astype(BF16)
+
+
+def qkv_grads(split, norm_one, d_q, d_kv):
+    count, width = norm_one.shape
+    size = d_q.shape[1]
+    shapes = [(split, width), (3 * size - split, width), (2, size)]
+    return token_call(
+        lambda *refs: qkv_grads_kernel(split, *refs),
+        count,
+        "qkv_grads",
+        [shaped(shapes[0]), shaped(shapes[1]), shaped(shapes[2], F32)],
+        [tiled(TILE, width), tiled(TILE, size), pl.BlockSpec((2, TILE, size), lambda i: (0, i, 0))],
+        [whole(shape) for shape in shapes],
+        [pltpu.VMEM((3 * size, width), F32)],
+        6 * count * width * size,
+        (norm_one, d_q, d_kv),
     )
 
 
@@ -911,33 +988,48 @@
             )
         )
         d_others.append(narrow_other(mlp_outs[i][4]))
-    norm_two, hidden, d_upper, d_branch, d_norm, branch_part = [
-        jnp.concatenate(parts, axis=0) for parts in zip(*mlp_outs)
+    norm_two, hidden, d_upper, d_branch = [
+        jnp.concatenate(parts, axis=0) for parts in list(zip(*mlp_outs))[:4]
     ]
+    d_norms = [outs[4] for outs in mlp_outs]
+    branch_parts = [outs[5] for outs in mlp_outs]
+    up_sum, down_sum = [sum(outs[i] for outs in mlp_outs)[0] for i in (6, 7)]
     up_grad = dot(d_upper, norm_two, ((0,), (0,)), BF16)
     down_grad = dot(hidden, d_branch, ((0,), (0,)), BF16)
-    up_grad, down_grad = lax.psum((up_grad, down_grad), "wide")
-    attn_part, attn_other, d_other = [
-        jnp.concatenate(parts, axis=0) for parts in (attn_parts, attn_others, d_others)
-    ]
-    branch = narrow_scatter(branch_part) + down_bias.astype(F32)
-
-    def image_sum(hot, term):
-        return dot(hot, term.astype(BF16), ((0,), (0,)))
-
+    halved = narrow_count == 2 and blocks == 2 and share == block
+
+    def own_of(parts, index):
+        if halved:
+            return jnp.where(index == 0, parts[0], parts[1])
+        return lax.dynamic_slice_in_dim(jnp.concatenate(parts, axis=0), index * share, share)
+
+    if halved:
+        branch_other = swap(own_of(branch_parts, 1 - narrow_index))
+    if ring_fits([up_grad]):
+        mine = ring_scatter([up_grad, down_grad], 1)
+        mine, d_others = lax.optimization_barrier((mine, d_others))
+        up_grad, down_grad = [
+            lax.all_gather(mine[lane], "wide", axis=0, tiled=True) for lane in range(2)
+        ]
+    else:
+        up_grad, down_grad = lax.psum((up_grad, down_grad), "wide")
+    if halved:
+        branch = own_of(branch_parts, narrow_index).astype(F32) + branch_other.astype(F32)
+    else:
+        branch = narrow_scatter(jnp.concatenate(branch_parts, axis=0))
+    branch = branch + down_bias.astype(F32)
     first_bias = jnp.where(narrow_index == 0, down_bias.astype(F32), 0.0)
-    d_gate_two = image_sum(
-        onehot_full, live * cotangent.astype(F32) * (branch_part.astype(F32) + first_bias)
-    )
+    d_gate_two = 0.0
+    for i in range(blocks):
+        term = rows_of(live, i) * rows_of(cotangent, i).astype(F32)
+        term = term * (branch_parts[i].astype(F32) + first_bias)
+        d_gate_two += dot(rows_of(onehot_full, i), term.astype(BF16), ((0,), (0,)))
     d_gate_two = narrow_scatter(d_gate_two.astype(BF16), 1)
     d_middle, d_context, out_weight_grad, images_two, out_bias_sum = middle_back(
         narrow_count,
+        [attn_parts, attn_others, d_norms, d_others],
         tok_full,
-        attn_part,
-        attn_other,
         cotangent,
-        d_norm,
-        d_other,
         context,
         ids_col,
         live,
@@ -960,19 +1052,10 @@
     rims = jnp.stack([to_right(d_rim[1]), to_left(d_rim[0])])
     lane_rows = (4 * part_width * width + 6 * img_row * mod_width) // (2 * width)
     split = min(lane_rows, 3 * part_width - 16)
-    d_norm_part, top, bottom, images_one, qv_sums = project_back(
-        narrow_count,
-        split,
-        img_row,
-        tok_full,
-        norm_one,
-        d_queries,
-        d_own,
-        rims,
-        tail_start[None],
-        ids_row,
-        flat_qkv,
-    )
+    d_norm_part, d_kv, images_one = project_back(
+        narrow_count, img_row, tok_full, d_queries, d_own, rims, tail_start[None], ids_row, flat_qkv
+    )
+    top, bottom, qv_sums = qkv_grads(split, norm_one, d_queries, d_kv)
 
     def mine_of(images):
         return lax.dynamic_index_in_dim(images, narrow_index, 0, keepdims=False)
@@ -984,17 +1067,17 @@
         early = mine_of(lax.psum(images_one, "narrow"))
     images_two = mine_of(images_two)
     loose_parts = [
-        jnp.sum(d_upper.astype(F32), axis=0),
-        jnp.sum(d_branch.astype(F32), axis=0),
+        up_sum,
+        down_sum,
         qv_sums[0],
         qv_sums[1],
         out_bias_sum[0],
     ]
     loose = jnp.concatenate(loose_parts)
     loose = jnp.pad(loose, (0, (-loose.shape[0]) % (8 * width))).reshape(-1, width)
-    terms = [early[0], early[1], images_two[0], images_two[1], images_two[2], d_gate_two]
-    terms = [term.astype(BF16) for term in terms]
-    d_mod = [jnp.concatenate(terms[2 * i : 2 * i + 2], axis=1) for i in range(3)]
+    terms = [images_two[0], images_two[1], images_two[2], d_gate_two.astype(BF16)]
+    d_mod = [early.astype(BF16)]
+    d_mod += [jnp.concatenate(terms[2 * i : 2 * i + 2], axis=1) for i in range(2)]
     if 2 * mod_width == width:
         d_mod_flat = jnp.concatenate(d_mod, axis=0)
     else:
@@ -1012,7 +1095,8 @@
     hot_own = own(onehot_full)
     scale_one = dot(hot_own, table_one[1], ((1,), (0,)))
     tokens_grad = own(d_middle) + norm_back(d_norm_one * (1.0 + scale_one), xhat_one, rstd_one)
-    attn_own = own(attn_part).astype(F32) + own(attn_other).astype(F32) + out_bias.astype(F32)
+    attn_own = sum(own_of(parts, narrow_index).astype(F32) for parts in (attn_parts, attn_others))
+    attn_own = attn_own + out_bias.astype(F32)
     live_own = own(live)
     gates = [dot(hot_own, table_two[j], ((1,), (0,))) for j in (0, 3)]
     layer_out = (tok_own + live_own * (gates[0] * attn_own + gates[1] * branch)).astype(BF16)

time: 573 us -> 569 us (level)
  waiting for transfers between devices: 17.7 us -> 35.6 us
  local copies, waits for them, and re-layouts: 91.9 us -> 78.2 us
  other arithmetic: 60.8 us -> 54.1 us
    ppermute x11, waiting for transfers between devices: 17.7 us -> 35.6 us  [swap(): return lax.ppermute(part, 'narrow', [(0, 1), (1, 0)])]
    concatenate x3 -> x0, other arithmetic: 9.81 us -> none  [body(): jnp.concatenate(parts, axis=0)]
    unnamed x127 -> x115, local copies, waits for them, and re-layouts: 29.7 us -> 22.7 us
    ppermute x2, starting transfers between devices: 10 us -> 3.49 us  [to_right(): lax.ppermute(rows, 'wide', [(i, i + 1) for i in range(wide_count - 1)])]
    convert_element_type x3 -> x4, other arithmetic: 2.5 us -> 8.23 us  [the longest x1 7.32 us: body(): up_weight_grad = up_grad.T.astype(F32)]
    pallas_call x5 -> x6, Pallas kernels: 108 us -> 111 us  [token_call(): pl.pallas_call(kernel, grid=(tokens // TILE,), out_shape=out_shape, in_sp...]
    dot_general x13 -> x14, matrix products: 47.9 us -> 49 us  [dot(): lax.dot_general(left, right, (dims, ((), ())), preferred_element_type=F32)]
    pallas_call x1 -> x2, Pallas kernels: 146 us -> 147 us  [the longest x1 86.4 us: ring_sum(): pl.pallas_call(lambda *refs: ring_kernel(chips, subs, True, *refs), out_s...]
  transfers between devices with their start and end apart: 16 -> 17, of which waited for: 2 -> 4; matrix products, arithmetic and copies ran while one was open for 30% -> 30% of each run, Pallas kernels for 52% -> 51%
where the time goes in v7:
time: 569 us; the launch traced here: 560 us
  Pallas kernels  297 us (52%)
  local copies, waits for them, and re-layouts  78.2 us (14%)
  matrix products  57.4 us (10%)
  other arithmetic  54.1 us (10%)
  waiting for transfers between devices  35.6 us (6%)
  starting transfers between devices  20.8 us (4%)
  between operations  17.1 us (3%)
    pallas_call x6, Pallas kernels, token_call(): pl.pallas_call(kernel, grid=(tokens // TILE,), out_shape=out_shape, in_sp...  111 us
    pallas_call x1, Pallas kernels, ring_sum(): pl.pallas_call(lambda *refs: ring_kernel(chips, subs, True, *refs), out_s...  86.4 us
    pallas_call x1, Pallas kernels, ring_scatter(): pl.pallas_call(lambda *refs: ring_kernel(chips, shard // UNIT, False, *re...  60.5 us
    dot_general x14, matrix products, dot(): lax.dot_general(left, right, (dims, ((), ())), preferred_element_type=F32)  49 us
    ppermute x11, waiting for transfers between devices, swap(): return lax.ppermute(part, 'narrow', [(0, 1), (1, 0)])  35.6 us
    pallas_call x1, Pallas kernels, attention_backward(): pl.pallas_call(lambda *refs: backward_kernel(tiles, *refs), grid=(tiles,)...  26.4 us
    unnamed x115, local copies, waits for them, and re-layouts  22.7 us
    ppermute x11, starting transfers between devices, swap(): return lax.ppermute(part, 'narrow', [(0, 1), (1, 0)])  14.1 us
  transfers between devices with their start and end apart: 17, of which 4 were waited for; matrix products, arithmetic and copies ran while one was open for 30% of the time, Pallas kernels for 51%

profile of v7, /device:TPU:0, one launch (start us, length us, event | category | flops | bytes accessed | tf_op | source)
XLA Modules:
  0.0 560.0 jit_solution(6858381593037513903)
XLA Ops:
  11.0 5.2 fusion.72
  19.2 5.3 slice.225
  33.0 5.4 fusion.6
  41.7 7.4 %collective-permute-done.2 = bf16[576,256,2]{1,0,2:T(8,128)(2,1)S(1)} collective-permute-done((bf16[576,256,2]{1,0,2:T(8,128)(2,1)S(1)}, bf16[576,256,2]{1,0,2:T(8,128)(2,1)S(1)}, u32[]{:S(2)}, u32[]{:S(2)}) %collective-permute-start.2) | collective-permute-done | bytes 589856 | tf_op jit(solution)/shard_map/ppermute | solution.py:21
  55.2 12.8 %project.1 = (bf16[1024,576]{1,0:T(8,128)(2,1)}, bf16[1024,576]{1,0:T(8,128)(2,1)}, bf16[1024,576]{1,0:T(8,128)(2,1)}, bf16[1024,1152]{1,0:T(8,128)(2,1)}) custom-call(bf16[1024,1152]{1,0:T(8,128)(2,1)} %maximum_select_fusion.tokens.refs_0_, s32[1024,1]{1,0:T(8,128)} %copy.54.ids.refs_3_, bf16[2,256,1152]{2,1,0:T(8,128)(2,1)} %fusion.36.table, ...), custom_call_target="tpu_custom_call" | custom-call | flops 4076863488 | bytes 11289984 | tf_op jit(solution)/shard_map/project/pallas_call | solution.py:610
  82.3 12.1 %attention_forward.1 = (bf16[1024,576]{1,0:T(8,128)(2,1)S(1)}, f32[8,1024]{1,0:T(8,128)S(1)}) custom-call(bf16[1024,576]{1,0:T(8,128)(2,1)S(1)} %copy-done.10, bf16[1024,576]{1,0:T(8,128)(2,1)S(1)} %copy-done.6, bf16[1024,576]{1,0:T(8,128)(2,1)S(1)} %copy-done.7, bf16[2,128,576]{2,1,0:T(8,128)(2,1)} %collective-permute-done.3.refs_3_, ...), custom_call_target="tpu_custom_call" | custom-call | flops 1207959552 | bytes 4718592 | tf_op jit(solution)/shard_map/attention_forward/pallas_call | solution.py:413
  109.4 5.2 fusion.23.table.refs_14_
  114.6 17.7 %collective-permute-done.6.theirs.refs_9_ = bf16[512,1152]{1,0:T(8,128)(2,1)} collective-permute-done((bf16[512,1152]{1,0:T(8,128)(2,1)}, bf16[512,1152]{1,0:T(8,128)(2,1)}, u32[]{:S(2)}, u32[]{:S(2)}) %collective-permute-start.6) | collective-permute-done | bytes 1179680 | tf_op jit(solution)/shard_map/ppermute | solution.py:21
  132.2 27.2 %mlp.3 = (bf16[512,1152]{1,0:T(8,128)(2,1)}, bf16[512,2304]{1,0:T(8,128)(2,1)}, bf16[512,2304]{1,0:T(8,128)(2,1)}, bf16[512,1152]{1,0:T(8,128)(2,1)}, bf16[512,1...) custom-call(bf16[512,1152]{1,0:T(8,128)(2,1)} %get-tuple-element.181.tokens, ...), custom_call_target="tpu_custom_call" | custom-call | flops 10871635968 | bytes 26558592 | tf_op jit(solution)/shard_map/mlp/pallas_call | solution.py:610
  161.5 27.0 %mlp.2 = (bf16[512,1152]{1,0:T(8,128)(2,1)}, bf16[512,2304]{1,0:T(8,128)(2,1)}, bf16[512,2304]{1,0:T(8,128)(2,1)}, bf16[512,1152]{1,0:T(8,128)(2,1)}, bf16[512,1...) custom-call(bf16[512,1152]{1,0:T(8,128)(2,1)} %get-tuple-element.180.tokens, ...), custom_call_target="tpu_custom_call" | custom-call | flops 10871635968 | bytes 26558592 | tf_op jit(solution)/shard_map/mlp/pallas_call | solution.py:610
  188.7 9.3 %convolution_convert_fusion.1 = bf16[2304,1152]{1,0:T(8,128)(2,1)S(1)} fusion(bf16[512,2304]{1,0:T(8,128)(2,1)} %get-tuple-element.68, bf16[512,2304]{1,0:T(8,128)(2,1)} %get-tuple-element.67, bf16[512,1152]{1,0:T(8,128)(2,1)} %get-tuple-element.70, bf16[512,1152]{1,0:T(8,128)(2,1)} %get-tuple-element.69), kind=kOutput, calls=%fused_computation.1 | convolution fusion | flops 5452627968 | bytes 12386304 | tf_op jit(solution)/shard_map/dot_general | solution.py:17
  198.1 6.7 %convolution_convert_fusion = bf16[2304,1152]{1,0:T(8,128)(2,1)S(1)} fusion(bf16[512,2304]{1,0:T(8,128)(2,1)S(1)} %copy-done.50, bf16[512,2304]{1,0:T(8,128)(2,1)S(1)} %copy-done.51, bf16[512,1152]{1,0:T(8,128)(2,1)S(1)} %copy-done.52, bf16[512,1152]{1,0:T(8,128)(2,1)S(1)} %copy-done.53), kind=kOutput, calls=%fused_computation | convolution fusion | flops 5452627968 | bytes 12386304 | tf_op jit(solution)/shard_map/dot_general | solution.py:17
  204.8 60.5 %ring_scatter.1 = bf16[2,144,1152]{2,1,0:T(8,128)(2,1)S(1)} custom-call(bf16[8,2,144,1152]{3,2,1,0:T(8,128)(2,1)S(1)} %bitcast.100, bf16[8,2,144,1152]{3,2,1,0:T(8,128)(2,1)S(1)} %bitcast.101), custom_call_target="tpu_custom_call" | custom-call | tf_op jit(solution)/shard_map/ring_scatter/pallas_call | solution.py:278
  279.5 6.8 %collective-permute-done.13 = bf16[256,576]{1,0:T(8,128)(2,1)S(1)} collective-permute-done((bf16[256,576]{1,0:T(8,128)(2,1)S(1)}, bf16[256,576]{1,0:T(8,128)(2,1)S(1)}, u32[]{:S(2)}, u32[]{:S(2)}) %collective-permute-start.13) | collective-permute-done | bytes 294944 | tf_op jit(solution)/shard_map/ppermute | solution.py:21
  287.1 19.0 %middle_back.1 = (f32[1024,1152]{1,0:T(8,128)}, bf16[1024,576]{1,0:T(8,128)(2,1)}, bf16[576,1152]{1,0:T(8,128)(2,1)}, bf16[2,3,256,576]{3,2,1,0:T(8,128)(2,1)}, f32[1,1152]{1,0:T(1,128)}) custom-call(bf16[1024,1152]{1,0:T(8,128)(2,1)} %maximum_select_fusion.tokens.refs_0_, bf16[1024,1152]{1,0:T(8,128)(2,1)} %refs_1_.1, bf16[1024,576]{1,0:T(8,128)(2,1)} %copy-done.3, ...), custom_call_target="tpu_custom_call" | custom-call | flops 2717908992 | bytes 28554624 | tf_op jit(solution)/shard_map/middle_back/pallas_call | solution.py:610
  306.2 26.4 %attention_backward.1 = (bf16[1024,576]{1,0:T(8,128)(2,1)S(1)}, bf16[2,1024,576]{2,1,0:T(8,128)(2,1)}, bf16[2,2,128,576]{3,2,1,0:T(8,128)(2,1)S(1)}) custom-call(bf16[1024,576]{1,0:T(8,128)(2,1)S(1)} %copy-done.11, bf16[1024,576]{1,0:T(8,128)(2,1)S(1)} %copy-done.6, bf16[1024,576]{1,0:T(8,128)(2,1)} %get-tuple-element.61.refs_2_, ...), custom_call_target="tpu_custom_call" | custom-call | flops 3019898880 | bytes 9437184 | tf_op jit(solution)/shard_map/attention_backward/pallas_call | solution.py:514
  336.4 6.5 %fusion.22 = bf16[512,1152]{1,0:T(8,128)(2,1)} fusion(bf16[512,1152]{1,0:T(8,128)(2,1)} %param.15, bf16[512,1152]{1,0:T(8,128)(2,1)} %collective-permute-done.7, f32[512,1152]{1,0:T(8,128)} %fusion.50, f32[1152]{0:T(1024)S(1)} %convert_element_type.152, bf16[512,1152]{1,0:T(8,128)(2,1)} %get-tuple-element.63, bf16[512,1152]{1,0:T(8,128)(2,1)} %get-tuple-element.64, ...), kind=kOutput, calls=%fused_computation.39 | convolution fusion | flops 312606720 | bytes 13708293 | tf_op jit(solution)/shard_map/dot_general | solution.py:17
  345.5 15.4 %project_back.1 = (bf16[1024,1152]{1,0:T(8,128)(2,1)}, bf16[2,1024,576]{2,1,0:T(8,128)(2,1)}, bf16[2,256,1152]{2,1,0:T(8,128)(2,1)}) custom-call(bf16[1024,1152]{1,0:T(8,128)(2,1)} %maximum_select_fusion.tokens.refs_0_, bf16[1024,576]{1,0:T(8,128)(2,1)} %copy-done.12, bf16[2,1024,576]{2,1,0:T(8,128)(2,1)} %get-tuple-element.81.refs_2_, ...), custom_call_target="tpu_custom_call" | custom-call | flops 4076863488 | bytes 15710214 | tf_op jit(solution)/shard_map/project_back/pallas_call | solution.py:610
  364.2 10.0 %qkv_grads.1 = (bf16[1536,1152]{1,0:T(8,128)(2,1)}, bf16[192,1152]{1,0:T(8,128)(2,1)}, f32[2,576]{1,0:T(2,128)}) custom-call(bf16[1024,1152]{1,0:T(8,128)(2,1)} %get-tuple-element.84.refs_0_, bf16[1024,576]{1,0:T(8,128)(2,1)} %copy-done.12, bf16[2,1024,576]{2,1,0:T(8,128)(2,1)} %get-tuple-element.85.refs_2_), custom_call_target="tpu_custom_call" | custom-call | flops 4076863488 | bytes 8847360 | tf_op jit(solution)/shard_map/qkv_grads/pallas_call | solution.py:610
  385.4 86.4 %ring_sum.1 = (bf16[2,8,2,96,1152]{4,3,2,1,0:T(8,128)(2,1)}, bf16[512,1152]{1,0:T(8,128)(2,1)S(1)}, f32[8,1152]{1,0:T(8,128)S(1)}) custom-call(bf16[8,2,96,1152]{3,2,1,0:T(8,128)(2,1)S(1)} %bitcast.103, bf16[8,2,96,1152]{3,2,1,0:T(8,128)(2,1)S(1)} %bitcast.102, bf16[1024,1152]{1,0:T(8,128)(2,1)S(1)} %copy-done.1, f32[8,1152]{1,0:T(8,128)S(1)} %copy-done.4), custom_call_target="tpu_custom_call" | custom-call | tf_op jit(solution)/shard_map/ring_sum/pallas_call | solution.py:298
  505.0 8.4 %fusion.51 = f32[1152,6,576]{0,2,1:T(8,128)} fusion(bf16[6,576,256]{2,1,0:T(8,128)(2,1)S(1)} %bitcast.114, bf16[256,1152]{1,0:T(8,128)(2,1)S(1)} %copy-done.34), kind=kOutput, calls=%fused_computation.88 | convolution fusion | flops 2040201216 | bytes 18284544 | tf_op jit(solution)/shard_map/dot_general | solution.py:1122
  525.5 7.3 %convert_bitcast_fusion = f32[1152,2304]{0,1:T(8,128)} fusion(bf16[1,2304,1152]{2,1,0:T(8,128)(2,1)} %all-gather.5.cloned.1.call-done), kind=kLoop, calls=%fused_computation.2 | loop fusion | flops 2654208 | bytes 15925248 | tf_op jit(solution)/shard_map/convert_element_type | solution.py:1103
  532.8 12.7 %copy.63 = f32[1152,2304]{1,0:T(8,128)} copy(f32[1152,2304]{0,1:T(8,128)} %convert_bitcast_fusion) | data formatting | bytes 21233664
  545.5 7.3 %bitcast_convert_fusion = f32[2304,1152]{1,0:T(8,128)} fusion(bf16[1,2304,1152]{2,1,0:T(8,128)(2,1)} %all-gather.7.cloned.1.call-done), kind=kLoop, calls=%fused_computation.4 | loop fusion | flops 2654208 | bytes 15925248 | tf_op jit(solution)/shard_map/convert_element_type | solution.py:1104
  (238 shorter events, 135.1 us)
Async XLA Ops:
  7.2 518.3 %all-gather.5.cloned.1.call-start = ((), (), s32[]{:S(2)}) async-start(), calls=%async_computation | async-start | bytes 5640192 | tf_op jit(solution)/shard_map/all_gather | solution.py:1012
  7.2 44.1 %collective-permute-start = (bf16[512,1152]{1,0:T(8,128)(2,1)}, bf16[512,1152]{1,0:T(8,128)(2,1)}, u32[]{:S(2)}, u32[]{:S(2)}) collective-permute-start(bf16[512,1152]{1,0:T(8,128)(2,1)} %param.15), channel_id=1, source_target_pairs={{0,1},{1,0},{2,3},{3,2},{4,5},{5,4},{6,7},{7,6},{8,9},{9,8},{10,11... | collective-permute-start | bytes 3538952 | tf_op jit(solution)/shard_map/ppermute | solution.py:21
  19.1 30.0 %collective-permute-start.2 = (bf16[576,256,2]{1,0,2:T(8,128)(2,1)S(1)}, bf16[576,256,2]{1,0,2:T(8,128)(2,1)S(1)}, u32[]{:S(2)}, u32[]{:S(2)}) collective-permute-start(bf16[576,256,2]{1,0,2:T(8,128)(2,1)S(1)} %bitcast.127), channel_id=1, source_target_pairs={{0,1},{1,0},{2,3},{3,2},{4,5},{5,4},{6,7},{7,6},{8,9},{9,8},{10,11... | collective-permute-start | bytes 1769480 | tf_op jit(solution)/shard_map/ppermute | solution.py:21
  28.7 241.2 %copy-start.37 = (s32[1024]{0:T(1024)}, s32[1024]{0:T(1024)S(1)}, u32[]{:S(2)}) copy-start(s32[1024]{0:T(1024)S(1)} %get-tuple-element.147) | copy-start | bytes 12292
  69.3 11.7 %copy-start.6 = (bf16[1024,576]{1,0:T(8,128)(2,1)S(1)}, bf16[1024,576]{1,0:T(8,128)(2,1)}, u32[]{:S(2)}) copy-start(bf16[1024,576]{1,0:T(8,128)(2,1)} %get-tuple-element.60.refs_1_) | copy-start | bytes 3538948
  69.3 11.7 %copy-start.7 = (bf16[1024,576]{1,0:T(8,128)(2,1)S(1)}, bf16[1024,576]{1,0:T(8,128)(2,1)}, u32[]{:S(2)}) copy-start(bf16[1024,576]{1,0:T(8,128)(2,1)} %get-tuple-element.61.refs_2_) | copy-start | bytes 3538948
  69.3 11.6 %collective-permute-start.3 = (bf16[2,128,576]{2,1,0:T(8,128)(2,1)S(1)}, bf16[2,128,576]{2,1,0:T(8,128)(2,1)}, u32[]{:S(2)}, u32[]{:S(2)}) collective-permute-start(bf16[2,128,576]{2,1,0:T(8,128)(2,1)S(1)} %pad_maximum_fusion.1), channel_id=1, source_target_pairs={{0,2},{2,4},{4,6},{6,8},{8,10},{10,12},{12,14},{14,16},{16,18},{18... | collective-permute-start | bytes 884744 | tf_op jit(solution)/shard_map/ppermute | solution.py:945
  72.3 8.7 %collective-permute-start.4 = (bf16[2,128,576]{2,1,0:T(8,128)(2,1)}, bf16[2,128,576]{2,1,0:T(8,128)(2,1)}, u32[]{:S(2)}, u32[]{:S(2)}) collective-permute-start(bf16[2,128,576]{2,1,0:T(8,128)(2,1)} %pad_maximum_fusion.2), channel_id=1, source_target_pairs={{2,0},{4,2},{6,4},{8,6},{10,8},{12,10},{14,12},{16,14},{18,16},{20... | collective-permute-start | bytes 884744 | tf_op jit(solution)/shard_map/ppermute | solution.py:948
  79.2 27.7 %collective-permute-start.1 = (bf16[576,256,4]{1,0,2:T(8,128)(2,1)}, bf16[576,256,4]{1,0,2:T(8,128)(2,1)}, u32[]{:S(2)}, u32[]{:S(2)}) collective-permute-start(bf16[576,256,4]{1,0,2:T(8,128)(2,1)} %copy.46), channel_id=1, source_target_pairs={{0,1},{1,0},{2,3},{3,2},{4,5},{5,4},{6,7},{7,6},{8,9},{9,8},{10,11... | collective-permute-start | bytes 3538952 | tf_op jit(solution)/shard_map/ppermute | solution.py:21
  82.3 12.1 %copy-start.25 = (bf16[576,1152]{1,0:T(8,128)(2,1)S(1)}, bf16[576,1152]{1,0:T(8,128)(2,1)}, u32[]{:S(2)}) copy-start(bf16[576,1152]{1,0:T(8,128)(2,1)} %refs_16_.1) | copy-start | bytes 3981316
  82.3 14.6 %copy-start.21 = (bf16[1024,1152]{1,0:T(8,128)(2,1)S(1)}, bf16[1024,1152]{1,0:T(8,128)(2,1)}, u32[]{:S(2)}) copy-start(bf16[1024,1152]{1,0:T(8,128)(2,1)} %refs_1_.1) | copy-start | bytes 7077892
  96.6 35.7 %collective-permute-start.6 = (bf16[512,1152]{1,0:T(8,128)(2,1)}, bf16[512,1152]{1,0:T(8,128)(2,1)}, u32[]{:S(2)}, u32[]{:S(2)}) collective-permute-start(bf16[512,1152]{1,0:T(8,128)(2,1)} %convolution_convert_fusion.2.mine.refs_7_), channel_id=1, source_target_pairs={{0,1},{1,0},{2,3},{3,2},{4,5},{5,4},{6,7},{7,6},{8,9},{9,8},{10,11... | collective-permute-start | bytes 3538952 | tf_op jit(solution)/shard_map/ppermute | solution.py:21
  101.5 60.1 %collective-permute-start.5 = (bf16[512,1152]{1,0:T(8,128)(2,1)}, bf16[512,1152]{1,0:T(8,128)(2,1)}, u32[]{:S(2)}, u32[]{:S(2)}) collective-permute-start(bf16[512,1152]{1,0:T(8,128)(2,1)} %convolution_convert_fusion.3.mine.refs_6_), channel_id=1, source_target_pairs={{0,1},{1,0},{2,3},{3,2},{4,5},{5,4},{6,7},{7,6},{8,9},{9,8},{10,11... | collective-permute-start | bytes 3538952 | tf_op jit(solution)/shard_map/ppermute | solution.py:21
  159.5 105.8 %collective-permute-start.9 = (bf16[512,1152]{1,0:T(8,128)(2,1)}, bf16[512,1152]{1,0:T(8,128)(2,1)}, u32[]{:S(2)}, u32[]{:S(2)}) collective-permute-start(bf16[512,1152]{1,0:T(8,128)(2,1)} %get-tuple-element.66.refs_11_), channel_id=1, source_target_pairs={{0,1},{1,0},{2,3},{3,2},{4,5},{5,4},{6,7},{7,6},{8,9},{9,8},{10,11... | collective-permute-start | bytes 3538952 | tf_op jit(solution)/shard_map/ppermute | solution.py:21
  188.6 76.7 %collective-permute-start.8 = (bf16[512,1152]{1,0:T(8,128)(2,1)}, bf16[512,1152]{1,0:T(8,128)(2,1)S(1)}, u32[]{:S(2)}, u32[]{:S(2)}) collective-permute-start(bf16[512,1152]{1,0:T(8,128)(2,1)} %get-tuple-element.65.refs_10_), channel_id=1, source_target_pairs={{0,1},{1,0},{2,3},{3,2},{4,5},{5,4},{6,7},{7,6},{8,9},{9,8},{10,11... | collective-permute-start | bytes 3538952 | tf_op jit(solution)/shard_map/ppermute | solution.py:21
  266.5 278.9 %all-gather.7.cloned.1.call-start = ((), (), s32[]{:S(2)}) async-start(), calls=%async_computation.1 | async-start | bytes 5640192 | tf_op jit(solution)/shard_map/all_gather | solution.py:1012
  275.6 10.7 %collective-permute-start.13 = (bf16[256,576]{1,0:T(8,128)(2,1)S(1)}, bf16[256,576]{1,0:T(8,128)(2,1)S(1)}, u32[]{:S(2)}, u32[]{:S(2)}) collective-permute-start(bf16[256,576]{1,0:T(8,128)(2,1)S(1)} %constant_dynamic-slice_fusion), channel_id=1, source_target_pairs={{0,1},{1,0},{2,3},{3,2},{4,5},{5,4},{6,7},{7,6},{8,9},{9,8},{10,11... | collective-permute-start | bytes 884744 | tf_op jit(solution)/shard_map/ppermute | solution.py:21
  278.3 58.1 %collective-permute-start.7 = (bf16[512,1152]{1,0:T(8,128)(2,1)}, bf16[512,1152]{1,0:T(8,128)(2,1)}, u32[]{:S(2)}, u32[]{:S(2)}) collective-permute-start(bf16[512,1152]{1,0:T(8,128)(2,1)} %broadcast_select_fusion), channel_id=1, source_target_pairs={{0,1},{1,0},{2,3},{3,2},{4,5},{5,4},{6,7},{7,6},{8,9},{9,8},{10,11... | collective-permute-start | bytes 3538952 | tf_op jit(solution)/shard_map/ppermute | solution.py:21
  287.1 19.0 %copy-start.11 = (bf16[1024,576]{1,0:T(8,128)(2,1)S(1)}, bf16[1024,576]{1,0:T(8,128)(2,1)}, u32[]{:S(2)}) copy-start(bf16[1024,576]{1,0:T(8,128)(2,1)} %get-tuple-element.59.refs_0_) | copy-start | bytes 3538948
  306.2 30.2 %copy-start.48 = (f32[512]{0:T(512)S(1)}, f32[512]{0:T(512)}, u32[]{:S(2)}) copy-start(f32[512]{0:T(512)} %get-tuple-element.170) | copy-start | bytes 6148
  333.7 10.8 %collective-permute-start.10 = (bf16[2,128,576]{2,1,0:T(8,128)(2,1)S(1)}, bf16[2,128,576]{2,1,0:T(8,128)(2,1)S(1)}, u32[]{:S(2)}, u32[]{:S(2)}) collective-permute-start(bf16[2,128,576]{2,1,0:T(8,128)(2,1)S(1)} %get-tuple-element.164), channel_id=1, source_target_pairs={{0,2},{2,4},{4,6},{6,8},{8,10},{10,12},{12,14},{14,16},{16,18},{18... | collective-permute-start | bytes 884744 | tf_op jit(solution)/shard_map/ppermute | solution.py:945
  335.0 9.5 %collective-permute-start.11 = (bf16[2,128,576]{2,1,0:T(8,128)(2,1)S(1)}, bf16[2,128,576]{2,1,0:T(8,128)(2,1)S(1)}, u32[]{:S(2)}, u32[]{:S(2)}) collective-permute-start(bf16[2,128,576]{2,1,0:T(8,128)(2,1)S(1)} %get-tuple-element.165), channel_id=1, source_target_pairs={{2,0},{4,2},{6,4},{8,6},{10,8},{12,10},{14,12},{16,14},{18,16},{20... | collective-permute-start | bytes 884744 | tf_op jit(solution)/shard_map/ppermute | solution.py:948
  362.8 19.7 %collective-permute-start.12 = (bf16[256,1152]{1,0:T(8,128)(2,1)}, bf16[256,1152]{1,0:T(8,128)(2,1)}, u32[]{:S(2)}, u32[]{:S(2)}) collective-permute-start(bf16[256,1152]{1,0:T(8,128)(2,1)} %dynamic-slice_bitcast_fusion), channel_id=1, source_target_pairs={{0,1},{1,0},{2,3},{3,2},{4,5},{5,4},{6,7},{7,6},{8,9},{9,8},{10,11... | collective-permute-start | bytes 1769480 | tf_op jit(solution)/shard_map/ppermute | solution.py:21
  490.5 32.6 %collective-permute-start.14 = (bf16[256,1152]{1,0:T(8,128)(2,1)}, bf16[256,1152]{1,0:T(8,128)(2,1)}, u32[]{:S(2)}, u32[]{:S(2)}) collective-permute-start(bf16[256,1152]{1,0:T(8,128)(2,1)} %fusion.15), channel_id=1, source_target_pairs={{0,1},{1,0},{2,3},{3,2},{4,5},{5,4},{6,7},{7,6},{8,9},{9,8},{10,11... | collective-permute-start | bytes 1769480 | tf_op jit(solution)/shard_map/ppermute | solution.py:21
  (49 other events, 246.6 us)
Sparse Core Ops, SparseCore 0:
  266.7 56.6 all-gather.4
  336.5 60.2 all-gather.6

commit v8 on v7

--- a/solution.py
+++ b/solution.py
@@ -878,6 +878,50 @@
     )
 
 
+def turned(part):
+    rows, width = part.shape
+    step = 384 if rows % 384 == 0 else rows
+
+    def kernel(source, out):
+        out[...] = source[...].astype(F32).T
+
+    return pl.pallas_call(
+        kernel,
+        grid=(rows // step,),
+        out_shape=shaped((width, rows), F32),
+        in_specs=[tiled(step, width)],
+        out_specs=pl.BlockSpec((width, step), lambda i: (0, i)),
+        name="turned",
+    )(part)
+
+
+def widened(flat, counts):
+    width = flat.shape[1]
+    step = next(n for n in (192, 96, 48, 16) if all(count % n == 0 for count in counts))
+    starts = [sum(counts[:i]) // step for i in range(len(counts))]
+    tiles = [count // step for count in counts]
+
+    def spec(start, size):
+        return pl.BlockSpec((step, width), lambda i: (jnp.clip(i - start, 0, size - 1), 0))
+
+    def kernel(source, *outs):
+        tile = pl.program_id(0)
+        for out, start, size in zip(outs, starts, tiles):
+
+            @pl.when((tile >= start) & (tile < start + size))
+            def _():
+                out[...] = source[...].astype(F32)
+
+    return pl.pallas_call(
+        kernel,
+        grid=(sum(tiles),),
+        out_shape=[shaped((count, width), F32) for count in counts],
+        in_specs=[tiled(step, width)],
+        out_specs=[spec(*pair) for pair in zip(starts, tiles)],
+        name="widened",
+    )(flat)
+
+
 def body(
     tokens,
     condition,
@@ -1018,13 +1062,6 @@
     else:
         branch = narrow_scatter(jnp.concatenate(branch_parts, axis=0))
     branch = branch + down_bias.astype(F32)
-    first_bias = jnp.where(narrow_index == 0, down_bias.astype(F32), 0.0)
-    d_gate_two = 0.0
-    for i in range(blocks):
-        term = rows_of(live, i) * rows_of(cotangent, i).astype(F32)
-        term = term * (branch_parts[i].astype(F32) + first_bias)
-        d_gate_two += dot(rows_of(onehot_full, i), term.astype(BF16), ((0,), (0,)))
-    d_gate_two = narrow_scatter(d_gate_two.astype(BF16), 1)
     d_middle, d_context, out_weight_grad, images_two, out_bias_sum = middle_back(
         narrow_count,
         [attn_parts, attn_others, d_norms, d_others],
@@ -1038,6 +1075,14 @@
         out_row,
         out_weight,
     )
+    d_context, branch_parts = lax.optimization_barrier((d_context, branch_parts))
+    first_bias = jnp.where(narrow_index == 0, down_bias.astype(F32), 0.0)
+    d_gate_two = 0.0
+    for i in range(blocks):
+        term = rows_of(live, i) * rows_of(cotangent, i).astype(F32)
+        term = term * (branch_parts[i].astype(F32) + first_bias)
+        d_gate_two += dot(rows_of(onehot_full, i), term.astype(BF16), ((0,), (0,)))
+    d_gate_two = narrow_scatter(d_gate_two.astype(BF16), 1)
     d_queries, d_own, d_rim = attention_backward(
         queries,
         key_rows,
@@ -1066,15 +1111,10 @@
     else:
         early = mine_of(lax.psum(images_one, "narrow"))
     images_two = mine_of(images_two)
-    loose_parts = [
-        up_sum,
-        down_sum,
-        qv_sums[0],
-        qv_sums[1],
-        out_bias_sum[0],
-    ]
-    loose = jnp.concatenate(loose_parts)
-    loose = jnp.pad(loose, (0, (-loose.shape[0]) % (8 * width))).reshape(-1, width)
+    loose_parts = [up_sum, down_sum, qv_sums[0], qv_sums[1], out_bias_sum[0]]
+    longest = max(part.shape[0] for part in loose_parts)
+    loose = [jnp.pad(part[None], ((0, 0), (0, longest - part.shape[0]))) for part in loose_parts]
+    loose = jnp.concatenate(loose + [jnp.zeros((3, longest), F32)], axis=0)
     terms = [images_two[0], images_two[1], images_two[2], d_gate_two.astype(BF16)]
     d_mod = [early.astype(BF16)]
     d_mod += [jnp.concatenate(terms[2 * i : 2 * i + 2], axis=1) for i in range(2)]
@@ -1100,18 +1140,13 @@
     live_own = own(live)
     gates = [dot(hot_own, table_two[j], ((1,), (0,))) for j in (0, 3)]
     layer_out = (tok_own + live_own * (gates[0] * attn_own + gates[1] * branch)).astype(BF16)
-    up_weight_grad = up_grad.T.astype(F32)
+    up_weight_grad = turned(up_grad)
     down_weight_grad = down_grad.astype(F32)
     keep = 3 * part_width
-    qkv_flat = flat[:keep].astype(F32)
+    qkv_flat, out_weight_grad = widened(flat, (keep, part_width))
     qkv_weight_grad = jnp.transpose(qkv_flat.reshape(3, part_width, width), (2, 0, 1))
-    out_weight_grad = flat[keep : keep + part_width].astype(F32)
-    loose = loose.reshape(-1)
-    bounds = [0]
-    for part in loose_parts:
-        bounds.append(bounds[-1] + part.shape[0])
     up_bias_grad, down_bias_grad, query_bias, value_bias, out_bias_grad = [
-        loose[bounds[i] : bounds[i + 1]] for i in range(5)
+        loose[i, : part.shape[0]] for i, part in enumerate(loose_parts)
     ]
     qv_bias_grad = jnp.stack([query_bias, value_bias])
     d_mod_flat = flat[keep + part_width :]

time: 569 us -> 545 us (0.958)
  Pallas kernels: 297 us -> 323 us
  local copies, waits for them, and re-layouts: 78.2 us -> 54.3 us
  other arithmetic: 54.1 us -> 36.5 us
  waiting for transfers between devices: 35.6 us -> 29.2 us
    pallas_call x0 -> x2, Pallas kernels: none -> 18.2 us  [the longest x1 10.3 us: widened(): pl.pallas_call(kernel, grid=(sum(tiles),), out_shape=[shaped((count, widt...]
    unnamed x115 -> x104, local copies, waits for them, and re-layouts: 22.7 us -> 9.87 us
    convert_element_type x2 -> x0, other arithmetic: 10.3 us -> none  [the longest x1 7.32 us: body(): up_weight_grad = up_grad.T.astype(F32)]
    pallas_call x1, Pallas kernels: 86.4 us -> 94 us  [ring_sum(): pl.pallas_call(lambda *refs: ring_kernel(chips, subs, True, *refs), out_s...]
    ppermute x11, waiting for transfers between devices: 35.6 us -> 29.2 us  [swap(): return lax.ppermute(part, 'narrow', [(0, 1), (1, 0)])]
    reshape x3 -> x0, local copies, waits for them, and re-layouts: 6.38 us -> none  [the longest x1 4.23 us: body(): d_mod = d_mod_flat.reshape(3, img_row, width)]
  transfers between devices with their start and end apart: 17 -> 17, of which waited for: 4 -> 4; matrix products, arithmetic and copies ran while one was open for 30% -> 24% of each run, Pallas kernels for 51% -> 58%
where the time goes in v8:
time: 545 us; the launch traced here: 537 us
  Pallas kernels  323 us (59%)
  matrix products  56.5 us (10%)
  local copies, waits for them, and re-layouts  54.3 us (10%)
  other arithmetic  36.5 us (7%)
  waiting for transfers between devices  29.2 us (5%)
  starting transfers between devices  20.8 us (4%)
  between operations  17 us (3%)
    pallas_call x6, Pallas kernels, token_call(): pl.pallas_call(kernel, grid=(tokens // TILE,), out_shape=out_shape, in_sp...  111 us
    pallas_call x1, Pallas kernels, ring_sum(): pl.pallas_call(lambda *refs: ring_kernel(chips, subs, True, *refs), out_s...  94 us
    pallas_call x1, Pallas kernels, ring_scatter(): pl.pallas_call(lambda *refs: ring_kernel(chips, shard // UNIT, False, *re...  61.9 us
    dot_general x14, matrix products, dot(): lax.dot_general(left, right, (dims, ((), ())), preferred_element_type=F32)  48.1 us
    ppermute x11, waiting for transfers between devices, swap(): return lax.ppermute(part, 'narrow', [(0, 1), (1, 0)])  29.2 us
    pallas_call x1, Pallas kernels, attention_backward(): pl.pallas_call(lambda *refs: backward_kernel(tiles, *refs), grid=(tiles,)...  26.6 us
    ppermute x11, starting transfers between devices, swap(): return lax.ppermute(part, 'narrow', [(0, 1), (1, 0)])  13.9 us
  transfers between devices with their start and end apart: 17, of which 4 were waited for; matrix products, arithmetic and copies ran while one was open for 24% of the time, Pallas kernels for 58%

profile of v8, /device:TPU:0, one launch (start us, length us, event | category | flops | bytes accessed | tf_op | source)
XLA Modules:
  0.0 536.9 jit_solution(13534108139588643058)
XLA Ops:
  11.0 5.2 fusion.72
  19.2 5.3 slice.200
  33.3 5.4 %fusion.6 = bf16[256,2304]{1,0:T(8,128)(2,1)} fusion(bf16[2304,1152]{1,0:T(8,128)(2,1)} %bitcast.114, f32[2304]{0:T(1024)S(1)} %reshape.141, bf16[256,1152]{1,0:T(8,128)(2,1)S(1)} %copy-done.31), kind=kOutput, calls=%fused_computation.10 | convolution fusion | flops 1361903616 | bytes 7087104 | tf_op jit(solution)/shard_map/dot_general | solution.py:17
  42.0 7.1 %collective-permute-done.2 = bf16[576,256,2]{1,0,2:T(8,128)(2,1)S(1)} collective-permute-done((bf16[576,256,2]{1,0,2:T(8,128)(2,1)S(1)}, bf16[576,256,2]{1,0,2:T(8,128)(2,1)S(1)}, u32[]{:S(2)}, u32[]{:S(2)}) %collective-permute-start.2) | collective-permute-done | bytes 589856 | tf_op jit(solution)/shard_map/ppermute | solution.py:21
  51.3 3.9 maximum_select_fusion.tokens.refs_0_
  55.2 12.8 %project.1 = (bf16[1024,576]{1,0:T(8,128)(2,1)}, bf16[1024,576]{1,0:T(8,128)(2,1)}, bf16[1024,576]{1,0:T(8,128)(2,1)}, bf16[1024,1152]{1,0:T(8,128)(2,1)}) custom-call(bf16[1024,1152]{1,0:T(8,128)(2,1)} %maximum_select_fusion.tokens.refs_0_, s32[1024,1]{1,0:T(8,128)} %copy.52.ids.refs_3_, bf16[2,256,1152]{2,1,0:T(8,128)(2,1)} %fusion.36.table, ...), custom_call_target="tpu_custom_call" | custom-call | flops 4076863488 | bytes 11289984 | tf_op jit(solution)/shard_map/project/pallas_call | solution.py:610
  81.8 10.8 %attention_forward.1 = (bf16[1024,576]{1,0:T(8,128)(2,1)S(1)}, f32[8,1024]{1,0:T(8,128)S(1)}) custom-call(bf16[1024,576]{1,0:T(8,128)(2,1)S(1)} %copy-done.6, bf16[1024,576]{1,0:T(8,128)(2,1)S(1)} %copy-done.3, bf16[1024,576]{1,0:T(8,128)(2,1)S(1)} %copy-done.4, bf16[2,128,576]{2,1,0:T(8,128)(2,1)S(1)} %collective-permute-done.3.refs_3_, ...), custom_call_target="tpu_custom_call" | custom-call | flops 1207959552 | bytes 4718592 | tf_op jit(solution)/shard_map/attention_forward/pallas_call | solution.py:413
  106.8 5.4 fusion.23.table.refs_14_
  112.2 17.5 %collective-permute-done.6.theirs.refs_9_ = bf16[512,1152]{1,0:T(8,128)(2,1)} collective-permute-done((bf16[512,1152]{1,0:T(8,128)(2,1)}, bf16[512,1152]{1,0:T(8,128)(2,1)}, u32[]{:S(2)}, u32[]{:S(2)}) %collective-permute-start.6) | collective-permute-done | bytes 1179680 | tf_op jit(solution)/shard_map/ppermute | solution.py:21
  129.7 27.1 %mlp.3 = (bf16[512,1152]{1,0:T(8,128)(2,1)}, bf16[512,2304]{1,0:T(8,128)(2,1)}, bf16[512,2304]{1,0:T(8,128)(2,1)}, bf16[512,1152]{1,0:T(8,128)(2,1)}, bf16[512,1...) custom-call(bf16[512,1152]{1,0:T(8,128)(2,1)} %get-tuple-element.150.tokens, ...), custom_call_target="tpu_custom_call" | custom-call | flops 10871635968 | bytes 26558592 | tf_op jit(solution)/shard_map/mlp/pallas_call | solution.py:610
  158.8 27.3 %mlp.2 = (bf16[512,1152]{1,0:T(8,128)(2,1)}, bf16[512,2304]{1,0:T(8,128)(2,1)}, bf16[512,2304]{1,0:T(8,128)(2,1)}, bf16[512,1152]{1,0:T(8,128)(2,1)}, bf16[512,1...) custom-call(bf16[512,1152]{1,0:T(8,128)(2,1)} %get-tuple-element.149.tokens, ...), custom_call_target="tpu_custom_call" | custom-call | flops 10871635968 | bytes 26558592 | tf_op jit(solution)/shard_map/mlp/pallas_call | solution.py:610
  186.3 9.3 %convolution_convert_fusion.1 = bf16[2304,1152]{1,0:T(8,128)(2,1)S(1)} fusion(bf16[512,2304]{1,0:T(8,128)(2,1)} %get-tuple-element.73, bf16[512,2304]{1,0:T(8,128)(2,1)} %get-tuple-element.72, bf16[512,1152]{1,0:T(8,128)(2,1)} %get-tuple-element.75, bf16[512,1152]{1,0:T(8,128)(2,1)} %get-tuple-element.74), kind=kOutput, calls=%fused_computation.1 | convolution fusion | flops 5452627968 | bytes 12386304 | tf_op jit(solution)/shard_map/dot_general | solution.py:17
  195.6 6.7 %convolution_convert_fusion = bf16[2304,1152]{1,0:T(8,128)(2,1)S(1)} fusion(bf16[512,2304]{1,0:T(8,128)(2,1)S(1)} %copy-done.47, bf16[512,2304]{1,0:T(8,128)(2,1)S(1)} %copy-done.48, bf16[512,1152]{1,0:T(8,128)(2,1)S(1)} %copy-done.49, bf16[512,1152]{1,0:T(8,128)(2,1)S(1)} %copy-done.50), kind=kOutput, calls=%fused_computation | convolution fusion | flops 5452627968 | bytes 12386304 | tf_op jit(solution)/shard_map/dot_general | solution.py:17
  202.3 61.9 %ring_scatter.1 = bf16[2,144,1152]{2,1,0:T(8,128)(2,1)S(1)} custom-call(bf16[8,2,144,1152]{3,2,1,0:T(8,128)(2,1)S(1)} %bitcast.95, bf16[8,2,144,1152]{3,2,1,0:T(8,128)(2,1)S(1)} %bitcast.96), custom_call_target="tpu_custom_call" | custom-call | tf_op jit(solution)/shard_map/ring_scatter/pallas_call | solution.py:278
  275.7 19.0 %middle_back.1 = (f32[1024,1152]{1,0:T(8,128)}, bf16[1024,576]{1,0:T(8,128)(2,1)}, bf16[576,1152]{1,0:T(8,128)(2,1)}, bf16[2,3,256,576]{3,2,1,0:T(8,128)(2,1)}, f32[1,1152]{1,0:T(1,128)}) custom-call(bf16[1024,1152]{1,0:T(8,128)(2,1)} %maximum_select_fusion.tokens.refs_0_, bf16[1024,1152]{1,0:T(8,128)(2,1)} %refs_1_.1, bf16[1024,576]{1,0:T(8,128)(2,1)} %copy-done.2, ...), custom_call_target="tpu_custom_call" | custom-call | flops 2717908992 | bytes 28554624 | tf_op jit(solution)/shard_map/middle_back/pallas_call | solution.py:610
  296.1 26.6 %attention_backward.1 = (bf16[1024,576]{1,0:T(8,128)(2,1)S(1)}, bf16[2,1024,576]{2,1,0:T(8,128)(2,1)}, bf16[2,2,128,576]{3,2,1,0:T(8,128)(2,1)S(1)}) custom-call(bf16[1024,576]{1,0:T(8,128)(2,1)S(1)} %copy-done.7, bf16[1024,576]{1,0:T(8,128)(2,1)S(1)} %copy-done.3, bf16[1024,576]{1,0:T(8,128)(2,1)} %get-tuple-element.66.refs_2_, ...), custom_call_target="tpu_custom_call" | custom-call | flops 3019898880 | bytes 9437184 | tf_op jit(solution)/shard_map/attention_backward/pallas_call | solution.py:514
  330.0 5.3 fusion.22
  337.1 15.0 %project_back.1 = (bf16[1024,1152]{1,0:T(8,128)(2,1)}, bf16[2,1024,576]{2,1,0:T(8,128)(2,1)}, bf16[2,256,1152]{2,1,0:T(8,128)(2,1)}) custom-call(bf16[1024,1152]{1,0:T(8,128)(2,1)} %maximum_select_fusion.tokens.refs_0_, bf16[1024,576]{1,0:T(8,128)(2,1)} %copy-done.8, bf16[2,1024,576]{2,1,0:T(8,128)(2,1)} %get-tuple-element.87.refs_2_, ...), custom_call_target="tpu_custom_call" | custom-call | flops 4076863488 | bytes 15710214 | tf_op jit(solution)/shard_map/project_back/pallas_call | solution.py:610
  355.4 10.0 %qkv_grads.1 = (bf16[1536,1152]{1,0:T(8,128)(2,1)}, bf16[192,1152]{1,0:T(8,128)(2,1)}, f32[2,576]{1,0:T(2,128)}) custom-call(bf16[1024,1152]{1,0:T(8,128)(2,1)} %get-tuple-element.90.refs_0_, bf16[1024,576]{1,0:T(8,128)(2,1)} %copy-done.8, bf16[2,1024,576]{2,1,0:T(8,128)(2,1)} %get-tuple-element.91.refs_2_), custom_call_target="tpu_custom_call" | custom-call | flops 4076863488 | bytes 8847360 | tf_op jit(solution)/shard_map/qkv_grads/pallas_call | solution.py:610
  372.3 94.0 %ring_sum.1 = (bf16[2,8,2,96,1152]{4,3,2,1,0:T(8,128)(2,1)}, bf16[512,1152]{1,0:T(8,128)(2,1)S(1)}, f32[8,2304]{1,0:T(8,128)S(1)}) custom-call(bf16[8,2,96,1152]{3,2,1,0:T(8,128)(2,1)S(1)} %bitcast.98, bf16[8,2,96,1152]{3,2,1,0:T(8,128)(2,1)S(1)} %bitcast.97, bf16[1024,1152]{1,0:T(8,128)(2,1)S(1)} %copy-done.1, f32[8,2304]{1,0:T(8,128)S(1)} %concatenate.59.refs_3_), custom_call_target="tpu_custom_call" | custom-call | tf_op jit(solution)/shard_map/ring_sum/pallas_call | solution.py:298
  470.1 10.3 %widened.1 = (f32[1728,1152]{1,0:T(8,128)}, f32[576,1152]{1,0:T(8,128)}) custom-call(bf16[3072,1152]{1,0:T(8,128)(2,1)} %bitcast.106), custom_call_target="tpu_custom_call" | custom-call | tf_op jit(solution)/shard_map/widened/pallas_call | solution.py:915
  503.9 8.4 %fusion.51 = f32[1152,6,576]{0,2,1:T(8,128)} fusion(bf16[6,576,256]{2,1,0:T(8,128)(2,1)S(1)} %bitcast.113, bf16[256,1152]{1,0:T(8,128)(2,1)S(1)} %copy-done.32), kind=kOutput, calls=%fused_computation.85 | convolution fusion | flops 2040201216 | bytes 18284544 | tf_op jit(solution)/shard_map/dot_general | solution.py:1157
  514.6 7.9 %turned.1 = f32[1152,2304]{1,0:T(8,128)} custom-call(bf16[2304,1152]{1,0:T(8,128)(2,1)} %bitcast.115), custom_call_target="tpu_custom_call" | custom-call | tf_op jit(solution)/shard_map/turned/pallas_call | solution.py:888
  522.5 7.3 %bitcast_convert_fusion = f32[2304,1152]{1,0:T(8,128)} fusion(bf16[1,2304,1152]{2,1,0:T(8,128)(2,1)} %all-gather.7.cloned.1.call-done), kind=kLoop, calls=%fused_computation.2 | loop fusion | flops 2654208 | bytes 15925248 | tf_op jit(solution)/shard_map/convert_element_type | solution.py:1144
  (221 shorter events, 110.5 us)
Async XLA Ops:
  7.2 507.5 %all-gather.5.cloned.1.call-start = ((), (), s32[]{:S(2)}) async-start(), calls=%async_computation | async-start | bytes 5640192 | tf_op jit(solution)/shard_map/all_gather | solution.py:1056
  7.2 44.1 %collective-permute-start = (bf16[512,1152]{1,0:T(8,128)(2,1)}, bf16[512,1152]{1,0:T(8,128)(2,1)}, u32[]{:S(2)}, u32[]{:S(2)}) collective-permute-start(bf16[512,1152]{1,0:T(8,128)(2,1)} %param.15), channel_id=1, source_target_pairs={{0,1},{1,0},{2,3},{3,2},{4,5},{5,4},{6,7},{7,6},{8,9},{9,8},{10,11... | collective-permute-start | bytes 3538952 | tf_op jit(solution)/shard_map/ppermute | solution.py:21
  19.1 30.0 %collective-permute-start.2 = (bf16[576,256,2]{1,0,2:T(8,128)(2,1)S(1)}, bf16[576,256,2]{1,0,2:T(8,128)(2,1)S(1)}, u32[]{:S(2)}, u32[]{:S(2)}) collective-permute-start(bf16[576,256,2]{1,0,2:T(8,128)(2,1)S(1)} %bitcast.121), channel_id=1, source_target_pairs={{0,1},{1,0},{2,3},{3,2},{4,5},{5,4},{6,7},{7,6},{8,9},{9,8},{10,11... | collective-permute-start | bytes 1769480 | tf_op jit(solution)/shard_map/ppermute | solution.py:21
  19.2 10.6 %copy-start.41 = (bf16[2304]{0:T(1024)(128)(2,1)S(1)}, bf16[2304]{0:T(1024)(128)(2,1)}, u32[]{:S(2)}) copy-start(bf16[2304]{0:T(1024)(128)(2,1)} %param.25) | copy-start | bytes 13828
  29.0 240.7 %copy-start.36 = (s32[1024]{0:T(1024)}, s32[1024]{0:T(1024)S(1)}, u32[]{:S(2)}) copy-start(s32[1024]{0:T(1024)S(1)} %get-tuple-element.116) | copy-start | bytes 12292
  69.3 9.8 %collective-permute-start.3 = (bf16[2,128,576]{2,1,0:T(8,128)(2,1)S(1)}, bf16[2,128,576]{2,1,0:T(8,128)(2,1)S(1)}, u32[]{:S(2)}, u32[]{:S(2)}) collective-permute-start(bf16[2,128,576]{2,1,0:T(8,128)(2,1)S(1)} %pad_maximum_fusion.1), channel_id=1, source_target_pairs={{0,2},{2,4},{4,6},{6,8},{8,10},{10,12},{12,14},{14,16},{16,18},{18... | collective-permute-start | bytes 884744 | tf_op jit(solution)/shard_map/ppermute | solution.py:989
  70.9 8.3 %collective-permute-start.4 = (bf16[2,128,576]{2,1,0:T(8,128)(2,1)S(1)}, bf16[2,128,576]{2,1,0:T(8,128)(2,1)S(1)}, u32[]{:S(2)}, u32[]{:S(2)}) collective-permute-start(bf16[2,128,576]{2,1,0:T(8,128)(2,1)S(1)} %pad_maximum_fusion.2), channel_id=1, source_target_pairs={{2,0},{4,2},{6,4},{8,6},{10,8},{12,10},{14,12},{16,14},{18,16},{20... | collective-permute-start | bytes 884744 | tf_op jit(solution)/shard_map/ppermute | solution.py:992
  77.4 27.0 %collective-permute-start.1 = (bf16[576,256,4]{1,0,2:T(8,128)(2,1)}, bf16[576,256,4]{1,0,2:T(8,128)(2,1)}, u32[]{:S(2)}, u32[]{:S(2)}) collective-permute-start(bf16[576,256,4]{1,0,2:T(8,128)(2,1)} %copy.44), channel_id=1, source_target_pairs={{0,1},{1,0},{2,3},{3,2},{4,5},{5,4},{6,7},{7,6},{8,9},{9,8},{10,11... | collective-permute-start | bytes 3538952 | tf_op jit(solution)/shard_map/ppermute | solution.py:21
  81.8 10.9 %copy-start.23 = (bf16[576,1152]{1,0:T(8,128)(2,1)S(1)}, bf16[576,1152]{1,0:T(8,128)(2,1)}, u32[]{:S(2)}) copy-start(bf16[576,1152]{1,0:T(8,128)(2,1)} %refs_16_.1) | copy-start | bytes 3981316
  81.8 13.3 %copy-start.18 = (bf16[1024,1152]{1,0:T(8,128)(2,1)S(1)}, bf16[1024,1152]{1,0:T(8,128)(2,1)}, u32[]{:S(2)}) copy-start(bf16[1024,1152]{1,0:T(8,128)(2,1)} %refs_1_.1) | copy-start | bytes 7077892
  94.8 34.9 %collective-permute-start.6 = (bf16[512,1152]{1,0:T(8,128)(2,1)}, bf16[512,1152]{1,0:T(8,128)(2,1)}, u32[]{:S(2)}, u32[]{:S(2)}) collective-permute-start(bf16[512,1152]{1,0:T(8,128)(2,1)} %convolution_convert_fusion.2.mine.refs_7_), channel_id=1, source_target_pairs={{0,1},{1,0},{2,3},{3,2},{4,5},{5,4},{6,7},{7,6},{8,9},{9,8},{10,11... | collective-permute-start | bytes 3538952 | tf_op jit(solution)/shard_map/ppermute | solution.py:21
  99.6 59.3 %collective-permute-start.5 = (bf16[512,1152]{1,0:T(8,128)(2,1)}, bf16[512,1152]{1,0:T(8,128)(2,1)}, u32[]{:S(2)}, u32[]{:S(2)}) collective-permute-start(bf16[512,1152]{1,0:T(8,128)(2,1)} %convolution_convert_fusion.3.mine.refs_6_), channel_id=1, source_target_pairs={{0,1},{1,0},{2,3},{3,2},{4,5},{5,4},{6,7},{7,6},{8,9},{9,8},{10,11... | collective-permute-start | bytes 3538952 | tf_op jit(solution)/shard_map/ppermute | solution.py:21
  156.8 107.4 %collective-permute-start.9 = (bf16[512,1152]{1,0:T(8,128)(2,1)}, bf16[512,1152]{1,0:T(8,128)(2,1)S(1)}, u32[]{:S(2)}, u32[]{:S(2)}) collective-permute-start(bf16[512,1152]{1,0:T(8,128)(2,1)} %get-tuple-element.71.refs_11_), channel_id=1, source_target_pairs={{0,1},{1,0},{2,3},{3,2},{4,5},{5,4},{6,7},{7,6},{8,9},{9,8},{10,11... | collective-permute-start | bytes 3538952 | tf_op jit(solution)/shard_map/ppermute | solution.py:21
  186.1 78.1 %collective-permute-start.8 = (bf16[512,1152]{1,0:T(8,128)(2,1)}, bf16[512,1152]{1,0:T(8,128)(2,1)S(1)}, u32[]{:S(2)}, u32[]{:S(2)}) collective-permute-start(bf16[512,1152]{1,0:T(8,128)(2,1)} %get-tuple-element.70.refs_10_), channel_id=1, source_target_pairs={{0,1},{1,0},{2,3},{3,2},{4,5},{5,4},{6,7},{7,6},{8,9},{9,8},{10,11... | collective-permute-start | bytes 3538952 | tf_op jit(solution)/shard_map/ppermute | solution.py:21
  265.5 257.1 %all-gather.7.cloned.1.call-start = ((), (), s32[]{:S(2)}) async-start(), calls=%async_computation.1 | async-start | bytes 5640192 | tf_op jit(solution)/shard_map/all_gather | solution.py:1056
  269.9 60.1 %copy-start.33 = (pred[1024,256]{1,0:T(32,128)(4,1)}, pred[1024,256]{1,0:T(32,128)(4,1)S(1)}, u32[]{:S(2)}) copy-start(pred[1024,256]{1,0:T(32,128)(4,1)S(1)} %iota_compare_fusion) | copy-start | bytes 786436
  274.1 55.9 %collective-permute-start.7 = (bf16[512,1152]{1,0:T(8,128)(2,1)}, bf16[512,1152]{1,0:T(8,128)(2,1)}, u32[]{:S(2)}, u32[]{:S(2)}) collective-permute-start(bf16[512,1152]{1,0:T(8,128)(2,1)} %broadcast_select_fusion), channel_id=1, source_target_pairs={{0,1},{1,0},{2,3},{3,2},{4,5},{5,4},{6,7},{7,6},{8,9},{9,8},{10,11... | collective-permute-start | bytes 3538952 | tf_op jit(solution)/shard_map/ppermute | solution.py:21
  296.1 30.6 %copy-start.19 = (bf16[1024,1152]{1,0:T(8,128)(2,1)S(1)}, bf16[1024,1152]{1,0:T(8,128)(2,1)}, u32[]{:S(2)}) copy-start(bf16[1024,1152]{1,0:T(8,128)(2,1)} %refs_1_.1) | copy-start | bytes 7077892
  296.1 30.6 %copy-start.30 = (bf16[512,1152]{1,0:T(8,128)(2,1)S(1)}, bf16[512,1152]{1,0:T(8,128)(2,1)}, u32[]{:S(2)}) copy-start(bf16[512,1152]{1,0:T(8,128)(2,1)} %get-tuple-element.97) | copy-start | bytes 3538948
  322.8 13.4 %collective-permute-start.10 = (bf16[2,128,576]{2,1,0:T(8,128)(2,1)S(1)}, bf16[2,128,576]{2,1,0:T(8,128)(2,1)S(1)}, u32[]{:S(2)}, u32[]{:S(2)}) collective-permute-start(bf16[2,128,576]{2,1,0:T(8,128)(2,1)S(1)} %get-tuple-element.133), channel_id=1, source_target_pairs={{0,2},{2,4},{4,6},{6,8},{8,10},{10,12},{12,14},{14,16},{16,18},{18... | collective-permute-start | bytes 884744 | tf_op jit(solution)/shard_map/ppermute | solution.py:989
  325.4 10.8 %collective-permute-start.11 = (bf16[2,128,576]{2,1,0:T(8,128)(2,1)S(1)}, bf16[2,128,576]{2,1,0:T(8,128)(2,1)S(1)}, u32[]{:S(2)}, u32[]{:S(2)}) collective-permute-start(bf16[2,128,576]{2,1,0:T(8,128)(2,1)S(1)} %get-tuple-element.134), channel_id=1, source_target_pairs={{2,0},{4,2},{6,4},{8,6},{10,8},{12,10},{14,12},{16,14},{18,16},{20... | collective-permute-start | bytes 884744 | tf_op jit(solution)/shard_map/ppermute | solution.py:992
  329.2 26.1 %collective-permute-start.13 = (bf16[256,576]{1,0:T(8,128)(2,1)}, bf16[256,576]{1,0:T(8,128)(2,1)S(1)}, u32[]{:S(2)}, u32[]{:S(2)}) collective-permute-start(bf16[256,576]{1,0:T(8,128)(2,1)} %constant_dynamic-slice_fusion), channel_id=1, source_target_pairs={{0,1},{1,0},{2,3},{3,2},{4,5},{5,4},{6,7},{7,6},{8,9},{9,8},{10,11... | collective-permute-start | bytes 884744 | tf_op jit(solution)/shard_map/ppermute | solution.py:21
  354.1 16.4 %collective-permute-start.12 = (bf16[256,1152]{1,0:T(8,128)(2,1)}, bf16[256,1152]{1,0:T(8,128)(2,1)}, u32[]{:S(2)}, u32[]{:S(2)}) collective-permute-start(bf16[256,1152]{1,0:T(8,128)(2,1)} %dynamic-slice_bitcast_fusion), channel_id=1, source_target_pairs={{0,1},{1,0},{2,3},{3,2},{4,5},{5,4},{6,7},{7,6},{8,9},{9,8},{10,11... | collective-permute-start | bytes 1769480 | tf_op jit(solution)/shard_map/ppermute | solution.py:21
  489.5 22.7 %collective-permute-start.14 = (bf16[256,1152]{1,0:T(8,128)(2,1)}, bf16[256,1152]{1,0:T(8,128)(2,1)}, u32[]{:S(2)}, u32[]{:S(2)}) collective-permute-start(bf16[256,1152]{1,0:T(8,128)(2,1)} %fusion.15), channel_id=1, source_target_pairs={{0,1},{1,0},{2,3},{3,2},{4,5},{5,4},{6,7},{7,6},{8,9},{9,8},{10,11... | collective-permute-start | bytes 1769480 | tf_op jit(solution)/shard_map/ppermute | solution.py:21
  (44 other events, 188.7 us)
Sparse Core Ops, SparseCore 0:
  265.6 56.6 all-gather.4
  324.4 55.2 all-gather.6

commit v9 on v8

--- a/solution.py
+++ b/solution.py
@@ -21,10 +21,10 @@
     return lax.ppermute(part, "narrow", [(0, 1), (1, 0)])
 
 
-def narrow_gather(part):
+def narrow_gather(part, other=None):
     if lax.axis_size("narrow") != 2:
         return lax.all_gather(part, "narrow", axis=0, tiled=True)
-    other = swap(part)
+    other = swap(part) if other is None else other
     first = lax.axis_index("narrow") == 0
     return jnp.where(
         first, jnp.concatenate([part, other], axis=0), jnp.concatenate([other, part], axis=0)
@@ -626,8 +626,16 @@
     return jax.ShapeDtypeStruct(shape, dtype)
 
 
-def project_kernel(tokens, ids, table, weight, bias, q, k, v, norm_one):
-    xhat, _ = norm(tokens[...].astype(F32))
+def project_kernel(split, *refs):
+    if split:
+        index, mine, theirs, *refs = refs
+        held = pl.program_id(0) // (pl.num_programs(0) // 2) == index[0]
+        rows = jnp.where(held, mine[...], theirs[...])
+    else:
+        tokens, *refs = refs
+        rows = tokens[...]
+    ids, table, weight, bias, q, k, v, norm_one = refs
+    xhat, _ = norm(rows.astype(F32))
     normed = (xhat * (1.0 + pick(ids[...], table[1])) + pick(ids[...], table[0])).astype(BF16)
     norm_one[...] = normed
     size = q.shape[1]
@@ -638,19 +646,24 @@
         out[...] = rows.astype(BF16)
 
 
-def project(tokens, ids, table, weight, bias):
-    count, width = tokens.shape
+def project(sources, ids, table, weight, bias):
+    split = len(sources) == 3
+    count, width = ids.shape[0], weight.shape[1]
     size = weight.shape[0] // 3
+    specs = [tiled(TILE, width)]
+    if split:
+        half = pl.BlockSpec((TILE, width), lambda i: (i % (count // TILE // 2), 0))
+        specs = [pl.BlockSpec(memory_space=pltpu.SMEM), half, half]
     return token_call(
-        project_kernel,
+        lambda *refs: project_kernel(split, *refs),
         count,
         "project",
         [shaped((count, size))] * 3 + [shaped((count, width))],
-        [tiled(TILE, width), tiled(TILE, 1), whole(table.shape), whole(weight.shape), whole(bias.shape)],
+        specs + [tiled(TILE, 1), whole(table.shape), whole(weight.shape), whole(bias.shape)],
         [tiled(TILE, size)] * 3 + [tiled(TILE, width)],
         [],
         6 * count * width * size,
-        (tokens, ids, table, weight, bias),
+        tuple(sources) + (ids, table, weight, bias),
     )
 
 
@@ -689,10 +702,13 @@
     branch[...] = ahead.astype(BF16)
 
 
-def mlp(tokens, mine, theirs, cotangent, ids, live, table, out_bias, up, up_bias, down):
-    count, width = tokens.shape
+def mlp(start, tokens, mine, theirs, cotangent, ids, live, table, out_bias, up, up_bias, down):
+    count, width = mine.shape
     size = up.shape[1]
-    row, col = tiled(TILE, width), tiled(TILE, 1)
+    first = start // TILE
+    here = tiled(TILE, width)
+    row = pl.BlockSpec((TILE, width), lambda i: (i + first, 0))
+    col = pl.BlockSpec((TILE, 1), lambda i: (i + first, 0))
     consts = (table, out_bias, up, up_bias, down)
     return token_call(
         mlp_kernel,
@@ -700,7 +716,7 @@
         "mlp",
         [shaped((count, n)) for n in (width, size, size, width, width, width)]
         + [shaped((1, n), F32) for n in (size, width)],
-        [row, row, row, row, col, col] + [whole(x.shape) for x in consts],
+        [row, here, here, row, col, col] + [whole(x.shape) for x in consts],
         [tiled(TILE, n) for n in (width, size, size, width, width, width)]
         + [whole((1, n)) for n in (size, width)],
         [],
@@ -963,23 +979,31 @@
     cond_rows = condition.astype(F32)
     sigmoid_rows = jax.nn.sigmoid(cond_rows)
     activated = (cond_rows * sigmoid_rows).astype(BF16)
-    tok_full = narrow_gather(tokens)
+    halves_held = narrow_count == 2 and share % TILE == 0
+    tok_other = swap(tokens) if halves_held else None
+    tok_full = narrow_gather(tokens, tok_other)
     mod_rows = jnp.transpose(modulator, (1, 2, 0)).reshape(6 * mod_width, width)
 
-    def vectors(lo, hi, after=None):
+    def vectors(lo, hi):
         part = dot(activated, mod_rows[lo * mod_width : hi * mod_width], ((1,), (1,)))
         part = part + modulator_bias[lo:hi].astype(F32).reshape(1, -1)
         rows = jnp.moveaxis(part.astype(BF16).reshape(img_row, hi - lo, -1), 2, 0)
-        if after is not None:
-            rows, after = lax.optimization_barrier((rows, after))
-        return jnp.transpose(narrow_gather(rows), (2, 1, 0)), after
-
-    table_one, _ = vectors(0, 2)
-    table_two, tok_full = vectors(2, 6, tok_full)
+        return rows
+
+    def table_of(rows, other=None):
+        return jnp.transpose(narrow_gather(rows, other), (2, 1, 0))
+
+    table_one = table_of(vectors(0, 2))
+    rows_two = vectors(2, 6)
+    sources = [narrow_index[None], tokens, tok_other] if halves_held else [tok_full]
+    rows_two, sources[-1] = lax.optimization_barrier((rows_two, sources[-1]))
+    other_two = swap(rows_two) if narrow_count == 2 else None
     flat_qkv = jnp.transpose(qkv_weight, (1, 2, 0)).reshape(3 * part_width, width)
     queries, key_rows, value_rows, norm_one = project(
-        tok_full, ids_col, table_one, flat_qkv, qv_bias
-    )
+        sources, ids_col, table_one, flat_qkv, qv_bias
+    )
+    other_two, queries = lax.optimization_barrier((other_two, queries))
+    table_two = table_of(rows_two, other_two)
     tail_start = own_count - span
 
     def tail_of(rows):
@@ -1017,13 +1041,15 @@
         attn_parts.append(dot(rows_of(context, i), out_weight, ((1,), (0,)), BF16))
         attn_others.append(narrow_other(attn_parts[i]))
     for i in range(blocks):
-        operands = [rows_of(rows, i) for rows in (tok_full, cotangent, ids_col, live)]
         mlp_outs.append(
             mlp(
-                operands[0],
+                i * block,
+                tok_full,
                 attn_parts[i],
                 attn_others[i],
-                *operands[1:],
+                cotangent,
+                ids_col,
+                live,
                 table_two,
                 out_row,
                 up_weight,

time: 545 us -> 537 us (0.985)
    unnamed x104 -> x120, local copies, waits for them, and re-layouts: 9.87 us -> 13.7 us
  transfers between devices with their start and end apart: 17 -> 17, of which waited for: 4 -> 3; matrix products, arithmetic and copies ran while one was open for 24% -> 23% of each run, Pallas kernels for 58% -> 59%
where the time goes in v9:
time: 537 us; the launch traced here: 529 us
  Pallas kernels  322 us (60%)
  matrix products  56.9 us (11%)
  local copies, waits for them, and re-layouts  50.7 us (9%)
  other arithmetic  35 us (7%)
  waiting for transfers between devices  27.7 us (5%)
  starting transfers between devices  19.7 us (4%)
  between operations  17.3 us (3%)
    pallas_call x6, Pallas kernels, token_call(): pl.pallas_call(kernel, grid=(tokens // TILE,), out_shape=out_shape, in_sp...  112 us
    pallas_call x1, Pallas kernels, ring_sum(): pl.pallas_call(lambda *refs: ring_kernel(chips, subs, True, *refs), out_s...  94.2 us
    pallas_call x1, Pallas kernels, ring_scatter(): pl.pallas_call(lambda *refs: ring_kernel(chips, shard // UNIT, False, *re...  59.9 us
    dot_general x14, matrix products, dot(): lax.dot_general(left, right, (dims, ((), ())), preferred_element_type=F32)  48.5 us
    ppermute x11, waiting for transfers between devices, swap(): return lax.ppermute(part, 'narrow', [(0, 1), (1, 0)])  27.6 us
    pallas_call x1, Pallas kernels, attention_backward(): pl.pallas_call(lambda *refs: backward_kernel(tiles, *refs), grid=(tiles,)...  27.2 us
    ppermute x11, starting transfers between devices, swap(): return lax.ppermute(part, 'narrow', [(0, 1), (1, 0)])  13.9 us
    unnamed x120, local copies, waits for them, and re-layouts  13.7 us
  transfers between devices with their start and end apart: 17, of which 3 were waited for; matrix products, arithmetic and copies ran while one was open for 23% of the time, Pallas kernels for 59%

profile of v9, /device:TPU:0, one launch (start us, length us, event | category | flops | bytes accessed | tf_op | source)
XLA Modules:
  0.0 529.5 jit_solution(14501784713410199909)
XLA Ops:
  11.0 5.2 fusion.72
  19.2 5.3 %slice.166 = bf16[4,576,1152]{2,1,0:T(8,128)(2,1)} slice(bf16[6,576,1152]{2,1,0:T(8,128)(2,1)} %bitcast.99), slice={[2:6], [0:576], [0:1152]} | slice | bytes 10616832 | tf_op jit(solution)/shard_map/slice | solution.py:988
  29.1 4.4 fusion.6
  35.1 14.1 %collective-permute-done.2 = bf16[576,256,2]{1,0,2:T(8,128)(2,1)} collective-permute-done((bf16[576,256,2]{1,0,2:T(8,128)(2,1)S(1)}, bf16[576,256,2]{1,0,2:T(8,128)(2,1)}, u32[]{:S(2)}, u32[]{:S(2)}) %collective-permute-start.2) | collective-permute-done | bytes 589856 | tf_op jit(solution)/shard_map/ppermute | solution.py:21
  55.6 13.2 %project.1 = (bf16[1024,576]{1,0:T(8,128)(2,1)}, bf16[1024,576]{1,0:T(8,128)(2,1)}, bf16[1024,576]{1,0:T(8,128)(2,1)}, bf16[1024,1152]{1,0:T(8,128)(2,1)}) custom-call(s32[1]{0:T(128)} %bitcast.5.refs_0_, bf16[512,1152]{1,0:T(8,128)(2,1)} %refs_1_.2, bf16[512,1152]{1,0:T(8,128)(2,1)} %collective-permute-done.refs_2_, s32[1024,1]{1,0:T(8,128)} %copy.48.refs_3_.ids, ...), custom_call_target="tpu_custom_call" | custom-call | flops 4076863488 | bytes 11289990 | tf_op jit(solution)/shard_map/project/pallas_call | solution.py:610
  74.9 4.6 collective-permute-done.1
  83.8 11.1 %attention_forward.1 = (bf16[1024,576]{1,0:T(8,128)(2,1)S(1)}, f32[8,1024]{1,0:T(8,128)S(1)}) custom-call(bf16[1024,576]{1,0:T(8,128)(2,1)S(1)} %copy-done.9, bf16[1024,576]{1,0:T(8,128)(2,1)S(1)} %copy-done.3, bf16[1024,576]{1,0:T(8,128)(2,1)S(1)} %copy-done.4, bf16[2,128,576]{2,1,0:T(8,128)(2,1)S(1)} %collective-permute-done.3.refs_3_, ...), custom_call_target="tpu_custom_call" | custom-call | flops 1207959552 | bytes 4718592 | tf_op jit(solution)/shard_map/attention_forward/pallas_call | solution.py:413
  101.5 4.0 maximum_select_fusion.1.tokens.refs_0_
  115.7 8.9 %collective-permute-done.6.theirs.refs_9_ = bf16[512,1152]{1,0:T(8,128)(2,1)} collective-permute-done((bf16[512,1152]{1,0:T(8,128)(2,1)}, bf16[512,1152]{1,0:T(8,128)(2,1)}, u32[]{:S(2)}, u32[]{:S(2)}) %collective-permute-start.6) | collective-permute-done | bytes 1179680 | tf_op jit(solution)/shard_map/ppermute | solution.py:21
  124.6 27.1 %mlp.3 = (bf16[512,1152]{1,0:T(8,128)(2,1)}, bf16[512,2304]{1,0:T(8,128)(2,1)}, bf16[512,2304]{1,0:T(8,128)(2,1)}, bf16[512,1152]{1,0:T(8,128)(2,1)}, bf16[512,1...) custom-call(bf16[1024,1152]{1,0:T(8,128)(2,1)} %maximum_select_fusion.1.tokens.refs_0_, ...), custom_call_target="tpu_custom_call" | custom-call | flops 10871635968 | bytes 30103680 | tf_op jit(solution)/shard_map/mlp/pallas_call | solution.py:610
  155.2 27.3 %mlp.2 = (bf16[512,1152]{1,0:T(8,128)(2,1)}, bf16[512,2304]{1,0:T(8,128)(2,1)}, bf16[512,2304]{1,0:T(8,128)(2,1)}, bf16[512,1152]{1,0:T(8,128)(2,1)}, bf16[512,1...) custom-call(bf16[1024,1152]{1,0:T(8,128)(2,1)} %maximum_select_fusion.1.tokens.refs_0_, ...), custom_call_target="tpu_custom_call" | custom-call | flops 10871635968 | bytes 30103680 | tf_op jit(solution)/shard_map/mlp/pallas_call | solution.py:610
  182.6 9.3 %convolution_convert_fusion.1 = bf16[2304,1152]{1,0:T(8,128)(2,1)S(1)} fusion(bf16[512,2304]{1,0:T(8,128)(2,1)} %get-tuple-element.77, bf16[512,2304]{1,0:T(8,128)(2,1)} %get-tuple-element.76, bf16[512,1152]{1,0:T(8,128)(2,1)} %get-tuple-element.79, bf16[512,1152]{1,0:T(8,128)(2,1)} %get-tuple-element.78), kind=kOutput, calls=%fused_computation.1 | convolution fusion | flops 5452627968 | bytes 12386304 | tf_op jit(solution)/shard_map/dot_general | solution.py:17
  191.9 6.7 %convolution_convert_fusion = bf16[2304,1152]{1,0:T(8,128)(2,1)S(1)} fusion(bf16[512,2304]{1,0:T(8,128)(2,1)S(1)} %copy-done.55, bf16[512,2304]{1,0:T(8,128)(2,1)S(1)} %copy-done.56, bf16[512,1152]{1,0:T(8,128)(2,1)S(1)} %copy-done.57, bf16[512,1152]{1,0:T(8,128)(2,1)S(1)} %copy-done.58), kind=kOutput, calls=%fused_computation | convolution fusion | flops 5452627968 | bytes 12386304 | tf_op jit(solution)/shard_map/dot_general | solution.py:17
  198.6 59.9 %ring_scatter.1 = bf16[2,144,1152]{2,1,0:T(8,128)(2,1)S(1)} custom-call(bf16[8,2,144,1152]{3,2,1,0:T(8,128)(2,1)S(1)} %bitcast.92, bf16[8,2,144,1152]{3,2,1,0:T(8,128)(2,1)S(1)} %bitcast.93), custom_call_target="tpu_custom_call" | custom-call | tf_op jit(solution)/shard_map/ring_scatter/pallas_call | solution.py:278
  269.1 19.0 %middle_back.1 = (f32[1024,1152]{1,0:T(8,128)}, bf16[1024,576]{1,0:T(8,128)(2,1)}, bf16[576,1152]{1,0:T(8,128)(2,1)}, bf16[2,3,256,576]{3,2,1,0:T(8,128)(2,1)}, f32[1,1152]{1,0:T(1,128)}) custom-call(bf16[1024,1152]{1,0:T(8,128)(2,1)} %maximum_select_fusion.1.tokens.refs_0_, bf16[1024,1152]{1,0:T(8,128)(2,1)} %refs_1_.3, bf16[1024,576]{1,0:T(8,128)(2,1)} %copy-done.2, ...), custom_call_target="tpu_custom_call" | custom-call | flops 2717908992 | bytes 28554624 | tf_op jit(solution)/shard_map/middle_back/pallas_call | solution.py:610
  289.5 27.2 %attention_backward.1 = (bf16[1024,576]{1,0:T(8,128)(2,1)S(1)}, bf16[2,1024,576]{2,1,0:T(8,128)(2,1)}, bf16[2,2,128,576]{3,2,1,0:T(8,128)(2,1)S(1)}) custom-call(bf16[1024,576]{1,0:T(8,128)(2,1)S(1)} %copy-done.10, bf16[1024,576]{1,0:T(8,128)(2,1)S(1)} %copy-done.3, bf16[1024,576]{1,0:T(8,128)(2,1)} %get-tuple-element.70.refs_2_, ...), custom_call_target="tpu_custom_call" | custom-call | flops 3019898880 | bytes 9437184 | tf_op jit(solution)/shard_map/attention_backward/pallas_call | solution.py:514
  323.2 5.2 fusion.22
  330.2 15.0 %project_back.1 = (bf16[1024,1152]{1,0:T(8,128)(2,1)}, bf16[2,1024,576]{2,1,0:T(8,128)(2,1)}, bf16[2,256,1152]{2,1,0:T(8,128)(2,1)}) custom-call(bf16[1024,1152]{1,0:T(8,128)(2,1)} %maximum_select_fusion.1.tokens.refs_0_, bf16[1024,576]{1,0:T(8,128)(2,1)} %copy-done.11, bf16[2,1024,576]{2,1,0:T(8,128)(2,1)} %get-tuple-element.91.refs_2_, ...), custom_call_target="tpu_custom_call" | custom-call | flops 4076863488 | bytes 15710214 | tf_op jit(solution)/shard_map/project_back/pallas_call | solution.py:610
  348.8 10.0 %qkv_grads.1 = (bf16[1536,1152]{1,0:T(8,128)(2,1)}, bf16[192,1152]{1,0:T(8,128)(2,1)}, f32[2,576]{1,0:T(2,128)}) custom-call(bf16[1024,1152]{1,0:T(8,128)(2,1)} %get-tuple-element.94.refs_0_, bf16[1024,576]{1,0:T(8,128)(2,1)} %copy-done.11, bf16[2,1024,576]{2,1,0:T(8,128)(2,1)} %get-tuple-element.95.refs_2_), custom_call_target="tpu_custom_call" | custom-call | flops 4076863488 | bytes 8847360 | tf_op jit(solution)/shard_map/qkv_grads/pallas_call | solution.py:610
  365.0 94.2 %ring_sum.1 = (bf16[2,8,2,96,1152]{4,3,2,1,0:T(8,128)(2,1)}, bf16[512,1152]{1,0:T(8,128)(2,1)S(1)}, f32[8,2304]{1,0:T(8,128)S(1)}) custom-call(bf16[8,2,96,1152]{3,2,1,0:T(8,128)(2,1)S(1)} %bitcast.95, bf16[8,2,96,1152]{3,2,1,0:T(8,128)(2,1)S(1)} %bitcast.94, bf16[1024,1152]{1,0:T(8,128)(2,1)S(1)} %copy-done.1, f32[8,2304]{1,0:T(8,128)S(1)} %concatenate.59.refs_3_), custom_call_target="tpu_custom_call" | custom-call | tf_op jit(solution)/shard_map/ring_sum/pallas_call | solution.py:298
  463.0 10.3 %widened.1 = (f32[1728,1152]{1,0:T(8,128)}, f32[576,1152]{1,0:T(8,128)}) custom-call(bf16[3072,1152]{1,0:T(8,128)(2,1)} %bitcast.103), custom_call_target="tpu_custom_call" | custom-call | tf_op jit(solution)/shard_map/widened/pallas_call | solution.py:931
  496.4 8.4 %fusion.53 = f32[1152,6,576]{0,2,1:T(8,128)} fusion(bf16[6,576,256]{2,1,0:T(8,128)(2,1)S(1)} %bitcast.110, bf16[256,1152]{1,0:T(8,128)(2,1)S(1)} %copy-done.35), kind=kOutput, calls=%fused_computation.87 | convolution fusion | flops 2040201216 | bytes 18284544 | tf_op jit(solution)/shard_map/dot_general | solution.py:1183
  507.2 7.9 %turned.1 = f32[1152,2304]{1,0:T(8,128)} custom-call(bf16[2304,1152]{1,0:T(8,128)(2,1)} %bitcast.112), custom_call_target="tpu_custom_call" | custom-call | tf_op jit(solution)/shard_map/turned/pallas_call | solution.py:904
  515.1 7.3 %bitcast_convert_fusion = f32[2304,1152]{1,0:T(8,128)} fusion(bf16[1,2304,1152]{2,1,0:T(8,128)(2,1)} %all-gather.7.cloned.1.call-done), kind=kLoop, calls=%fused_computation.2 | loop fusion | flops 2654208 | bytes 15925248 | tf_op jit(solution)/shard_map/convert_element_type | solution.py:1170
  (231 shorter events, 106.8 us)
Async XLA Ops:
  7.2 500.0 %all-gather.5.cloned.1.call-start = ((), (), s32[]{:S(2)}) async-start(), calls=%async_computation | async-start | bytes 5640192 | tf_op jit(solution)/shard_map/all_gather | solution.py:1082
  7.2 43.3 %collective-permute-start = (bf16[512,1152]{1,0:T(8,128)(2,1)}, bf16[512,1152]{1,0:T(8,128)(2,1)}, u32[]{:S(2)}, u32[]{:S(2)}) collective-permute-start(bf16[512,1152]{1,0:T(8,128)(2,1)} %refs_1_.2), channel_id=1, source_target_pairs={{0,1},{1,0},{2,3},{3,2},{4,5},{5,4},{6,7},{7,6},{8,9},{9,8},{10,11... | collective-permute-start | bytes 3538952 | tf_op jit(solution)/shard_map/ppermute | solution.py:21
  19.0 30.1 %collective-permute-start.2 = (bf16[576,256,2]{1,0,2:T(8,128)(2,1)S(1)}, bf16[576,256,2]{1,0,2:T(8,128)(2,1)}, u32[]{:S(2)}, u32[]{:S(2)}) collective-permute-start(bf16[576,256,2]{1,0,2:T(8,128)(2,1)S(1)} %bitcast.118), channel_id=1, source_target_pairs={{0,1},{1,0},{2,3},{3,2},{4,5},{5,4},{6,7},{7,6},{8,9},{9,8},{10,11... | collective-permute-start | bytes 1769480 | tf_op jit(solution)/shard_map/ppermute | solution.py:21
  28.0 235.3 %copy-start.40 = (s32[1024]{0:T(1024)}, s32[1024]{0:T(1024)S(1)}, u32[]{:S(2)}) copy-start(s32[1024]{0:T(1024)S(1)} %get-tuple-element.120) | copy-start | bytes 12292
  52.0 27.4 %collective-permute-start.1 = (bf16[576,256,4]{1,0,2:T(8,128)(2,1)}, bf16[576,256,4]{1,0,2:T(8,128)(2,1)}, u32[]{:S(2)}, u32[]{:S(2)}) collective-permute-start(bf16[576,256,4]{1,0,2:T(8,128)(2,1)} %copy.42), channel_id=1, source_target_pairs={{0,1},{1,0},{2,3},{3,2},{4,5},{5,4},{6,7},{7,6},{8,9},{9,8},{10,11... | collective-permute-start | bytes 3538952 | tf_op jit(solution)/shard_map/ppermute | solution.py:21
  70.2 9.2 %collective-permute-start.3 = (bf16[2,128,576]{2,1,0:T(8,128)(2,1)S(1)}, bf16[2,128,576]{2,1,0:T(8,128)(2,1)S(1)}, u32[]{:S(2)}, u32[]{:S(2)}) collective-permute-start(bf16[2,128,576]{2,1,0:T(8,128)(2,1)S(1)} %pad_maximum_fusion.1), channel_id=1, source_target_pairs={{0,2},{2,4},{4,6},{6,8},{8,10},{10,12},{12,14},{14,16},{16,18},{18... | collective-permute-start | bytes 884744 | tf_op jit(solution)/shard_map/ppermute | solution.py:1013
  71.6 7.8 %collective-permute-start.4 = (bf16[2,128,576]{2,1,0:T(8,128)(2,1)S(1)}, bf16[2,128,576]{2,1,0:T(8,128)(2,1)S(1)}, u32[]{:S(2)}, u32[]{:S(2)}) collective-permute-start(bf16[2,128,576]{2,1,0:T(8,128)(2,1)S(1)} %pad_maximum_fusion.2), channel_id=1, source_target_pairs={{2,0},{4,2},{6,4},{8,6},{10,8},{12,10},{14,12},{16,14},{18,16},{20... | collective-permute-start | bytes 884744 | tf_op jit(solution)/shard_map/ppermute | solution.py:1016
  97.3 27.3 %collective-permute-start.6 = (bf16[512,1152]{1,0:T(8,128)(2,1)}, bf16[512,1152]{1,0:T(8,128)(2,1)}, u32[]{:S(2)}, u32[]{:S(2)}) collective-permute-start(bf16[512,1152]{1,0:T(8,128)(2,1)} %convolution_convert_fusion.2.mine.refs_7_), channel_id=1, source_target_pairs={{0,1},{1,0},{2,3},{3,2},{4,5},{5,4},{6,7},{7,6},{8,9},{9,8},{10,11... | collective-permute-start | bytes 3538952 | tf_op jit(solution)/shard_map/ppermute | solution.py:21
  111.5 42.6 %collective-permute-start.5 = (bf16[512,1152]{1,0:T(8,128)(2,1)}, bf16[512,1152]{1,0:T(8,128)(2,1)S(1)}, u32[]{:S(2)}, u32[]{:S(2)}) collective-permute-start(bf16[512,1152]{1,0:T(8,128)(2,1)} %convolution_convert_fusion.3.mine.refs_6_), channel_id=1, source_target_pairs={{0,1},{1,0},{2,3},{3,2},{4,5},{5,4},{6,7},{7,6},{8,9},{9,8},{10,11... | collective-permute-start | bytes 3538952 | tf_op jit(solution)/shard_map/ppermute | solution.py:21
  151.6 106.9 %collective-permute-start.9 = (bf16[512,1152]{1,0:T(8,128)(2,1)}, bf16[512,1152]{1,0:T(8,128)(2,1)}, u32[]{:S(2)}, u32[]{:S(2)}) collective-permute-start(bf16[512,1152]{1,0:T(8,128)(2,1)} %get-tuple-element.75.refs_11_), channel_id=1, source_target_pairs={{0,1},{1,0},{2,3},{3,2},{4,5},{5,4},{6,7},{7,6},{8,9},{9,8},{10,11... | collective-permute-start | bytes 3538952 | tf_op jit(solution)/shard_map/ppermute | solution.py:21
  182.4 76.1 %collective-permute-start.8 = (bf16[512,1152]{1,0:T(8,128)(2,1)}, bf16[512,1152]{1,0:T(8,128)(2,1)S(1)}, u32[]{:S(2)}, u32[]{:S(2)}) collective-permute-start(bf16[512,1152]{1,0:T(8,128)(2,1)} %get-tuple-element.74.refs_10_), channel_id=1, source_target_pairs={{0,1},{1,0},{2,3},{3,2},{4,5},{5,4},{6,7},{7,6},{8,9},{9,8},{10,11... | collective-permute-start | bytes 3538952 | tf_op jit(solution)/shard_map/ppermute | solution.py:21
  259.8 255.3 %all-gather.7.cloned.1.call-start = ((), (), s32[]{:S(2)}) async-start(), calls=%async_computation.1 | async-start | bytes 5640192 | tf_op jit(solution)/shard_map/all_gather | solution.py:1082
  268.5 54.7 %collective-permute-start.7 = (bf16[512,1152]{1,0:T(8,128)(2,1)}, bf16[512,1152]{1,0:T(8,128)(2,1)}, u32[]{:S(2)}, u32[]{:S(2)}) collective-permute-start(bf16[512,1152]{1,0:T(8,128)(2,1)} %broadcast_select_fusion), channel_id=1, source_target_pairs={{0,1},{1,0},{2,3},{3,2},{4,5},{5,4},{6,7},{7,6},{8,9},{9,8},{10,11... | collective-permute-start | bytes 3538952 | tf_op jit(solution)/shard_map/ppermute | solution.py:21
  269.1 19.0 %copy-start.8 = (bf16[2,128,576]{2,1,0:T(8,128)(2,1)S(1)}, bf16[2,128,576]{2,1,0:T(8,128)(2,1)}, u32[]{:S(2)}) copy-start(bf16[2,128,576]{2,1,0:T(8,128)(2,1)} %copy-done.6) | copy-start | bytes 884740
  289.5 30.3 %copy-start.23 = (bf16[1024,1152]{1,0:T(8,128)(2,1)S(1)}, bf16[1024,1152]{1,0:T(8,128)(2,1)}, u32[]{:S(2)}) copy-start(bf16[1024,1152]{1,0:T(8,128)(2,1)} %refs_1_.3) | copy-start | bytes 7077892
  289.5 30.3 %copy-start.33 = (bf16[512,1152]{1,0:T(8,128)(2,1)S(1)}, bf16[512,1152]{1,0:T(8,128)(2,1)}, u32[]{:S(2)}) copy-start(bf16[512,1152]{1,0:T(8,128)(2,1)} %get-tuple-element.101) | copy-start | bytes 3538948
  289.5 30.3 %copy-start.37 = (pred[1024,256]{1,0:T(32,128)(4,1)S(1)}, pred[1024,256]{1,0:T(32,128)(4,1)}, u32[]{:S(2)}) copy-start(pred[1024,256]{1,0:T(32,128)(4,1)} %copy-done.36) | copy-start | bytes 786436
  289.5 30.3 %copy-start.46 = (f32[1152]{0:T(1024)S(1)}, f32[1152]{0:T(1024)}, u32[]{:S(2)}) copy-start(f32[1152]{0:T(1024)} %broadcast_select_fusion.1) | copy-start | bytes 13828
  289.5 30.3 %copy-start.53 = (f32[512]{0:T(512)S(1)}, f32[512]{0:T(512)}, u32[]{:S(2)}) copy-start(f32[512]{0:T(512)} %get-tuple-element.140) | copy-start | bytes 6148
  316.7 12.5 %collective-permute-start.10 = (bf16[2,128,576]{2,1,0:T(8,128)(2,1)S(1)}, bf16[2,128,576]{2,1,0:T(8,128)(2,1)S(1)}, u32[]{:S(2)}, u32[]{:S(2)}) collective-permute-start(bf16[2,128,576]{2,1,0:T(8,128)(2,1)S(1)} %get-tuple-element.133), channel_id=1, source_target_pairs={{0,2},{2,4},{4,6},{6,8},{8,10},{10,12},{12,14},{14,16},{16,18},{18... | collective-permute-start | bytes 884744 | tf_op jit(solution)/shard_map/ppermute | solution.py:1013
  318.4 10.8 %collective-permute-start.11 = (bf16[2,128,576]{2,1,0:T(8,128)(2,1)S(1)}, bf16[2,128,576]{2,1,0:T(8,128)(2,1)S(1)}, u32[]{:S(2)}, u32[]{:S(2)}) collective-permute-start(bf16[2,128,576]{2,1,0:T(8,128)(2,1)S(1)} %get-tuple-element.134), channel_id=1, source_target_pairs={{2,0},{4,2},{6,4},{8,6},{10,8},{12,10},{14,12},{16,14},{18,16},{20... | collective-permute-start | bytes 884744 | tf_op jit(solution)/shard_map/ppermute | solution.py:1016
  321.6 27.0 %collective-permute-start.13 = (bf16[256,576]{1,0:T(8,128)(2,1)S(1)}, bf16[256,576]{1,0:T(8,128)(2,1)S(1)}, u32[]{:S(2)}, u32[]{:S(2)}) collective-permute-start(bf16[256,576]{1,0:T(8,128)(2,1)S(1)} %constant_dynamic-slice_fusion), channel_id=1, source_target_pairs={{0,1},{1,0},{2,3},{3,2},{4,5},{5,4},{6,7},{7,6},{8,9},{9,8},{10,11... | collective-permute-start | bytes 884744 | tf_op jit(solution)/shard_map/ppermute | solution.py:21
  347.2 15.2 %collective-permute-start.12 = (bf16[256,1152]{1,0:T(8,128)(2,1)}, bf16[256,1152]{1,0:T(8,128)(2,1)}, u32[]{:S(2)}, u32[]{:S(2)}) collective-permute-start(bf16[256,1152]{1,0:T(8,128)(2,1)} %dynamic-slice_bitcast_fusion), channel_id=1, source_target_pairs={{0,1},{1,0},{2,3},{3,2},{4,5},{5,4},{6,7},{7,6},{8,9},{9,8},{10,11... | collective-permute-start | bytes 1769480 | tf_op jit(solution)/shard_map/ppermute | solution.py:21
  482.4 22.4 %collective-permute-start.14 = (bf16[256,1152]{1,0:T(8,128)(2,1)}, bf16[256,1152]{1,0:T(8,128)(2,1)}, u32[]{:S(2)}, u32[]{:S(2)}) collective-permute-start(bf16[256,1152]{1,0:T(8,128)(2,1)} %fusion.15), channel_id=1, source_target_pairs={{0,1},{1,0},{2,3},{3,2},{4,5},{5,4},{6,7},{7,6},{8,9},{9,8},{10,11... | collective-permute-start | bytes 1769480 | tf_op jit(solution)/shard_map/ppermute | solution.py:21
  (52 other events, 233.9 us)
Sparse Core Ops, SparseCore 0:
  259.9 54.6 all-gather.4
  316.8 56.4 all-gather.6

commit v10 on v9

--- a/solution.py
+++ b/solution.py
@@ -683,7 +683,7 @@
     column = jnp.sum(pulled.astype(F32), axis=0, keepdims=True)
     down_sum[...] = jnp.where(first, 0.0, down_sum[...]) + column
     width = up.shape[1]
-    step = 384 if width % 384 == 0 else width
+    step = 768 if width % 768 == 0 else width
     back = ahead = 0.0
     for lo in range(0, width, step):
         cols = slice(lo, lo + step)
@@ -913,7 +913,7 @@
 
 def widened(flat, counts):
     width = flat.shape[1]
-    step = next(n for n in (192, 96, 48, 16) if all(count % n == 0 for count in counts))
+    step = next(n for n in (576, 192, 96, 48, 16) if all(count % n == 0 for count in counts))
     starts = [sum(counts[:i]) // step for i in range(len(counts))]
     tiles = [count // step for count in counts]
 
@@ -934,6 +934,7 @@
         out_shape=[shaped((count, width), F32) for count in counts],
         in_specs=[tiled(step, width)],
         out_specs=[spec(*pair) for pair in zip(starts, tiles)],
+        compiler_params=pltpu.CompilerParams(vmem_limit_bytes=40 << 20),
         name="widened",
     )(flat)
 

time: 537 us -> 523 us (0.974)
  Pallas kernels: 322 us -> 307 us
    pallas_call x6, Pallas kernels: 112 us -> 103 us  [token_call(): pl.pallas_call(kernel, grid=(tokens // TILE,), out_shape=out_shape, in_sp...]
    unnamed x120 -> x124, local copies, waits for them, and re-layouts: 13.7 us -> 17.2 us
  transfers between devices with their start and end apart: 17 -> 17, of which waited for: 3 -> 3; matrix products, arithmetic and copies ran while one was open for 23% -> 22% of each run, Pallas kernels for 59% -> 57%
where the time goes in v10:
time: 523 us; the launch traced here: 515 us
  Pallas kernels  307 us (59%)
  local copies, waits for them, and re-layouts  53.4 us (10%)
  matrix products  52.4 us (10%)
  other arithmetic  34.7 us (7%)
  waiting for transfers between devices  28 us (5%)
  starting transfers between devices  23 us (4%)
  between operations  17.1 us (3%)
    pallas_call x6, Pallas kernels, token_call(): pl.pallas_call(kernel, grid=(tokens // TILE,), out_shape=out_shape, in_sp...  103 us
    pallas_call x1, Pallas kernels, ring_sum(): pl.pallas_call(lambda *refs: ring_kernel(chips, subs, True, *refs), out_s...  93.4 us
    pallas_call x1, Pallas kernels, ring_scatter(): pl.pallas_call(lambda *refs: ring_kernel(chips, shard // UNIT, False, *re...  58.4 us
    dot_general x14, matrix products, dot(): lax.dot_general(left, right, (dims, ((), ())), preferred_element_type=F32)  44.1 us
    ppermute x11, waiting for transfers between devices, swap(): return lax.ppermute(part, 'narrow', [(0, 1), (1, 0)])  28 us
    pallas_call x1, Pallas kernels, attention_backward(): pl.pallas_call(lambda *refs: backward_kernel(tiles, *refs), grid=(tiles,)...  27.2 us
    unnamed x124, local copies, waits for them, and re-layouts  17.2 us
    ppermute x11, starting transfers between devices, swap(): return lax.ppermute(part, 'narrow', [(0, 1), (1, 0)])  16.7 us
  transfers between devices with their start and end apart: 17, of which 3 were waited for; matrix products, arithmetic and copies ran while one was open for 22% of the time, Pallas kernels for 57%

profile of v10, /device:TPU:0, one launch (start us, length us, event | category | flops | bytes accessed | tf_op | source)
XLA Modules:
  0.0 515.4 jit_solution(3225574748958144098)
XLA Ops:
  11.0 5.2 %fusion.72 = (bf16[2,576,1152]{2,1,0:T(8,128)(2,1)}, bf16[2,576,1152]{2,1,0:T(8,128)(2,1)}, bf16[2,576,1152]{2,1,0:T(8,128)(2,1)S(1)}) fusion(bf16[6,576,1152]{2,1,0:T(8,128)(2,1)} %bitcast.103), kind=kLoop, calls=%fused_computation.133 | loop fusion | bytes 15925248 | tf_op jit(solution)/shard_map/slice | solution.py:1190
  19.1 5.3 %slice.166 = bf16[4,576,1152]{2,1,0:T(8,128)(2,1)} slice(bf16[6,576,1152]{2,1,0:T(8,128)(2,1)} %bitcast.104), slice={[2:6], [0:576], [0:1152]} | slice | bytes 10616832 | tf_op jit(solution)/shard_map/slice | solution.py:989
  28.8 4.4 fusion.6
  34.9 14.3 %collective-permute-done.2 = bf16[576,256,2]{1,0,2:T(8,128)(2,1)} collective-permute-done((bf16[576,256,2]{1,0,2:T(8,128)(2,1)S(1)}, bf16[576,256,2]{1,0,2:T(8,128)(2,1)}, u32[]{:S(2)}, u32[]{:S(2)}) %collective-permute-start.2) | collective-permute-done | bytes 589856 | tf_op jit(solution)/shard_map/ppermute | solution.py:21
  55.6 13.2 %project.1 = (bf16[1024,576]{1,0:T(8,128)(2,1)}, bf16[1024,576]{1,0:T(8,128)(2,1)}, bf16[1024,576]{1,0:T(8,128)(2,1)}, bf16[1024,1152]{1,0:T(8,128)(2,1)}) custom-call(s32[1]{0:T(128)} %bitcast.5.refs_0_, bf16[512,1152]{1,0:T(8,128)(2,1)} %refs_1_.2, bf16[512,1152]{1,0:T(8,128)(2,1)} %collective-permute-done.refs_2_, s32[1024,1]{1,0:T(8,128)} %copy.48.refs_3_.ids, ...), custom_call_target="tpu_custom_call" | custom-call | flops 4076863488 | bytes 11289990 | tf_op jit(solution)/shard_map/project/pallas_call | solution.py:610
  74.9 4.6 collective-permute-done.1
  83.8 11.1 %attention_forward.1 = (bf16[1024,576]{1,0:T(8,128)(2,1)S(1)}, f32[8,1024]{1,0:T(8,128)S(1)}) custom-call(bf16[1024,576]{1,0:T(8,128)(2,1)S(1)} %copy-done.10, bf16[1024,576]{1,0:T(8,128)(2,1)S(1)} %copy-done.4, bf16[1024,576]{1,0:T(8,128)(2,1)S(1)} %copy-done.5, bf16[2,128,576]{2,1,0:T(8,128)(2,1)S(1)} %collective-permute-done.3.refs_3_, ...), custom_call_target="tpu_custom_call" | custom-call | flops 1207959552 | bytes 4718592 | tf_op jit(solution)/shard_map/attention_forward/pallas_call | solution.py:413
  115.5 9.0 %collective-permute-done.6.theirs.refs_9_ = bf16[512,1152]{1,0:T(8,128)(2,1)} collective-permute-done((bf16[512,1152]{1,0:T(8,128)(2,1)}, bf16[512,1152]{1,0:T(8,128)(2,1)}, u32[]{:S(2)}, u32[]{:S(2)}) %collective-permute-start.6) | collective-permute-done | bytes 1179680 | tf_op jit(solution)/shard_map/ppermute | solution.py:21
  124.6 22.9 %mlp.3 = (bf16[512,1152]{1,0:T(8,128)(2,1)}, bf16[512,2304]{1,0:T(8,128)(2,1)}, bf16[512,2304]{1,0:T(8,128)(2,1)}, bf16[512,1152]{1,0:T(8,128)(2,1)}, bf16[512,1...) custom-call(bf16[1024,1152]{1,0:T(8,128)(2,1)} %maximum_select_fusion.1.tokens.refs_0_, ...), custom_call_target="tpu_custom_call" | custom-call | flops 10871635968 | bytes 30103680 | tf_op jit(solution)/shard_map/mlp/pallas_call | solution.py:610
  151.0 23.1 %mlp.2 = (bf16[512,1152]{1,0:T(8,128)(2,1)}, bf16[512,2304]{1,0:T(8,128)(2,1)}, bf16[512,2304]{1,0:T(8,128)(2,1)}, bf16[512,1152]{1,0:T(8,128)(2,1)}, bf16[512,1...) custom-call(bf16[1024,1152]{1,0:T(8,128)(2,1)} %maximum_select_fusion.1.tokens.refs_0_, ...), custom_call_target="tpu_custom_call" | custom-call | flops 10871635968 | bytes 30103680 | tf_op jit(solution)/shard_map/mlp/pallas_call | solution.py:610
  176.4 9.1 %convolution_convert_fusion.1 = bf16[2304,1152]{1,0:T(8,128)(2,1)S(1)} fusion(bf16[512,2304]{1,0:T(8,128)(2,1)} %get-tuple-element.77, bf16[512,2304]{1,0:T(8,128)(2,1)} %get-tuple-element.76, bf16[512,1152]{1,0:T(8,128)(2,1)} %get-tuple-element.79, bf16[512,1152]{1,0:T(8,128)(2,1)} %get-tuple-element.78), kind=kOutput, calls=%fused_computation.1 | convolution fusion | flops 5452627968 | bytes 12386304 | tf_op jit(solution)/shard_map/dot_general | solution.py:17
  185.5 6.9 %convolution_convert_fusion = bf16[2304,1152]{1,0:T(8,128)(2,1)S(1)} fusion(bf16[512,2304]{1,0:T(8,128)(2,1)S(1)} %copy-done.57, bf16[512,2304]{1,0:T(8,128)(2,1)S(1)} %copy-done.58, bf16[512,1152]{1,0:T(8,128)(2,1)S(1)} %copy-done.59, bf16[512,1152]{1,0:T(8,128)(2,1)S(1)} %copy-done.60), kind=kOutput, calls=%fused_computation | convolution fusion | flops 5452627968 | bytes 12386304 | tf_op jit(solution)/shard_map/dot_general | solution.py:17
  192.4 58.4 %ring_scatter.1 = bf16[2,144,1152]{2,1,0:T(8,128)(2,1)S(1)} custom-call(bf16[8,2,144,1152]{3,2,1,0:T(8,128)(2,1)S(1)} %bitcast.97, bf16[8,2,144,1152]{3,2,1,0:T(8,128)(2,1)S(1)} %bitcast.98), custom_call_target="tpu_custom_call" | custom-call | tf_op jit(solution)/shard_map/ring_scatter/pallas_call | solution.py:278
  262.3 19.0 %middle_back.1 = (f32[1024,1152]{1,0:T(8,128)}, bf16[1024,576]{1,0:T(8,128)(2,1)}, bf16[576,1152]{1,0:T(8,128)(2,1)}, bf16[2,3,256,576]{3,2,1,0:T(8,128)(2,1)}, f32[1,1152]{1,0:T(1,128)}) custom-call(bf16[1024,1152]{1,0:T(8,128)(2,1)} %maximum_select_fusion.1.tokens.refs_0_, bf16[1024,1152]{1,0:T(8,128)(2,1)} %refs_1_.3, bf16[1024,576]{1,0:T(8,128)(2,1)} %copy-done.3, ...), custom_call_target="tpu_custom_call" | custom-call | flops 2717908992 | bytes 28554624 | tf_op jit(solution)/shard_map/middle_back/pallas_call | solution.py:610
  282.7 27.2 %attention_backward.1 = (bf16[1024,576]{1,0:T(8,128)(2,1)S(1)}, bf16[2,1024,576]{2,1,0:T(8,128)(2,1)}, bf16[2,2,128,576]{3,2,1,0:T(8,128)(2,1)S(1)}) custom-call(bf16[1024,576]{1,0:T(8,128)(2,1)S(1)} %copy-done.11, bf16[1024,576]{1,0:T(8,128)(2,1)S(1)} %copy-done.4, bf16[1024,576]{1,0:T(8,128)(2,1)} %get-tuple-element.70.refs_2_, ...), custom_call_target="tpu_custom_call" | custom-call | flops 3019898880 | bytes 9437184 | tf_op jit(solution)/shard_map/attention_backward/pallas_call | solution.py:514
  316.4 5.2 %fusion.22 = bf16[512,1152]{1,0:T(8,128)(2,1)} fusion(bf16[512,1152]{1,0:T(8,128)(2,1)S(1)} %copy-done.14, bf16[512,1152]{1,0:T(8,128)(2,1)} %collective-permute-done.7, f32[512,1152]{1,0:T(8,128)S(1)} %copy-done.26, f32[1152]{0:T(1024)S(1)} %copy-done.47, bf16[512,1152]{1,0:T(8,128)(2,1)S(1)} %copy-done.35, bf16[512,1152]{1,0:T(8,128)(2,1)S(1)} %copy-done.33, ...), kind=kOutput, calls=%fused_computation.37 | convolution fusion | flops 312606720 | bytes 13715461 | tf_op jit(solution)/shard_map/dot_general | solution.py:17
  323.4 15.0 %project_back.1 = (bf16[1024,1152]{1,0:T(8,128)(2,1)}, bf16[2,1024,576]{2,1,0:T(8,128)(2,1)}, bf16[2,256,1152]{2,1,0:T(8,128)(2,1)}) custom-call(bf16[1024,1152]{1,0:T(8,128)(2,1)} %maximum_select_fusion.1.tokens.refs_0_, bf16[1024,576]{1,0:T(8,128)(2,1)} %copy-done.12, bf16[2,1024,576]{2,1,0:T(8,128)(2,1)} %get-tuple-element.91.refs_2_, ...), custom_call_target="tpu_custom_call" | custom-call | flops 4076863488 | bytes 15710214 | tf_op jit(solution)/shard_map/project_back/pallas_call | solution.py:610
  342.0 10.0 %qkv_grads.1 = (bf16[1536,1152]{1,0:T(8,128)(2,1)}, bf16[192,1152]{1,0:T(8,128)(2,1)}, f32[2,576]{1,0:T(2,128)}) custom-call(bf16[1024,1152]{1,0:T(8,128)(2,1)} %get-tuple-element.94.refs_0_, bf16[1024,576]{1,0:T(8,128)(2,1)} %copy-done.12, bf16[2,1024,576]{2,1,0:T(8,128)(2,1)} %get-tuple-element.95.refs_2_), custom_call_target="tpu_custom_call" | custom-call | flops 4076863488 | bytes 8847360 | tf_op jit(solution)/shard_map/qkv_grads/pallas_call | solution.py:610
  358.2 93.4 %ring_sum.1 = (bf16[2,8,2,96,1152]{4,3,2,1,0:T(8,128)(2,1)}, bf16[512,1152]{1,0:T(8,128)(2,1)S(1)}, f32[8,2304]{1,0:T(8,128)S(1)}) custom-call(bf16[8,2,96,1152]{3,2,1,0:T(8,128)(2,1)S(1)} %bitcast.100, bf16[8,2,96,1152]{3,2,1,0:T(8,128)(2,1)S(1)} %bitcast.99, bf16[1024,1152]{1,0:T(8,128)(2,1)S(1)} %copy-done.2, f32[8,2304]{1,0:T(8,128)S(1)} %concatenate.59.refs_3_), custom_call_target="tpu_custom_call" | custom-call | tf_op jit(solution)/shard_map/ring_sum/pallas_call | solution.py:298
  456.7 5.5 %widened.1 = (f32[1728,1152]{1,0:T(8,128)}, f32[576,1152]{1,0:T(8,128)}) custom-call(bf16[3072,1152]{1,0:T(8,128)(2,1)S(1)} %bitcast.93), custom_call_target="tpu_custom_call" | custom-call | tf_op jit(solution)/shard_map/widened/pallas_call | solution.py:931
  478.4 4.0 fusion.20
  482.4 8.4 %fusion.53 = f32[1152,6,576]{0,2,1:T(8,128)} fusion(bf16[6,576,256]{2,1,0:T(8,128)(2,1)S(1)} %bitcast.110, bf16[256,1152]{1,0:T(8,128)(2,1)S(1)} %copy-done.37), kind=kOutput, calls=%fused_computation.87 | convolution fusion | flops 2040201216 | bytes 18284544 | tf_op jit(solution)/shard_map/dot_general | solution.py:1184
  493.1 7.9 %turned.1 = f32[1152,2304]{1,0:T(8,128)} custom-call(bf16[2304,1152]{1,0:T(8,128)(2,1)} %bitcast.112), custom_call_target="tpu_custom_call" | custom-call | tf_op jit(solution)/shard_map/turned/pallas_call | solution.py:904
  501.1 7.3 %bitcast_convert_fusion = f32[2304,1152]{1,0:T(8,128)} fusion(bf16[1,2304,1152]{2,1,0:T(8,128)(2,1)} %all-gather.7.cloned.1.call-done), kind=kLoop, calls=%fused_computation.2 | loop fusion | flops 2654208 | bytes 15925248 | tf_op jit(solution)/shard_map/convert_element_type | solution.py:1171
  (235 shorter events, 108.0 us)
Async XLA Ops:
  7.2 486.0 %all-gather.5.cloned.1.call-start = ((), (), s32[]{:S(2)}) async-start(), calls=%async_computation | async-start | bytes 5640192 | tf_op jit(solution)/shard_map/all_gather | solution.py:1083
  7.2 43.3 %collective-permute-start = (bf16[512,1152]{1,0:T(8,128)(2,1)}, bf16[512,1152]{1,0:T(8,128)(2,1)}, u32[]{:S(2)}, u32[]{:S(2)}) collective-permute-start(bf16[512,1152]{1,0:T(8,128)(2,1)} %refs_1_.2), channel_id=1, source_target_pairs={{0,1},{1,0},{2,3},{3,2},{4,5},{5,4},{6,7},{7,6},{8,9},{9,8},{10,11... | collective-permute-start | bytes 3538952 | tf_op jit(solution)/shard_map/ppermute | solution.py:21
  19.0 30.1 %collective-permute-start.2 = (bf16[576,256,2]{1,0,2:T(8,128)(2,1)S(1)}, bf16[576,256,2]{1,0,2:T(8,128)(2,1)}, u32[]{:S(2)}, u32[]{:S(2)}) collective-permute-start(bf16[576,256,2]{1,0,2:T(8,128)(2,1)S(1)} %bitcast.118), channel_id=1, source_target_pairs={{0,1},{1,0},{2,3},{3,2},{4,5},{5,4},{6,7},{7,6},{8,9},{9,8},{10,11... | collective-permute-start | bytes 1769480 | tf_op jit(solution)/shard_map/ppermute | solution.py:21
  27.8 227.9 %copy-start.42 = (s32[1024]{0:T(1024)}, s32[1024]{0:T(1024)S(1)}, u32[]{:S(2)}) copy-start(s32[1024]{0:T(1024)S(1)} %get-tuple-element.120) | copy-start | bytes 12292
  52.0 27.4 %collective-permute-start.1 = (bf16[576,256,4]{1,0,2:T(8,128)(2,1)}, bf16[576,256,4]{1,0,2:T(8,128)(2,1)}, u32[]{:S(2)}, u32[]{:S(2)}) collective-permute-start(bf16[576,256,4]{1,0,2:T(8,128)(2,1)} %copy.42), channel_id=1, source_target_pairs={{0,1},{1,0},{2,3},{3,2},{4,5},{5,4},{6,7},{7,6},{8,9},{9,8},{10,11... | collective-permute-start | bytes 3538952 | tf_op jit(solution)/shard_map/ppermute | solution.py:21
  70.2 9.2 %collective-permute-start.3 = (bf16[2,128,576]{2,1,0:T(8,128)(2,1)S(1)}, bf16[2,128,576]{2,1,0:T(8,128)(2,1)S(1)}, u32[]{:S(2)}, u32[]{:S(2)}) collective-permute-start(bf16[2,128,576]{2,1,0:T(8,128)(2,1)S(1)} %pad_maximum_fusion.1), channel_id=1, source_target_pairs={{0,2},{2,4},{4,6},{6,8},{8,10},{10,12},{12,14},{14,16},{16,18},{18... | collective-permute-start | bytes 884744 | tf_op jit(solution)/shard_map/ppermute | solution.py:1014
  71.6 7.8 %collective-permute-start.4 = (bf16[2,128,576]{2,1,0:T(8,128)(2,1)S(1)}, bf16[2,128,576]{2,1,0:T(8,128)(2,1)S(1)}, u32[]{:S(2)}, u32[]{:S(2)}) collective-permute-start(bf16[2,128,576]{2,1,0:T(8,128)(2,1)S(1)} %pad_maximum_fusion.2), channel_id=1, source_target_pairs={{2,0},{4,2},{6,4},{8,6},{10,8},{12,10},{14,12},{16,14},{18,16},{20... | collective-permute-start | bytes 884744 | tf_op jit(solution)/shard_map/ppermute | solution.py:1017
  97.3 27.3 %collective-permute-start.6 = (bf16[512,1152]{1,0:T(8,128)(2,1)}, bf16[512,1152]{1,0:T(8,128)(2,1)}, u32[]{:S(2)}, u32[]{:S(2)}) collective-permute-start(bf16[512,1152]{1,0:T(8,128)(2,1)} %convolution_convert_fusion.2.mine.refs_7_), channel_id=1, source_target_pairs={{0,1},{1,0},{2,3},{3,2},{4,5},{5,4},{6,7},{7,6},{8,9},{9,8},{10,11... | collective-permute-start | bytes 3538952 | tf_op jit(solution)/shard_map/ppermute | solution.py:21
  111.4 38.5 %collective-permute-start.5 = (bf16[512,1152]{1,0:T(8,128)(2,1)}, bf16[512,1152]{1,0:T(8,128)(2,1)S(1)}, u32[]{:S(2)}, u32[]{:S(2)}) collective-permute-start(bf16[512,1152]{1,0:T(8,128)(2,1)} %convolution_convert_fusion.3.mine.refs_6_), channel_id=1, source_target_pairs={{0,1},{1,0},{2,3},{3,2},{4,5},{5,4},{6,7},{7,6},{8,9},{9,8},{10,11... | collective-permute-start | bytes 3538952 | tf_op jit(solution)/shard_map/ppermute | solution.py:21
  147.5 103.4 %collective-permute-start.9 = (bf16[512,1152]{1,0:T(8,128)(2,1)}, bf16[512,1152]{1,0:T(8,128)(2,1)}, u32[]{:S(2)}, u32[]{:S(2)}) collective-permute-start(bf16[512,1152]{1,0:T(8,128)(2,1)} %get-tuple-element.75.refs_11_), channel_id=1, source_target_pairs={{0,1},{1,0},{2,3},{3,2},{4,5},{5,4},{6,7},{7,6},{8,9},{9,8},{10,11... | collective-permute-start | bytes 3538952 | tf_op jit(solution)/shard_map/ppermute | solution.py:21
  174.1 76.8 %collective-permute-start.8 = (bf16[512,1152]{1,0:T(8,128)(2,1)}, bf16[512,1152]{1,0:T(8,128)(2,1)S(1)}, u32[]{:S(2)}, u32[]{:S(2)}) collective-permute-start(bf16[512,1152]{1,0:T(8,128)(2,1)} %get-tuple-element.74.refs_10_), channel_id=1, source_target_pairs={{0,1},{1,0},{2,3},{3,2},{4,5},{5,4},{6,7},{7,6},{8,9},{9,8},{10,11... | collective-permute-start | bytes 3538952 | tf_op jit(solution)/shard_map/ppermute | solution.py:21
  252.2 248.9 %all-gather.7.cloned.1.call-start = ((), (), s32[]{:S(2)}) async-start(), calls=%async_computation.1 | async-start | bytes 5640192 | tf_op jit(solution)/shard_map/all_gather | solution.py:1083
  260.8 55.2 %collective-permute-start.7 = (bf16[512,1152]{1,0:T(8,128)(2,1)}, bf16[512,1152]{1,0:T(8,128)(2,1)}, u32[]{:S(2)}, u32[]{:S(2)}) collective-permute-start(bf16[512,1152]{1,0:T(8,128)(2,1)} %broadcast_select_fusion), channel_id=1, source_target_pairs={{0,1},{1,0},{2,3},{3,2},{4,5},{5,4},{6,7},{7,6},{8,9},{9,8},{10,11... | collective-permute-start | bytes 3538952 | tf_op jit(solution)/shard_map/ppermute | solution.py:21
  262.3 19.0 %copy-start.9 = (bf16[2,128,576]{2,1,0:T(8,128)(2,1)S(1)}, bf16[2,128,576]{2,1,0:T(8,128)(2,1)}, u32[]{:S(2)}) copy-start(bf16[2,128,576]{2,1,0:T(8,128)(2,1)} %copy-done.7) | copy-start | bytes 884740
  282.7 30.7 %copy-start.25 = (bf16[1024,1152]{1,0:T(8,128)(2,1)S(1)}, bf16[1024,1152]{1,0:T(8,128)(2,1)}, u32[]{:S(2)}) copy-start(bf16[1024,1152]{1,0:T(8,128)(2,1)} %refs_1_.3) | copy-start | bytes 7077892
  282.7 30.8 %copy-start.35 = (bf16[512,1152]{1,0:T(8,128)(2,1)S(1)}, bf16[512,1152]{1,0:T(8,128)(2,1)}, u32[]{:S(2)}) copy-start(bf16[512,1152]{1,0:T(8,128)(2,1)} %get-tuple-element.101) | copy-start | bytes 3538948
  282.7 30.8 %copy-start.39 = (pred[1024,256]{1,0:T(32,128)(4,1)S(1)}, pred[1024,256]{1,0:T(32,128)(4,1)}, u32[]{:S(2)}) copy-start(pred[1024,256]{1,0:T(32,128)(4,1)} %copy-done.38) | copy-start | bytes 786436
  282.7 30.8 %copy-start.48 = (f32[1152]{0:T(1024)S(1)}, f32[1152]{0:T(1024)}, u32[]{:S(2)}) copy-start(f32[1152]{0:T(1024)} %broadcast_select_fusion.1) | copy-start | bytes 13828
  282.7 30.8 %copy-start.55 = (f32[512]{0:T(512)S(1)}, f32[512]{0:T(512)}, u32[]{:S(2)}) copy-start(f32[512]{0:T(512)} %get-tuple-element.140) | copy-start | bytes 6148
  310.0 12.5 %collective-permute-start.10 = (bf16[2,128,576]{2,1,0:T(8,128)(2,1)S(1)}, bf16[2,128,576]{2,1,0:T(8,128)(2,1)S(1)}, u32[]{:S(2)}, u32[]{:S(2)}) collective-permute-start(bf16[2,128,576]{2,1,0:T(8,128)(2,1)S(1)} %get-tuple-element.133), channel_id=1, source_target_pairs={{0,2},{2,4},{4,6},{6,8},{8,10},{10,12},{12,14},{14,16},{16,18},{18... | collective-permute-start | bytes 884744 | tf_op jit(solution)/shard_map/ppermute | solution.py:1014
  312.1 10.3 %collective-permute-start.11 = (bf16[2,128,576]{2,1,0:T(8,128)(2,1)S(1)}, bf16[2,128,576]{2,1,0:T(8,128)(2,1)S(1)}, u32[]{:S(2)}, u32[]{:S(2)}) collective-permute-start(bf16[2,128,576]{2,1,0:T(8,128)(2,1)S(1)} %get-tuple-element.134), channel_id=1, source_target_pairs={{2,0},{4,2},{6,4},{8,6},{10,8},{12,10},{14,12},{16,14},{18,16},{20... | collective-permute-start | bytes 884744 | tf_op jit(solution)/shard_map/ppermute | solution.py:1017
  315.3 26.5 %collective-permute-start.13 = (bf16[256,576]{1,0:T(8,128)(2,1)S(1)}, bf16[256,576]{1,0:T(8,128)(2,1)S(1)}, u32[]{:S(2)}, u32[]{:S(2)}) collective-permute-start(bf16[256,576]{1,0:T(8,128)(2,1)S(1)} %constant_dynamic-slice_fusion), channel_id=1, source_target_pairs={{0,1},{1,0},{2,3},{3,2},{4,5},{5,4},{6,7},{7,6},{8,9},{9,8},{10,11... | collective-permute-start | bytes 884744 | tf_op jit(solution)/shard_map/ppermute | solution.py:21
  340.3 15.3 %collective-permute-start.12 = (bf16[256,1152]{1,0:T(8,128)(2,1)}, bf16[256,1152]{1,0:T(8,128)(2,1)}, u32[]{:S(2)}, u32[]{:S(2)}) collective-permute-start(bf16[256,1152]{1,0:T(8,128)(2,1)} %dynamic-slice_bitcast_fusion), channel_id=1, source_target_pairs={{0,1},{1,0},{2,3},{3,2},{4,5},{5,4},{6,7},{7,6},{8,9},{9,8},{10,11... | collective-permute-start | bytes 1769480 | tf_op jit(solution)/shard_map/ppermute | solution.py:21
  467.8 23.0 %collective-permute-start.14 = (bf16[256,1152]{1,0:T(8,128)(2,1)}, bf16[256,1152]{1,0:T(8,128)(2,1)}, u32[]{:S(2)}, u32[]{:S(2)}) collective-permute-start(bf16[256,1152]{1,0:T(8,128)(2,1)} %fusion.15), channel_id=1, source_target_pairs={{0,1},{1,0},{2,3},{3,2},{4,5},{5,4},{6,7},{7,6},{8,9},{9,8},{10,11... | collective-permute-start | bytes 1769480 | tf_op jit(solution)/shard_map/ppermute | solution.py:21
  (54 other events, 260.5 us)
Sparse Core Ops, SparseCore 0:
  252.3 55.4 all-gather.4
  310.0 56.1 all-gather.6
